TPU v7x, 512 devices: a whole 4x4x16 slice. The times are simulated.
512 devices in a mesh: tm: 256 (over z, y, x), state: 2 (over core).
Axes of the slice: x: 4, y: 4, z: 16, core: 2. Of those that a mesh axis runs over, the one named last changes fastest.
Arguments:
- record: bfloat16 [32768, 4096], P('tm', 'state'), may hold values from -24 to 24
- gain: bfloat16 [2, 256, 4096], P(None, 'state'), may hold values from -0.0625 to 0.0625
- rate: float32 [256, 32768], P('state', 'tm'), as said below
- leak: float32 [256], P('state'), may hold values from 1.5258789e-05 to 0.05
- dilation: int32 [2], replicated, may hold values from 0 to 64, as said below
Outputs:
- smoothed: float32 [256, 32768], P('state', 'tm')
- grad: float32 [4096, 512], P(('state', 'tm'))
Inputs may be any that keep to these rules, and one draw needn't show every extreme that they name: `dilation`: delays of the taps; the largest of them equals 64. `rate`: positive rates.
All inputs are finite; a program needn't handle non-finite values.
Results may differ from a plain program's by a relative error of at most 0.0014.
Values may be sent and summed in bfloat16 or wider, within the bound.
No kernel may reach another device: no remote copies, remote signals or barrier semaphores. Data moves between devices by JAX's collectives and lax.ppermute only.
A program may use at most 64 MiB of HBM per device.

v0:
```python
import jax
import jax.numpy as jnp
from jax import lax
from jax.sharding import Mesh
from jax.sharding import PartitionSpec as P

TAPS = 2
DMAX = 64
TM = ("tm_0", "tm_1", "tm_2")
STATE_TM = ("state", "tm_0", "tm_1", "tm_2")


def from_behind(x, axis, by):
    peers = lax.axis_size(axis)
    pairs = [(i, i + by) for i in range(peers) if 0 <= i + by < peers]
    return lax.ppermute(x, axis, pairs)


def copy_for_each(x, axis):
    copies = jnp.broadcast_to(x, (lax.axis_size(axis), *x.shape))
    return lax.all_to_all(copies, axis, split_axis=0, concat_axis=0, tiled=True)


def of_everyone(x, axis):
    everything = copy_for_each(x, axis)
    return jnp.sum(everything, axis=0)


def laid_out(blocks, dim):
    blocks = jnp.moveaxis(blocks, 0, dim)
    lengths = blocks.shape
    return blocks.reshape(*lengths[:dim], lengths[dim] * lengths[dim + 1], *lengths[dim + 2 :])


def gathered_by_axis(x, axes, dim):
    far, near = axes
    blocks = copy_for_each(copy_for_each(x, far), near)
    return laid_out(blocks.swapaxes(0, 1).reshape(-1, *x.shape), dim)


def in_one_piece(arrays, axis, dim, along):
    widths = [a.shape[along] for a in arrays]
    both = jnp.concatenate(arrays, axis=along)
    whole = gathered_by_axis(both, axis, dim)
    return tuple(jnp.split(whole, [sum(widths[:k]) for k in range(1, len(widths))], axis=along))


def gather_directly(x, axis, dim):
    return laid_out(copy_for_each(x, axis), dim)


def in_blocks(x, dim, peers):
    lengths = x.shape
    blocks = x.reshape(*lengths[:dim], peers, lengths[dim] // peers, *lengths[dim + 1 :])
    return jnp.moveaxis(blocks, dim, 0)


def summed_on_arrival(x, axis, dim):
    peers = lax.axis_size(axis)
    blocks = lax.all_to_all(in_blocks(x, dim, peers), axis, 0, 0, tiled=True)
    return jnp.sum(blocks, axis=0)


def sum_by_axis(x, axes, dim):
    far, near = axes
    own = summed_on_arrival(in_blocks(x, dim, lax.axis_size(far)), near, dim + 1)
    return jnp.sum(lax.all_to_all(own, far, 0, 0, tiled=True), axis=0)


def affine(first, second):
    return (first[0] * second[0], second[0] * first[1] + second[1])


def entry_from_all(pair, backward, position, count):
    inclusive = lax.associative_scan(affine, pair, reverse=backward, axis=0)
    if backward:
        pick = position + 1
        valid = position < count - 1
    else:
        pick = position - 1
        valid = position > 0
    safe = jnp.clip(pick, 0, count - 1)
    value = lax.dynamic_index_in_dim(inclusive[1], safe, 0, keepdims=False)
    return jnp.where(valid, value, 0.0)


def running_sum(values, triangle):
    return jnp.dot(
        values, triangle, precision=lax.Precision.HIGHEST, preferred_element_type=jnp.float32
    )


def block_recursion(log_sums, inputs, keep):
    differ = jnp.where(keep[None], log_sums[:, :, None] - log_sums[:, None, :], 0.0)
    kernel = jnp.where(keep[None], jnp.exp(-jnp.abs(differ)), 0.0)
    return jnp.einsum(
        "hts,hs->ht",
        kernel,
        inputs,
        precision=lax.Precision.HIGHEST,
        preferred_element_type=jnp.float32,
    )


def per_device(record, gain, rate, leak, dilation):
    frames = record.shape[0]
    tail = record[frames - DMAX :]
    rim_rows = from_behind(tail, TM, 1)
    local_rows = jnp.concatenate([rim_rows, record], 0)
    local_taps = [
        lax.dynamic_slice_in_dim(local_rows, DMAX - dilation[k], frames, 0) for k in range(TAPS)
    ]
    gain_cols = lax.all_to_all(gain, "state", split_axis=2, concat_axis=1, tiled=True)
    local_view = jnp.stack(local_taps, 1)
    partial_drive = jnp.einsum(
        "lky,khy->hl", local_view, gain_cols, preferred_element_type=jnp.float32
    )
    total_drive = of_everyone(partial_drive, "state")
    own_modes = gain.shape[1]
    drive_in = lax.dynamic_slice_in_dim(
        total_drive, lax.axis_index("state") * own_modes, own_modes, 0
    )
    decay = jnp.exp(-rate)
    scale = jnp.sqrt(-jnp.expm1(-2.0 * rate))
    drive = scale * drive_in
    position = lax.axis_index(TM)
    count = lax.axis_size(TM)
    steps_idx = lax.iota(jnp.int32, frames)
    upper_incl = (steps_idx[:, None] <= steps_idx[None, :]).astype(jnp.float32)
    upper_excl = (steps_idx[:, None] < steps_idx[None, :]).astype(jnp.float32)
    lower_keep = steps_idx[:, None] >= steps_idx[None, :]
    upper_keep = steps_idx[:, None] <= steps_idx[None, :]
    rate_sums = running_sum(rate, upper_incl)
    offsets = block_recursion(rate_sums, drive, lower_keep)
    prods = jnp.exp(-rate_sums)
    summary = (prods[:, -1], offsets[:, -1])
    every = in_one_piece((summary[0][None], summary[1][None]), (("tm_0", "tm_1"), "tm_2"), 0, 1)
    entering = entry_from_all(every, False, position, count)
    filtered = prods * entering[:, None] + offsets
    kappa = 1.0 - leak
    weight = (1.0 - kappa[:, None] * decay * decay) * filtered
    link_rate = rate - jnp.log(kappa)[:, None]
    link_sums = running_sum(link_rate, upper_excl)
    weights = block_recursion(link_sums, weight, upper_keep)
    link_total = link_sums[:, -1:] + link_rate[:, -1:]
    links = jnp.exp(-(link_total - link_sums))
    closing = (links[:, 0], weights[:, 0])
    every_back = in_one_piece(
        (closing[0][None], closing[1][None]), (("tm_0", "tm_1"), "tm_2"), 0, 1
    )
    after = entry_from_all(every_back, True, position, count)
    smoothed = links * after[:, None] + weights
    prior = from_behind(smoothed[:, -1:], TM, 1)
    shifted = jnp.concatenate([prior, smoothed[:, :-1]], 1)
    resid = (smoothed - decay * shifted - drive).astype(jnp.bfloat16)
    resid_all = gather_directly(resid, "state", 0)
    pieces = []
    for k in range(TAPS):
        columns = local_taps[k]
        pieces.append(
            lax.dot_general(
                columns, resid_all, (((0,), (1,)), ((), ())), preferred_element_type=jnp.float32
            )
        )
    grad = sum_by_axis(jnp.concatenate(pieces, 1), (("tm_0", "tm_1"), "tm_2"), 0)
    return (smoothed, grad)


def solution(mesh):
    split = Mesh(
        mesh.devices.reshape(16, 4, 4, mesh.shape["state"]), ("tm_0", "tm_1", "tm_2", "state")
    )
    return jax.shard_map(
        per_device,
        mesh=split,
        in_specs=(P(TM, "state"), P(None, "state", None), P("state", TM), P("state"), P()),
        out_specs=(P("state", TM), P(STATE_TM, None)),
        check_vma=False,
    )
```

profile of v0, /device:TPU:1, one launch (start us, length us, event | category | flops | bytes accessed | tf_op | source)
XLA Modules:
  0.0 257.8 jit_solution(2452550016362452787)
XLA Ops:
  0.6 1.0 slice.424
  1.6 4.1 %collective-permute-start = (bf16[64,2048]{1,0:T(8,128)(2,1)S(1)}, bf16[64,2048]{1,0:T(8,128)(2,1)S(1)}, u32[]{:S(2)}, u32[]{:S(2)}) collective-permute-start(bf16[64,2048]{1,0:T(8,128)(2,1)S(1)} %slice.424), channel_id=1, source_target_pairs={{0,2},{2,4},{4,6},{6,8},{8,10},{10,12},{12,14},{14,16},{16,18},{18... | collective-permute-start | bytes 786440 | tf_op jit(solution)/shard_map/ppermute | solution.py:16
  5.7 6.2 %copy.67 = bf16[2,128,4096]{1,0,2:T(2,128)(2,1)} copy(bf16[2,128,4096]{2,1,0:T(8,128)(2,1)} %param.6) | data formatting | bytes 4194304 | tf_op args[1]
  11.9 8.1 %all-to-all-start = ((bf16[2,128,4096]{1,0,2:T(2,128)(2,1)}), bf16[2,128,4096]{1,0,2:T(2,128)(2,1)S(1)}, u32[]{:S(2)}, u32[]{:S(2)}) async-start(bf16[2,128,4096]{1,0,2:T(2,128)(2,1)} %copy.67), calls=%async_computation | async-start | bytes 4194304 | tf_op jit(solution)/shard_map/all_to_all | solution.py:113
  20.0 0.6 fusion.48
  23.6 3.9 %copy.68 = bf16[2,128,2,2048]{3,1,2,0:T(8,128)(2,1)} copy(bf16[2,128,2,2048]{1,0,3,2:T(2,128)(2,1)S(1)} %bitcast.61) | data formatting | bytes 4194304 | tf_op jit(solution)/shard_map/all_to_all | solution.py:113
  27.9 2.4 convolution_bitcast_fusion
  30.5 3.6 %all_to_all.64 = f32[2,256,128]{2,1,0:T(8,128)S(1)} all-to-all(f32[2,256,128]{2,1,0:T(8,128)S(1)} %broadcast_in_dim.76), channel_id=1, replica_groups=mesh['tm_0'=16,'tm_1'=4,'tm_2'=4,'state'=2] {'state'}, dimensions={0} | all-to-all | bytes 524288 | tf_op jit(solution)/shard_map/all_to_all | solution.py:21
  34.4 4.7 %multiply_reduce_fusion.1 = f32[128,128]{1,0:T(8,128)S(1)} fusion(f32[128,128]{1,0:T(8,128)S(1)} %copy.91, f32[128,128]{1,0:T(8,128)S(1)} %copy.64, pred[128,128]{1,0:T(8,128)(4,1)S(1)} %iota_compare_fusion), kind=kLoop, calls=%fused_computation.1 | loop fusion | flops 14663680 | bytes 212992
  39.2 0.7 broadcast_in_dim.77
  39.9 15.2 %all-to-all-start.2 = ((f32[64,1,256]{2,1,0:T(1,128)}), f32[64,1,256]{2,1,0:T(1,128)S(1)}, u32[]{:S(2)}, u32[]{:S(2)}) async-start(f32[64,1,256]{2,1,0:T(1,128)} %broadcast_in_dim.77), calls=%async_computation.2 | async-start | bytes 131072 | tf_op jit(solution)/shard_map/all_to_all | solution.py:21
  55.1 14.0 %all-to-all-done.2 = f32[64,1,256]{2,1,0:T(1,128)S(1)} async-done(((f32[64,1,256]{2,1,0:T(1,128)}), f32[64,1,256]{2,1,0:T(1,128)S(1)}, u32[]{:S(2)}, u32[]{:S(2)}) %all-to-all-start.2) | async-done | bytes 65568 | tf_op jit(solution)/shard_map/all_to_all | solution.py:21
  69.1 0.7 broadcast_in_dim.78
  69.8 3.7 %all-to-all-start.3 = ((f32[4,64,1,256]{3,1,2,0:T(8,128)}), f32[4,64,1,256]{3,1,2,0:T(8,128)S(1)}, u32[]{:S(2)}, u32[]{:S(2)}) async-start(f32[4,64,1,256]{3,1,2,0:T(8,128)} %broadcast_in_dim.78), calls=%async_computation.3 | async-start | bytes 524288 | tf_op jit(solution)/shard_map/all_to_all | solution.py:21
  73.5 5.5 %all-to-all-done.3 = f32[4,64,1,256]{3,1,2,0:T(8,128)S(1)} async-done(((f32[4,64,1,256]{3,1,2,0:T(8,128)}), f32[4,64,1,256]{3,1,2,0:T(8,128)S(1)}, u32[]{:S(2)}, u32[]{:S(2)}) %all-to-all-start.3) | async-done | bytes 262176 | tf_op jit(solution)/shard_map/all_to_all | solution.py:21
  81.3 4.7 %multiply_reduce_fusion = f32[128,128]{1,0:T(8,128)S(1)} fusion(f32[128,128]{1,0:T(8,128)S(1)} %copy.92, f32[128,128]{1,0:T(8,128)S(1)} %copy.61, pred[128,128]{1,0:T(8,128)(4,1)S(1)} %iota_compare_fusion.1), kind=kLoop, calls=%fused_computation | loop fusion | flops 14663680 | bytes 212992
  86.2 18.5 %all_to_all.65 = f32[64,1,256]{2,1,0:T(1,128)S(1)} all-to-all(f32[64,1,256]{2,1,0:T(1,128)S(1)} %broadcast_in_dim.80), channel_id=1, replica_groups=mesh['tm_0'=16,'tm_1'=4,'tm_2'=4,'state'=2] {'tm_0','tm_1'}, dimensions={0} | all-to-all | bytes 131072 | tf_op jit(solution)/shard_map/all_to_all | solution.py:21
  104.7 0.7 broadcast_in_dim.81
  105.4 3.4 %all-to-all-start.5 = ((f32[4,64,1,256]{3,1,2,0:T(8,128)}), f32[4,64,1,256]{3,1,2,0:T(8,128)S(1)}, u32[]{:S(2)}, u32[]{:S(2)}) async-start(f32[4,64,1,256]{3,1,2,0:T(8,128)} %broadcast_in_dim.81), calls=%async_computation.5 | async-start | bytes 524288 | tf_op jit(solution)/shard_map/all_to_all | solution.py:21
  108.8 5.5 %all-to-all-done.5 = f32[4,64,1,256]{3,1,2,0:T(8,128)S(1)} async-done(((f32[4,64,1,256]{3,1,2,0:T(8,128)}), f32[4,64,1,256]{3,1,2,0:T(8,128)S(1)}, u32[]{:S(2)}, u32[]{:S(2)}) %all-to-all-start.5) | async-done | bytes 262176 | tf_op jit(solution)/shard_map/all_to_all | solution.py:21
  116.4 2.2 collective-permute-start.1
  118.6 0.7 collective-permute-done.1
  119.5 9.4 %all_to_all.66 = bf16[2,128,128]{2,1,0:T(8,128)(2,1)S(1)} all-to-all(bf16[2,128,128]{2,1,0:T(8,128)(2,1)S(1)} %broadcast_in_dim.82), channel_id=1, replica_groups=mesh['tm_0'=16,'tm_1'=4,'tm_2'=4,'state'=2] {'state'}, dimensions={0} | all-to-all | bytes 131072 | tf_op jit(solution)/shard_map/all_to_all | solution.py:21
  129.8 2.4 pad_maximum_fusion
  132.2 5.4 %copy.74 = f32[2048,512]{1,0:T(8,128)} copy(f32[2048,512]{0,1:T(8,128)} %pad_maximum_fusion) | data formatting | bytes 8388608 | tf_op jit(solution)/shard_map/concatenate | solution.py:165
  137.7 2.8 %copy.75 = f32[4,64,8,512]{3,2,1,0:T(8,128)S(1)} copy(f32[4,64,8,512]{3,2,0,1:T(8,128)} %bitcast.60) | data formatting | bytes 8388608 | tf_op jit(solution)/shard_map/transpose | solution.py:55
  140.4 51.7 %all_to_all.67 = f32[4,64,8,512]{3,2,1,0:T(8,128)} all-to-all(f32[4,64,8,512]{3,2,1,0:T(8,128)S(1)} %copy.75), channel_id=1, replica_groups=mesh['tm_0'=16,'tm_1'=4,'tm_2'=4,'state'=2] {'tm_2'}, dimensions={0} | all-to-all | bytes 8388608 | tf_op jit(solution)/shard_map/all_to_all | solution.py:60
  192.2 3.8 %reduce_sum.28 = f32[64,8,512]{2,1,0:T(8,128)} reduce(f32[4,64,8,512]{3,2,1,0:T(8,128)} %all_to_all.67, f32[]{:T(128)} %constant.49.clone.1), dimensions={0}, to_apply=%region_1.2 | reduce | flops 786432 | bytes 5242884 | tf_op jit(solution)/shard_map/reduce_sum | solution.py:61
  195.9 10.3 %all-to-all-start.8 = ((f32[64,8,512]{2,1,0:T(8,128)}), f32[64,8,512]{2,1,0:T(8,128)S(1)}, u32[]{:S(2)}, u32[]{:S(2)}) async-start(f32[64,8,512]{2,1,0:T(8,128)} %reduce_sum.28), calls=%async_computation.8 | async-start | bytes 2097152 | tf_op jit(solution)/shard_map/all_to_all | solution.py:67
  206.2 0.7 copy.76
  207.0 50.1 %all-to-all-done.8 = f32[64,8,512]{2,1,0:T(8,128)S(1)} async-done(((f32[64,8,512]{2,1,0:T(8,128)}), f32[64,8,512]{2,1,0:T(8,128)S(1)}, u32[]{:S(2)}, u32[]{:S(2)}) %all-to-all-start.8) | async-done | bytes 1048608 | tf_op jit(solution)/shard_map/all_to_all | solution.py:67
  257.1 0.7 reduce_sum.29
  (243 shorter events, 5.8 us)
Async XLA Ops:
  1.6 18.4 %copy-start.2 = (s32[2]{0:T(128)S(1)}, s32[2]{0:T(128)}, u32[]{:S(2)}) copy-start(s32[2]{0:T(128)} %param.9) | copy-start | bytes 28
  1.6 21.6 %copy-start.1 = (f32[128,128]{1,0:T(8,128)S(1)}, f32[128,128]{1,0:T(8,128)}, u32[]{:S(2)}) copy-start(f32[128,128]{1,0:T(8,128)} %param.7) | copy-start | bytes 196612
  1.6 25.9 %collective-permute-start = (bf16[64,2048]{1,0:T(8,128)(2,1)S(1)}, bf16[64,2048]{1,0:T(8,128)(2,1)S(1)}, u32[]{:S(2)}, u32[]{:S(2)}) collective-permute-start(bf16[64,2048]{1,0:T(8,128)(2,1)S(1)} %slice.424), channel_id=1, source_target_pairs={{0,2},{2,4},{4,6},{6,8},{8,10},{10,12},{12,14},{14,16},{16,18},{18... | collective-permute-start | bytes 786440 | tf_op jit(solution)/shard_map/ppermute | solution.py:16
  11.9 15.7 %copy-start = (bf16[128,2048]{1,0:T(8,128)(2,1)S(1)}, bf16[128,2048]{1,0:T(8,128)(2,1)}, u32[]{:S(2)}) copy-start(bf16[128,2048]{1,0:T(8,128)(2,1)} %param.5) | copy-start | bytes 1572868
  11.9 11.8 %all-to-all-start = ((bf16[2,128,4096]{1,0,2:T(2,128)(2,1)}), bf16[2,128,4096]{1,0,2:T(2,128)(2,1)S(1)}, u32[]{:S(2)}, u32[]{:S(2)}) async-start(bf16[2,128,4096]{1,0,2:T(2,128)(2,1)} %copy.67), calls=%async_computation | async-start | bytes 4194304 | tf_op jit(solution)/shard_map/all_to_all | solution.py:113
  30.3 43.2 %copy-start.3 = (f32[128]{0:T(128)S(1)}, f32[128]{0:T(128)}, u32[]{:S(2)}) copy-start(f32[128]{0:T(128)} %param.8) | copy-start | bytes 1540
  39.9 29.2 %all-to-all-start.2 = ((f32[64,1,256]{2,1,0:T(1,128)}), f32[64,1,256]{2,1,0:T(1,128)S(1)}, u32[]{:S(2)}, u32[]{:S(2)}) async-start(f32[64,1,256]{2,1,0:T(1,128)} %broadcast_in_dim.77), calls=%async_computation.2 | async-start | bytes 131072 | tf_op jit(solution)/shard_map/all_to_all | solution.py:21
  69.8 9.3 %all-to-all-start.3 = ((f32[4,64,1,256]{3,1,2,0:T(8,128)}), f32[4,64,1,256]{3,1,2,0:T(8,128)S(1)}, u32[]{:S(2)}, u32[]{:S(2)}) async-start(f32[4,64,1,256]{3,1,2,0:T(8,128)} %broadcast_in_dim.78), calls=%async_computation.3 | async-start | bytes 524288 | tf_op jit(solution)/shard_map/all_to_all | solution.py:21
  105.4 8.9 %all-to-all-start.5 = ((f32[4,64,1,256]{3,1,2,0:T(8,128)}), f32[4,64,1,256]{3,1,2,0:T(8,128)S(1)}, u32[]{:S(2)}, u32[]{:S(2)}) async-start(f32[4,64,1,256]{3,1,2,0:T(8,128)} %broadcast_in_dim.81), calls=%async_computation.5 | async-start | bytes 524288 | tf_op jit(solution)/shard_map/all_to_all | solution.py:21
  116.4 2.9 %collective-permute-start.1 = (f32[128,1]{0,1:T(1,128)S(1)}, f32[128,1]{0,1:T(1,128)S(1)}, u32[]{:S(2)}, u32[]{:S(2)}) collective-permute-start(f32[128,1]{0,1:T(1,128)S(1)} %slice.587), channel_id=1, source_target_pairs={{0,2},{2,4},{4,6},{6,8},{8,10},{10,12},{12,14},{14,16},{16,18},{18... | collective-permute-start | bytes 1544 | tf_op jit(solution)/shard_map/ppermute | solution.py:16
  195.9 61.1 %all-to-all-start.8 = ((f32[64,8,512]{2,1,0:T(8,128)}), f32[64,8,512]{2,1,0:T(8,128)S(1)}, u32[]{:S(2)}, u32[]{:S(2)}) async-start(f32[64,8,512]{2,1,0:T(8,128)} %reduce_sum.28), calls=%async_computation.8 | async-start | bytes 2097152 | tf_op jit(solution)/shard_map/all_to_all | solution.py:67
where the time goes:
time: 263 us; the launch traced here: 258 us
  blocking collectives  83.2 us (32%)
  waiting for transfers between devices  75.8 us (29%)
  starting transfers between devices  47 us (18%)
  local copies, waits for them, and re-layouts  26.3 us (10%)
  other arithmetic  17.2 us (7%)
  between operations  4.54 us (2%)
  matrix products  3.8 us (1%)
    all_to_all x1, blocking collectives, summed_on_arrival(): blocks = lax.all_to_all(in_blocks(x, dim, peers), axis, 0, 0, tiled=True)  51.7 us
    all_to_all x1, waiting for transfers between devices, sum_by_axis(): return jnp.sum(lax.all_to_all(own, far, 0, 0, tiled=True), axis=0)  50.1 us
    all_to_all x3, blocking collectives, copy_for_each(): return lax.all_to_all(copies, axis, split_axis=0, concat_axis=0, tiled=True)  31.5 us
    all_to_all x3, waiting for transfers between devices, copy_for_each(): return lax.all_to_all(copies, axis, split_axis=0, concat_axis=0, tiled=True)  25 us
    all_to_all x3, starting transfers between devices, copy_for_each(): return lax.all_to_all(copies, axis, split_axis=0, concat_axis=0, tiled=True)  22.3 us
    all_to_all x1, starting transfers between devices, sum_by_axis(): return jnp.sum(lax.all_to_all(own, far, 0, 0, tiled=True), axis=0)  10.3 us
    unnamed x2, other arithmetic  9.43 us
    all_to_all x1, starting transfers between devices, per_device(): lax.all_to_all(gain, 'state', split_axis=2, concat_axis=1, tiled=True)  8.11 us
  transfers between devices with their start and end apart: 7, of which 5 were waited for; matrix products, arithmetic and copies ran while one was open for 5% of the time, Pallas kernels for 0%

commit v1 on v0

v1 whole, which is shorter than its diff:
```python
import jax
import jax.numpy as jnp
from jax import lax
from jax.experimental import pallas as pl
from jax.experimental.pallas import tpu as pltpu
from jax.sharding import Mesh
from jax.sharding import PartitionSpec as P

TAPS = 2
DMAX = 64
Z = "tm_0"
YX = ("tm_1", "tm_2")
TM = ("tm_0", "tm_1", "tm_2")
STATE_TM = ("state", "tm_0", "tm_1", "tm_2")
F32 = jnp.float32
BF16 = jnp.bfloat16
VMEM = pl.BlockSpec(memory_space=pltpu.VMEM)
SMEM = pl.BlockSpec(memory_space=pltpu.SMEM)
NT = (((1,), (1,)), ((), ()))


def call(body, outs, scratch=(), smem=(0,), n_in=1):
    specs = [SMEM if i in smem else VMEM for i in range(n_in)]
    return pl.pallas_call(
        body,
        out_shape=outs,
        in_specs=specs,
        out_specs=jax.tree.map(lambda _: VMEM, outs),
        scratch_shapes=scratch,
        compiler_params=pltpu.CompilerParams(vmem_limit_bytes=48 << 20),
    )


def later(x, k, fill):
    if k % 8 == 0:
        return jnp.concatenate([jnp.full((k, x.shape[1]), fill, x.dtype), x[:-k]], 0)
    row = lax.broadcasted_iota(jnp.int32, x.shape, 0)
    return jnp.where(row < k, fill, pltpu.roll(x, k, 0))


def earlier(x, k, fill):
    n = x.shape[0]
    if k % 8 == 0:
        return jnp.concatenate([x[k:], jnp.full((k, x.shape[1]), fill, x.dtype)], 0)
    row = lax.broadcasted_iota(jnp.int32, x.shape, 0)
    return jnp.where(row >= n - k, fill, pltpu.roll(x, n - k, 0))


def recur(link, sums, shift):
    k = 1
    while k < link.shape[0]:
        sums = [s + link * shift(s, k, 0.0) for s in sums]
        link = link * shift(link, k, 1.0)
        k *= 2
    return link, sums


def taps_body(where, own, other, gain, out):
    modes = gain.shape[1]
    half = own.shape[1]
    mine = pl.multiple_of(where[2] * half, half)
    theirs = pl.multiple_of((1 - where[2]) * half, half)
    for k in range(TAPS):
        out[:, k * modes : (k + 1) * modes] = lax.dot_general(
            own[...], gain[k, :, pl.ds(mine, half)], NT, preferred_element_type=F32
        ) + lax.dot_general(
            other[...], gain[k, :, pl.ds(theirs, half)], NT, preferred_element_type=F32
        )


def local_body(where, u, tail, decay_ref, scale, leak, keep, summary, ext):
    frames, modes = decay_ref.shape
    ext[:DMAX] = tail[...]
    ext[DMAX:] = u[...]
    drive_in = jnp.zeros((frames, modes), F32)
    for k in range(TAPS):
        rolled = pltpu.roll(ext[:, k * modes : (k + 1) * modes], frames + where[3 + k], 0)
        drive_in += rolled[:frames]
    drive = scale[...] * drive_in
    decay = decay_ref[...]
    prods, (offsets,) = recur(decay, [drive], later)
    kappa = 1.0 - leak[...]
    weight = 1.0 - kappa * decay * decay
    links, (base, slope) = recur(kappa * decay, [weight * offsets, weight * prods], earlier)
    keep[0] = prods
    keep[1] = offsets
    keep[2] = links
    keep[3] = base
    keep[4] = slope
    keep[5] = drive
    summary[...] = jnp.zeros_like(summary)
    rows = [prods[-1:], offsets[-1:], links[:1], base[:1], slope[:1], decay[-1:]]
    for r, row in enumerate(rows):
        for i in range(summary.shape[0]):
            summary[i, r : r + 1] = row


def joined(first, second):
    p1, o1, l1, b1, s1 = first
    p2, o2, l2, b2, s2 = second
    return (p1 * p2, p2 * o1 + o2, l1 * l2, b1 + l1 * (b2 + s2 * o1), s1 + l1 * s2 * p1)


def five(ref, i):
    return tuple(ref[i, r : r + 1] for r in range(5))


def plane_body(every, out):
    n = every.shape[0]
    parts = [five(every, i) for i in range(n)]
    while len(parts) > 1:
        parts = [joined(parts[i], parts[i + 1]) for i in range(0, len(parts), 2)]
    out[...] = jnp.zeros_like(out)
    rows = list(parts[0]) + [every[n - 1, 5:6]]
    for r, row in enumerate(rows):
        for i in range(out.shape[0]):
            out[i, r : r + 1] = row


def ends(every, position, entering, closing, last):
    n = every.shape[0]
    states = []
    state = entering
    before = last
    own_state = jnp.zeros_like(entering)
    own_last = jnp.zeros_like(entering)
    for i in range(n):
        states.append(state)
        own_state = jnp.where(position == i, state, own_state)
        own_last = jnp.where(position == i, before, own_last)
        state = every[i, 0:1] * state + every[i, 1:2]
        before = every[i, 5:6]
    after = closing
    own_after = jnp.zeros_like(entering)
    for i in reversed(range(n)):
        own_after = jnp.where(position == i, after, own_after)
        after = every[i, 2:3] * after + every[i, 3:4] + every[i, 4:5] * states[i]
    return own_state, own_after, own_last


def finish_body(where, plane, planes, keep, decay_ref, leak, smoothed_out, resid_out):
    zero = jnp.zeros((1, decay_ref.shape[1]), F32)
    entering, after, last = ends(planes, where[0], zero, zero, zero)
    entering, after, last = ends(plane, where[1], entering, after, last)
    smoothed = keep[3] + keep[4] * entering + keep[2] * after
    decay = decay_ref[...]
    kappa = 1.0 - leak[...]
    prior = (1.0 - kappa * last * last) * entering + kappa * last * smoothed[:1]
    first = jnp.logical_and(where[0] == 0, where[1] == 0)
    prior = jnp.where(first, 0.0, prior)
    row = lax.broadcasted_iota(jnp.int32, smoothed.shape, 0)
    shifted = jnp.where(row == 0, prior, pltpu.roll(smoothed, 1, 0))
    resid = (smoothed - decay * shifted - keep[5]).astype(BF16)
    smoothed_out[...] = smoothed.T
    for i in range(resid_out.shape[0]):
        resid_out[i] = resid


def gradient_body(where, tail, own, tail_other, other, resid, out, padded):
    blocks, frames, modes = resid.shape
    row = lax.broadcasted_iota(jnp.int32, (frames, 2 * frames), 0)
    column = lax.broadcasted_iota(jnp.int32, (frames, 2 * frames), 1)
    picks = [(column == row + where[3 + k]).astype(F32).astype(BF16) for k in range(TAPS)]
    nothing = jnp.zeros((frames, modes), BF16)
    for b in range(blocks + 1):
        pair = jnp.concatenate(
            [resid[b - 1] if b > 0 else nothing, resid[b] if b < blocks else nothing], 0
        )
        for k in range(TAPS):
            moved = jnp.dot(picks[k], pair, preferred_element_type=F32)
            padded[b * frames : (b + 1) * frames, k * modes : (k + 1) * modes] = moved.astype(BF16)
    rhs = padded[...]
    for which, (before, rows) in enumerate(((tail, own), (tail_other, other))):
        lhs = jnp.concatenate([before[...]] + [rows[i] for i in range(blocks)], 1)
        sums = jnp.dot(lhs, rhs, preferred_element_type=F32)
        half = jnp.where(where[2] == which, 0, 1)
        for i in range(out.shape[0]):
            out[i, half] = sums[i * 8 : (i + 1) * 8]


def swapped(x):
    return lax.ppermute(x, "state", [(0, 1), (1, 0)])


def per_device(record, gain, rate, leak, dilation):
    frames, sensors = record.shape
    modes = rate.shape[0]
    planes = lax.axis_size(Z)
    blocks = lax.axis_size(YX)
    core = lax.axis_index("state")
    where = jnp.concatenate(
        [
            jnp.stack([lax.axis_index(Z), lax.axis_index(YX), core]).astype(jnp.int32),
            dilation,
        ]
    )
    other = swapped(record)
    group = sensors // planes // blocks
    by_sensor = record.T.reshape(planes, blocks, group, frames).swapaxes(0, 1)
    by_sensor = by_sensor.reshape(blocks, planes * group, frames)
    mine = lax.all_to_all(by_sensor, YX, 0, 0, tiled=True)
    tail = lax.ppermute(mine[-1], Z, [(i, i + 1) for i in range(planes - 1)])
    rate_t = rate.T
    decay = jnp.exp(-rate_t)
    scale = jnp.sqrt(-jnp.expm1(-2.0 * rate_t))
    leak_row = leak[None]

    u = call(taps_body, jax.ShapeDtypeStruct((frames, TAPS * modes), F32), n_in=4)(
        where, record, other, gain
    )
    u_tail = lax.ppermute(u[frames - DMAX :], TM, [(i, i + 1) for i in range(planes * blocks - 1)])
    keep, summary = call(
        local_body,
        (
            jax.ShapeDtypeStruct((6, frames, modes), F32),
            jax.ShapeDtypeStruct((blocks, 8, modes), F32),
        ),
        scratch=[pltpu.VMEM((DMAX + frames, TAPS * modes), F32)],
        n_in=6,
    )(where, u, u_tail, decay, scale, leak_row)
    plane = lax.all_to_all(summary, YX, 0, 0, tiled=True)
    plane_summary = call(
        plane_body, jax.ShapeDtypeStruct((planes, 8, modes), F32), smem=(), n_in=1
    )(plane)
    every_plane = lax.all_to_all(plane_summary, Z, 0, 0, tiled=True)
    smoothed, resid = call(
        finish_body,
        (
            jax.ShapeDtypeStruct((modes, frames), F32),
            jax.ShapeDtypeStruct((blocks, frames, modes), BF16),
        ),
        n_in=6,
    )(where, plane, every_plane, keep, decay, leak_row)
    resid_all = lax.all_to_all(resid, YX, 0, 0, tiled=True)
    theirs = swapped(jnp.concatenate([tail[None], mine]))
    partial = call(
        gradient_body,
        jax.ShapeDtypeStruct((planes, 2, group, TAPS * modes), F32),
        scratch=[pltpu.VMEM(((blocks + 1) * frames, TAPS * modes), BF16)],
        n_in=6,
    )(where, tail, mine, theirs[0], theirs[1:], resid_all)
    summed = jnp.sum(lax.all_to_all(partial, Z, 0, 0, tiled=True), axis=0)
    ours = lax.dynamic_index_in_dim(summed, core, 0, keepdims=False)
    given = swapped(lax.dynamic_index_in_dim(summed, 1 - core, 0, keepdims=False))
    ours = ours.reshape(group, TAPS, modes)
    given = given.reshape(group, TAPS, modes)
    low = jnp.where(core == 0, ours, given)
    high = jnp.where(core == 0, given, ours)
    grad = jnp.stack([low, high], 2).reshape(group, TAPS * 2 * modes)
    return (smoothed, grad)


def solution(mesh):
    split = Mesh(
        mesh.devices.reshape(16, 4, 4, mesh.shape["state"]), ("tm_0", "tm_1", "tm_2", "state")
    )
    return jax.shard_map(
        per_device,
        mesh=split,
        in_specs=(P(TM, "state"), P(None, "state", None), P("state", TM), P("state"), P()),
        out_specs=(P("state", TM), P(STATE_TM, None)),
        check_vma=False,
    )
```

time: 263 us -> 121 us (0.46); the launches traced: 258 us -> 120 us
  blocking collectives: 83.2 us -> 28.5 us
  waiting for transfers between devices: 75.8 us -> 29.2 us
  local copies, waits for them, and re-layouts: 26.3 us -> 2.58 us
  other arithmetic: 17.2 us -> 0.82 us
  Pallas kernels: 0 us -> 7.02 us
  starting transfers between devices: 47 us -> 51.3 us
  matrix products: 3.8 us -> 0 us
  between operations: 4.54 us -> 0.9 us
    all_to_all x4 -> x1, blocking collectives: 83.2 us -> 28.5 us  [per_device(): every_plane = lax.all_to_all(plane_summary, Z, 0, 0, tiled=True)]
    all_to_all x5 -> x4, waiting for transfers between devices: 75.1 us -> 27.1 us  [the longest x1 12.8 us: per_device(): summed = jnp.sum(lax.all_to_all(partial, Z, 0, 0, tiled=True), axis=0)]
    ppermute x2 -> x5, starting transfers between devices: 6.28 us -> 27 us  [the longest x3 19.9 us: swapped(): return lax.ppermute(x, 'state', [(0, 1), (1, 0)])]
    all_to_all x5 -> x4, starting transfers between devices: 40.7 us -> 24.3 us  [the longest x1 7.58 us: per_device(): mine = lax.all_to_all(by_sensor, YX, 0, 0, tiled=True)]
    unnamed x2 -> x0, other arithmetic: 9.43 us -> none
    pallas_call x0 -> x5, Pallas kernels: none -> 7.02 us  [the longest x1 2.28 us: per_device(): call(gradient_body, jax.ShapeDtypeStruct((planes, 2, group, TAPS * modes)...]
    unnamed x17 -> x12, local copies, waits for them, and re-layouts: 7.29 us -> 1.57 us
    concatenate x2 -> x0, local copies, waits for them, and re-layouts: 5.48 us -> none  [the longest x1 5.44 us: per_device(): jnp.concatenate(pieces, 1)]
  transfers between devices with their start and end apart: 7 -> 9, of which waited for: 5 -> 6; matrix products, arithmetic and copies ran while one was open for 5% -> 0% of each run, Pallas kernels for 0% -> 4%
where the time goes in v1:
time: 121 us; the launch traced here: 120 us
  starting transfers between devices  51.3 us (42%)
  waiting for transfers between devices  29.2 us (24%)
  blocking collectives  28.5 us (24%)
  Pallas kernels  7.02 us (6%)
  local copies, waits for them, and re-layouts  2.58 us (2%)
    all_to_all x1, blocking collectives, per_device(): every_plane = lax.all_to_all(plane_summary, Z, 0, 0, tiled=True)  28.5 us
    ppermute x3, starting transfers between devices, swapped(): return lax.ppermute(x, 'state', [(0, 1), (1, 0)])  19.9 us
    all_to_all x1, waiting for transfers between devices, per_device(): summed = jnp.sum(lax.all_to_all(partial, Z, 0, 0, tiled=True), axis=0)  12.8 us
    all_to_all x1, waiting for transfers between devices, per_device(): resid_all = lax.all_to_all(resid, YX, 0, 0, tiled=True)  9.22 us
    all_to_all x1, starting transfers between devices, per_device(): mine = lax.all_to_all(by_sensor, YX, 0, 0, tiled=True)  7.58 us
    all_to_all x1, starting transfers between devices, per_device(): plane = lax.all_to_all(summary, YX, 0, 0, tiled=True)  7.3 us
    all_to_all x1, starting transfers between devices, per_device(): resid_all = lax.all_to_all(resid, YX, 0, 0, tiled=True)  5.85 us
    ppermute x1, starting transfers between devices, per_device(): tail = lax.ppermute(mine[-1], Z, [(i, i + 1) for i in range(planes - 1)])  5.03 us
  transfers between devices with their start and end apart: 9, of which 6 were waited for; matrix products, arithmetic and copies ran while one was open for 0% of the time, Pallas kernels for 4%

profile of v1, /device:TPU:1, one launch (start us, length us, event | category | flops | bytes accessed | tf_op | source)
XLA Modules:
  0.0 120.3 jit_solution(11857400579839238875)
XLA Ops:
  0.7 1.5 %copy.12 = bf16[128,2048]{0,1:T(8,128)(2,1)S(1)} copy(bf16[128,2048]{1,0:T(8,128)(2,1)} %own.1) | data formatting | bytes 1048576 | tf_op args[0]
  2.1 0.9 copy.15
  3.1 7.6 %all-to-all-start.2 = ((bf16[16,128,128]{2,1,0:T(8,128)(2,1)}), bf16[16,128,128]{2,1,0:T(8,128)(2,1)S(1)}, u32[]{:S(2)}, u32[]{:S(2)}) async-start(bf16[16,128,128]{2,1,0:T(8,128)(2,1)} %bitcast.33), calls=%async_computation.2 | async-start | bytes 1048576 | tf_op jit(solution)/shard_map/all_to_all | solution.py:201
  10.7 0.0 copy-done.1
  10.7 0.0 copy-start.2
  10.7 4.8 %collective-permute-start = (bf16[128,2048]{1,0:T(8,128)(2,1)S(1)}, bf16[128,2048]{1,0:T(8,128)(2,1)}, u32[]{:S(2)}, u32[]{:S(2)}) collective-permute-start(bf16[128,2048]{1,0:T(8,128)(2,1)S(1)} %copy-done.1), channel_id=1, source_target_pairs={{0,1},{1,0},{2,3},{3,2},{4,5},{5,4},{6,7},{7,6},{8,9},{9,8},{10,11... | collective-permute-start | bytes 1572872 | tf_op jit(solution)/shard_map/ppermute | solution.py:182
  15.5 0.1 copy.10
  15.6 0.1 pad_add_fusion.where
  15.7 4.0 %all-to-all-done.2.own = bf16[16,128,128]{2,1,0:T(8,128)(2,1)S(1)} async-done(((bf16[16,128,128]{2,1,0:T(8,128)(2,1)}), bf16[16,128,128]{2,1,0:T(8,128)(2,1)S(1)}, u32[]{:S(2)}, u32[]{:S(2)}) %all-to-all-start.2) | async-done | bytes 524320 | tf_op jit(solution)/shard_map/all_to_all | solution.py:201
  19.7 5.0 %collective-permute-start.2 = (bf16[128,128]{1,0:T(8,128)(2,1)S(1)}, bf16[128,128]{1,0:T(8,128)(2,1)S(1)}, u32[]{:S(2)}, u32[]{:S(2)}) collective-permute-start(bf16[128,128]{1,0:T(8,128)(2,1)S(1)} %slice_bitcast_fusion.1), channel_id=1, source_target_pairs={{0,32},{32,64},{64,96},{96,128},{128,160},{160,192},{192,224},{224... | collective-permute-start | bytes 98312 | tf_op jit(solution)/shard_map/ppermute | solution.py:202
  24.7 0.0 collective-permute-done.other
  24.7 1.8 %shard_map.68.u = f32[128,256]{1,0:T(8,128)S(1)} custom-call(s32[5]{0:T(128)S(1)} %pad_add_fusion.where, bf16[128,2048]{1,0:T(8,128)(2,1)S(1)} %copy-done.1, bf16[128,2048]{1,0:T(8,128)(2,1)} %collective-permute-done.other, bf16[2,128,4096]{2,1,0:T(8,128)(2,1)S(1)} %copy-done), custom_call_target="tpu_custom_call" | custom-call | tf_op jit(solution)/shard_map/pallas_call | solution.py:208
  26.5 2.1 %collective-permute-start.1 = (f32[64,256]{1,0:T(8,128)S(1)}, f32[64,256]{1,0:T(8,128)S(1)}, u32[]{:S(2)}, u32[]{:S(2)}) collective-permute-start(f32[64,256]{1,0:T(8,128)S(1)} %slice.16), channel_id=1, source_target_pairs={{0,2},{2,4},{4,6},{6,8},{8,10},{10,12},{12,14},{14,16},{16,18},{18... | collective-permute-start | bytes 196616 | tf_op jit(solution)/shard_map/ppermute | solution.py:211
  28.7 0.1 sqrt_bitcast_fusion
  28.7 1.3 %collective-permute-done.1.tail = f32[64,256]{1,0:T(8,128)S(1)} collective-permute-done((f32[64,256]{1,0:T(8,128)S(1)}, f32[64,256]{1,0:T(8,128)S(1)}, u32[]{:S(2)}, u32[]{:S(2)}) %collective-permute-start.1) | collective-permute-done | bytes 65568 | tf_op jit(solution)/shard_map/ppermute | solution.py:211
  30.0 1.4 %shard_map.69 = (f32[6,128,128]{2,1,0:T(8,128)S(1)}, f32[16,8,128]{2,1,0:T(8,128)}) custom-call(s32[5]{0:T(128)S(1)} %pad_add_fusion.where, f32[128,256]{1,0:T(8,128)S(1)} %shard_map.68.u, f32[64,256]{1,0:T(8,128)S(1)} %collective-permute-done.1.tail, f32[128,128]{1,0:T(8,128)S(1)} %get-tuple-element.11.decay_ref, f32[128,128]{1,0:T(8,128)S(1)} %get-tuple-element.10.scale, ...), custom_call_target="tpu_custom_call" | custom-call | tf_op jit(solution)/shard_map/pallas_call | solution.py:212
  31.4 7.3 %all-to-all-start = ((f32[16,8,128]{2,1,0:T(8,128)}), f32[16,8,128]{2,1,0:T(8,128)S(1)}, u32[]{:S(2)}, u32[]{:S(2)}) async-start(f32[16,8,128]{2,1,0:T(8,128)} %get-tuple-element.6), calls=%async_computation | async-start | bytes 131072 | tf_op jit(solution)/shard_map/all_to_all | solution.py:221
  38.7 0.0 collective-permute-done.2.tail
  38.7 0.1 pad_maximum_fusion
  38.8 5.3 %collective-permute-start.3 = (bf16[17,128,128]{2,1,0:T(8,128)(2,1)S(1)}, bf16[17,128,128]{2,1,0:T(8,128)(2,1)S(1)}, u32[]{:S(2)}, u32[]{:S(2)}) collective-permute-start(bf16[17,128,128]{2,1,0:T(8,128)(2,1)S(1)} %pad_maximum_fusion), channel_id=1, source_target_pairs={{0,1},{1,0},{2,3},{3,2},{4,5},{5,4},{6,7},{7,6},{8,9},{9,8},{10,11... | collective-permute-start | bytes 1671176 | tf_op jit(solution)/shard_map/ppermute | solution.py:182
  44.1 1.1 all-to-all-done.every.plane
  45.3 28.5 %all_to_all.25.planes = f32[16,8,128]{2,1,0:T(8,128)S(1)} all-to-all(f32[16,8,128]{2,1,0:T(8,128)S(1)} %shard_map.70), channel_id=1, replica_groups=mesh['tm_0'=16,'tm_1'=4,'tm_2'=4,'state'=2] {'tm_0'}, dimensions={0} | all-to-all | bytes 131072 | tf_op jit(solution)/shard_map/all_to_all | solution.py:225
  73.8 1.5 %shard_map.71 = (f32[128,128]{1,0:T(8,128)}, bf16[16,128,128]{2,1,0:T(8,128)(2,1)}) custom-call(s32[5]{0:T(128)S(1)} %pad_add_fusion.where, f32[16,8,128]{2,1,0:T(8,128)S(1)} %all-to-all-done.every.plane, f32[16,8,128]{2,1,0:T(8,128)S(1)} %all_to_all.25.planes, f32[6,128,128]{2,1,0:T(8,128)S(1)} %get-tuple-element.7.keep, ...), custom_call_target="tpu_custom_call" | custom-call | tf_op jit(solution)/shard_map/pallas_call | solution.py:226
  75.3 5.9 %all-to-all-start.3 = ((bf16[16,128,128]{2,1,0:T(8,128)(2,1)}), bf16[16,128,128]{2,1,0:T(8,128)(2,1)S(1)}, u32[]{:S(2)}, u32[]{:S(2)}) async-start(bf16[16,128,128]{2,1,0:T(8,128)(2,1)} %get-tuple-element.9), calls=%async_computation.3 | async-start | bytes 1048576 | tf_op jit(solution)/shard_map/all_to_all | solution.py:234
  81.2 0.0 collective-permute-done.3
  81.2 9.2 %all-to-all-done.3.resid = bf16[16,128,128]{2,1,0:T(8,128)(2,1)S(1)} async-done(((bf16[16,128,128]{2,1,0:T(8,128)(2,1)}), bf16[16,128,128]{2,1,0:T(8,128)(2,1)S(1)}, u32[]{:S(2)}, u32[]{:S(2)}) %all-to-all-start.3) | async-done | bytes 524320 | tf_op jit(solution)/shard_map/all_to_all | solution.py:234
  90.5 2.3 %shard_map.72 = f32[16,2,8,256]{3,2,1,0:T(8,128)} custom-call(s32[5]{0:T(128)S(1)} %pad_add_fusion.where, bf16[128,128]{1,0:T(8,128)(2,1)S(1)} %collective-permute-done.2.tail, bf16[16,128,128]{2,1,0:T(8,128)(2,1)S(1)} %all-to-all-done.2.own, bf16[128,128]{1,0:T(8,128)(2,1)S(1)} %slice_bitcast_fusion.tail_other, bf16[16,128,128]{2,1,0:T(8,128)(2,1)S(1)} %slice.19.other, ...), custom_call_target="tpu_custom_call" | custom-call | tf_op jit(solution)/shard_map/pallas_call | solution.py:236
  92.7 3.5 %all-to-all-start.4 = ((f32[16,2,8,256]{3,2,1,0:T(8,128)}), f32[16,2,8,256]{3,2,1,0:T(8,128)S(1)}, u32[]{:S(2)}, u32[]{:S(2)}) async-start(f32[16,2,8,256]{3,2,1,0:T(8,128)} %shard_map.72), calls=%async_computation.4 | async-start | bytes 524288 | tf_op jit(solution)/shard_map/all_to_all | solution.py:242
  96.3 12.8 %all-to-all-done.4 = f32[16,2,8,256]{3,2,1,0:T(8,128)S(1)} async-done(((f32[16,2,8,256]{3,2,1,0:T(8,128)}), f32[16,2,8,256]{3,2,1,0:T(8,128)S(1)}, u32[]{:S(2)}, u32[]{:S(2)}) %all-to-all-start.4) | async-done | bytes 262176 | tf_op jit(solution)/shard_map/all_to_all | solution.py:242
  109.1 9.8 %collective-permute-start.4 = (f32[8,256]{1,0:T(8,128)S(1)}, f32[8,256]{1,0:T(8,128)S(1)}, u32[]{:S(2)}, u32[]{:S(2)}) collective-permute-start(f32[8,256]{1,0:T(8,128)S(1)} %dynamic-slice_bitcast_fusion), channel_id=1, source_target_pairs={{0,1},{1,0},{2,3},{3,2},{4,5},{5,4},{6,7},{7,6},{8,9},{9,8},{10,11... | collective-permute-start | bytes 24584 | tf_op jit(solution)/shard_map/ppermute | solution.py:182
  118.9 0.8 collective-permute-done.4
  119.7 0.6 pad_maximum_fusion.1
  (16 shorter events, 0.2 us)
Async XLA Ops:
  0.6 10.0 %copy-start.1 = (bf16[128,2048]{1,0:T(8,128)(2,1)S(1)}, bf16[128,2048]{1,0:T(8,128)(2,1)}, u32[]{:S(2)}) copy-start(bf16[128,2048]{1,0:T(8,128)(2,1)} %own.1) | copy-start | bytes 1572868
  0.6 14.8 %copy-start.3 = (f32[128,128]{1,0:T(8,128)S(1)}, f32[128,128]{1,0:T(8,128)}, u32[]{:S(2)}) copy-start(f32[128,128]{1,0:T(8,128)} %param.7) | copy-start | bytes 196612
  0.7 14.9 %copy-start.4 = (s32[2]{0:T(128)S(1)}, s32[2]{0:T(128)}, u32[]{:S(2)}) copy-start(s32[2]{0:T(128)} %param.9) | copy-start | bytes 28
  0.7 24.1 %copy-start = (bf16[2,128,4096]{2,1,0:T(8,128)(2,1)S(1)}, bf16[2,128,4096]{2,1,0:T(8,128)(2,1)}, u32[]{:S(2)}) copy-start(bf16[2,128,4096]{2,1,0:T(8,128)(2,1)} %gain.1) | copy-start | bytes 6291460
  3.1 16.6 %all-to-all-start.2 = ((bf16[16,128,128]{2,1,0:T(8,128)(2,1)}), bf16[16,128,128]{2,1,0:T(8,128)(2,1)S(1)}, u32[]{:S(2)}, u32[]{:S(2)}) async-start(bf16[16,128,128]{2,1,0:T(8,128)(2,1)} %bitcast.33), calls=%async_computation.2 | async-start | bytes 1048576 | tf_op jit(solution)/shard_map/all_to_all | solution.py:201
  10.7 19.3 %copy-start.2 = (f32[128]{0:T(128)S(1)}, f32[128]{0:T(128)}, u32[]{:S(2)}) copy-start(f32[128]{0:T(128)} %param.8) | copy-start | bytes 1540
  10.7 14.0 %collective-permute-start = (bf16[128,2048]{1,0:T(8,128)(2,1)S(1)}, bf16[128,2048]{1,0:T(8,128)(2,1)}, u32[]{:S(2)}, u32[]{:S(2)}) collective-permute-start(bf16[128,2048]{1,0:T(8,128)(2,1)S(1)} %copy-done.1), channel_id=1, source_target_pairs={{0,1},{1,0},{2,3},{3,2},{4,5},{5,4},{6,7},{7,6},{8,9},{9,8},{10,11... | collective-permute-start | bytes 1572872 | tf_op jit(solution)/shard_map/ppermute | solution.py:182
  19.7 19.0 %collective-permute-start.2 = (bf16[128,128]{1,0:T(8,128)(2,1)S(1)}, bf16[128,128]{1,0:T(8,128)(2,1)S(1)}, u32[]{:S(2)}, u32[]{:S(2)}) collective-permute-start(bf16[128,128]{1,0:T(8,128)(2,1)S(1)} %slice_bitcast_fusion.1), channel_id=1, source_target_pairs={{0,32},{32,64},{64,96},{96,128},{128,160},{160,192},{192,224},{224... | collective-permute-start | bytes 98312 | tf_op jit(solution)/shard_map/ppermute | solution.py:202
  26.5 3.5 %collective-permute-start.1 = (f32[64,256]{1,0:T(8,128)S(1)}, f32[64,256]{1,0:T(8,128)S(1)}, u32[]{:S(2)}, u32[]{:S(2)}) collective-permute-start(f32[64,256]{1,0:T(8,128)S(1)} %slice.16), channel_id=1, source_target_pairs={{0,2},{2,4},{4,6},{6,8},{8,10},{10,12},{12,14},{14,16},{16,18},{18... | collective-permute-start | bytes 196616 | tf_op jit(solution)/shard_map/ppermute | solution.py:211
  31.4 13.8 %all-to-all-start = ((f32[16,8,128]{2,1,0:T(8,128)}), f32[16,8,128]{2,1,0:T(8,128)S(1)}, u32[]{:S(2)}, u32[]{:S(2)}) async-start(f32[16,8,128]{2,1,0:T(8,128)} %get-tuple-element.6), calls=%async_computation | async-start | bytes 131072 | tf_op jit(solution)/shard_map/all_to_all | solution.py:221
  38.8 42.4 %collective-permute-start.3 = (bf16[17,128,128]{2,1,0:T(8,128)(2,1)S(1)}, bf16[17,128,128]{2,1,0:T(8,128)(2,1)S(1)}, u32[]{:S(2)}, u32[]{:S(2)}) collective-permute-start(bf16[17,128,128]{2,1,0:T(8,128)(2,1)S(1)} %pad_maximum_fusion), channel_id=1, source_target_pairs={{0,1},{1,0},{2,3},{3,2},{4,5},{5,4},{6,7},{7,6},{8,9},{9,8},{10,11... | collective-permute-start | bytes 1671176 | tf_op jit(solution)/shard_map/ppermute | solution.py:182
  75.3 15.1 %all-to-all-start.3 = ((bf16[16,128,128]{2,1,0:T(8,128)(2,1)}), bf16[16,128,128]{2,1,0:T(8,128)(2,1)S(1)}, u32[]{:S(2)}, u32[]{:S(2)}) async-start(bf16[16,128,128]{2,1,0:T(8,128)(2,1)} %get-tuple-element.9), calls=%async_computation.3 | async-start | bytes 1048576 | tf_op jit(solution)/shard_map/all_to_all | solution.py:234
  92.7 16.3 %all-to-all-start.4 = ((f32[16,2,8,256]{3,2,1,0:T(8,128)}), f32[16,2,8,256]{3,2,1,0:T(8,128)S(1)}, u32[]{:S(2)}, u32[]{:S(2)}) async-start(f32[16,2,8,256]{3,2,1,0:T(8,128)} %shard_map.72), calls=%async_computation.4 | async-start | bytes 524288 | tf_op jit(solution)/shard_map/all_to_all | solution.py:242
  109.1 10.6 %collective-permute-start.4 = (f32[8,256]{1,0:T(8,128)S(1)}, f32[8,256]{1,0:T(8,128)S(1)}, u32[]{:S(2)}, u32[]{:S(2)}) collective-permute-start(f32[8,256]{1,0:T(8,128)S(1)} %dynamic-slice_bitcast_fusion), channel_id=1, source_target_pairs={{0,1},{1,0},{2,3},{3,2},{4,5},{5,4},{6,7},{7,6},{8,9},{9,8},{10,11... | collective-permute-start | bytes 24584 | tf_op jit(solution)/shard_map/ppermute | solution.py:182

commit v2 on v1

--- a/solution.py
+++ b/solution.py
@@ -156,7 +156,7 @@
         resid_out[i] = resid
 
 
-def gradient_body(where, tail, own, tail_other, other, resid, out, padded):
+def gradient_body(where, tails, own, other, resid, out, padded):
     blocks, frames, modes = resid.shape
     row = lax.broadcasted_iota(jnp.int32, (frames, 2 * frames), 0)
     column = lax.broadcasted_iota(jnp.int32, (frames, 2 * frames), 1)
@@ -170,12 +170,27 @@
             moved = jnp.dot(picks[k], pair, preferred_element_type=F32)
             padded[b * frames : (b + 1) * frames, k * modes : (k + 1) * modes] = moved.astype(BF16)
     rhs = padded[...]
-    for which, (before, rows) in enumerate(((tail, own), (tail_other, other))):
-        lhs = jnp.concatenate([before[...]] + [rows[i] for i in range(blocks)], 1)
+    for which, rows in enumerate((own, other)):
+        lhs = jnp.concatenate([tails[which]] + [rows[i] for i in range(blocks)], 1)
         sums = jnp.dot(lhs, rhs, preferred_element_type=F32)
         half = jnp.where(where[2] == which, 0, 1)
         for i in range(out.shape[0]):
             out[i, half] = sums[i * 8 : (i + 1) * 8]
+
+
+def total_body(pieces, out):
+    modes = out.shape[1] // TAPS // 2
+    for core in range(2):
+        total = pieces[core]
+        for i in range(2 + core, pieces.shape[0], 2):
+            total += pieces[i]
+        for k in range(TAPS):
+            column = (2 * k + core) * modes
+            out[:, column : column + modes] = total[:, k * modes : (k + 1) * modes]
+
+
+def behind(x, first):
+    return lax.optimization_barrier((x, first))[0]
 
 
 def swapped(x):
@@ -187,10 +202,9 @@
     modes = rate.shape[0]
     planes = lax.axis_size(Z)
     blocks = lax.axis_size(YX)
-    core = lax.axis_index("state")
     where = jnp.concatenate(
         [
-            jnp.stack([lax.axis_index(Z), lax.axis_index(YX), core]).astype(jnp.int32),
+            jnp.stack([lax.axis_index(Z), lax.axis_index(YX), lax.axis_index("state")]).astype(jnp.int32),
             dilation,
         ]
     )
@@ -199,7 +213,6 @@
     by_sensor = record.T.reshape(planes, blocks, group, frames).swapaxes(0, 1)
     by_sensor = by_sensor.reshape(blocks, planes * group, frames)
     mine = lax.all_to_all(by_sensor, YX, 0, 0, tiled=True)
-    tail = lax.ppermute(mine[-1], Z, [(i, i + 1) for i in range(planes - 1)])
     rate_t = rate.T
     decay = jnp.exp(-rate_t)
     scale = jnp.sqrt(-jnp.expm1(-2.0 * rate_t))
@@ -218,6 +231,8 @@
         scratch=[pltpu.VMEM((DMAX + frames, TAPS * modes), F32)],
         n_in=6,
     )(where, u, u_tail, decay, scale, leak_row)
+    summary, mine = lax.optimization_barrier((summary, mine))
+    theirs = swapped(mine)
     plane = lax.all_to_all(summary, YX, 0, 0, tiled=True)
     plane_summary = call(
         plane_body, jax.ShapeDtypeStruct((planes, 8, modes), F32), smem=(), n_in=1
@@ -232,21 +247,19 @@
         n_in=6,
     )(where, plane, every_plane, keep, decay, leak_row)
     resid_all = lax.all_to_all(resid, YX, 0, 0, tiled=True)
-    theirs = swapped(jnp.concatenate([tail[None], mine]))
+    tails = behind(jnp.stack([mine[-1], theirs[-1]]), resid)
+    tails = lax.ppermute(tails, Z, [(i, i + 1) for i in range(planes - 1)])
     partial = call(
         gradient_body,
         jax.ShapeDtypeStruct((planes, 2, group, TAPS * modes), F32),
         scratch=[pltpu.VMEM(((blocks + 1) * frames, TAPS * modes), BF16)],
-        n_in=6,
-    )(where, tail, mine, theirs[0], theirs[1:], resid_all)
-    summed = jnp.sum(lax.all_to_all(partial, Z, 0, 0, tiled=True), axis=0)
-    ours = lax.dynamic_index_in_dim(summed, core, 0, keepdims=False)
-    given = swapped(lax.dynamic_index_in_dim(summed, 1 - core, 0, keepdims=False))
-    ours = ours.reshape(group, TAPS, modes)
-    given = given.reshape(group, TAPS, modes)
-    low = jnp.where(core == 0, ours, given)
-    high = jnp.where(core == 0, given, ours)
-    grad = jnp.stack([low, high], 2).reshape(group, TAPS * 2 * modes)
+        n_in=5,
+    )(where, tails, mine, theirs, resid_all)
+    pieces = partial.reshape(planes * 2, group, TAPS * modes)
+    pieces = lax.all_to_all(pieces, (Z, "state"), 0, 0, tiled=True)
+    grad = call(
+        total_body, jax.ShapeDtypeStruct((group, TAPS * 2 * modes), F32), smem=(), n_in=1
+    )(pieces)
     return (smoothed, grad)
 
 

time: 121 us -> 111 us (0.917)
  blocking collectives: 28.5 us -> 41.9 us
  starting transfers between devices: 51.3 us -> 39.5 us
  waiting for transfers between devices: 29.2 us -> 18.4 us
    all_to_all x1 -> x2, blocking collectives: 28.5 us -> 41.9 us  [the longest x1 30.5 us: per_device(): pieces = lax.all_to_all(pieces, (Z, 'state'), 0, 0, tiled=True)]
    all_to_all x2 -> x1, waiting for transfers between devices: 13.9 us -> 6.8 us  [per_device(): every_plane = lax.all_to_all(plane_summary, Z, 0, 0, tiled=True)]
    ppermute x3 -> x2, starting transfers between devices: 19.9 us -> 13.8 us  [swapped(): return lax.ppermute(x, 'state', [(0, 1), (1, 0)])]
    all_to_all x1, waiting for transfers between devices: 9.22 us -> 4.99 us  [per_device(): resid_all = lax.all_to_all(resid, YX, 0, 0, tiled=True)]
    all_to_all x1, starting transfers between devices: 7.58 us -> 3.57 us  [per_device(): mine = lax.all_to_all(by_sensor, YX, 0, 0, tiled=True)]
    ppermute x1, starting transfers between devices: 5.03 us -> 2.66 us  [per_device(): tails = lax.ppermute(tails, Z, [(i, i + 1) for i in range(planes - 1)])]
    all_to_all x1, starting transfers between devices: 5.85 us -> 3.57 us  [per_device(): resid_all = lax.all_to_all(resid, YX, 0, 0, tiled=True)]
    all_to_all x2 -> x1, starting transfers between devices: 10.8 us -> 12.7 us  [per_device(): every_plane = lax.all_to_all(plane_summary, Z, 0, 0, tiled=True)]
  transfers between devices with their start and end apart: 9 -> 7, of which waited for: 6 -> 5; matrix products, arithmetic and copies ran while one was open for 0% -> 2% of each run, Pallas kernels for 4% -> 4%
where the time goes in v2:
time: 111 us; the launch traced here: 110 us
  blocking collectives  41.9 us (38%)
  starting transfers between devices  39.5 us (36%)
  waiting for transfers between devices  18.4 us (17%)
  Pallas kernels  6.99 us (6%)
  local copies, waits for them, and re-layouts  2.38 us (2%)
    all_to_all x1, blocking collectives, per_device(): pieces = lax.all_to_all(pieces, (Z, 'state'), 0, 0, tiled=True)  30.5 us
    ppermute x2, starting transfers between devices, swapped(): return lax.ppermute(x, 'state', [(0, 1), (1, 0)])  13.8 us
    all_to_all x1, starting transfers between devices, per_device(): every_plane = lax.all_to_all(plane_summary, Z, 0, 0, tiled=True)  12.7 us
    all_to_all x1, blocking collectives, per_device(): plane = lax.all_to_all(summary, YX, 0, 0, tiled=True)  11.3 us
    all_to_all x1, waiting for transfers between devices, per_device(): every_plane = lax.all_to_all(plane_summary, Z, 0, 0, tiled=True)  6.8 us
    all_to_all x1, waiting for transfers between devices, per_device(): resid_all = lax.all_to_all(resid, YX, 0, 0, tiled=True)  4.99 us
    all_to_all x1, starting transfers between devices, per_device(): resid_all = lax.all_to_all(resid, YX, 0, 0, tiled=True)  3.57 us
    all_to_all x1, starting transfers between devices, per_device(): mine = lax.all_to_all(by_sensor, YX, 0, 0, tiled=True)  3.57 us
  transfers between devices with their start and end apart: 7, of which 5 were waited for; matrix products, arithmetic and copies ran while one was open for 2% of the time, Pallas kernels for 4%

profile of v2, /device:TPU:1, one launch (start us, length us, event | category | flops | bytes accessed | tf_op | source)
XLA Modules:
  0.0 110.1 jit_solution(12887285881659606672)
XLA Ops:
  0.6 0.0 copy-start.1
  0.6 0.0 copy-start.3
  0.7 0.0 copy-start.4
  0.7 0.0 copy-start
  0.7 9.1 %collective-permute-start = (bf16[128,2048]{1,0:T(8,128)(2,1)}, bf16[128,2048]{1,0:T(8,128)(2,1)}, u32[]{:S(2)}, u32[]{:S(2)}) collective-permute-start(bf16[128,2048]{1,0:T(8,128)(2,1)} %own.1), channel_id=1, source_target_pairs={{0,1},{1,0},{2,3},{3,2},{4,5},{5,4},{6,7},{7,6},{8,9},{9,8},{10,11... | collective-permute-start | bytes 1572872 | tf_op jit(solution)/shard_map/ppermute | solution.py:197
  9.7 1.3 %copy.12 = bf16[128,2048]{0,1:T(8,128)(2,1)S(1)} copy(bf16[128,2048]{1,0:T(8,128)(2,1)} %own.1) | data formatting | bytes 1048576 | tf_op args[0]
  11.0 0.9 copy.15
  12.0 3.6 %all-to-all-start = ((bf16[16,128,128]{2,1,0:T(8,128)(2,1)}), bf16[16,128,128]{2,1,0:T(8,128)(2,1)S(1)}, u32[]{:S(2)}, u32[]{:S(2)}) async-start(bf16[16,128,128]{2,1,0:T(8,128)(2,1)} %bitcast.20), calls=%async_computation | async-start | bytes 1048576 | tf_op jit(solution)/shard_map/all_to_all | solution.py:215
  15.6 0.0 copy-start.2
  15.6 0.1 copy.10
  15.7 0.1 pad_add_fusion.where
  15.8 0.0 collective-permute-done.other
  15.8 1.8 %shard_map.68.u = f32[128,256]{1,0:T(8,128)S(1)} custom-call(s32[5]{0:T(128)S(1)} %pad_add_fusion.where, bf16[128,2048]{1,0:T(8,128)(2,1)S(1)} %copy-done.1, bf16[128,2048]{1,0:T(8,128)(2,1)} %collective-permute-done.other, bf16[2,128,4096]{2,1,0:T(8,128)(2,1)S(1)} %copy-done), custom_call_target="tpu_custom_call" | custom-call | tf_op jit(solution)/shard_map/pallas_call | solution.py:221
  17.6 3.1 %collective-permute-start.1 = (f32[64,256]{1,0:T(8,128)S(1)}, f32[64,256]{1,0:T(8,128)S(1)}, u32[]{:S(2)}, u32[]{:S(2)}) collective-permute-start(f32[64,256]{1,0:T(8,128)S(1)} %slice.12), channel_id=1, source_target_pairs={{0,2},{2,4},{4,6},{6,8},{8,10},{10,12},{12,14},{14,16},{16,18},{18... | collective-permute-start | bytes 196616 | tf_op jit(solution)/shard_map/ppermute | solution.py:224
  20.7 0.1 sqrt_bitcast_fusion
  20.8 2.2 %collective-permute-done.1.tail = f32[64,256]{1,0:T(8,128)S(1)} collective-permute-done((f32[64,256]{1,0:T(8,128)S(1)}, f32[64,256]{1,0:T(8,128)S(1)}, u32[]{:S(2)}, u32[]{:S(2)}) %collective-permute-start.1) | collective-permute-done | bytes 65568 | tf_op jit(solution)/shard_map/ppermute | solution.py:224
  23.0 0.8 shard_map.69
  23.9 3.1 %all-to-all-done.own = bf16[16,128,128]{2,1,0:T(8,128)(2,1)S(1)} async-done(((bf16[16,128,128]{2,1,0:T(8,128)(2,1)}), bf16[16,128,128]{2,1,0:T(8,128)(2,1)S(1)}, u32[]{:S(2)}, u32[]{:S(2)}) %all-to-all-start) | async-done | bytes 524320 | tf_op jit(solution)/shard_map/all_to_all | solution.py:215
  26.9 11.3 %all_to_all.25.every.plane = f32[16,8,128]{2,1,0:T(8,128)S(1)} all-to-all(f32[16,8,128]{2,1,0:T(8,128)S(1)} %get-tuple-element.10), channel_id=1, replica_groups=mesh['tm_0'=16,'tm_1'=4,'tm_2'=4,'state'=2] {'tm_1','tm_2'}, dimensions={0} | all-to-all | bytes 131072 | tf_op jit(solution)/shard_map/all_to_all | solution.py:236
  38.3 0.7 shard_map.70
  38.9 12.7 %all-to-all-start.2 = ((f32[16,8,128]{2,1,0:T(8,128)}), f32[16,8,128]{2,1,0:T(8,128)S(1)}, u32[]{:S(2)}, u32[]{:S(2)}) async-start(f32[16,8,128]{2,1,0:T(8,128)} %shard_map.70), calls=%async_computation.2 | async-start | bytes 131072 | tf_op jit(solution)/shard_map/all_to_all | solution.py:240
  51.7 4.8 %collective-permute-start.2 = (bf16[16,128,128]{2,1,0:T(8,128)(2,1)S(1)}, bf16[16,128,128]{2,1,0:T(8,128)(2,1)S(1)}, u32[]{:S(2)}, u32[]{:S(2)}) collective-permute-start(bf16[16,128,128]{2,1,0:T(8,128)(2,1)S(1)} %all-to-all-done.own), channel_id=1, source_target_pairs={{0,1},{1,0},{2,3},{3,2},{4,5},{5,4},{6,7},{7,6},{8,9},{9,8},{10,11... | collective-permute-start | bytes 1572872 | tf_op jit(solution)/shard_map/ppermute | solution.py:197
  56.4 6.8 %all-to-all-done.2.planes = f32[16,8,128]{2,1,0:T(8,128)S(1)} async-done(((f32[16,8,128]{2,1,0:T(8,128)}), f32[16,8,128]{2,1,0:T(8,128)S(1)}, u32[]{:S(2)}, u32[]{:S(2)}) %all-to-all-start.2) | async-done | bytes 65568 | tf_op jit(solution)/shard_map/all_to_all | solution.py:240
  63.2 1.5 %shard_map.71 = (f32[128,128]{1,0:T(8,128)}, bf16[16,128,128]{2,1,0:T(8,128)(2,1)}) custom-call(s32[5]{0:T(128)S(1)} %pad_add_fusion.where, f32[16,8,128]{2,1,0:T(8,128)S(1)} %all_to_all.25.every.plane, f32[16,8,128]{2,1,0:T(8,128)S(1)} %all-to-all-done.2.planes, f32[6,128,128]{2,1,0:T(8,128)S(1)} %get-tuple-element.11.keep, ...), custom_call_target="tpu_custom_call" | custom-call | tf_op jit(solution)/shard_map/pallas_call | solution.py:241
  64.8 3.6 %all-to-all-start.3 = ((bf16[16,128,128]{2,1,0:T(8,128)(2,1)}), bf16[16,128,128]{2,1,0:T(8,128)(2,1)S(1)}, u32[]{:S(2)}, u32[]{:S(2)}) async-start(bf16[16,128,128]{2,1,0:T(8,128)(2,1)} %get-tuple-element.14), calls=%async_computation.3 | async-start | bytes 1048576 | tf_op jit(solution)/shard_map/all_to_all | solution.py:249
  68.4 0.0 collective-permute-done.2.other
  68.4 2.7 %collective-permute-start.3 = (bf16[2,128,128]{2,1,0:T(8,128)(2,1)S(1)}, bf16[2,128,128]{2,1,0:T(8,128)(2,1)S(1)}, u32[]{:S(2)}, u32[]{:S(2)}) collective-permute-start(bf16[2,128,128]{2,1,0:T(8,128)(2,1)S(1)} %pad_maximum_fusion), channel_id=1, source_target_pairs={{0,32},{32,64},{64,96},{96,128},{128,160},{160,192},{192,224},{224... | collective-permute-start | bytes 196616 | tf_op jit(solution)/shard_map/ppermute | solution.py:251
  71.1 1.3 %collective-permute-done.3.tails = bf16[2,128,128]{2,1,0:T(8,128)(2,1)S(1)} collective-permute-done((bf16[2,128,128]{2,1,0:T(8,128)(2,1)S(1)}, bf16[2,128,128]{2,1,0:T(8,128)(2,1)S(1)}, u32[]{:S(2)}, u32[]{:S(2)}) %collective-permute-start.3) | collective-permute-done | bytes 65568 | tf_op jit(solution)/shard_map/ppermute | solution.py:251
  72.4 5.0 %all-to-all-done.3.resid = bf16[16,128,128]{2,1,0:T(8,128)(2,1)S(1)} async-done(((bf16[16,128,128]{2,1,0:T(8,128)(2,1)}), bf16[16,128,128]{2,1,0:T(8,128)(2,1)S(1)}, u32[]{:S(2)}, u32[]{:S(2)}) %all-to-all-start.3) | async-done | bytes 524320 | tf_op jit(solution)/shard_map/all_to_all | solution.py:249
  77.4 1.6 %shard_map.72 = f32[16,2,8,256]{3,2,1,0:T(8,128)S(1)} custom-call(s32[5]{0:T(128)S(1)} %pad_add_fusion.where, bf16[2,128,128]{2,1,0:T(8,128)(2,1)S(1)} %collective-permute-done.3.tails, bf16[16,128,128]{2,1,0:T(8,128)(2,1)S(1)} %all-to-all-done.own, bf16[16,128,128]{2,1,0:T(8,128)(2,1)S(1)} %collective-permute-done.2.other, ...), custom_call_target="tpu_custom_call" | custom-call | tf_op jit(solution)/shard_map/pallas_call | solution.py:252
  79.0 30.5 %all_to_all.26.pieces = f32[32,8,256]{2,1,0:T(8,128)S(1)} all-to-all(f32[32,8,256]{2,1,0:T(8,128)S(1)} %bitcast.17), channel_id=1, replica_groups=mesh['tm_0'=16,'tm_1'=4,'tm_2'=4,'state'=2] {'tm_0','state'}, dimensions={0} | all-to-all | bytes 524288 | tf_op jit(solution)/shard_map/all_to_all | solution.py:259
  109.5 0.6 shard_map.73
  (9 shorter events, 0.0 us)
Async XLA Ops:
  0.6 15.2 %copy-start.1 = (bf16[128,2048]{1,0:T(8,128)(2,1)S(1)}, bf16[128,2048]{1,0:T(8,128)(2,1)}, u32[]{:S(2)}) copy-start(bf16[128,2048]{1,0:T(8,128)(2,1)} %own.1) | copy-start | bytes 1572868
  0.6 15.0 %copy-start.3 = (f32[128,128]{1,0:T(8,128)S(1)}, f32[128,128]{1,0:T(8,128)}, u32[]{:S(2)}) copy-start(f32[128,128]{1,0:T(8,128)} %param.7) | copy-start | bytes 196612
  0.7 15.1 %copy-start.4 = (s32[2]{0:T(128)S(1)}, s32[2]{0:T(128)}, u32[]{:S(2)}) copy-start(s32[2]{0:T(128)} %param.9) | copy-start | bytes 28
  0.7 15.1 %copy-start = (bf16[2,128,4096]{2,1,0:T(8,128)(2,1)S(1)}, bf16[2,128,4096]{2,1,0:T(8,128)(2,1)}, u32[]{:S(2)}) copy-start(bf16[2,128,4096]{2,1,0:T(8,128)(2,1)} %gain.1) | copy-start | bytes 6291460
  0.7 15.1 %collective-permute-start = (bf16[128,2048]{1,0:T(8,128)(2,1)}, bf16[128,2048]{1,0:T(8,128)(2,1)}, u32[]{:S(2)}, u32[]{:S(2)}) collective-permute-start(bf16[128,2048]{1,0:T(8,128)(2,1)} %own.1), channel_id=1, source_target_pairs={{0,1},{1,0},{2,3},{3,2},{4,5},{5,4},{6,7},{7,6},{8,9},{9,8},{10,11... | collective-permute-start | bytes 1572872 | tf_op jit(solution)/shard_map/ppermute | solution.py:197
  12.0 14.9 %all-to-all-start = ((bf16[16,128,128]{2,1,0:T(8,128)(2,1)}), bf16[16,128,128]{2,1,0:T(8,128)(2,1)S(1)}, u32[]{:S(2)}, u32[]{:S(2)}) async-start(bf16[16,128,128]{2,1,0:T(8,128)(2,1)} %bitcast.20), calls=%async_computation | async-start | bytes 1048576 | tf_op jit(solution)/shard_map/all_to_all | solution.py:215
  15.6 7.5 %copy-start.2 = (f32[128]{0:T(128)S(1)}, f32[128]{0:T(128)}, u32[]{:S(2)}) copy-start(f32[128]{0:T(128)} %param.8) | copy-start | bytes 1540
  17.6 5.4 %collective-permute-start.1 = (f32[64,256]{1,0:T(8,128)S(1)}, f32[64,256]{1,0:T(8,128)S(1)}, u32[]{:S(2)}, u32[]{:S(2)}) collective-permute-start(f32[64,256]{1,0:T(8,128)S(1)} %slice.12), channel_id=1, source_target_pairs={{0,2},{2,4},{4,6},{6,8},{8,10},{10,12},{12,14},{14,16},{16,18},{18... | collective-permute-start | bytes 196616 | tf_op jit(solution)/shard_map/ppermute | solution.py:224
  38.9 24.3 %all-to-all-start.2 = ((f32[16,8,128]{2,1,0:T(8,128)}), f32[16,8,128]{2,1,0:T(8,128)S(1)}, u32[]{:S(2)}, u32[]{:S(2)}) async-start(f32[16,8,128]{2,1,0:T(8,128)} %shard_map.70), calls=%async_computation.2 | async-start | bytes 131072 | tf_op jit(solution)/shard_map/all_to_all | solution.py:240
  51.7 16.7 %collective-permute-start.2 = (bf16[16,128,128]{2,1,0:T(8,128)(2,1)S(1)}, bf16[16,128,128]{2,1,0:T(8,128)(2,1)S(1)}, u32[]{:S(2)}, u32[]{:S(2)}) collective-permute-start(bf16[16,128,128]{2,1,0:T(8,128)(2,1)S(1)} %all-to-all-done.own), channel_id=1, source_target_pairs={{0,1},{1,0},{2,3},{3,2},{4,5},{5,4},{6,7},{7,6},{8,9},{9,8},{10,11... | collective-permute-start | bytes 1572872 | tf_op jit(solution)/shard_map/ppermute | solution.py:197
  64.8 12.6 %all-to-all-start.3 = ((bf16[16,128,128]{2,1,0:T(8,128)(2,1)}), bf16[16,128,128]{2,1,0:T(8,128)(2,1)S(1)}, u32[]{:S(2)}, u32[]{:S(2)}) async-start(bf16[16,128,128]{2,1,0:T(8,128)(2,1)} %get-tuple-element.14), calls=%async_computation.3 | async-start | bytes 1048576 | tf_op jit(solution)/shard_map/all_to_all | solution.py:249
  68.4 4.0 %collective-permute-start.3 = (bf16[2,128,128]{2,1,0:T(8,128)(2,1)S(1)}, bf16[2,128,128]{2,1,0:T(8,128)(2,1)S(1)}, u32[]{:S(2)}, u32[]{:S(2)}) collective-permute-start(bf16[2,128,128]{2,1,0:T(8,128)(2,1)S(1)} %pad_maximum_fusion), channel_id=1, source_target_pairs={{0,32},{32,64},{64,96},{96,128},{128,160},{160,192},{192,224},{224... | collective-permute-start | bytes 196616 | tf_op jit(solution)/shard_map/ppermute | solution.py:251

commit v3 on v2

--- a/solution.py
+++ b/solution.py
@@ -68,7 +68,7 @@
         )
 
 
-def local_body(where, u, tail, decay_ref, scale, leak, keep, summary, ext):
+def local_body(where, u, tail, decay_ref, scale, leak, by_sensor, keep, sent, ext):
     frames, modes = decay_ref.shape
     ext[:DMAX] = tail[...]
     ext[DMAX:] = u[...]
@@ -88,11 +88,25 @@
     keep[3] = base
     keep[4] = slope
     keep[5] = drive
-    summary[...] = jnp.zeros_like(summary)
     rows = [prods[-1:], offsets[-1:], links[:1], base[:1], slope[:1], decay[-1:]]
-    for r, row in enumerate(rows):
-        for i in range(summary.shape[0]):
-            summary[i, r : r + 1] = row
+    rest = jnp.concatenate(rows + [jnp.zeros((2, modes), F32)], 0)
+    frames_rows = by_sensor.shape[1]
+    parts = []
+    for _ in range(3):
+        part = rest.astype(BF16)
+        parts.append(part.astype(F32))
+        rest = rest - parts[-1]
+    coded = jnp.concatenate(parts, 0).astype(BF16)
+    for i in range(sent.shape[0]):
+        sent[i, :frames_rows] = by_sensor[i]
+        sent[i, frames_rows:] = coded
+
+
+def decoded(every, out):
+    at = every.shape[1] - 24
+    for i in range(every.shape[0]):
+        rows = every[i, at:].astype(F32)
+        out[i] = rows[:8] + rows[8:16] + rows[16:]
 
 
 def joined(first, second):
@@ -105,8 +119,9 @@
     return tuple(ref[i, r : r + 1] for r in range(5))
 
 
-def plane_body(every, out):
-    n = every.shape[0]
+def plane_body(sent, every, out):
+    n = sent.shape[0]
+    decoded(sent, every)
     parts = [five(every, i) for i in range(n)]
     while len(parts) > 1:
         parts = [joined(parts[i], parts[i + 1]) for i in range(0, len(parts), 2)]
@@ -171,7 +186,7 @@
             padded[b * frames : (b + 1) * frames, k * modes : (k + 1) * modes] = moved.astype(BF16)
     rhs = padded[...]
     for which, rows in enumerate((own, other)):
-        lhs = jnp.concatenate([tails[which]] + [rows[i] for i in range(blocks)], 1)
+        lhs = jnp.concatenate([tails[which]] + [rows[i, :-24] for i in range(blocks)], 1)
         sums = jnp.dot(lhs, rhs, preferred_element_type=F32)
         half = jnp.where(where[2] == which, 0, 1)
         for i in range(out.shape[0]):
@@ -210,9 +225,6 @@
     )
     other = swapped(record)
     group = sensors // planes // blocks
-    by_sensor = record.T.reshape(planes, blocks, group, frames).swapaxes(0, 1)
-    by_sensor = by_sensor.reshape(blocks, planes * group, frames)
-    mine = lax.all_to_all(by_sensor, YX, 0, 0, tiled=True)
     rate_t = rate.T
     decay = jnp.exp(-rate_t)
     scale = jnp.sqrt(-jnp.expm1(-2.0 * rate_t))
@@ -222,21 +234,28 @@
         where, record, other, gain
     )
     u_tail = lax.ppermute(u[frames - DMAX :], TM, [(i, i + 1) for i in range(planes * blocks - 1)])
-    keep, summary = call(
+    by_sensor = behind(record, u).T.reshape(planes, blocks, group, frames).swapaxes(0, 1)
+    by_sensor = by_sensor.reshape(blocks, planes * group, frames)
+    keep, sent = call(
         local_body,
         (
             jax.ShapeDtypeStruct((6, frames, modes), F32),
-            jax.ShapeDtypeStruct((blocks, 8, modes), F32),
+            jax.ShapeDtypeStruct((blocks, planes * group + 24, frames), BF16),
         ),
         scratch=[pltpu.VMEM((DMAX + frames, TAPS * modes), F32)],
-        n_in=6,
-    )(where, u, u_tail, decay, scale, leak_row)
-    summary, mine = lax.optimization_barrier((summary, mine))
+        n_in=7,
+    )(where, u, u_tail, decay, scale, leak_row, by_sensor)
+    mine = lax.all_to_all(sent, YX, 0, 0, tiled=True)
+    plane, plane_summary = call(
+        plane_body,
+        (
+            jax.ShapeDtypeStruct((blocks, 8, modes), F32),
+            jax.ShapeDtypeStruct((planes, 8, modes), F32),
+        ),
+        smem=(),
+        n_in=1,
+    )(mine)
     theirs = swapped(mine)
-    plane = lax.all_to_all(summary, YX, 0, 0, tiled=True)
-    plane_summary = call(
-        plane_body, jax.ShapeDtypeStruct((planes, 8, modes), F32), smem=(), n_in=1
-    )(plane)
     every_plane = lax.all_to_all(plane_summary, Z, 0, 0, tiled=True)
     smoothed, resid = call(
         finish_body,
@@ -247,7 +266,7 @@
         n_in=6,
     )(where, plane, every_plane, keep, decay, leak_row)
     resid_all = lax.all_to_all(resid, YX, 0, 0, tiled=True)
-    tails = behind(jnp.stack([mine[-1], theirs[-1]]), resid)
+    tails = behind(jnp.stack([mine[-1, :-24], theirs[-1, :-24]]), resid)
     tails = lax.ppermute(tails, Z, [(i, i + 1) for i in range(planes - 1)])
     partial = call(
         gradient_body,

time: 111 us -> 112 us (level)
  blocking collectives: 41.9 us -> 71 us
  starting transfers between devices: 39.5 us -> 21.2 us
  waiting for transfers between devices: 18.4 us -> 7.64 us
  local copies, waits for them, and re-layouts: 2.38 us -> 3.98 us
    all_to_all x1 -> x2, blocking collectives: 11.3 us -> 42.1 us  [the longest x1 27.8 us: per_device(): every_plane = lax.all_to_all(plane_summary, Z, 0, 0, tiled=True)]
    all_to_all x2 -> x0, starting transfers between devices: 16.3 us -> none  [the longest x1 12.7 us: per_device(): every_plane = lax.all_to_all(plane_summary, Z, 0, 0, tiled=True)]
    all_to_all x2 -> x0, waiting for transfers between devices: 9.88 us -> none  [the longest x1 6.8 us: per_device(): every_plane = lax.all_to_all(plane_summary, Z, 0, 0, tiled=True)]
    unnamed x12 -> x9, local copies, waits for them, and re-layouts: 1.42 us -> 3.57 us
    ppermute x1, starting transfers between devices: 3.15 us -> 1.29 us  [per_device(): lax.ppermute(u[frames - DMAX:], TM, [(i, i + 1) for i in range(planes * b...]
    all_to_all x1, blocking collectives: 30.5 us -> 29 us  [per_device(): pieces = lax.all_to_all(pieces, (Z, 'state'), 0, 0, tiled=True)]
    ppermute x1, waiting for transfers between devices: 2.23 us -> 0.83 us  [per_device(): lax.ppermute(u[frames - DMAX:], TM, [(i, i + 1) for i in range(planes * b...]
  transfers between devices with their start and end apart: 7 -> 5, of which waited for: 5 -> 3; matrix products, arithmetic and copies ran while one was open for 2% -> 2% of each run, Pallas kernels for 4% -> 1%
where the time goes in v3:
time: 112 us; the launch traced here: 111 us
  blocking collectives  71 us (63%)
  starting transfers between devices  21.2 us (19%)
  waiting for transfers between devices  7.64 us (7%)
  Pallas kernels  5.88 us (5%)
  local copies, waits for them, and re-layouts  3.98 us (4%)
    all_to_all x1, blocking collectives, per_device(): pieces = lax.all_to_all(pieces, (Z, 'state'), 0, 0, tiled=True)  29 us
    all_to_all x1, blocking collectives, per_device(): every_plane = lax.all_to_all(plane_summary, Z, 0, 0, tiled=True)  27.8 us
    all_to_all x1, blocking collectives, per_device(): mine = lax.all_to_all(sent, YX, 0, 0, tiled=True)  14.3 us
    ppermute x2, starting transfers between devices, swapped(): return lax.ppermute(x, 'state', [(0, 1), (1, 0)])  13.6 us
    all_to_all x1, waiting for transfers between devices, per_device(): resid_all = lax.all_to_all(resid, YX, 0, 0, tiled=True)  5.47 us
    all_to_all x1, starting transfers between devices, per_device(): resid_all = lax.all_to_all(resid, YX, 0, 0, tiled=True)  3.57 us
    unnamed x9, local copies, waits for them, and re-layouts  3.57 us
    ppermute x1, starting transfers between devices, per_device(): tails = lax.ppermute(tails, Z, [(i, i + 1) for i in range(planes - 1)])  2.74 us
  transfers between devices with their start and end apart: 5, of which 3 were waited for; matrix products, arithmetic and copies ran while one was open for 2% of the time, Pallas kernels for 1%

profile of v3, /device:TPU:1, one launch (start us, length us, event | category | flops | bytes accessed | tf_op | source)
XLA Modules:
  0.0 111.3 jit_solution(10879233597274990251)
XLA Ops:
  0.6 8.8 %collective-permute-start = (bf16[128,2048]{1,0:T(8,128)(2,1)}, bf16[128,2048]{1,0:T(8,128)(2,1)S(1)}, u32[]{:S(2)}, u32[]{:S(2)}) collective-permute-start(bf16[128,2048]{1,0:T(8,128)(2,1)} %own.1), channel_id=1, source_target_pairs={{0,1},{1,0},{2,3},{3,2},{4,5},{5,4},{6,7},{7,6},{8,9},{9,8},{10,11... | collective-permute-start | bytes 1572872 | tf_op jit(solution)/shard_map/ppermute | solution.py:212
  9.4 0.9 copy.10
  10.4 0.7 pad_add_fusion.where
  11.1 0.0 collective-permute-done.other
  11.2 0.0 copy-start
  11.2 1.6 %copy-done = bf16[2,128,4096]{2,1,0:T(8,128)(2,1)S(1)} copy-done((bf16[2,128,4096]{2,1,0:T(8,128)(2,1)S(1)}, bf16[2,128,4096]{2,1,0:T(8,128)(2,1)}, u32[]{:S(2)}) %copy-start) | copy-done | bytes 2097176
  12.7 0.0 copy-start.1
  12.7 1.0 copy-done.1
  13.8 0.0 copy-start.2
  13.8 0.0 copy-start.3
  13.8 1.2 %shard_map.68.u = f32[128,256]{1,0:T(8,128)S(1)} custom-call(s32[5]{0:T(128)S(1)} %pad_add_fusion.where, bf16[128,2048]{1,0:T(8,128)(2,1)S(1)} %copy-done.1, bf16[128,2048]{1,0:T(8,128)(2,1)S(1)} %collective-permute-done.other, bf16[2,128,4096]{2,1,0:T(8,128)(2,1)S(1)} %copy-done), custom_call_target="tpu_custom_call" | custom-call | tf_op jit(solution)/shard_map/pallas_call | solution.py:233
  15.1 1.3 %collective-permute-start.1 = (f32[64,256]{1,0:T(8,128)S(1)}, f32[64,256]{1,0:T(8,128)S(1)}, u32[]{:S(2)}, u32[]{:S(2)}) collective-permute-start(f32[64,256]{1,0:T(8,128)S(1)} %slice.12), channel_id=1, source_target_pairs={{0,2},{2,4},{4,6},{6,8},{8,10},{10,12},{12,14},{14,16},{16,18},{18... | collective-permute-start | bytes 196616 | tf_op jit(solution)/shard_map/ppermute | solution.py:236
  16.4 0.1 sqrt_bitcast_fusion
  16.4 0.0 copy-done.2
  16.4 0.3 copy.12
  16.7 0.1 copy.15
  16.8 0.8 collective-permute-done.1.tail
  17.7 0.0 copy-done.3
  17.7 0.8 shard_map.69
  18.5 14.3 %all_to_all.20.sent.own = bf16[16,152,128]{2,1,0:T(8,128)(2,1)S(1)} all-to-all(bf16[16,152,128]{2,1,0:T(8,128)(2,1)S(1)} %get-tuple-element.11), channel_id=1, replica_groups=mesh['tm_0'=16,'tm_1'=4,'tm_2'=4,'state'=2] {'tm_1','tm_2'}, dimensions={0} | all-to-all | bytes 1245184 | tf_op jit(solution)/shard_map/all_to_all | solution.py:248
  32.8 4.8 %collective-permute-start.2 = (bf16[16,152,128]{2,1,0:T(8,128)(2,1)S(1)}, bf16[16,152,128]{2,1,0:T(8,128)(2,1)S(1)}, u32[]{:S(2)}, u32[]{:S(2)}) collective-permute-start(bf16[16,152,128]{2,1,0:T(8,128)(2,1)S(1)} %all_to_all.20.sent.own), channel_id=1, source_target_pairs={{0,1},{1,0},{2,3},{3,2},{4,5},{5,4},{6,7},{7,6},{8,9},{9,8},{10,11... | collective-permute-start | bytes 1867784 | tf_op jit(solution)/shard_map/ppermute | solution.py:212
  37.6 0.1 shard_map.70
  37.7 27.8 %all_to_all.21.planes = f32[16,8,128]{2,1,0:T(8,128)S(1)} all-to-all(f32[16,8,128]{2,1,0:T(8,128)S(1)} %get-tuple-element.13), channel_id=1, replica_groups=mesh['tm_0'=16,'tm_1'=4,'tm_2'=4,'state'=2] {'tm_0'}, dimensions={0} | all-to-all | bytes 131072 | tf_op jit(solution)/shard_map/all_to_all | solution.py:259
  65.4 1.5 %shard_map.71 = (f32[128,128]{1,0:T(8,128)}, bf16[16,128,128]{2,1,0:T(8,128)(2,1)}) custom-call(s32[5]{0:T(128)S(1)} %pad_add_fusion.where, f32[16,8,128]{2,1,0:T(8,128)S(1)} %get-tuple-element.12.plane, f32[16,8,128]{2,1,0:T(8,128)S(1)} %all_to_all.21.planes, f32[6,128,128]{2,1,0:T(8,128)S(1)} %get-tuple-element.14.keep, ...), custom_call_target="tpu_custom_call" | custom-call | tf_op jit(solution)/shard_map/pallas_call | solution.py:260
  67.0 3.6 %all-to-all-start.2 = ((bf16[16,128,128]{2,1,0:T(8,128)(2,1)}), bf16[16,128,128]{2,1,0:T(8,128)(2,1)S(1)}, u32[]{:S(2)}, u32[]{:S(2)}) async-start(bf16[16,128,128]{2,1,0:T(8,128)(2,1)} %get-tuple-element.16), calls=%async_computation.2 | async-start | bytes 1048576 | tf_op jit(solution)/shard_map/all_to_all | solution.py:268
  70.5 0.0 collective-permute-done.2.other
  70.6 2.7 %collective-permute-start.3 = (bf16[2,128,128]{2,1,0:T(8,128)(2,1)S(1)}, bf16[2,128,128]{2,1,0:T(8,128)(2,1)S(1)}, u32[]{:S(2)}, u32[]{:S(2)}) collective-permute-start(bf16[2,128,128]{2,1,0:T(8,128)(2,1)S(1)} %pad_maximum_fusion), channel_id=1, source_target_pairs={{0,32},{32,64},{64,96},{96,128},{128,160},{160,192},{192,224},{224... | collective-permute-start | bytes 196616 | tf_op jit(solution)/shard_map/ppermute | solution.py:270
  73.3 1.3 %collective-permute-done.3.tails = bf16[2,128,128]{2,1,0:T(8,128)(2,1)S(1)} collective-permute-done((bf16[2,128,128]{2,1,0:T(8,128)(2,1)S(1)}, bf16[2,128,128]{2,1,0:T(8,128)(2,1)S(1)}, u32[]{:S(2)}, u32[]{:S(2)}) %collective-permute-start.3) | collective-permute-done | bytes 65568 | tf_op jit(solution)/shard_map/ppermute | solution.py:270
  74.6 5.5 %all-to-all-done.2.resid = bf16[16,128,128]{2,1,0:T(8,128)(2,1)S(1)} async-done(((bf16[16,128,128]{2,1,0:T(8,128)(2,1)}), bf16[16,128,128]{2,1,0:T(8,128)(2,1)S(1)}, u32[]{:S(2)}, u32[]{:S(2)}) %all-to-all-start.2) | async-done | bytes 524320 | tf_op jit(solution)/shard_map/all_to_all | solution.py:268
  80.1 1.6 %shard_map.72 = f32[16,2,8,256]{3,2,1,0:T(8,128)S(1)} custom-call(s32[5]{0:T(128)S(1)} %pad_add_fusion.where, bf16[2,128,128]{2,1,0:T(8,128)(2,1)S(1)} %collective-permute-done.3.tails, bf16[16,152,128]{2,1,0:T(8,128)(2,1)S(1)} %all_to_all.20.sent.own, bf16[16,152,128]{2,1,0:T(8,128)(2,1)S(1)} %collective-permute-done.2.other, ...), custom_call_target="tpu_custom_call" | custom-call | tf_op jit(solution)/shard_map/pallas_call | solution.py:271
  81.7 29.0 %all_to_all.22.pieces = f32[32,8,256]{2,1,0:T(8,128)S(1)} all-to-all(f32[32,8,256]{2,1,0:T(8,128)S(1)} %bitcast.18), channel_id=1, replica_groups=mesh['tm_0'=16,'tm_1'=4,'tm_2'=4,'state'=2] {'tm_0','state'}, dimensions={0} | all-to-all | bytes 524288 | tf_op jit(solution)/shard_map/all_to_all | solution.py:278
  110.7 0.6 shard_map.73
  (4 shorter events, 0.0 us)
Async XLA Ops:
  0.6 10.5 %collective-permute-start = (bf16[128,2048]{1,0:T(8,128)(2,1)}, bf16[128,2048]{1,0:T(8,128)(2,1)S(1)}, u32[]{:S(2)}, u32[]{:S(2)}) collective-permute-start(bf16[128,2048]{1,0:T(8,128)(2,1)} %own.1), channel_id=1, source_target_pairs={{0,1},{1,0},{2,3},{3,2},{4,5},{5,4},{6,7},{7,6},{8,9},{9,8},{10,11... | collective-permute-start | bytes 1572872 | tf_op jit(solution)/shard_map/ppermute | solution.py:212
  11.2 1.6 %copy-start = (bf16[2,128,4096]{2,1,0:T(8,128)(2,1)S(1)}, bf16[2,128,4096]{2,1,0:T(8,128)(2,1)}, u32[]{:S(2)}) copy-start(bf16[2,128,4096]{2,1,0:T(8,128)(2,1)} %gain.1) | copy-start | bytes 6291460
  12.7 1.0 copy-start.1
  13.8 2.6 %copy-start.2 = (bf16[128,2048]{1,0:T(8,128)(2,1)S(1)}, bf16[128,2048]{1,0:T(8,128)(2,1)}, u32[]{:S(2)}) copy-start(bf16[128,2048]{1,0:T(8,128)(2,1)} %own.1) | copy-start | bytes 1572868
  13.8 3.9 %copy-start.3 = (f32[128]{0:T(128)S(1)}, f32[128]{0:T(128)}, u32[]{:S(2)}) copy-start(f32[128]{0:T(128)} %param.8) | copy-start | bytes 1540
  15.1 2.6 %collective-permute-start.1 = (f32[64,256]{1,0:T(8,128)S(1)}, f32[64,256]{1,0:T(8,128)S(1)}, u32[]{:S(2)}, u32[]{:S(2)}) collective-permute-start(f32[64,256]{1,0:T(8,128)S(1)} %slice.12), channel_id=1, source_target_pairs={{0,2},{2,4},{4,6},{6,8},{8,10},{10,12},{12,14},{14,16},{16,18},{18... | collective-permute-start | bytes 196616 | tf_op jit(solution)/shard_map/ppermute | solution.py:236
  32.8 37.7 %collective-permute-start.2 = (bf16[16,152,128]{2,1,0:T(8,128)(2,1)S(1)}, bf16[16,152,128]{2,1,0:T(8,128)(2,1)S(1)}, u32[]{:S(2)}, u32[]{:S(2)}) collective-permute-start(bf16[16,152,128]{2,1,0:T(8,128)(2,1)S(1)} %all_to_all.20.sent.own), channel_id=1, source_target_pairs={{0,1},{1,0},{2,3},{3,2},{4,5},{5,4},{6,7},{7,6},{8,9},{9,8},{10,11... | collective-permute-start | bytes 1867784 | tf_op jit(solution)/shard_map/ppermute | solution.py:212
  67.0 13.2 %all-to-all-start.2 = ((bf16[16,128,128]{2,1,0:T(8,128)(2,1)}), bf16[16,128,128]{2,1,0:T(8,128)(2,1)S(1)}, u32[]{:S(2)}, u32[]{:S(2)}) async-start(bf16[16,128,128]{2,1,0:T(8,128)(2,1)} %get-tuple-element.16), calls=%async_computation.2 | async-start | bytes 1048576 | tf_op jit(solution)/shard_map/all_to_all | solution.py:268
  70.6 4.1 %collective-permute-start.3 = (bf16[2,128,128]{2,1,0:T(8,128)(2,1)S(1)}, bf16[2,128,128]{2,1,0:T(8,128)(2,1)S(1)}, u32[]{:S(2)}, u32[]{:S(2)}) collective-permute-start(bf16[2,128,128]{2,1,0:T(8,128)(2,1)S(1)} %pad_maximum_fusion), channel_id=1, source_target_pairs={{0,32},{32,64},{64,96},{96,128},{128,160},{160,192},{192,224},{224... | collective-permute-start | bytes 196616 | tf_op jit(solution)/shard_map/ppermute | solution.py:270

commit v4 on v3

--- a/solution.py
+++ b/solution.py
@@ -55,16 +55,24 @@
     return link, sums
 
 
-def taps_body(where, own, other, gain, out):
+def own_body(where, own, gain, out):
     modes = gain.shape[1]
     half = own.shape[1]
-    mine = pl.multiple_of(where[2] * half, half)
-    theirs = pl.multiple_of((1 - where[2]) * half, half)
+    at = pl.multiple_of(where[2] * half, half)
     for k in range(TAPS):
         out[:, k * modes : (k + 1) * modes] = lax.dot_general(
-            own[...], gain[k, :, pl.ds(mine, half)], NT, preferred_element_type=F32
-        ) + lax.dot_general(
-            other[...], gain[k, :, pl.ds(theirs, half)], NT, preferred_element_type=F32
+            own[...], gain[k, :, pl.ds(at, half)], NT, preferred_element_type=F32
+        )
+
+
+def rest_body(where, other, gain, part, out):
+    modes = gain.shape[1]
+    half = other.shape[1]
+    at = pl.multiple_of((1 - where[2]) * half, half)
+    for k in range(TAPS):
+        columns = slice(k * modes, (k + 1) * modes)
+        out[:, columns] = part[:, columns] + lax.dot_general(
+            other[...], gain[k, :, pl.ds(at, half)], NT, preferred_element_type=F32
         )
 
 
@@ -186,7 +194,7 @@
             padded[b * frames : (b + 1) * frames, k * modes : (k + 1) * modes] = moved.astype(BF16)
     rhs = padded[...]
     for which, rows in enumerate((own, other)):
-        lhs = jnp.concatenate([tails[which]] + [rows[i, :-24] for i in range(blocks)], 1)
+        lhs = jnp.concatenate([tails[which]] + [rows[i, : tails.shape[1]] for i in range(blocks)], 1)
         sums = jnp.dot(lhs, rhs, preferred_element_type=F32)
         half = jnp.where(where[2] == which, 0, 1)
         for i in range(out.shape[0]):
@@ -230,9 +238,9 @@
     scale = jnp.sqrt(-jnp.expm1(-2.0 * rate_t))
     leak_row = leak[None]
 
-    u = call(taps_body, jax.ShapeDtypeStruct((frames, TAPS * modes), F32), n_in=4)(
-        where, record, other, gain
-    )
+    both = jax.ShapeDtypeStruct((frames, TAPS * modes), F32)
+    part = call(own_body, both, n_in=3)(where, record, gain)
+    u = call(rest_body, both, n_in=4)(where, other, gain, part)
     u_tail = lax.ppermute(u[frames - DMAX :], TM, [(i, i + 1) for i in range(planes * blocks - 1)])
     by_sensor = behind(record, u).T.reshape(planes, blocks, group, frames).swapaxes(0, 1)
     by_sensor = by_sensor.reshape(blocks, planes * group, frames)
@@ -255,7 +263,7 @@
         smem=(),
         n_in=1,
     )(mine)
-    theirs = swapped(mine)
+    theirs = swapped(mine[:, :-24])
     every_plane = lax.all_to_all(plane_summary, Z, 0, 0, tiled=True)
     smoothed, resid = call(
         finish_body,
@@ -266,7 +274,7 @@
         n_in=6,
     )(where, plane, every_plane, keep, decay, leak_row)
     resid_all = lax.all_to_all(resid, YX, 0, 0, tiled=True)
-    tails = behind(jnp.stack([mine[-1, :-24], theirs[-1, :-24]]), resid)
+    tails = behind(jnp.stack([mine[-1, :-24], theirs[-1]]), resid)
     tails = lax.ppermute(tails, Z, [(i, i + 1) for i in range(planes - 1)])
     partial = call(
         gradient_body,

time: 112 us -> 111 us (level)
  blocking collectives: 71 us -> 45.1 us
  starting transfers between devices: 21.2 us -> 37.1 us
  waiting for transfers between devices: 7.64 us -> 14.9 us
  Pallas kernels: 5.88 us -> 7.21 us
    all_to_all x1 -> x0, blocking collectives: 27.8 us -> none  [per_device(): every_plane = lax.all_to_all(plane_summary, Z, 0, 0, tiled=True)]
    all_to_all x0 -> x1, starting transfers between devices: none -> 16.7 us  [per_device(): every_plane = lax.all_to_all(plane_summary, Z, 0, 0, tiled=True)]
    all_to_all x0 -> x1, waiting for transfers between devices: none -> 7.41 us  [per_device(): every_plane = lax.all_to_all(plane_summary, Z, 0, 0, tiled=True)]
    unnamed x9 -> x11, local copies, waits for them, and re-layouts: 3.57 us -> 4.15 us
  transfers between devices with their start and end apart: 5 -> 6, of which waited for: 3 -> 4; matrix products, arithmetic and copies ran while one was open for 2% -> 2% of each run, Pallas kernels for 1% -> 2%
where the time goes in v4:
time: 111 us
  blocking collectives  45.1 us (41%)
  starting transfers between devices  37.1 us (33%)
  waiting for transfers between devices  14.9 us (13%)
  Pallas kernels  7.21 us (6%)
  local copies, waits for them, and re-layouts  4.61 us (4%)
    all_to_all x1, blocking collectives, per_device(): pieces = lax.all_to_all(pieces, (Z, 'state'), 0, 0, tiled=True)  30 us
    all_to_all x1, starting transfers between devices, per_device(): every_plane = lax.all_to_all(plane_summary, Z, 0, 0, tiled=True)  16.7 us
    all_to_all x1, blocking collectives, per_device(): mine = lax.all_to_all(sent, YX, 0, 0, tiled=True)  15.1 us
    ppermute x2, starting transfers between devices, swapped(): return lax.ppermute(x, 'state', [(0, 1), (1, 0)])  12.9 us
    all_to_all x1, waiting for transfers between devices, per_device(): every_plane = lax.all_to_all(plane_summary, Z, 0, 0, tiled=True)  7.41 us
    all_to_all x1, waiting for transfers between devices, per_device(): resid_all = lax.all_to_all(resid, YX, 0, 0, tiled=True)  4.93 us
    unnamed x11, local copies, waits for them, and re-layouts  4.15 us
    all_to_all x1, starting transfers between devices, per_device(): resid_all = lax.all_to_all(resid, YX, 0, 0, tiled=True)  3.57 us
  transfers between devices with their start and end apart: 6, of which 4 were waited for; matrix products, arithmetic and copies ran while one was open for 2% of the time, Pallas kernels for 2%

profile of v4, /device:TPU:1, one launch (start us, length us, event | category | flops | bytes accessed | tf_op | source)
XLA Modules:
  0.0 110.5 jit_solution(6142477926989110803)
XLA Ops:
  0.6 8.8 %collective-permute-start = (bf16[128,2048]{1,0:T(8,128)(2,1)}, bf16[128,2048]{1,0:T(8,128)(2,1)S(1)}, u32[]{:S(2)}, u32[]{:S(2)}) collective-permute-start(bf16[128,2048]{1,0:T(8,128)(2,1)} %own.1), channel_id=1, source_target_pairs={{0,1},{1,0},{2,3},{3,2},{4,5},{5,4},{6,7},{7,6},{8,9},{9,8},{10,11... | collective-permute-start | bytes 1572872 | tf_op jit(solution)/shard_map/ppermute | solution.py:220
  9.4 0.9 copy.10
  10.4 0.7 pad_add_fusion.where
  11.1 1.6 %copy-done = bf16[2,128,4096]{2,1,0:T(8,128)(2,1)S(1)} copy-done((bf16[2,128,4096]{2,1,0:T(8,128)(2,1)S(1)}, bf16[2,128,4096]{2,1,0:T(8,128)(2,1)}, u32[]{:S(2)}) %copy-start) | copy-done | bytes 2097176
  12.7 1.0 copy-done.2
  13.8 1.0 shard_map.68.part
  14.7 0.0 copy-start.3
  14.7 0.0 copy-start.4
  14.8 0.0 collective-permute-done.other
  14.8 0.6 copy-done.1
  15.3 1.0 shard_map.69.u
  16.3 1.3 %collective-permute-start.1 = (f32[64,256]{1,0:T(8,128)S(1)}, f32[64,256]{1,0:T(8,128)S(1)}, u32[]{:S(2)}, u32[]{:S(2)}) collective-permute-start(f32[64,256]{1,0:T(8,128)S(1)} %slice.16), channel_id=1, source_target_pairs={{0,2},{2,4},{4,6},{6,8},{8,10},{10,12},{12,14},{14,16},{16,18},{18... | collective-permute-start | bytes 196616 | tf_op jit(solution)/shard_map/ppermute | solution.py:244
  17.6 0.1 sqrt_bitcast_fusion
  17.7 0.0 copy-done.3
  17.7 0.3 copy.12
  18.0 0.1 copy.15
  18.1 1.2 %collective-permute-done.1.tail = f32[64,256]{1,0:T(8,128)S(1)} collective-permute-done((f32[64,256]{1,0:T(8,128)S(1)}, f32[64,256]{1,0:T(8,128)S(1)}, u32[]{:S(2)}, u32[]{:S(2)}) %collective-permute-start.1) | collective-permute-done | bytes 65568 | tf_op jit(solution)/shard_map/ppermute | solution.py:244
  19.3 0.8 shard_map.70
  20.2 15.1 %all_to_all.20.sent.own = bf16[16,152,128]{2,1,0:T(8,128)(2,1)S(1)} all-to-all(bf16[16,152,128]{2,1,0:T(8,128)(2,1)S(1)} %get-tuple-element.11), channel_id=1, replica_groups=mesh['tm_0'=16,'tm_1'=4,'tm_2'=4,'state'=2] {'tm_1','tm_2'}, dimensions={0} | all-to-all | bytes 1245184 | tf_op jit(solution)/shard_map/all_to_all | solution.py:256
  35.3 0.7 shard_map.71
  36.0 16.7 %all-to-all-start.1 = ((f32[16,8,128]{2,1,0:T(8,128)}), f32[16,8,128]{2,1,0:T(8,128)S(1)}, u32[]{:S(2)}, u32[]{:S(2)}) async-start(f32[16,8,128]{2,1,0:T(8,128)} %get-tuple-element.13), calls=%async_computation.1 | async-start | bytes 131072 | tf_op jit(solution)/shard_map/all_to_all | solution.py:267
  52.7 4.1 %collective-permute-start.2 = (bf16[16,128,128]{2,1,0:T(8,128)(2,1)S(1)}, bf16[16,128,128]{2,1,0:T(8,128)(2,1)S(1)}, u32[]{:S(2)}, u32[]{:S(2)}) collective-permute-start(bf16[16,128,128]{2,1,0:T(8,128)(2,1)S(1)} %slice.18), channel_id=1, source_target_pairs={{0,1},{1,0},{2,3},{3,2},{4,5},{5,4},{6,7},{7,6},{8,9},{9,8},{10,11... | collective-permute-start | bytes 1572872 | tf_op jit(solution)/shard_map/ppermute | solution.py:220
  56.8 7.4 %all-to-all-done.1.planes = f32[16,8,128]{2,1,0:T(8,128)S(1)} async-done(((f32[16,8,128]{2,1,0:T(8,128)}), f32[16,8,128]{2,1,0:T(8,128)S(1)}, u32[]{:S(2)}, u32[]{:S(2)}) %all-to-all-start.1) | async-done | bytes 65568 | tf_op jit(solution)/shard_map/all_to_all | solution.py:267
  64.3 1.5 %shard_map.72 = (f32[128,128]{1,0:T(8,128)}, bf16[16,128,128]{2,1,0:T(8,128)(2,1)}) custom-call(s32[5]{0:T(128)S(1)} %pad_add_fusion.where, f32[16,8,128]{2,1,0:T(8,128)S(1)} %get-tuple-element.12.plane, f32[16,8,128]{2,1,0:T(8,128)S(1)} %all-to-all-done.1.planes, f32[6,128,128]{2,1,0:T(8,128)S(1)} %get-tuple-element.14.keep, ...), custom_call_target="tpu_custom_call" | custom-call | tf_op jit(solution)/shard_map/pallas_call | solution.py:268
  65.8 3.6 %all-to-all-start.2 = ((bf16[16,128,128]{2,1,0:T(8,128)(2,1)}), bf16[16,128,128]{2,1,0:T(8,128)(2,1)S(1)}, u32[]{:S(2)}, u32[]{:S(2)}) async-start(bf16[16,128,128]{2,1,0:T(8,128)(2,1)} %get-tuple-element.16), calls=%async_computation.2 | async-start | bytes 1048576 | tf_op jit(solution)/shard_map/all_to_all | solution.py:276
  69.4 0.0 collective-permute-done.2.other
  69.4 2.6 %collective-permute-start.3 = (bf16[2,128,128]{2,1,0:T(8,128)(2,1)S(1)}, bf16[2,128,128]{2,1,0:T(8,128)(2,1)S(1)}, u32[]{:S(2)}, u32[]{:S(2)}) collective-permute-start(bf16[2,128,128]{2,1,0:T(8,128)(2,1)S(1)} %pad_maximum_fusion), channel_id=1, source_target_pairs={{0,32},{32,64},{64,96},{96,128},{128,160},{160,192},{192,224},{224... | collective-permute-start | bytes 196616 | tf_op jit(solution)/shard_map/ppermute | solution.py:278
  72.1 1.3 %collective-permute-done.3.tails = bf16[2,128,128]{2,1,0:T(8,128)(2,1)S(1)} collective-permute-done((bf16[2,128,128]{2,1,0:T(8,128)(2,1)S(1)}, bf16[2,128,128]{2,1,0:T(8,128)(2,1)S(1)}, u32[]{:S(2)}, u32[]{:S(2)}) %collective-permute-start.3) | collective-permute-done | bytes 65568 | tf_op jit(solution)/shard_map/ppermute | solution.py:278
  73.4 4.9 %all-to-all-done.2.resid = bf16[16,128,128]{2,1,0:T(8,128)(2,1)S(1)} async-done(((bf16[16,128,128]{2,1,0:T(8,128)(2,1)}), bf16[16,128,128]{2,1,0:T(8,128)(2,1)S(1)}, u32[]{:S(2)}, u32[]{:S(2)}) %all-to-all-start.2) | async-done | bytes 524320 | tf_op jit(solution)/shard_map/all_to_all | solution.py:276
  78.3 1.6 %shard_map.73 = f32[16,2,8,256]{3,2,1,0:T(8,128)S(1)} custom-call(s32[5]{0:T(128)S(1)} %pad_add_fusion.where, bf16[2,128,128]{2,1,0:T(8,128)(2,1)S(1)} %collective-permute-done.3.tails, bf16[16,152,128]{2,1,0:T(8,128)(2,1)S(1)} %all_to_all.20.sent.own, bf16[16,128,128]{2,1,0:T(8,128)(2,1)S(1)} %collective-permute-done.2.other, ...), custom_call_target="tpu_custom_call" | custom-call | tf_op jit(solution)/shard_map/pallas_call | solution.py:279
  79.9 30.0 %all_to_all.21.pieces = f32[32,8,256]{2,1,0:T(8,128)S(1)} all-to-all(f32[32,8,256]{2,1,0:T(8,128)S(1)} %bitcast.18), channel_id=1, replica_groups=mesh['tm_0'=16,'tm_1'=4,'tm_2'=4,'state'=2] {'tm_0','state'}, dimensions={0} | all-to-all | bytes 524288 | tf_op jit(solution)/shard_map/all_to_all | solution.py:286
  109.9 0.6 shard_map.74
  (9 shorter events, 0.1 us)
Async XLA Ops:
  0.6 14.1 %collective-permute-start = (bf16[128,2048]{1,0:T(8,128)(2,1)}, bf16[128,2048]{1,0:T(8,128)(2,1)S(1)}, u32[]{:S(2)}, u32[]{:S(2)}) collective-permute-start(bf16[128,2048]{1,0:T(8,128)(2,1)} %own.1), channel_id=1, source_target_pairs={{0,1},{1,0},{2,3},{3,2},{4,5},{5,4},{6,7},{7,6},{8,9},{9,8},{10,11... | collective-permute-start | bytes 1572872 | tf_op jit(solution)/shard_map/ppermute | solution.py:220
  11.1 1.6 %copy-start = (bf16[2,128,4096]{2,1,0:T(8,128)(2,1)S(1)}, bf16[2,128,4096]{2,1,0:T(8,128)(2,1)}, u32[]{:S(2)}) copy-start(bf16[2,128,4096]{2,1,0:T(8,128)(2,1)} %gain.3) | copy-start | bytes 6291460
  12.7 1.0 copy-start.2
  13.7 1.6 %copy-start.1 = (bf16[2,128,4096]{2,1,0:T(8,128)(2,1)S(1)}, bf16[2,128,4096]{2,1,0:T(8,128)(2,1)}, u32[]{:S(2)}) copy-start(bf16[2,128,4096]{2,1,0:T(8,128)(2,1)} %gain.3) | copy-start | bytes 6291460
  14.7 3.0 %copy-start.3 = (bf16[128,2048]{1,0:T(8,128)(2,1)S(1)}, bf16[128,2048]{1,0:T(8,128)(2,1)}, u32[]{:S(2)}) copy-start(bf16[128,2048]{1,0:T(8,128)(2,1)} %own.1) | copy-start | bytes 1572868
  14.7 4.6 %copy-start.4 = (f32[128]{0:T(128)S(1)}, f32[128]{0:T(128)}, u32[]{:S(2)}) copy-start(f32[128]{0:T(128)} %param.8) | copy-start | bytes 1540
  16.3 3.0 %collective-permute-start.1 = (f32[64,256]{1,0:T(8,128)S(1)}, f32[64,256]{1,0:T(8,128)S(1)}, u32[]{:S(2)}, u32[]{:S(2)}) collective-permute-start(f32[64,256]{1,0:T(8,128)S(1)} %slice.16), channel_id=1, source_target_pairs={{0,2},{2,4},{4,6},{6,8},{8,10},{10,12},{12,14},{14,16},{16,18},{18... | collective-permute-start | bytes 196616 | tf_op jit(solution)/shard_map/ppermute | solution.py:244
  36.0 28.3 %all-to-all-start.1 = ((f32[16,8,128]{2,1,0:T(8,128)}), f32[16,8,128]{2,1,0:T(8,128)S(1)}, u32[]{:S(2)}, u32[]{:S(2)}) async-start(f32[16,8,128]{2,1,0:T(8,128)} %get-tuple-element.13), calls=%async_computation.1 | async-start | bytes 131072 | tf_op jit(solution)/shard_map/all_to_all | solution.py:267
  52.7 16.7 %collective-permute-start.2 = (bf16[16,128,128]{2,1,0:T(8,128)(2,1)S(1)}, bf16[16,128,128]{2,1,0:T(8,128)(2,1)S(1)}, u32[]{:S(2)}, u32[]{:S(2)}) collective-permute-start(bf16[16,128,128]{2,1,0:T(8,128)(2,1)S(1)} %slice.18), channel_id=1, source_target_pairs={{0,1},{1,0},{2,3},{3,2},{4,5},{5,4},{6,7},{7,6},{8,9},{9,8},{10,11... | collective-permute-start | bytes 1572872 | tf_op jit(solution)/shard_map/ppermute | solution.py:220
  65.8 12.5 %all-to-all-start.2 = ((bf16[16,128,128]{2,1,0:T(8,128)(2,1)}), bf16[16,128,128]{2,1,0:T(8,128)(2,1)S(1)}, u32[]{:S(2)}, u32[]{:S(2)}) async-start(bf16[16,128,128]{2,1,0:T(8,128)(2,1)} %get-tuple-element.16), calls=%async_computation.2 | async-start | bytes 1048576 | tf_op jit(solution)/shard_map/all_to_all | solution.py:276
  69.4 4.0 %collective-permute-start.3 = (bf16[2,128,128]{2,1,0:T(8,128)(2,1)S(1)}, bf16[2,128,128]{2,1,0:T(8,128)(2,1)S(1)}, u32[]{:S(2)}, u32[]{:S(2)}) collective-permute-start(bf16[2,128,128]{2,1,0:T(8,128)(2,1)S(1)} %pad_maximum_fusion), channel_id=1, source_target_pairs={{0,32},{32,64},{64,96},{96,128},{128,160},{160,192},{192,224},{224... | collective-permute-start | bytes 196616 | tf_op jit(solution)/shard_map/ppermute | solution.py:278

commit v5 on v4

--- a/solution.py
+++ b/solution.py
@@ -16,11 +16,12 @@
 BF16 = jnp.bfloat16
 VMEM = pl.BlockSpec(memory_space=pltpu.VMEM)
 SMEM = pl.BlockSpec(memory_space=pltpu.SMEM)
+WHOLE = pl.BlockSpec(memory_space=pltpu.HBM)
 NT = (((1,), (1,)), ((), ()))
 
 
-def call(body, outs, scratch=(), smem=(0,), n_in=1):
-    specs = [SMEM if i in smem else VMEM for i in range(n_in)]
+def call(body, outs, scratch=(), smem=(0,), whole=(), n_in=1):
+    specs = [WHOLE if i in whole else SMEM if i in smem else VMEM for i in range(n_in)]
     return pl.pallas_call(
         body,
         out_shape=outs,
@@ -55,24 +56,38 @@
     return link, sums
 
 
-def own_body(where, own, gain, out):
+def own_body(record, gain, out, gain_rest, own, gain_own, arrived):
+    modes = gain_own.shape[1]
+    half = own.shape[1]
+    core = lax.axis_index("state")
+    mine = pl.multiple_of(core * half, half)
+    theirs = pl.multiple_of((1 - core) * half, half)
+    copies = [pltpu.make_async_copy(record, own, arrived.at[0])]
+    for k in range(TAPS):
+        copies.append(
+            pltpu.make_async_copy(
+                gain.at[k, :, pl.ds(mine, half)], gain_own.at[k], arrived.at[1 + k]
+            )
+        )
+    rest = pltpu.make_async_copy(gain.at[:, :, pl.ds(theirs, half)], gain_rest, arrived.at[1 + TAPS])
+    for copy in copies:
+        copy.start()
+    rest.start()
+    copies[0].wait()
+    for k in range(TAPS):
+        copies[1 + k].wait()
+        out[:, k * modes : (k + 1) * modes] = lax.dot_general(
+            own[...], gain_own[k], NT, preferred_element_type=F32
+        )
+    rest.wait()
+
+
+def rest_body(other, gain, part, out):
     modes = gain.shape[1]
-    half = own.shape[1]
-    at = pl.multiple_of(where[2] * half, half)
-    for k in range(TAPS):
-        out[:, k * modes : (k + 1) * modes] = lax.dot_general(
-            own[...], gain[k, :, pl.ds(at, half)], NT, preferred_element_type=F32
-        )
-
-
-def rest_body(where, other, gain, part, out):
-    modes = gain.shape[1]
-    half = other.shape[1]
-    at = pl.multiple_of((1 - where[2]) * half, half)
     for k in range(TAPS):
         columns = slice(k * modes, (k + 1) * modes)
         out[:, columns] = part[:, columns] + lax.dot_general(
-            other[...], gain[k, :, pl.ds(at, half)], NT, preferred_element_type=F32
+            other[...], gain[k], NT, preferred_element_type=F32
         )
 
 
@@ -233,15 +248,26 @@
     )
     other = swapped(record)
     group = sensors // planes // blocks
-    rate_t = rate.T
+    both = jax.ShapeDtypeStruct((frames, TAPS * modes), F32)
+    half_gain = (TAPS, modes, sensors)
+    part, gain_rest = call(
+        own_body,
+        (both, jax.ShapeDtypeStruct(half_gain, BF16)),
+        scratch=[
+            pltpu.VMEM((frames, sensors), BF16),
+            pltpu.VMEM(half_gain, BF16),
+            pltpu.SemaphoreType.DMA((2 + TAPS,)),
+        ],
+        smem=(),
+        whole=(0, 1),
+        n_in=2,
+    )(*(pltpu.with_memory_space_constraint(x, pltpu.HBM) for x in (record, gain)))
+    u = call(rest_body, both, smem=(), n_in=3)(other, gain_rest, part)
+    u_tail = lax.ppermute(u[frames - DMAX :], TM, [(i, i + 1) for i in range(planes * blocks - 1)])
+    rate_t = behind(rate, u).T
     decay = jnp.exp(-rate_t)
     scale = jnp.sqrt(-jnp.expm1(-2.0 * rate_t))
     leak_row = leak[None]
-
-    both = jax.ShapeDtypeStruct((frames, TAPS * modes), F32)
-    part = call(own_body, both, n_in=3)(where, record, gain)
-    u = call(rest_body, both, n_in=4)(where, other, gain, part)
-    u_tail = lax.ppermute(u[frames - DMAX :], TM, [(i, i + 1) for i in range(planes * blocks - 1)])
     by_sensor = behind(record, u).T.reshape(planes, blocks, group, frames).swapaxes(0, 1)
     by_sensor = by_sensor.reshape(blocks, planes * group, frames)
     keep, sent = call(

time: 111 us -> 107 us (0.964)
  local copies, waits for them, and re-layouts: 4.61 us -> 0.57 us
    unnamed x11 -> x8, local copies, waits for them, and re-layouts: 4.15 us -> 0.02 us
  transfers between devices with their start and end apart: 6 -> 6, of which waited for: 4 -> 4; matrix products, arithmetic and copies ran while one was open for 2% -> 1% of each run, Pallas kernels for 2% -> 3%
where the time goes in v5:
time: 107 us; the launch traced here: 106 us
  blocking collectives  45.2 us (42%)
  starting transfers between devices  37 us (35%)
  waiting for transfers between devices  14.8 us (14%)
  Pallas kernels  7.83 us (7%)
    all_to_all x1, blocking collectives, per_device(): pieces = lax.all_to_all(pieces, (Z, 'state'), 0, 0, tiled=True)  30 us
    all_to_all x1, starting transfers between devices, per_device(): every_plane = lax.all_to_all(plane_summary, Z, 0, 0, tiled=True)  16.6 us
    all_to_all x1, blocking collectives, per_device(): mine = lax.all_to_all(sent, YX, 0, 0, tiled=True)  15.1 us
    ppermute x2, starting transfers between devices, swapped(): return lax.ppermute(x, 'state', [(0, 1), (1, 0)])  12.9 us
    all_to_all x1, waiting for transfers between devices, per_device(): every_plane = lax.all_to_all(plane_summary, Z, 0, 0, tiled=True)  7.4 us
    all_to_all x1, waiting for transfers between devices, per_device(): resid_all = lax.all_to_all(resid, YX, 0, 0, tiled=True)  4.93 us
    all_to_all x1, starting transfers between devices, per_device(): resid_all = lax.all_to_all(resid, YX, 0, 0, tiled=True)  3.57 us
    ppermute x1, starting transfers between devices, per_device(): tails = lax.ppermute(tails, Z, [(i, i + 1) for i in range(planes - 1)])  2.65 us
  transfers between devices with their start and end apart: 6, of which 4 were waited for; matrix products, arithmetic and copies ran while one was open for 1% of the time, Pallas kernels for 3%

profile of v5, /device:TPU:1, one launch (start us, length us, event | category | flops | bytes accessed | tf_op | source)
XLA Modules:
  0.0 106.4 jit_solution(9435654280878505116)
XLA Ops:
  0.6 0.0 copy-start.3
  0.6 8.8 %collective-permute-start = (bf16[128,2048]{1,0:T(8,128)(2,1)}, bf16[128,2048]{1,0:T(8,128)(2,1)S(1)}, u32[]{:S(2)}, u32[]{:S(2)}) collective-permute-start(bf16[128,2048]{1,0:T(8,128)(2,1)} %record.1), channel_id=1, source_target_pairs={{0,1},{1,0},{2,3},{3,2},{4,5},{5,4},{6,7},{7,6},{8,9},{9,8},{10,11... | collective-permute-start | bytes 1572872 | tf_op jit(solution)/shard_map/ppermute | solution.py:235
  9.4 0.0 copy-start.2
  9.5 0.0 copy-start.1
  9.5 2.1 %shard_map.68 = (f32[128,256]{1,0:T(8,128)S(1)}, bf16[2,128,2048]{2,1,0:T(8,128)(2,1)S(1)}) custom-call(bf16[128,2048]{1,0:T(8,128)(2,1)} %record.1, bf16[2,128,4096]{2,1,0:T(8,128)(2,1)} %gain.1), custom_call_target="tpu_custom_call" | custom-call | tf_op jit(solution)/shard_map/pallas_call | solution.py:253
  11.6 0.0 copy-done.3
  11.6 0.1 pad_add_fusion.where
  11.7 0.0 collective-permute-done.other
  11.7 0.4 shard_map.69.u
  12.2 1.3 %collective-permute-start.1 = (f32[64,256]{1,0:T(8,128)S(1)}, f32[64,256]{1,0:T(8,128)S(1)}, u32[]{:S(2)}, u32[]{:S(2)}) collective-permute-start(f32[64,256]{1,0:T(8,128)S(1)} %slice.16), channel_id=1, source_target_pairs={{0,2},{2,4},{4,6},{6,8},{8,10},{10,12},{12,14},{14,16},{16,18},{18... | collective-permute-start | bytes 196616 | tf_op jit(solution)/shard_map/ppermute | solution.py:266
  13.5 0.0 copy-done.2
  13.5 0.1 copy.10
  13.6 0.1 sqrt_bitcast_fusion
  13.6 0.0 copy-done.1
  13.6 0.3 copy.12
  13.9 0.1 copy.15
  14.1 1.1 %collective-permute-done.1.tail = f32[64,256]{1,0:T(8,128)S(1)} collective-permute-done((f32[64,256]{1,0:T(8,128)S(1)}, f32[64,256]{1,0:T(8,128)S(1)}, u32[]{:S(2)}, u32[]{:S(2)}) %collective-permute-start.1) | collective-permute-done | bytes 65568 | tf_op jit(solution)/shard_map/ppermute | solution.py:266
  15.2 0.8 shard_map.70
  16.0 15.1 %all_to_all.20.sent.own = bf16[16,152,128]{2,1,0:T(8,128)(2,1)S(1)} all-to-all(bf16[16,152,128]{2,1,0:T(8,128)(2,1)S(1)} %get-tuple-element.17), channel_id=1, replica_groups=mesh['tm_0'=16,'tm_1'=4,'tm_2'=4,'state'=2] {'tm_1','tm_2'}, dimensions={0} | all-to-all | bytes 1245184 | tf_op jit(solution)/shard_map/all_to_all | solution.py:282
  31.2 0.7 shard_map.71
  31.8 16.6 %all-to-all-start.1 = ((f32[16,8,128]{2,1,0:T(8,128)}), f32[16,8,128]{2,1,0:T(8,128)S(1)}, u32[]{:S(2)}, u32[]{:S(2)}) async-start(f32[16,8,128]{2,1,0:T(8,128)} %get-tuple-element.19), calls=%async_computation.1 | async-start | bytes 131072 | tf_op jit(solution)/shard_map/all_to_all | solution.py:293
  48.5 4.1 %collective-permute-start.2 = (bf16[16,128,128]{2,1,0:T(8,128)(2,1)S(1)}, bf16[16,128,128]{2,1,0:T(8,128)(2,1)S(1)}, u32[]{:S(2)}, u32[]{:S(2)}) collective-permute-start(bf16[16,128,128]{2,1,0:T(8,128)(2,1)S(1)} %slice.18), channel_id=1, source_target_pairs={{0,1},{1,0},{2,3},{3,2},{4,5},{5,4},{6,7},{7,6},{8,9},{9,8},{10,11... | collective-permute-start | bytes 1572872 | tf_op jit(solution)/shard_map/ppermute | solution.py:235
  52.7 7.4 %all-to-all-done.1.planes = f32[16,8,128]{2,1,0:T(8,128)S(1)} async-done(((f32[16,8,128]{2,1,0:T(8,128)}), f32[16,8,128]{2,1,0:T(8,128)S(1)}, u32[]{:S(2)}, u32[]{:S(2)}) %all-to-all-start.1) | async-done | bytes 65568 | tf_op jit(solution)/shard_map/all_to_all | solution.py:293
  60.1 1.5 %shard_map.72 = (f32[128,128]{1,0:T(8,128)}, bf16[16,128,128]{2,1,0:T(8,128)(2,1)}) custom-call(s32[5]{0:T(128)S(1)} %pad_add_fusion.where, f32[16,8,128]{2,1,0:T(8,128)S(1)} %get-tuple-element.18.plane, f32[16,8,128]{2,1,0:T(8,128)S(1)} %all-to-all-done.1.planes, f32[6,128,128]{2,1,0:T(8,128)S(1)} %get-tuple-element.20.keep, ...), custom_call_target="tpu_custom_call" | custom-call | tf_op jit(solution)/shard_map/pallas_call | solution.py:294
  61.6 3.6 %all-to-all-start.2 = ((bf16[16,128,128]{2,1,0:T(8,128)(2,1)}), bf16[16,128,128]{2,1,0:T(8,128)(2,1)S(1)}, u32[]{:S(2)}, u32[]{:S(2)}) async-start(bf16[16,128,128]{2,1,0:T(8,128)(2,1)} %get-tuple-element.22), calls=%async_computation.2 | async-start | bytes 1048576 | tf_op jit(solution)/shard_map/all_to_all | solution.py:302
  65.2 0.0 collective-permute-done.2.other
  65.2 2.6 %collective-permute-start.3 = (bf16[2,128,128]{2,1,0:T(8,128)(2,1)S(1)}, bf16[2,128,128]{2,1,0:T(8,128)(2,1)S(1)}, u32[]{:S(2)}, u32[]{:S(2)}) collective-permute-start(bf16[2,128,128]{2,1,0:T(8,128)(2,1)S(1)} %pad_maximum_fusion), channel_id=1, source_target_pairs={{0,32},{32,64},{64,96},{96,128},{128,160},{160,192},{192,224},{224... | collective-permute-start | bytes 196616 | tf_op jit(solution)/shard_map/ppermute | solution.py:304
  67.9 1.3 %collective-permute-done.3.tails = bf16[2,128,128]{2,1,0:T(8,128)(2,1)S(1)} collective-permute-done((bf16[2,128,128]{2,1,0:T(8,128)(2,1)S(1)}, bf16[2,128,128]{2,1,0:T(8,128)(2,1)S(1)}, u32[]{:S(2)}, u32[]{:S(2)}) %collective-permute-start.3) | collective-permute-done | bytes 65568 | tf_op jit(solution)/shard_map/ppermute | solution.py:304
  69.2 4.9 %all-to-all-done.2.resid = bf16[16,128,128]{2,1,0:T(8,128)(2,1)S(1)} async-done(((bf16[16,128,128]{2,1,0:T(8,128)(2,1)}), bf16[16,128,128]{2,1,0:T(8,128)(2,1)S(1)}, u32[]{:S(2)}, u32[]{:S(2)}) %all-to-all-start.2) | async-done | bytes 524320 | tf_op jit(solution)/shard_map/all_to_all | solution.py:302
  74.1 1.6 %shard_map.73 = f32[16,2,8,256]{3,2,1,0:T(8,128)S(1)} custom-call(s32[5]{0:T(128)S(1)} %pad_add_fusion.where, bf16[2,128,128]{2,1,0:T(8,128)(2,1)S(1)} %collective-permute-done.3.tails, bf16[16,152,128]{2,1,0:T(8,128)(2,1)S(1)} %all_to_all.20.sent.own, bf16[16,128,128]{2,1,0:T(8,128)(2,1)S(1)} %collective-permute-done.2.other, ...), custom_call_target="tpu_custom_call" | custom-call | tf_op jit(solution)/shard_map/pallas_call | solution.py:305
  75.7 30.0 %all_to_all.21.pieces = f32[32,8,256]{2,1,0:T(8,128)S(1)} all-to-all(f32[32,8,256]{2,1,0:T(8,128)S(1)} %bitcast.18), channel_id=1, replica_groups=mesh['tm_0'=16,'tm_1'=4,'tm_2'=4,'state'=2] {'tm_0','state'}, dimensions={0} | all-to-all | bytes 524288 | tf_op jit(solution)/shard_map/all_to_all | solution.py:312
  105.7 0.6 shard_map.74
  (7 shorter events, 0.1 us)
Async XLA Ops:
  0.6 11.0 %copy-start.3 = (s32[2]{0:T(128)S(1)}, s32[2]{0:T(128)}, u32[]{:S(2)}) copy-start(s32[2]{0:T(128)} %param.9) | copy-start | bytes 28
  0.6 11.1 %collective-permute-start = (bf16[128,2048]{1,0:T(8,128)(2,1)}, bf16[128,2048]{1,0:T(8,128)(2,1)S(1)}, u32[]{:S(2)}, u32[]{:S(2)}) collective-permute-start(bf16[128,2048]{1,0:T(8,128)(2,1)} %record.1), channel_id=1, source_target_pairs={{0,1},{1,0},{2,3},{3,2},{4,5},{5,4},{6,7},{7,6},{8,9},{9,8},{10,11... | collective-permute-start | bytes 1572872 | tf_op jit(solution)/shard_map/ppermute | solution.py:235
  9.4 4.0 %copy-start.2 = (f32[128,128]{1,0:T(8,128)S(1)}, f32[128,128]{1,0:T(8,128)}, u32[]{:S(2)}) copy-start(f32[128,128]{1,0:T(8,128)} %param.7) | copy-start | bytes 196612
  9.5 4.2 %copy-start.1 = (bf16[128,2048]{1,0:T(8,128)(2,1)S(1)}, bf16[128,2048]{1,0:T(8,128)(2,1)}, u32[]{:S(2)}) copy-start(bf16[128,2048]{1,0:T(8,128)(2,1)} %record.1) | copy-start | bytes 1572868
  11.7 3.5 %copy-start = (f32[128]{0:T(128)S(1)}, f32[128]{0:T(128)}, u32[]{:S(2)}) copy-start(f32[128]{0:T(128)} %param.8) | copy-start | bytes 1540
  12.2 3.0 %collective-permute-start.1 = (f32[64,256]{1,0:T(8,128)S(1)}, f32[64,256]{1,0:T(8,128)S(1)}, u32[]{:S(2)}, u32[]{:S(2)}) collective-permute-start(f32[64,256]{1,0:T(8,128)S(1)} %slice.16), channel_id=1, source_target_pairs={{0,2},{2,4},{4,6},{6,8},{8,10},{10,12},{12,14},{14,16},{16,18},{18... | collective-permute-start | bytes 196616 | tf_op jit(solution)/shard_map/ppermute | solution.py:266
  31.8 28.2 %all-to-all-start.1 = ((f32[16,8,128]{2,1,0:T(8,128)}), f32[16,8,128]{2,1,0:T(8,128)S(1)}, u32[]{:S(2)}, u32[]{:S(2)}) async-start(f32[16,8,128]{2,1,0:T(8,128)} %get-tuple-element.19), calls=%async_computation.1 | async-start | bytes 131072 | tf_op jit(solution)/shard_map/all_to_all | solution.py:293
  48.5 16.7 %collective-permute-start.2 = (bf16[16,128,128]{2,1,0:T(8,128)(2,1)S(1)}, bf16[16,128,128]{2,1,0:T(8,128)(2,1)S(1)}, u32[]{:S(2)}, u32[]{:S(2)}) collective-permute-start(bf16[16,128,128]{2,1,0:T(8,128)(2,1)S(1)} %slice.18), channel_id=1, source_target_pairs={{0,1},{1,0},{2,3},{3,2},{4,5},{5,4},{6,7},{7,6},{8,9},{9,8},{10,11... | collective-permute-start | bytes 1572872 | tf_op jit(solution)/shard_map/ppermute | solution.py:235
  61.6 12.5 %all-to-all-start.2 = ((bf16[16,128,128]{2,1,0:T(8,128)(2,1)}), bf16[16,128,128]{2,1,0:T(8,128)(2,1)S(1)}, u32[]{:S(2)}, u32[]{:S(2)}) async-start(bf16[16,128,128]{2,1,0:T(8,128)(2,1)} %get-tuple-element.22), calls=%async_computation.2 | async-start | bytes 1048576 | tf_op jit(solution)/shard_map/all_to_all | solution.py:302
  65.2 4.0 %collective-permute-start.3 = (bf16[2,128,128]{2,1,0:T(8,128)(2,1)S(1)}, bf16[2,128,128]{2,1,0:T(8,128)(2,1)S(1)}, u32[]{:S(2)}, u32[]{:S(2)}) collective-permute-start(bf16[2,128,128]{2,1,0:T(8,128)(2,1)S(1)} %pad_maximum_fusion), channel_id=1, source_target_pairs={{0,32},{32,64},{64,96},{96,128},{128,160},{160,192},{192,224},{224... | collective-permute-start | bytes 196616 | tf_op jit(solution)/shard_map/ppermute | solution.py:304

commit v6 on v5

--- a/solution.py
+++ b/solution.py
@@ -1,3 +1,5 @@
+import functools
+
 import jax
 import jax.numpy as jnp
 from jax import lax
@@ -7,6 +9,7 @@
 from jax.sharding import PartitionSpec as P
 
 TAPS = 2
+TOP = 32768.0
 DMAX = 64
 Z = "tm_0"
 YX = ("tm_1", "tm_2")
@@ -56,7 +59,7 @@
     return link, sums
 
 
-def own_body(record, gain, out, gain_rest, own, gain_own, arrived):
+def own_body(record, gain, out, gain_rest, peak, own, gain_own, arrived):
     modes = gain_own.shape[1]
     half = own.shape[1]
     core = lax.axis_index("state")
@@ -74,6 +77,8 @@
         copy.start()
     rest.start()
     copies[0].wait()
+    largest = jnp.max(jnp.abs(own[...].astype(F32)), axis=0, keepdims=True)
+    peak[...] = jnp.broadcast_to(jnp.max(largest, axis=1, keepdims=True), peak.shape)
     for k in range(TAPS):
         copies[1 + k].wait()
         out[:, k * modes : (k + 1) * modes] = lax.dot_general(
@@ -91,7 +96,7 @@
         )
 
 
-def local_body(where, u, tail, decay_ref, scale, leak, by_sensor, keep, sent, ext):
+def local_body(where, u, tail, decay_ref, scale, leak, by_sensor, peak, keep, sent, ext):
     frames, modes = decay_ref.shape
     ext[:DMAX] = tail[...]
     ext[DMAX:] = u[...]
@@ -112,7 +117,8 @@
     keep[4] = slope
     keep[5] = drive
     rows = [prods[-1:], offsets[-1:], links[:1], base[:1], slope[:1], decay[-1:]]
-    rest = jnp.concatenate(rows + [jnp.zeros((2, modes), F32)], 0)
+    rows += [jnp.max(jnp.abs(offsets), axis=0, keepdims=True), peak[:1]]
+    rest = jnp.concatenate(rows, 0)
     frames_rows = by_sensor.shape[1]
     parts = []
     for _ in range(3):
@@ -148,8 +154,14 @@
     parts = [five(every, i) for i in range(n)]
     while len(parts) > 1:
         parts = [joined(parts[i], parts[i + 1]) for i in range(0, len(parts), 2)]
-    out[...] = jnp.zeros_like(out)
-    rows = list(parts[0]) + [every[n - 1, 5:6]]
+    state = jnp.zeros_like(every[0, :1])
+    reach = state
+    peak = state
+    for i in range(n):
+        reach = jnp.maximum(reach, every[i, 6:7] + jnp.abs(state))
+        peak = jnp.maximum(peak, every[i, 7:8])
+        state = every[i, 0:1] * state + every[i, 1:2]
+    rows = list(parts[0]) + [every[n - 1, 5:6], reach, peak]
     for r, row in enumerate(rows):
         for i in range(out.shape[0]):
             out[i, r : r + 1] = row
@@ -169,17 +181,25 @@
         state = every[i, 0:1] * state + every[i, 1:2]
         before = every[i, 5:6]
     after = closing
+    afters = [after] * n
     own_after = jnp.zeros_like(entering)
     for i in reversed(range(n)):
+        afters[i] = after
         own_after = jnp.where(position == i, after, own_after)
         after = every[i, 2:3] * after + every[i, 3:4] + every[i, 4:5] * states[i]
-    return own_state, own_after, own_last
-
-
-def finish_body(where, plane, planes, keep, decay_ref, leak, smoothed_out, resid_out):
+    return own_state, own_after, own_last, states, afters
+
+
+def finish_body(where, plane, planes, keep, decay_ref, leak, smoothed_out, resid_out, reach):
     zero = jnp.zeros((1, decay_ref.shape[1]), F32)
-    entering, after, last = ends(planes, where[0], zero, zero, zero)
-    entering, after, last = ends(plane, where[1], entering, after, last)
+    entering, after, last, states, afters = ends(planes, where[0], zero, zero, zero)
+    peak = zero
+    for i in range(planes.shape[0]):
+        bound = 6.0 * (planes[i, 6:7] + jnp.abs(states[i])) + 2.0 * jnp.abs(afters[i])
+        reach[0, i : i + 1] = jnp.broadcast_to(jnp.max(bound, axis=1, keepdims=True), zero.shape)
+        reach[1, i : i + 1] = jnp.maximum(peak, planes[i, 7:8])
+        peak = planes[i, 7:8]
+    entering, after, last, _, _ = ends(plane, where[1], entering, after, last)
     smoothed = keep[3] + keep[4] * entering + keep[2] * after
     decay = decay_ref[...]
     kappa = 1.0 - leak[...]
@@ -194,7 +214,11 @@
         resid_out[i] = resid
 
 
-def gradient_body(where, tails, own, other, resid, out, padded):
+def bounds(first, second, span):
+    return jnp.maximum(span * first[0] * jnp.maximum(first[1], second[1]), 1e-30)
+
+
+def gradient_body(where, tails, tails_other, own, other, resid, reach, reach_other, out, padded):
     blocks, frames, modes = resid.shape
     row = lax.broadcasted_iota(jnp.int32, (frames, 2 * frames), 0)
     column = lax.broadcasted_iota(jnp.int32, (frames, 2 * frames), 1)
@@ -208,20 +232,29 @@
             moved = jnp.dot(picks[k], pair, preferred_element_type=F32)
             padded[b * frames : (b + 1) * frames, k * modes : (k + 1) * modes] = moved.astype(BF16)
     rhs = padded[...]
-    for which, rows in enumerate((own, other)):
-        lhs = jnp.concatenate([tails[which]] + [rows[i, : tails.shape[1]] for i in range(blocks)], 1)
-        sums = jnp.dot(lhs, rhs, preferred_element_type=F32)
+    bound = bounds(reach, reach_other, float(blocks * frames))
+    plane = lax.broadcasted_iota(jnp.int32, bound.shape, 0)
+    factor = jnp.sum(jnp.where(plane == where[0], TOP / bound, 0.0), axis=0, keepdims=True)
+    factor = jnp.concatenate([factor] * TAPS, 1)
+    for which, (before, rows) in enumerate(((tails, own), (tails_other, other))):
+        lhs = jnp.concatenate(
+            [before[...]] + [rows[i, : before.shape[0]] for i in range(blocks)], 1
+        )
+        sums = jnp.dot(lhs, rhs, preferred_element_type=F32) * factor
         half = jnp.where(where[2] == which, 0, 1)
         for i in range(out.shape[0]):
             out[i, half] = sums[i * 8 : (i + 1) * 8]
 
 
-def total_body(pieces, out):
+def total_body(where, pieces, reach, reach_other, out, *, span):
     modes = out.shape[1] // TAPS // 2
+    pair = (bounds(reach, reach_other, span) / TOP, bounds(reach_other, reach, span) / TOP)
     for core in range(2):
-        total = pieces[core]
-        for i in range(2 + core, pieces.shape[0], 2):
-            total += pieces[i]
+        factor = jnp.where(where[2] == core, pair[0], pair[1])
+        factor = jnp.concatenate([factor] * TAPS, 1)
+        total = pieces[core] * factor[:1]
+        for i in range(1, factor.shape[0]):
+            total += pieces[2 * i + core] * factor[i : i + 1]
         for k in range(TAPS):
             column = (2 * k + core) * modes
             out[:, column : column + modes] = total[:, k * modes : (k + 1) * modes]
@@ -250,9 +283,13 @@
     group = sensors // planes // blocks
     both = jax.ShapeDtypeStruct((frames, TAPS * modes), F32)
     half_gain = (TAPS, modes, sensors)
-    part, gain_rest = call(
+    part, gain_rest, peak = call(
         own_body,
-        (both, jax.ShapeDtypeStruct(half_gain, BF16)),
+        (
+            both,
+            jax.ShapeDtypeStruct(half_gain, BF16),
+            jax.ShapeDtypeStruct((8, modes), F32),
+        ),
         scratch=[
             pltpu.VMEM((frames, sensors), BF16),
             pltpu.VMEM(half_gain, BF16),
@@ -277,8 +314,8 @@
             jax.ShapeDtypeStruct((blocks, planes * group + 24, frames), BF16),
         ),
         scratch=[pltpu.VMEM((DMAX + frames, TAPS * modes), F32)],
-        n_in=7,
-    )(where, u, u_tail, decay, scale, leak_row, by_sensor)
+        n_in=8,
+    )(where, u, u_tail, decay, scale, leak_row, by_sensor, peak)
     mine = lax.all_to_all(sent, YX, 0, 0, tiled=True)
     plane, plane_summary = call(
         plane_body,
@@ -289,30 +326,38 @@
         smem=(),
         n_in=1,
     )(mine)
-    theirs = swapped(mine[:, :-24])
+    ready = behind(mine, plane_summary)[:, :-24]
+    theirs = swapped(ready)
+    onward = [(2 * i + c, 2 * i + 2 + c) for i in range(planes - 1) for c in range(2)]
+    across = [(2 * i + c, 2 * i + 3 - c) for i in range(planes - 1) for c in range(2)]
+    tails = lax.ppermute(ready[-1], (Z, "state"), onward)
+    tails_other = lax.ppermute(ready[-1], (Z, "state"), across)
     every_plane = lax.all_to_all(plane_summary, Z, 0, 0, tiled=True)
-    smoothed, resid = call(
+    every_plane = behind(every_plane, (tails, tails_other))
+    smoothed, resid, reach = call(
         finish_body,
         (
             jax.ShapeDtypeStruct((modes, frames), F32),
             jax.ShapeDtypeStruct((blocks, frames, modes), BF16),
+            jax.ShapeDtypeStruct((2, planes, modes), F32),
         ),
         n_in=6,
     )(where, plane, every_plane, keep, decay, leak_row)
     resid_all = lax.all_to_all(resid, YX, 0, 0, tiled=True)
-    tails = behind(jnp.stack([mine[-1, :-24], theirs[-1]]), resid)
-    tails = lax.ppermute(tails, Z, [(i, i + 1) for i in range(planes - 1)])
+    reach_other = swapped(reach)
     partial = call(
         gradient_body,
         jax.ShapeDtypeStruct((planes, 2, group, TAPS * modes), F32),
         scratch=[pltpu.VMEM(((blocks + 1) * frames, TAPS * modes), BF16)],
-        n_in=5,
-    )(where, tails, mine, theirs, resid_all)
-    pieces = partial.reshape(planes * 2, group, TAPS * modes)
+        n_in=8,
+    )(where, tails, tails_other, mine, theirs, resid_all, reach, reach_other)
+    pieces = partial.reshape(planes * 2, group, TAPS * modes).astype(jnp.float16)
     pieces = lax.all_to_all(pieces, (Z, "state"), 0, 0, tiled=True)
     grad = call(
-        total_body, jax.ShapeDtypeStruct((group, TAPS * 2 * modes), F32), smem=(), n_in=1
-    )(pieces)
+        functools.partial(total_body, span=float(blocks * frames)),
+        jax.ShapeDtypeStruct((group, TAPS * 2 * modes), F32),
+        n_in=4,
+    )(where, pieces.astype(F32), reach, reach_other)
     return (smoothed, grad)
 
 

time: 107 us -> 108 us (level)
  starting transfers between devices: 37 us -> 46.3 us
  waiting for transfers between devices: 14.8 us -> 5.68 us
    all_to_all x1, waiting for transfers between devices: 7.4 us -> 0.74 us  [per_device(): every_plane = lax.all_to_all(plane_summary, Z, 0, 0, tiled=True)]
    ppermute x1 -> x2, starting transfers between devices: 2.65 us -> 9.02 us  [the longest x1 5.75 us: per_device(): tails_other = lax.ppermute(ready[-1], (Z, 'state'), across)]
    ppermute x2 -> x3, starting transfers between devices: 12.9 us -> 15.8 us  [swapped(): return lax.ppermute(x, 'state', [(0, 1), (1, 0)])]
    all_to_all x1, waiting for transfers between devices: 4.93 us -> 3.01 us  [per_device(): resid_all = lax.all_to_all(resid, YX, 0, 0, tiled=True)]
    ppermute x1 -> x2, waiting for transfers between devices: 1.31 us -> 0.01 us  [the longest x1 0.01 us: per_device(): tails = lax.ppermute(ready[-1], (Z, 'state'), onward)]
  transfers between devices with their start and end apart: 6 -> 8, of which waited for: 4 -> 4; matrix products, arithmetic and copies ran while one was open for 1% -> 1% of each run, Pallas kernels for 3% -> 3%
where the time goes in v6:
time: 108 us
  starting transfers between devices  46.3 us (43%)
  blocking collectives  45.7 us (42%)
  Pallas kernels  8.42 us (8%)
  waiting for transfers between devices  5.68 us (5%)
    all_to_all x1, blocking collectives, per_device(): pieces = lax.all_to_all(pieces, (Z, 'state'), 0, 0, tiled=True)  30.5 us
    all_to_all x1, starting transfers between devices, per_device(): every_plane = lax.all_to_all(plane_summary, Z, 0, 0, tiled=True)  16.6 us
    ppermute x3, starting transfers between devices, swapped(): return lax.ppermute(x, 'state', [(0, 1), (1, 0)])  15.8 us
    all_to_all x1, blocking collectives, per_device(): mine = lax.all_to_all(sent, YX, 0, 0, tiled=True)  15.1 us
    ppermute x1, starting transfers between devices, per_device(): tails_other = lax.ppermute(ready[-1], (Z, 'state'), across)  5.75 us
    all_to_all x1, starting transfers between devices, per_device(): resid_all = lax.all_to_all(resid, YX, 0, 0, tiled=True)  3.57 us
    ppermute x1, starting transfers between devices, per_device(): tails = lax.ppermute(ready[-1], (Z, 'state'), onward)  3.27 us
    all_to_all x1, waiting for transfers between devices, per_device(): resid_all = lax.all_to_all(resid, YX, 0, 0, tiled=True)  3.01 us
  transfers between devices with their start and end apart: 8, of which 4 were waited for; matrix products, arithmetic and copies ran while one was open for 1% of the time, Pallas kernels for 3%

profile of v6, /device:TPU:1, one launch (start us, length us, event | category | flops | bytes accessed | tf_op | source)
XLA Modules:
  0.0 107.7 jit_solution(6485993769123743121)
XLA Ops:
  0.6 0.0 copy-start.3
  0.6 8.8 %collective-permute-start = (bf16[128,2048]{1,0:T(8,128)(2,1)}, bf16[128,2048]{1,0:T(8,128)(2,1)S(1)}, u32[]{:S(2)}, u32[]{:S(2)}) collective-permute-start(bf16[128,2048]{1,0:T(8,128)(2,1)} %record.1), channel_id=1, source_target_pairs={{0,1},{1,0},{2,3},{3,2},{4,5},{5,4},{6,7},{7,6},{8,9},{9,8},{10,11... | collective-permute-start | bytes 1572872 | tf_op jit(solution)/shard_map/ppermute | solution.py:268
  9.4 0.0 copy-start.2
  9.5 2.1 %shard_map.68 = (f32[128,256]{1,0:T(8,128)S(1)}, bf16[2,128,2048]{2,1,0:T(8,128)(2,1)S(1)}, f32[8,128]{1,0:T(8,128)S(1)}) custom-call(bf16[128,2048]{1,0:T(8,128)(2,1)} %record.1, bf16[2,128,4096]{2,1,0:T(8,128)(2,1)} %gain.1), custom_call_target="tpu_custom_call" | custom-call | tf_op jit(solution)/shard_map/pallas_call | solution.py:286
  11.6 0.1 pad_add_fusion.where
  11.7 0.0 collective-permute-done.other
  11.7 0.4 shard_map.69.u
  12.2 1.3 %collective-permute-start.1 = (f32[64,256]{1,0:T(8,128)S(1)}, f32[64,256]{1,0:T(8,128)S(1)}, u32[]{:S(2)}, u32[]{:S(2)}) collective-permute-start(f32[64,256]{1,0:T(8,128)S(1)} %slice.14), channel_id=1, source_target_pairs={{0,2},{2,4},{4,6},{6,8},{8,10},{10,12},{12,14},{14,16},{16,18},{18... | collective-permute-start | bytes 196616 | tf_op jit(solution)/shard_map/ppermute | solution.py:303
  13.5 0.1 copy.10
  13.6 0.1 sqrt_bitcast_fusion
  13.6 0.3 copy.12
  13.9 0.1 copy.15
  14.1 1.1 %collective-permute-done.1.tail = f32[64,256]{1,0:T(8,128)S(1)} collective-permute-done((f32[64,256]{1,0:T(8,128)S(1)}, f32[64,256]{1,0:T(8,128)S(1)}, u32[]{:S(2)}, u32[]{:S(2)}) %collective-permute-start.1) | collective-permute-done | bytes 65568 | tf_op jit(solution)/shard_map/ppermute | solution.py:303
  15.2 0.8 shard_map.70
  16.0 15.1 %all_to_all.20.sent.own = bf16[16,152,128]{2,1,0:T(8,128)(2,1)S(1)} all-to-all(bf16[16,152,128]{2,1,0:T(8,128)(2,1)S(1)} %get-tuple-element.21), channel_id=1, replica_groups=mesh['tm_0'=16,'tm_1'=4,'tm_2'=4,'state'=2] {'tm_1','tm_2'}, dimensions={0} | all-to-all | bytes 1245184 | tf_op jit(solution)/shard_map/all_to_all | solution.py:319
  31.2 0.7 shard_map.71
  31.9 16.6 %all-to-all-start.1 = ((f32[16,8,128]{2,1,0:T(8,128)}), f32[16,8,128]{2,1,0:T(8,128)S(1)}, u32[]{:S(2)}, u32[]{:S(2)}) async-start(f32[16,8,128]{2,1,0:T(8,128)} %get-tuple-element.23), calls=%async_computation.1 | async-start | bytes 131072 | tf_op jit(solution)/shard_map/all_to_all | solution.py:335
  48.5 3.3 %collective-permute-start.2 = (bf16[128,128]{1,0:T(8,128)(2,1)S(1)}, bf16[128,128]{1,0:T(8,128)(2,1)S(1)}, u32[]{:S(2)}, u32[]{:S(2)}) collective-permute-start(bf16[128,128]{1,0:T(8,128)(2,1)S(1)} %slice_bitcast_fusion), channel_id=1, source_target_pairs={{0,32},{1,33},{32,64},{33,65},{64,96},{65,97},{96,128},{97,129},{1... | collective-permute-start | bytes 98312 | tf_op jit(solution)/shard_map/ppermute | solution.py:333
  51.8 5.8 %collective-permute-start.3 = (bf16[128,128]{1,0:T(8,128)(2,1)S(1)}, bf16[128,128]{1,0:T(8,128)(2,1)S(1)}, u32[]{:S(2)}, u32[]{:S(2)}) collective-permute-start(bf16[128,128]{1,0:T(8,128)(2,1)S(1)} %slice_bitcast_fusion), channel_id=1, source_target_pairs={{0,33},{1,32},{32,65},{33,64},{64,97},{65,96},{96,129},{97,128},{1... | collective-permute-start | bytes 98312 | tf_op jit(solution)/shard_map/ppermute | solution.py:334
  57.6 1.9 %collective-permute-start.4 = (bf16[16,128,128]{2,1,0:T(8,128)(2,1)S(1)}, bf16[16,128,128]{2,1,0:T(8,128)(2,1)S(1)}, u32[]{:S(2)}, u32[]{:S(2)}) collective-permute-start(bf16[16,128,128]{2,1,0:T(8,128)(2,1)S(1)} %slice.13), channel_id=1, source_target_pairs={{0,1},{1,0},{2,3},{3,2},{4,5},{5,4},{6,7},{7,6},{8,9},{9,8},{10,11... | collective-permute-start | bytes 1572872 | tf_op jit(solution)/shard_map/ppermute | solution.py:268
  59.5 0.0 collective-permute-done.2.tails
  59.5 0.0 collective-permute-done.3.tails_other
  59.5 0.7 all-to-all-done.1.planes
  60.3 1.6 %shard_map.72 = (f32[128,128]{1,0:T(8,128)}, bf16[16,128,128]{2,1,0:T(8,128)(2,1)}, f32[2,16,128]{2,1,0:T(8,128)S(1)}) custom-call(s32[5]{0:T(128)S(1)} %pad_add_fusion.where, f32[16,8,128]{2,1,0:T(8,128)S(1)} %get-tuple-element.22.plane, f32[16,8,128]{2,1,0:T(8,128)S(1)} %all-to-all-done.1.planes, f32[6,128,128]{2,1,0:T(8,128)S(1)} %get-tuple-element.26.keep, ...), custom_call_target="tpu_custom_call" | custom-call | tf_op jit(solution)/shard_map/pallas_call | solution.py:337
  61.8 3.6 %all-to-all-start.2 = ((bf16[16,128,128]{2,1,0:T(8,128)(2,1)}), bf16[16,128,128]{2,1,0:T(8,128)(2,1)S(1)}, u32[]{:S(2)}, u32[]{:S(2)}) async-start(bf16[16,128,128]{2,1,0:T(8,128)(2,1)} %get-tuple-element.28), calls=%async_computation.2 | async-start | bytes 1048576 | tf_op jit(solution)/shard_map/all_to_all | solution.py:346
  65.4 5.1 %collective-permute-start.5 = (f32[2,16,128]{2,1,0:T(8,128)S(1)}, f32[2,16,128]{2,1,0:T(8,128)S(1)}, u32[]{:S(2)}, u32[]{:S(2)}) collective-permute-start(f32[2,16,128]{2,1,0:T(8,128)S(1)} %get-tuple-element.29.reach), channel_id=1, source_target_pairs={{0,1},{1,0},{2,3},{3,2},{4,5},{5,4},{6,7},{7,6},{8,9},{9,8},{10,11... | collective-permute-start | bytes 49160 | tf_op jit(solution)/shard_map/ppermute | solution.py:268
  70.5 0.8 collective-permute-done.5.reach_other
  71.4 0.0 collective-permute-done.4.other
  71.4 3.0 %all-to-all-done.2.resid = bf16[16,128,128]{2,1,0:T(8,128)(2,1)S(1)} async-done(((bf16[16,128,128]{2,1,0:T(8,128)(2,1)}), bf16[16,128,128]{2,1,0:T(8,128)(2,1)S(1)}, u32[]{:S(2)}, u32[]{:S(2)}) %all-to-all-start.2) | async-done | bytes 524320 | tf_op jit(solution)/shard_map/all_to_all | solution.py:346
  74.4 1.6 %shard_map.73 = f32[16,2,8,256]{3,2,1,0:T(8,128)S(1)} custom-call(s32[5]{0:T(128)S(1)} %pad_add_fusion.where, bf16[128,128]{1,0:T(8,128)(2,1)S(1)} %collective-permute-done.2.tails, bf16[128,128]{1,0:T(8,128)(2,1)S(1)} %collective-permute-done.3.tails_other, bf16[16,152,128]{2,1,0:T(8,128)(2,1)S(1)} %all_to_all.20.sent.own, ...), custom_call_target="tpu_custom_call" | custom-call | tf_op jit(solution)/shard_map/pallas_call | solution.py:348
  76.0 30.5 %all_to_all.21 = f16[32,8,256]{2,1,0:T(8,128)(2,1)S(1)} all-to-all(f16[32,8,256]{2,1,0:T(8,128)(2,1)S(1)} %bitcast.23), channel_id=1, replica_groups=mesh['tm_0'=16,'tm_1'=4,'tm_2'=4,'state'=2] {'tm_0','state'}, dimensions={0} | all-to-all | bytes 262144 | tf_op jit(solution)/shard_map/all_to_all | solution.py:355
  106.5 1.2 %shard_map.74 = f32[8,512]{1,0:T(8,128)} custom-call(s32[5]{0:T(128)S(1)} %pad_add_fusion.where, f32[32,8,256]{2,1,0:T(8,128)S(1)} %convert_element_type.11.pieces, f32[2,16,128]{2,1,0:T(8,128)S(1)} %get-tuple-element.29.reach, f32[2,16,128]{2,1,0:T(8,128)S(1)} %collective-permute-done.5.reach_other), custom_call_target="tpu_custom_call" | custom-call | tf_op jit(solution)/shard_map/pallas_call | solution.py:356
  (11 shorter events, 0.1 us)
Async XLA Ops:
  0.6 11.0 %copy-start.3 = (s32[2]{0:T(128)S(1)}, s32[2]{0:T(128)}, u32[]{:S(2)}) copy-start(s32[2]{0:T(128)} %param.9) | copy-start | bytes 28
  0.6 11.1 %collective-permute-start = (bf16[128,2048]{1,0:T(8,128)(2,1)}, bf16[128,2048]{1,0:T(8,128)(2,1)S(1)}, u32[]{:S(2)}, u32[]{:S(2)}) collective-permute-start(bf16[128,2048]{1,0:T(8,128)(2,1)} %record.1), channel_id=1, source_target_pairs={{0,1},{1,0},{2,3},{3,2},{4,5},{5,4},{6,7},{7,6},{8,9},{9,8},{10,11... | collective-permute-start | bytes 1572872 | tf_op jit(solution)/shard_map/ppermute | solution.py:268
  9.4 4.0 %copy-start.2 = (f32[128,128]{1,0:T(8,128)S(1)}, f32[128,128]{1,0:T(8,128)}, u32[]{:S(2)}) copy-start(f32[128,128]{1,0:T(8,128)} %param.7) | copy-start | bytes 196612
  9.5 4.2 %copy-start.1 = (bf16[128,2048]{1,0:T(8,128)(2,1)S(1)}, bf16[128,2048]{1,0:T(8,128)(2,1)}, u32[]{:S(2)}) copy-start(bf16[128,2048]{1,0:T(8,128)(2,1)} %record.1) | copy-start | bytes 1572868
  11.7 3.5 %copy-start = (f32[128]{0:T(128)S(1)}, f32[128]{0:T(128)}, u32[]{:S(2)}) copy-start(f32[128]{0:T(128)} %param.8) | copy-start | bytes 1540
  12.2 3.0 %collective-permute-start.1 = (f32[64,256]{1,0:T(8,128)S(1)}, f32[64,256]{1,0:T(8,128)S(1)}, u32[]{:S(2)}, u32[]{:S(2)}) collective-permute-start(f32[64,256]{1,0:T(8,128)S(1)} %slice.14), channel_id=1, source_target_pairs={{0,2},{2,4},{4,6},{6,8},{8,10},{10,12},{12,14},{14,16},{16,18},{18... | collective-permute-start | bytes 196616 | tf_op jit(solution)/shard_map/ppermute | solution.py:303
  31.9 28.4 %all-to-all-start.1 = ((f32[16,8,128]{2,1,0:T(8,128)}), f32[16,8,128]{2,1,0:T(8,128)S(1)}, u32[]{:S(2)}, u32[]{:S(2)}) async-start(f32[16,8,128]{2,1,0:T(8,128)} %get-tuple-element.23), calls=%async_computation.1 | async-start | bytes 131072 | tf_op jit(solution)/shard_map/all_to_all | solution.py:335
  48.5 11.0 %collective-permute-start.2 = (bf16[128,128]{1,0:T(8,128)(2,1)S(1)}, bf16[128,128]{1,0:T(8,128)(2,1)S(1)}, u32[]{:S(2)}, u32[]{:S(2)}) collective-permute-start(bf16[128,128]{1,0:T(8,128)(2,1)S(1)} %slice_bitcast_fusion), channel_id=1, source_target_pairs={{0,32},{1,33},{32,64},{33,65},{64,96},{65,97},{96,128},{97,129},{1... | collective-permute-start | bytes 98312 | tf_op jit(solution)/shard_map/ppermute | solution.py:333
  51.8 7.8 %collective-permute-start.3 = (bf16[128,128]{1,0:T(8,128)(2,1)S(1)}, bf16[128,128]{1,0:T(8,128)(2,1)S(1)}, u32[]{:S(2)}, u32[]{:S(2)}) collective-permute-start(bf16[128,128]{1,0:T(8,128)(2,1)S(1)} %slice_bitcast_fusion), channel_id=1, source_target_pairs={{0,33},{1,32},{32,65},{33,64},{64,97},{65,96},{96,129},{97,128},{1... | collective-permute-start | bytes 98312 | tf_op jit(solution)/shard_map/ppermute | solution.py:334
  57.6 13.8 %collective-permute-start.4 = (bf16[16,128,128]{2,1,0:T(8,128)(2,1)S(1)}, bf16[16,128,128]{2,1,0:T(8,128)(2,1)S(1)}, u32[]{:S(2)}, u32[]{:S(2)}) collective-permute-start(bf16[16,128,128]{2,1,0:T(8,128)(2,1)S(1)} %slice.13), channel_id=1, source_target_pairs={{0,1},{1,0},{2,3},{3,2},{4,5},{5,4},{6,7},{7,6},{8,9},{9,8},{10,11... | collective-permute-start | bytes 1572872 | tf_op jit(solution)/shard_map/ppermute | solution.py:268
  61.8 12.5 %all-to-all-start.2 = ((bf16[16,128,128]{2,1,0:T(8,128)(2,1)}), bf16[16,128,128]{2,1,0:T(8,128)(2,1)S(1)}, u32[]{:S(2)}, u32[]{:S(2)}) async-start(bf16[16,128,128]{2,1,0:T(8,128)(2,1)} %get-tuple-element.28), calls=%async_computation.2 | async-start | bytes 1048576 | tf_op jit(solution)/shard_map/all_to_all | solution.py:346
  65.4 5.9 %collective-permute-start.5 = (f32[2,16,128]{2,1,0:T(8,128)S(1)}, f32[2,16,128]{2,1,0:T(8,128)S(1)}, u32[]{:S(2)}, u32[]{:S(2)}) collective-permute-start(f32[2,16,128]{2,1,0:T(8,128)S(1)} %get-tuple-element.29.reach), channel_id=1, source_target_pairs={{0,1},{1,0},{2,3},{3,2},{4,5},{5,4},{6,7},{7,6},{8,9},{9,8},{10,11... | collective-permute-start | bytes 49160 | tf_op jit(solution)/shard_map/ppermute | solution.py:268

commit v7 on v6

--- a/solution.py
+++ b/solution.py
@@ -218,7 +218,7 @@
     return jnp.maximum(span * first[0] * jnp.maximum(first[1], second[1]), 1e-30)
 
 
-def gradient_body(where, tails, tails_other, own, other, resid, reach, reach_other, out, padded):
+def gradient_body(where, tails, own, other, resid, reach, reach_other, out, padded):
     blocks, frames, modes = resid.shape
     row = lax.broadcasted_iota(jnp.int32, (frames, 2 * frames), 0)
     column = lax.broadcasted_iota(jnp.int32, (frames, 2 * frames), 1)
@@ -236,9 +236,9 @@
     plane = lax.broadcasted_iota(jnp.int32, bound.shape, 0)
     factor = jnp.sum(jnp.where(plane == where[0], TOP / bound, 0.0), axis=0, keepdims=True)
     factor = jnp.concatenate([factor] * TAPS, 1)
-    for which, (before, rows) in enumerate(((tails, own), (tails_other, other))):
+    for which, (before, rows) in enumerate(((tails[0], own), (tails[1], other))):
         lhs = jnp.concatenate(
-            [before[...]] + [rows[i, : before.shape[0]] for i in range(blocks)], 1
+            [before] + [rows[i, : before.shape[0]] for i in range(blocks)], 1
         )
         sums = jnp.dot(lhs, rhs, preferred_element_type=F32) * factor
         half = jnp.where(where[2] == which, 0, 1)
@@ -326,14 +326,8 @@
         smem=(),
         n_in=1,
     )(mine)
-    ready = behind(mine, plane_summary)[:, :-24]
-    theirs = swapped(ready)
-    onward = [(2 * i + c, 2 * i + 2 + c) for i in range(planes - 1) for c in range(2)]
-    across = [(2 * i + c, 2 * i + 3 - c) for i in range(planes - 1) for c in range(2)]
-    tails = lax.ppermute(ready[-1], (Z, "state"), onward)
-    tails_other = lax.ppermute(ready[-1], (Z, "state"), across)
+    theirs = swapped(mine[:, :-24])
     every_plane = lax.all_to_all(plane_summary, Z, 0, 0, tiled=True)
-    every_plane = behind(every_plane, (tails, tails_other))
     smoothed, resid, reach = call(
         finish_body,
         (
@@ -344,13 +338,15 @@
         n_in=6,
     )(where, plane, every_plane, keep, decay, leak_row)
     resid_all = lax.all_to_all(resid, YX, 0, 0, tiled=True)
+    tails = behind(jnp.stack([mine[-1, :-24], theirs[-1]]), resid)
+    tails = lax.ppermute(tails, Z, [(i, i + 1) for i in range(planes - 1)])
     reach_other = swapped(reach)
     partial = call(
         gradient_body,
         jax.ShapeDtypeStruct((planes, 2, group, TAPS * modes), F32),
         scratch=[pltpu.VMEM(((blocks + 1) * frames, TAPS * modes), BF16)],
-        n_in=8,
-    )(where, tails, tails_other, mine, theirs, resid_all, reach, reach_other)
+        n_in=7,
+    )(where, tails, mine, theirs, resid_all, reach, reach_other)
     pieces = partial.reshape(planes * 2, group, TAPS * modes).astype(jnp.float16)
     pieces = lax.all_to_all(pieces, (Z, "state"), 0, 0, tiled=True)
     grad = call(

time: 108 us -> 101 us (0.935)
  blocking collectives: 45.7 us -> 39 us
  starting transfers between devices: 46.3 us -> 42.4 us
  waiting for transfers between devices: 5.68 us -> 9.35 us
    all_to_all x1, waiting for transfers between devices: 0.74 us -> 7.4 us  [per_device(): every_plane = lax.all_to_all(plane_summary, Z, 0, 0, tiled=True)]
    all_to_all x1, blocking collectives: 30.5 us -> 23.9 us  [per_device(): pieces = lax.all_to_all(pieces, (Z, 'state'), 0, 0, tiled=True)]
    ppermute x2 -> x1, starting transfers between devices: 9.02 us -> 2.65 us  [per_device(): tails = lax.ppermute(tails, Z, [(i, i + 1) for i in range(planes - 1)])]
    all_to_all x1, waiting for transfers between devices: 3.01 us -> 0.03 us  [per_device(): resid_all = lax.all_to_all(resid, YX, 0, 0, tiled=True)]
    ppermute x3, starting transfers between devices: 15.8 us -> 18.3 us  [swapped(): return lax.ppermute(x, 'state', [(0, 1), (1, 0)])]
  transfers between devices with their start and end apart: 8 -> 7, of which waited for: 4 -> 3; matrix products, arithmetic and copies ran while one was open for 1% -> 1% of each run, Pallas kernels for 3% -> 4%
where the time goes in v7:
time: 101 us
  starting transfers between devices  42.4 us (42%)
  blocking collectives  39 us (39%)
  waiting for transfers between devices  9.35 us (9%)
  Pallas kernels  8.42 us (8%)
    all_to_all x1, blocking collectives, per_device(): pieces = lax.all_to_all(pieces, (Z, 'state'), 0, 0, tiled=True)  23.9 us
    ppermute x3, starting transfers between devices, swapped(): return lax.ppermute(x, 'state', [(0, 1), (1, 0)])  18.3 us
    all_to_all x1, starting transfers between devices, per_device(): every_plane = lax.all_to_all(plane_summary, Z, 0, 0, tiled=True)  16.6 us
    all_to_all x1, blocking collectives, per_device(): mine = lax.all_to_all(sent, YX, 0, 0, tiled=True)  15.1 us
    all_to_all x1, waiting for transfers between devices, per_device(): every_plane = lax.all_to_all(plane_summary, Z, 0, 0, tiled=True)  7.4 us
    all_to_all x1, starting transfers between devices, per_device(): resid_all = lax.all_to_all(resid, YX, 0, 0, tiled=True)  3.57 us
    ppermute x1, starting transfers between devices, per_device(): tails = lax.ppermute(tails, Z, [(i, i + 1) for i in range(planes - 1)])  2.65 us
    pallas_call x1, Pallas kernels, per_device(): call(own_body, (both, jax.ShapeDtypeStruct(half_gain, BF16), jax.ShapeDty...  2.13 us
  transfers between devices with their start and end apart: 7, of which 3 were waited for; matrix products, arithmetic and copies ran while one was open for 1% of the time, Pallas kernels for 4%

profile of v7, /device:TPU:1, one launch (start us, length us, event | category | flops | bytes accessed | tf_op | source)
XLA Modules:
  0.0 100.8 jit_solution(9874284626560701550)
XLA Ops:
  0.6 0.0 copy-start.3
  0.6 8.8 %collective-permute-start = (bf16[128,2048]{1,0:T(8,128)(2,1)}, bf16[128,2048]{1,0:T(8,128)(2,1)S(1)}, u32[]{:S(2)}, u32[]{:S(2)}) collective-permute-start(bf16[128,2048]{1,0:T(8,128)(2,1)} %record.1), channel_id=1, source_target_pairs={{0,1},{1,0},{2,3},{3,2},{4,5},{5,4},{6,7},{7,6},{8,9},{9,8},{10,11... | collective-permute-start | bytes 1572872 | tf_op jit(solution)/shard_map/ppermute | solution.py:268
  9.4 0.0 copy-start.2
  9.5 0.0 copy-start.1
  9.5 2.1 %shard_map.68 = (f32[128,256]{1,0:T(8,128)S(1)}, bf16[2,128,2048]{2,1,0:T(8,128)(2,1)S(1)}, f32[8,128]{1,0:T(8,128)S(1)}) custom-call(bf16[128,2048]{1,0:T(8,128)(2,1)} %record.1, bf16[2,128,4096]{2,1,0:T(8,128)(2,1)} %gain.1), custom_call_target="tpu_custom_call" | custom-call | tf_op jit(solution)/shard_map/pallas_call | solution.py:286
  11.6 0.0 copy-done.3
  11.6 0.1 pad_add_fusion.where
  11.7 0.0 collective-permute-done.other
  11.7 0.4 shard_map.69.u
  12.2 1.3 %collective-permute-start.1 = (f32[64,256]{1,0:T(8,128)S(1)}, f32[64,256]{1,0:T(8,128)S(1)}, u32[]{:S(2)}, u32[]{:S(2)}) collective-permute-start(f32[64,256]{1,0:T(8,128)S(1)} %slice.16), channel_id=1, source_target_pairs={{0,2},{2,4},{4,6},{6,8},{8,10},{10,12},{12,14},{14,16},{16,18},{18... | collective-permute-start | bytes 196616 | tf_op jit(solution)/shard_map/ppermute | solution.py:303
  13.5 0.1 copy.10
  13.6 0.1 sqrt_bitcast_fusion
  13.6 0.3 copy.12
  13.9 0.1 copy.15
  14.1 1.1 %collective-permute-done.1.tail = f32[64,256]{1,0:T(8,128)S(1)} collective-permute-done((f32[64,256]{1,0:T(8,128)S(1)}, f32[64,256]{1,0:T(8,128)S(1)}, u32[]{:S(2)}, u32[]{:S(2)}) %collective-permute-start.1) | collective-permute-done | bytes 65568 | tf_op jit(solution)/shard_map/ppermute | solution.py:303
  15.2 0.8 shard_map.70
  16.0 15.1 %all_to_all.20.sent.own = bf16[16,152,128]{2,1,0:T(8,128)(2,1)S(1)} all-to-all(bf16[16,152,128]{2,1,0:T(8,128)(2,1)S(1)} %get-tuple-element.20), channel_id=1, replica_groups=mesh['tm_0'=16,'tm_1'=4,'tm_2'=4,'state'=2] {'tm_1','tm_2'}, dimensions={0} | all-to-all | bytes 1245184 | tf_op jit(solution)/shard_map/all_to_all | solution.py:319
  31.2 0.7 shard_map.71
  31.9 16.6 %all-to-all-start.1 = ((f32[16,8,128]{2,1,0:T(8,128)}), f32[16,8,128]{2,1,0:T(8,128)S(1)}, u32[]{:S(2)}, u32[]{:S(2)}) async-start(f32[16,8,128]{2,1,0:T(8,128)} %get-tuple-element.22), calls=%async_computation.1 | async-start | bytes 131072 | tf_op jit(solution)/shard_map/all_to_all | solution.py:330
  48.5 4.1 %collective-permute-start.2 = (bf16[16,128,128]{2,1,0:T(8,128)(2,1)S(1)}, bf16[16,128,128]{2,1,0:T(8,128)(2,1)S(1)}, u32[]{:S(2)}, u32[]{:S(2)}) collective-permute-start(bf16[16,128,128]{2,1,0:T(8,128)(2,1)S(1)} %slice.18), channel_id=1, source_target_pairs={{0,1},{1,0},{2,3},{3,2},{4,5},{5,4},{6,7},{7,6},{8,9},{9,8},{10,11... | collective-permute-start | bytes 1572872 | tf_op jit(solution)/shard_map/ppermute | solution.py:268
  52.7 7.4 %all-to-all-done.1.planes = f32[16,8,128]{2,1,0:T(8,128)S(1)} async-done(((f32[16,8,128]{2,1,0:T(8,128)}), f32[16,8,128]{2,1,0:T(8,128)S(1)}, u32[]{:S(2)}, u32[]{:S(2)}) %all-to-all-start.1) | async-done | bytes 65568 | tf_op jit(solution)/shard_map/all_to_all | solution.py:330
  60.1 1.6 %shard_map.72 = (f32[128,128]{1,0:T(8,128)}, bf16[16,128,128]{2,1,0:T(8,128)(2,1)}, f32[2,16,128]{2,1,0:T(8,128)S(1)}) custom-call(s32[5]{0:T(128)S(1)} %pad_add_fusion.where, f32[16,8,128]{2,1,0:T(8,128)S(1)} %get-tuple-element.21.plane, f32[16,8,128]{2,1,0:T(8,128)S(1)} %all-to-all-done.1.planes, f32[6,128,128]{2,1,0:T(8,128)S(1)} %get-tuple-element.23.keep, ...), custom_call_target="tpu_custom_call" | custom-call | tf_op jit(solution)/shard_map/pallas_call | solution.py:331
  61.6 3.6 %all-to-all-start.2 = ((bf16[16,128,128]{2,1,0:T(8,128)(2,1)}), bf16[16,128,128]{2,1,0:T(8,128)(2,1)S(1)}, u32[]{:S(2)}, u32[]{:S(2)}) async-start(bf16[16,128,128]{2,1,0:T(8,128)(2,1)} %get-tuple-element.25), calls=%async_computation.2 | async-start | bytes 1048576 | tf_op jit(solution)/shard_map/all_to_all | solution.py:340
  65.2 0.0 collective-permute-done.2.other
  65.3 2.6 %collective-permute-start.3 = (bf16[2,128,128]{2,1,0:T(8,128)(2,1)S(1)}, bf16[2,128,128]{2,1,0:T(8,128)(2,1)S(1)}, u32[]{:S(2)}, u32[]{:S(2)}) collective-permute-start(bf16[2,128,128]{2,1,0:T(8,128)(2,1)S(1)} %pad_maximum_fusion), channel_id=1, source_target_pairs={{0,32},{32,64},{64,96},{96,128},{128,160},{160,192},{192,224},{224... | collective-permute-start | bytes 196616 | tf_op jit(solution)/shard_map/ppermute | solution.py:342
  67.9 5.4 %collective-permute-start.4 = (f32[2,16,128]{2,1,0:T(8,128)S(1)}, f32[2,16,128]{2,1,0:T(8,128)S(1)}, u32[]{:S(2)}, u32[]{:S(2)}) collective-permute-start(f32[2,16,128]{2,1,0:T(8,128)S(1)} %get-tuple-element.27.reach), channel_id=1, source_target_pairs={{0,1},{1,0},{2,3},{3,2},{4,5},{5,4},{6,7},{7,6},{8,9},{9,8},{10,11... | collective-permute-start | bytes 49160 | tf_op jit(solution)/shard_map/ppermute | solution.py:268
  73.3 0.8 collective-permute-done.4.reach_other
  74.1 0.0 collective-permute-done.3.tails
  74.1 0.0 all-to-all-done.2.resid
  74.2 1.6 %shard_map.73 = f32[16,2,8,256]{3,2,1,0:T(8,128)S(1)} custom-call(s32[5]{0:T(128)S(1)} %pad_add_fusion.where, bf16[2,128,128]{2,1,0:T(8,128)(2,1)S(1)} %collective-permute-done.3.tails, bf16[16,152,128]{2,1,0:T(8,128)(2,1)S(1)} %all_to_all.20.sent.own, bf16[16,128,128]{2,1,0:T(8,128)(2,1)S(1)} %collective-permute-done.2.other, ...), custom_call_target="tpu_custom_call" | custom-call | tf_op jit(solution)/shard_map/pallas_call | solution.py:344
  75.8 23.9 %all_to_all.21 = f16[32,8,256]{2,1,0:T(8,128)(2,1)S(1)} all-to-all(f16[32,8,256]{2,1,0:T(8,128)(2,1)S(1)} %bitcast.21), channel_id=1, replica_groups=mesh['tm_0'=16,'tm_1'=4,'tm_2'=4,'state'=2] {'tm_0','state'}, dimensions={0} | all-to-all | bytes 262144 | tf_op jit(solution)/shard_map/all_to_all | solution.py:351
  99.7 1.2 %shard_map.74 = f32[8,512]{1,0:T(8,128)} custom-call(s32[5]{0:T(128)S(1)} %pad_add_fusion.where, f32[32,8,256]{2,1,0:T(8,128)S(1)} %convert_element_type.11.pieces, f32[2,16,128]{2,1,0:T(8,128)S(1)} %get-tuple-element.27.reach, f32[2,16,128]{2,1,0:T(8,128)S(1)} %collective-permute-done.4.reach_other), custom_call_target="tpu_custom_call" | custom-call | tf_op jit(solution)/shard_map/pallas_call | solution.py:352
  (11 shorter events, 0.1 us)
Async XLA Ops:
  0.6 11.0 %copy-start.3 = (s32[2]{0:T(128)S(1)}, s32[2]{0:T(128)}, u32[]{:S(2)}) copy-start(s32[2]{0:T(128)} %param.9) | copy-start | bytes 28
  0.6 11.1 %collective-permute-start = (bf16[128,2048]{1,0:T(8,128)(2,1)}, bf16[128,2048]{1,0:T(8,128)(2,1)S(1)}, u32[]{:S(2)}, u32[]{:S(2)}) collective-permute-start(bf16[128,2048]{1,0:T(8,128)(2,1)} %record.1), channel_id=1, source_target_pairs={{0,1},{1,0},{2,3},{3,2},{4,5},{5,4},{6,7},{7,6},{8,9},{9,8},{10,11... | collective-permute-start | bytes 1572872 | tf_op jit(solution)/shard_map/ppermute | solution.py:268
  9.4 4.0 %copy-start.2 = (f32[128,128]{1,0:T(8,128)S(1)}, f32[128,128]{1,0:T(8,128)}, u32[]{:S(2)}) copy-start(f32[128,128]{1,0:T(8,128)} %param.7) | copy-start | bytes 196612
  9.5 4.2 %copy-start.1 = (bf16[128,2048]{1,0:T(8,128)(2,1)S(1)}, bf16[128,2048]{1,0:T(8,128)(2,1)}, u32[]{:S(2)}) copy-start(bf16[128,2048]{1,0:T(8,128)(2,1)} %record.1) | copy-start | bytes 1572868
  11.7 3.5 %copy-start = (f32[128]{0:T(128)S(1)}, f32[128]{0:T(128)}, u32[]{:S(2)}) copy-start(f32[128]{0:T(128)} %param.8) | copy-start | bytes 1540
  12.2 3.0 %collective-permute-start.1 = (f32[64,256]{1,0:T(8,128)S(1)}, f32[64,256]{1,0:T(8,128)S(1)}, u32[]{:S(2)}, u32[]{:S(2)}) collective-permute-start(f32[64,256]{1,0:T(8,128)S(1)} %slice.16), channel_id=1, source_target_pairs={{0,2},{2,4},{4,6},{6,8},{8,10},{10,12},{12,14},{14,16},{16,18},{18... | collective-permute-start | bytes 196616 | tf_op jit(solution)/shard_map/ppermute | solution.py:303
  31.9 28.2 %all-to-all-start.1 = ((f32[16,8,128]{2,1,0:T(8,128)}), f32[16,8,128]{2,1,0:T(8,128)S(1)}, u32[]{:S(2)}, u32[]{:S(2)}) async-start(f32[16,8,128]{2,1,0:T(8,128)} %get-tuple-element.22), calls=%async_computation.1 | async-start | bytes 131072 | tf_op jit(solution)/shard_map/all_to_all | solution.py:330
  48.5 16.7 %collective-permute-start.2 = (bf16[16,128,128]{2,1,0:T(8,128)(2,1)S(1)}, bf16[16,128,128]{2,1,0:T(8,128)(2,1)S(1)}, u32[]{:S(2)}, u32[]{:S(2)}) collective-permute-start(bf16[16,128,128]{2,1,0:T(8,128)(2,1)S(1)} %slice.18), channel_id=1, source_target_pairs={{0,1},{1,0},{2,3},{3,2},{4,5},{5,4},{6,7},{7,6},{8,9},{9,8},{10,11... | collective-permute-start | bytes 1572872 | tf_op jit(solution)/shard_map/ppermute | solution.py:268
  61.6 12.5 %all-to-all-start.2 = ((bf16[16,128,128]{2,1,0:T(8,128)(2,1)}), bf16[16,128,128]{2,1,0:T(8,128)(2,1)S(1)}, u32[]{:S(2)}, u32[]{:S(2)}) async-start(bf16[16,128,128]{2,1,0:T(8,128)(2,1)} %get-tuple-element.25), calls=%async_computation.2 | async-start | bytes 1048576 | tf_op jit(solution)/shard_map/all_to_all | solution.py:340
  65.3 8.9 %collective-permute-start.3 = (bf16[2,128,128]{2,1,0:T(8,128)(2,1)S(1)}, bf16[2,128,128]{2,1,0:T(8,128)(2,1)S(1)}, u32[]{:S(2)}, u32[]{:S(2)}) collective-permute-start(bf16[2,128,128]{2,1,0:T(8,128)(2,1)S(1)} %pad_maximum_fusion), channel_id=1, source_target_pairs={{0,32},{32,64},{64,96},{96,128},{128,160},{160,192},{192,224},{224... | collective-permute-start | bytes 196616 | tf_op jit(solution)/shard_map/ppermute | solution.py:342
  67.9 6.2 %collective-permute-start.4 = (f32[2,16,128]{2,1,0:T(8,128)S(1)}, f32[2,16,128]{2,1,0:T(8,128)S(1)}, u32[]{:S(2)}, u32[]{:S(2)}) collective-permute-start(f32[2,16,128]{2,1,0:T(8,128)S(1)} %get-tuple-element.27.reach), channel_id=1, source_target_pairs={{0,1},{1,0},{2,3},{3,2},{4,5},{5,4},{6,7},{7,6},{8,9},{9,8},{10,11... | collective-permute-start | bytes 49160 | tf_op jit(solution)/shard_map/ppermute | solution.py:268

commit v8 on v7

--- a/solution.py
+++ b/solution.py
@@ -10,6 +10,7 @@
 
 TAPS = 2
 TOP = 32768.0
+PIECES = 4
 DMAX = 64
 Z = "tm_0"
 YX = ("tm_1", "tm_2")
@@ -61,49 +62,61 @@
 
 def own_body(record, gain, out, gain_rest, peak, own, gain_own, arrived):
     modes = gain_own.shape[1]
-    half = own.shape[1]
+    frames, half = own.shape
     core = lax.axis_index("state")
     mine = pl.multiple_of(core * half, half)
     theirs = pl.multiple_of((1 - core) * half, half)
-    copies = [pltpu.make_async_copy(record, own, arrived.at[0])]
+    record_copies = []
+    gain_copies = []
+    rest_copies = []
+    for piece in range(PIECES):
+        rows = pl.ds(piece * (frames // PIECES), frames // PIECES)
+        record_copies.append((record.at[rows], own.at[rows]))
     for k in range(TAPS):
-        copies.append(
-            pltpu.make_async_copy(
-                gain.at[k, :, pl.ds(mine, half)], gain_own.at[k], arrived.at[1 + k]
-            )
-        )
-    rest = pltpu.make_async_copy(gain.at[:, :, pl.ds(theirs, half)], gain_rest, arrived.at[1 + TAPS])
+        for piece in range(PIECES):
+            rows = pl.ds(piece * (modes // PIECES), modes // PIECES)
+            gain_copies.append((gain.at[k, rows, pl.ds(mine, half)], gain_own.at[k, rows]))
+            rest_copies.append((gain.at[k, rows, pl.ds(theirs, half)], gain_rest.at[k, rows]))
+    copies = [
+        pltpu.make_async_copy(source, target, arrived.at[n])
+        for n, (source, target) in enumerate(record_copies + gain_copies + rest_copies)
+    ]
     for copy in copies:
         copy.start()
-    rest.start()
-    copies[0].wait()
+    for copy in copies[:PIECES]:
+        copy.wait()
     largest = jnp.max(jnp.abs(own[...].astype(F32)), axis=0, keepdims=True)
     peak[...] = jnp.broadcast_to(jnp.max(largest, axis=1, keepdims=True), peak.shape)
     for k in range(TAPS):
-        copies[1 + k].wait()
+        for copy in copies[(1 + k) * PIECES : (2 + k) * PIECES]:
+            copy.wait()
         out[:, k * modes : (k + 1) * modes] = lax.dot_general(
             own[...], gain_own[k], NT, preferred_element_type=F32
         )
-    rest.wait()
-
-
-def rest_body(other, gain, part, out):
+    for copy in copies[(1 + TAPS) * PIECES :]:
+        copy.wait()
+
+
+def rest_body(where, other, gain, part, out, tail):
     modes = gain.shape[1]
+    row = lax.broadcasted_iota(jnp.int32, out.shape, 0)
+    here = jnp.zeros(out.shape, F32)
+    onward = jnp.zeros(out.shape, F32)
     for k in range(TAPS):
-        columns = slice(k * modes, (k + 1) * modes)
-        out[:, columns] = part[:, columns] + lax.dot_general(
+        u = part[:, k * modes : (k + 1) * modes] + lax.dot_general(
             other[...], gain[k], NT, preferred_element_type=F32
         )
-
-
-def local_body(where, u, tail, decay_ref, scale, leak, by_sensor, peak, keep, sent, ext):
+        delayed = pltpu.roll(u, where[3 + k], 0)
+        here += jnp.where(row >= where[3 + k], delayed, 0.0)
+        onward += jnp.where(row < where[3 + k], delayed, 0.0)
+    out[...] = here
+    tail[...] = onward[:DMAX]
+
+
+def local_body(here, tail, decay_ref, scale, leak, by_sensor, peak, keep, sent):
     frames, modes = decay_ref.shape
-    ext[:DMAX] = tail[...]
-    ext[DMAX:] = u[...]
-    drive_in = jnp.zeros((frames, modes), F32)
-    for k in range(TAPS):
-        rolled = pltpu.roll(ext[:, k * modes : (k + 1) * modes], frames + where[3 + k], 0)
-        drive_in += rolled[:frames]
+    nothing = jnp.zeros((frames - DMAX, modes), F32)
+    drive_in = here[...] + jnp.concatenate([tail[...], nothing], 0)
     drive = scale[...] * drive_in
     decay = decay_ref[...]
     prods, (offsets,) = recur(decay, [drive], later)
@@ -293,19 +306,26 @@
         scratch=[
             pltpu.VMEM((frames, sensors), BF16),
             pltpu.VMEM(half_gain, BF16),
-            pltpu.SemaphoreType.DMA((2 + TAPS,)),
+            pltpu.SemaphoreType.DMA(((1 + 2 * TAPS) * PIECES,)),
         ],
         smem=(),
         whole=(0, 1),
         n_in=2,
     )(*(pltpu.with_memory_space_constraint(x, pltpu.HBM) for x in (record, gain)))
-    u = call(rest_body, both, smem=(), n_in=3)(other, gain_rest, part)
-    u_tail = lax.ppermute(u[frames - DMAX :], TM, [(i, i + 1) for i in range(planes * blocks - 1)])
-    rate_t = behind(rate, u).T
+    here, onward = call(
+        rest_body,
+        (
+            jax.ShapeDtypeStruct((frames, modes), F32),
+            jax.ShapeDtypeStruct((DMAX, modes), F32),
+        ),
+        n_in=4,
+    )(where, other, gain_rest, part)
+    tail = lax.ppermute(onward, TM, [(i, i + 1) for i in range(planes * blocks - 1)])
+    rate_t = behind(rate, here).T
     decay = jnp.exp(-rate_t)
     scale = jnp.sqrt(-jnp.expm1(-2.0 * rate_t))
     leak_row = leak[None]
-    by_sensor = behind(record, u).T.reshape(planes, blocks, group, frames).swapaxes(0, 1)
+    by_sensor = behind(record, here).T.reshape(planes, blocks, group, frames).swapaxes(0, 1)
     by_sensor = by_sensor.reshape(blocks, planes * group, frames)
     keep, sent = call(
         local_body,
@@ -313,9 +333,9 @@
             jax.ShapeDtypeStruct((6, frames, modes), F32),
             jax.ShapeDtypeStruct((blocks, planes * group + 24, frames), BF16),
         ),
-        scratch=[pltpu.VMEM((DMAX + frames, TAPS * modes), F32)],
-        n_in=8,
-    )(where, u, u_tail, decay, scale, leak_row, by_sensor, peak)
+        smem=(),
+        n_in=7,
+    )(here, tail, decay, scale, leak_row, by_sensor, peak)
     mine = lax.all_to_all(sent, YX, 0, 0, tiled=True)
     plane, plane_summary = call(
         plane_body,

time: 101 us -> 101 us (level)
  waiting for transfers between devices: 9.35 us -> 8.23 us
where the time goes in v8:
time: 101 us; the launch traced here: 100 us
  starting transfers between devices  43.1 us (43%)
  blocking collectives  38.5 us (38%)
  Pallas kernels  8.64 us (9%)
  waiting for transfers between devices  8.23 us (8%)
    all_to_all x1, blocking collectives, per_device(): pieces = lax.all_to_all(pieces, (Z, 'state'), 0, 0, tiled=True)  23.7 us
    ppermute x3, starting transfers between devices, swapped(): return lax.ppermute(x, 'state', [(0, 1), (1, 0)])  19.3 us
    all_to_all x1, starting transfers between devices, per_device(): every_plane = lax.all_to_all(plane_summary, Z, 0, 0, tiled=True)  16.3 us
    all_to_all x1, blocking collectives, per_device(): mine = lax.all_to_all(sent, YX, 0, 0, tiled=True)  14.8 us
    all_to_all x1, waiting for transfers between devices, per_device(): every_plane = lax.all_to_all(plane_summary, Z, 0, 0, tiled=True)  6.99 us
    all_to_all x1, starting transfers between devices, per_device(): resid_all = lax.all_to_all(resid, YX, 0, 0, tiled=True)  3.57 us
    ppermute x1, starting transfers between devices, per_device(): tails = lax.ppermute(tails, Z, [(i, i + 1) for i in range(planes - 1)])  2.66 us
    pallas_call x1, Pallas kernels, per_device(): call(own_body, (both, jax.ShapeDtypeStruct(half_gain, BF16), jax.ShapeDty...  2.37 us
  transfers between devices with their start and end apart: 7, of which 3 were waited for; matrix products, arithmetic and copies ran while one was open for 1% of the time, Pallas kernels for 4%

profile of v8, /device:TPU:1, one launch (start us, length us, event | category | flops | bytes accessed | tf_op | source)
XLA Modules:
  0.0 100.1 jit_solution(14474903154869043376)
XLA Ops:
  0.6 0.0 copy-start.3
  0.6 8.8 %collective-permute-start = (bf16[128,2048]{1,0:T(8,128)(2,1)}, bf16[128,2048]{1,0:T(8,128)(2,1)S(1)}, u32[]{:S(2)}, u32[]{:S(2)}) collective-permute-start(bf16[128,2048]{1,0:T(8,128)(2,1)} %record.1), channel_id=1, source_target_pairs={{0,1},{1,0},{2,3},{3,2},{4,5},{5,4},{6,7},{7,6},{8,9},{9,8},{10,11... | collective-permute-start | bytes 1572872 | tf_op jit(solution)/shard_map/ppermute | solution.py:281
  9.4 0.0 copy-start.2
  9.5 2.4 %shard_map.68 = (f32[128,256]{1,0:T(8,128)S(1)}, bf16[2,128,2048]{2,1,0:T(8,128)(2,1)S(1)}, f32[8,128]{1,0:T(8,128)S(1)}) custom-call(bf16[128,2048]{1,0:T(8,128)(2,1)} %record.1, bf16[2,128,4096]{2,1,0:T(8,128)(2,1)} %gain.1), custom_call_target="tpu_custom_call" | custom-call | tf_op jit(solution)/shard_map/pallas_call | solution.py:299
  11.8 0.0 copy-start
  11.9 0.0 copy-done.3
  11.9 0.1 pad_add_fusion.where
  11.9 0.0 collective-permute-done.other
  12.0 1.0 %shard_map.69 = (f32[128,128]{1,0:T(8,128)S(1)}, f32[64,128]{1,0:T(8,128)S(1)}) custom-call(s32[5]{0:T(128)S(1)} %pad_add_fusion.where, bf16[128,2048]{1,0:T(8,128)(2,1)S(1)} %collective-permute-done.other, bf16[2,128,2048]{2,1,0:T(8,128)(2,1)S(1)} %get-tuple-element.17.gain, f32[128,256]{1,0:T(8,128)S(1)} %get-tuple-element.18.part), custom_call_target="tpu_custom_call" | custom-call | tf_op jit(solution)/shard_map/pallas_call | solution.py:315
  13.0 1.3 %collective-permute-start.1 = (f32[64,128]{1,0:T(8,128)S(1)}, f32[64,128]{1,0:T(8,128)S(1)}, u32[]{:S(2)}, u32[]{:S(2)}) collective-permute-start(f32[64,128]{1,0:T(8,128)S(1)} %get-tuple-element.20), channel_id=1, source_target_pairs={{0,2},{2,4},{4,6},{6,8},{8,10},{10,12},{12,14},{14,16},{16,18},{18... | collective-permute-start | bytes 98312 | tf_op jit(solution)/shard_map/ppermute | solution.py:323
  14.3 0.1 copy.10
  14.4 0.1 sqrt_bitcast_fusion
  14.4 0.3 copy.12
  14.7 0.1 copy.15
  14.9 0.4 collective-permute-done.1.tail
  15.3 0.2 shard_map.70
  15.5 14.8 %all_to_all.20.sent.own = bf16[16,152,128]{2,1,0:T(8,128)(2,1)S(1)} all-to-all(bf16[16,152,128]{2,1,0:T(8,128)(2,1)S(1)} %get-tuple-element.24), channel_id=1, replica_groups=mesh['tm_0'=16,'tm_1'=4,'tm_2'=4,'state'=2] {'tm_1','tm_2'}, dimensions={0} | all-to-all | bytes 1245184 | tf_op jit(solution)/shard_map/all_to_all | solution.py:339
  30.3 0.7 shard_map.71
  31.0 16.3 %all-to-all-start.1 = ((f32[16,8,128]{2,1,0:T(8,128)}), f32[16,8,128]{2,1,0:T(8,128)S(1)}, u32[]{:S(2)}, u32[]{:S(2)}) async-start(f32[16,8,128]{2,1,0:T(8,128)} %get-tuple-element.26), calls=%async_computation.1 | async-start | bytes 131072 | tf_op jit(solution)/shard_map/all_to_all | solution.py:350
  47.4 4.5 %collective-permute-start.2 = (bf16[16,128,128]{2,1,0:T(8,128)(2,1)S(1)}, bf16[16,128,128]{2,1,0:T(8,128)(2,1)S(1)}, u32[]{:S(2)}, u32[]{:S(2)}) collective-permute-start(bf16[16,128,128]{2,1,0:T(8,128)(2,1)S(1)} %slice.13), channel_id=1, source_target_pairs={{0,1},{1,0},{2,3},{3,2},{4,5},{5,4},{6,7},{7,6},{8,9},{9,8},{10,11... | collective-permute-start | bytes 1572872 | tf_op jit(solution)/shard_map/ppermute | solution.py:281
  51.9 7.0 %all-to-all-done.1.planes = f32[16,8,128]{2,1,0:T(8,128)S(1)} async-done(((f32[16,8,128]{2,1,0:T(8,128)}), f32[16,8,128]{2,1,0:T(8,128)S(1)}, u32[]{:S(2)}, u32[]{:S(2)}) %all-to-all-start.1) | async-done | bytes 65568 | tf_op jit(solution)/shard_map/all_to_all | solution.py:350
  58.9 1.6 %shard_map.72 = (f32[128,128]{1,0:T(8,128)}, bf16[16,128,128]{2,1,0:T(8,128)(2,1)}, f32[2,16,128]{2,1,0:T(8,128)S(1)}) custom-call(s32[5]{0:T(128)S(1)} %pad_add_fusion.where, f32[16,8,128]{2,1,0:T(8,128)S(1)} %get-tuple-element.25.plane, f32[16,8,128]{2,1,0:T(8,128)S(1)} %all-to-all-done.1.planes, f32[6,128,128]{2,1,0:T(8,128)S(1)} %get-tuple-element.27.keep, ...), custom_call_target="tpu_custom_call" | custom-call | tf_op jit(solution)/shard_map/pallas_call | solution.py:351
  60.5 3.6 %all-to-all-start.2 = ((bf16[16,128,128]{2,1,0:T(8,128)(2,1)}), bf16[16,128,128]{2,1,0:T(8,128)(2,1)S(1)}, u32[]{:S(2)}, u32[]{:S(2)}) async-start(bf16[16,128,128]{2,1,0:T(8,128)(2,1)} %get-tuple-element.29), calls=%async_computation.2 | async-start | bytes 1048576 | tf_op jit(solution)/shard_map/all_to_all | solution.py:360
  64.1 0.0 collective-permute-done.2.other
  64.1 2.7 %collective-permute-start.3 = (bf16[2,128,128]{2,1,0:T(8,128)(2,1)S(1)}, bf16[2,128,128]{2,1,0:T(8,128)(2,1)S(1)}, u32[]{:S(2)}, u32[]{:S(2)}) collective-permute-start(bf16[2,128,128]{2,1,0:T(8,128)(2,1)S(1)} %pad_maximum_fusion), channel_id=1, source_target_pairs={{0,32},{32,64},{64,96},{96,128},{128,160},{160,192},{192,224},{224... | collective-permute-start | bytes 196616 | tf_op jit(solution)/shard_map/ppermute | solution.py:362
  66.8 5.9 %collective-permute-start.4 = (f32[2,16,128]{2,1,0:T(8,128)S(1)}, f32[2,16,128]{2,1,0:T(8,128)S(1)}, u32[]{:S(2)}, u32[]{:S(2)}) collective-permute-start(f32[2,16,128]{2,1,0:T(8,128)S(1)} %get-tuple-element.31.reach), channel_id=1, source_target_pairs={{0,1},{1,0},{2,3},{3,2},{4,5},{5,4},{6,7},{7,6},{8,9},{9,8},{10,11... | collective-permute-start | bytes 49160 | tf_op jit(solution)/shard_map/ppermute | solution.py:281
  72.7 0.8 collective-permute-done.4.reach_other
  73.6 0.0 collective-permute-done.3.tails
  73.6 0.0 all-to-all-done.2.resid
  73.6 1.6 %shard_map.73 = f32[16,2,8,256]{3,2,1,0:T(8,128)S(1)} custom-call(s32[5]{0:T(128)S(1)} %pad_add_fusion.where, bf16[2,128,128]{2,1,0:T(8,128)(2,1)S(1)} %collective-permute-done.3.tails, bf16[16,152,128]{2,1,0:T(8,128)(2,1)S(1)} %all_to_all.20.sent.own, bf16[16,128,128]{2,1,0:T(8,128)(2,1)S(1)} %collective-permute-done.2.other, ...), custom_call_target="tpu_custom_call" | custom-call | tf_op jit(solution)/shard_map/pallas_call | solution.py:364
  75.2 23.7 %all_to_all.21 = f16[32,8,256]{2,1,0:T(8,128)(2,1)S(1)} all-to-all(f16[32,8,256]{2,1,0:T(8,128)(2,1)S(1)} %bitcast.21), channel_id=1, replica_groups=mesh['tm_0'=16,'tm_1'=4,'tm_2'=4,'state'=2] {'tm_0','state'}, dimensions={0} | all-to-all | bytes 262144 | tf_op jit(solution)/shard_map/all_to_all | solution.py:371
  98.9 1.2 %shard_map.74 = f32[8,512]{1,0:T(8,128)} custom-call(s32[5]{0:T(128)S(1)} %pad_add_fusion.where, f32[32,8,256]{2,1,0:T(8,128)S(1)} %convert_element_type.11.pieces, f32[2,16,128]{2,1,0:T(8,128)S(1)} %get-tuple-element.31.reach, f32[2,16,128]{2,1,0:T(8,128)S(1)} %collective-permute-done.4.reach_other), custom_call_target="tpu_custom_call" | custom-call | tf_op jit(solution)/shard_map/pallas_call | solution.py:372
  (10 shorter events, 0.1 us)
Async XLA Ops:
  0.6 11.2 %copy-start.3 = (s32[2]{0:T(128)S(1)}, s32[2]{0:T(128)}, u32[]{:S(2)}) copy-start(s32[2]{0:T(128)} %param.9) | copy-start | bytes 28
  0.6 11.3 %collective-permute-start = (bf16[128,2048]{1,0:T(8,128)(2,1)}, bf16[128,2048]{1,0:T(8,128)(2,1)S(1)}, u32[]{:S(2)}, u32[]{:S(2)}) collective-permute-start(bf16[128,2048]{1,0:T(8,128)(2,1)} %record.1), channel_id=1, source_target_pairs={{0,1},{1,0},{2,3},{3,2},{4,5},{5,4},{6,7},{7,6},{8,9},{9,8},{10,11... | collective-permute-start | bytes 1572872 | tf_op jit(solution)/shard_map/ppermute | solution.py:281
  9.4 4.8 %copy-start.2 = (f32[128,128]{1,0:T(8,128)S(1)}, f32[128,128]{1,0:T(8,128)}, u32[]{:S(2)}) copy-start(f32[128,128]{1,0:T(8,128)} %param.7) | copy-start | bytes 196612
  9.5 5.0 %copy-start.1 = (bf16[128,2048]{1,0:T(8,128)(2,1)S(1)}, bf16[128,2048]{1,0:T(8,128)(2,1)}, u32[]{:S(2)}) copy-start(bf16[128,2048]{1,0:T(8,128)(2,1)} %record.1) | copy-start | bytes 1572868
  11.8 3.4 %copy-start = (f32[128]{0:T(128)S(1)}, f32[128]{0:T(128)}, u32[]{:S(2)}) copy-start(f32[128]{0:T(128)} %param.8) | copy-start | bytes 1540
  13.0 2.3 %collective-permute-start.1 = (f32[64,128]{1,0:T(8,128)S(1)}, f32[64,128]{1,0:T(8,128)S(1)}, u32[]{:S(2)}, u32[]{:S(2)}) collective-permute-start(f32[64,128]{1,0:T(8,128)S(1)} %get-tuple-element.20), channel_id=1, source_target_pairs={{0,2},{2,4},{4,6},{6,8},{8,10},{10,12},{12,14},{14,16},{16,18},{18... | collective-permute-start | bytes 98312 | tf_op jit(solution)/shard_map/ppermute | solution.py:323
  31.0 27.9 %all-to-all-start.1 = ((f32[16,8,128]{2,1,0:T(8,128)}), f32[16,8,128]{2,1,0:T(8,128)S(1)}, u32[]{:S(2)}, u32[]{:S(2)}) async-start(f32[16,8,128]{2,1,0:T(8,128)} %get-tuple-element.26), calls=%async_computation.1 | async-start | bytes 131072 | tf_op jit(solution)/shard_map/all_to_all | solution.py:350
  47.4 16.7 %collective-permute-start.2 = (bf16[16,128,128]{2,1,0:T(8,128)(2,1)S(1)}, bf16[16,128,128]{2,1,0:T(8,128)(2,1)S(1)}, u32[]{:S(2)}, u32[]{:S(2)}) collective-permute-start(bf16[16,128,128]{2,1,0:T(8,128)(2,1)S(1)} %slice.13), channel_id=1, source_target_pairs={{0,1},{1,0},{2,3},{3,2},{4,5},{5,4},{6,7},{7,6},{8,9},{9,8},{10,11... | collective-permute-start | bytes 1572872 | tf_op jit(solution)/shard_map/ppermute | solution.py:281
  60.5 13.1 %all-to-all-start.2 = ((bf16[16,128,128]{2,1,0:T(8,128)(2,1)}), bf16[16,128,128]{2,1,0:T(8,128)(2,1)S(1)}, u32[]{:S(2)}, u32[]{:S(2)}) async-start(bf16[16,128,128]{2,1,0:T(8,128)(2,1)} %get-tuple-element.29), calls=%async_computation.2 | async-start | bytes 1048576 | tf_op jit(solution)/shard_map/all_to_all | solution.py:360
  64.1 9.4 %collective-permute-start.3 = (bf16[2,128,128]{2,1,0:T(8,128)(2,1)S(1)}, bf16[2,128,128]{2,1,0:T(8,128)(2,1)S(1)}, u32[]{:S(2)}, u32[]{:S(2)}) collective-permute-start(bf16[2,128,128]{2,1,0:T(8,128)(2,1)S(1)} %pad_maximum_fusion), channel_id=1, source_target_pairs={{0,32},{32,64},{64,96},{96,128},{128,160},{160,192},{192,224},{224... | collective-permute-start | bytes 196616 | tf_op jit(solution)/shard_map/ppermute | solution.py:362
  66.8 6.8 %collective-permute-start.4 = (f32[2,16,128]{2,1,0:T(8,128)S(1)}, f32[2,16,128]{2,1,0:T(8,128)S(1)}, u32[]{:S(2)}, u32[]{:S(2)}) collective-permute-start(f32[2,16,128]{2,1,0:T(8,128)S(1)} %get-tuple-element.31.reach), channel_id=1, source_target_pairs={{0,1},{1,0},{2,3},{3,2},{4,5},{5,4},{6,7},{7,6},{8,9},{9,8},{10,11... | collective-permute-start | bytes 49160 | tf_op jit(solution)/shard_map/ppermute | solution.py:281

commit v9 on v8

--- a/solution.py
+++ b/solution.py
@@ -10,7 +10,8 @@
 
 TAPS = 2
 TOP = 32768.0
-PIECES = 4
+PIECES = 1
+ROWS = 16
 DMAX = 64
 Z = "tm_0"
 YX = ("tm_1", "tm_2")
@@ -113,25 +114,38 @@
     tail[...] = onward[:DMAX]
 
 
-def local_body(here, tail, decay_ref, scale, leak, by_sensor, peak, keep, sent):
-    frames, modes = decay_ref.shape
-    nothing = jnp.zeros((frames - DMAX, modes), F32)
-    drive_in = here[...] + jnp.concatenate([tail[...], nothing], 0)
-    drive = scale[...] * drive_in
+def response_body(decay_ref, scale_ref, leak, out):
     decay = decay_ref[...]
-    prods, (offsets,) = recur(decay, [drive], later)
+    scale = scale_ref[...]
     kappa = 1.0 - leak[...]
     weight = 1.0 - kappa * decay * decay
+    links, _ = recur(kappa * decay, [], later)
+    to_end, (to_start,) = recur(earlier(decay, 1, 1.0), [later(links, 1, 1.0) * weight], earlier)
+    out[:DMAX] = (scale * to_end)[:DMAX]
+    out[DMAX : 2 * DMAX] = (scale * to_start)[:DMAX]
+    largest = jnp.max(scale, axis=0, keepdims=True)
+    out[2 * DMAX :] = jnp.broadcast_to(largest, (8, decay.shape[1]))
+
+
+def recursions(decay, kappa, drive):
+    prods, (offsets,) = recur(decay, [drive], later)
+    weight = 1.0 - kappa * decay * decay
     links, (base, slope) = recur(kappa * decay, [weight * offsets, weight * prods], earlier)
-    keep[0] = prods
-    keep[1] = offsets
-    keep[2] = links
-    keep[3] = base
-    keep[4] = slope
-    keep[5] = drive
+    return prods, offsets, links, base, slope
+
+
+def local_body(here, onward, response, decay_ref, scale, leak, by_sensor, peak, sent):
+    decay = decay_ref[...]
+    modes = decay.shape[1]
+    kappa = 1.0 - leak[...]
+    prods, offsets, links, base, slope = recursions(decay, kappa, scale[...] * here[...])
     rows = [prods[-1:], offsets[-1:], links[:1], base[:1], slope[:1], decay[-1:]]
     rows += [jnp.max(jnp.abs(offsets), axis=0, keepdims=True), peak[:1]]
-    rest = jnp.concatenate(rows, 0)
+    tail = onward[...]
+    rows.append(jnp.sum(response[:DMAX] * tail, axis=0, keepdims=True))
+    rows.append(jnp.sum(response[DMAX : 2 * DMAX] * tail, axis=0, keepdims=True))
+    rows.append(response[2 * DMAX : 2 * DMAX + 1] * jnp.sum(jnp.abs(tail), axis=0, keepdims=True))
+    rest = jnp.concatenate(rows + [jnp.zeros((ROWS - len(rows), modes), F32)], 0)
     frames_rows = by_sensor.shape[1]
     parts = []
     for _ in range(3):
@@ -144,44 +158,53 @@
         sent[i, frames_rows:] = coded
 
 
-def decoded(every, out):
-    at = every.shape[1] - 24
-    for i in range(every.shape[0]):
-        rows = every[i, at:].astype(F32)
-        out[i] = rows[:8] + rows[8:16] + rows[16:]
-
-
 def joined(first, second):
     p1, o1, l1, b1, s1 = first
     p2, o2, l2, b2, s2 = second
     return (p1 * p2, p2 * o1 + o2, l1 * l2, b1 + l1 * (b2 + s2 * o1), s1 + l1 * s2 * p1)
 
 
-def five(ref, i):
-    return tuple(ref[i, r : r + 1] for r in range(5))
+def rows_of(ref, i, count):
+    return [ref[i, r : r + 1] for r in range(count)]
 
 
 def plane_body(sent, every, out):
     n = sent.shape[0]
-    decoded(sent, every)
-    parts = [five(every, i) for i in range(n)]
+    at = sent.shape[1] - 3 * ROWS
+    blocks = []
+    for i in range(n):
+        coded = sent[i, at:].astype(F32)
+        every[i] = coded[:ROWS] + coded[ROWS : 2 * ROWS] + coded[2 * ROWS :]
+        block = rows_of(every, i, 11)
+        if i > 0:
+            before = blocks[-1]
+            for to, source in ((1, 8), (3, 9), (6, 10)):
+                block[to] = block[to] + before[source]
+            every[i, 1:2] = block[1]
+            every[i, 3:4] = block[3]
+        blocks.append(block)
+    parts = [tuple(block[:5]) for block in blocks[1:]]
     while len(parts) > 1:
-        parts = [joined(parts[i], parts[i + 1]) for i in range(0, len(parts), 2)]
-    state = jnp.zeros_like(every[0, :1])
+        pairs = [joined(parts[i], parts[i + 1]) for i in range(0, len(parts) - 1, 2)]
+        parts = pairs + parts[len(pairs) * 2 :]
+    whole = joined(tuple(blocks[0][:5]), parts[0])
+    state = jnp.zeros_like(blocks[0][0])
     reach = state
     peak = state
-    for i in range(n):
-        reach = jnp.maximum(reach, every[i, 6:7] + jnp.abs(state))
-        peak = jnp.maximum(peak, every[i, 7:8])
-        state = every[i, 0:1] * state + every[i, 1:2]
-    rows = list(parts[0]) + [every[n - 1, 5:6], reach, peak]
-    for r, row in enumerate(rows):
-        for i in range(out.shape[0]):
-            out[i, r : r + 1] = row
+    for block in blocks:
+        reach = jnp.maximum(reach, block[6] + jnp.abs(state))
+        peak = jnp.maximum(peak, block[7])
+        state = block[0] * state + block[1]
+    last = blocks[-1]
+    rows = list(whole) + [last[5], reach, peak, last[8], last[9], last[10]]
+    rows += [parts[0][0], blocks[0][2] * parts[0][4]]
+    rows = jnp.concatenate(rows + [jnp.zeros((ROWS - len(rows), state.shape[1]), F32)], 0)
+    for i in range(out.shape[0]):
+        out[i] = rows
 
 
 def ends(every, position, entering, closing, last):
-    n = every.shape[0]
+    n = len(every)
     states = []
     state = entering
     before = last
@@ -191,37 +214,57 @@
         states.append(state)
         own_state = jnp.where(position == i, state, own_state)
         own_last = jnp.where(position == i, before, own_last)
-        state = every[i, 0:1] * state + every[i, 1:2]
-        before = every[i, 5:6]
+        state = every[i][0] * state + every[i][1]
+        before = every[i][5]
     after = closing
     afters = [after] * n
     own_after = jnp.zeros_like(entering)
     for i in reversed(range(n)):
         afters[i] = after
         own_after = jnp.where(position == i, after, own_after)
-        after = every[i, 2:3] * after + every[i, 3:4] + every[i, 4:5] * states[i]
+        after = every[i][2] * after + every[i][3] + every[i][4] * states[i]
     return own_state, own_after, own_last, states, afters
 
 
-def finish_body(where, plane, planes, keep, decay_ref, leak, smoothed_out, resid_out, reach):
-    zero = jnp.zeros((1, decay_ref.shape[1]), F32)
+def finish_body(
+    where, plane_ref, planes_ref, here, tail, decay_ref, scale, leak, smoothed_out, resid_out, reach
+):
+    frames, modes = decay_ref.shape
+    zero = jnp.zeros((1, modes), F32)
+    planes = [rows_of(planes_ref, i, 13) for i in range(planes_ref.shape[0])]
+    moved = (zero, zero)
+    spread = [zero]
+    for i in range(1, len(planes)):
+        state, closing, more = planes[i - 1][8:11]
+        planes[i][1] = planes[i][1] + planes[i][11] * state
+        planes[i][3] = planes[i][3] + closing + planes[i][12] * state
+        spread.append(more)
+        moved = tuple(
+            jnp.where(where[0] == i, new, old) for new, old in zip((state, closing), moved)
+        )
     entering, after, last, states, afters = ends(planes, where[0], zero, zero, zero)
     peak = zero
-    for i in range(planes.shape[0]):
-        bound = 6.0 * (planes[i, 6:7] + jnp.abs(states[i])) + 2.0 * jnp.abs(afters[i])
+    for i in range(len(planes)):
+        bound = 6.0 * (planes[i][6] + spread[i] + jnp.abs(states[i])) + 2.0 * jnp.abs(afters[i])
         reach[0, i : i + 1] = jnp.broadcast_to(jnp.max(bound, axis=1, keepdims=True), zero.shape)
-        reach[1, i : i + 1] = jnp.maximum(peak, planes[i, 7:8])
-        peak = planes[i, 7:8]
+        reach[1, i : i + 1] = jnp.maximum(peak, planes[i][7])
+        peak = planes[i][7]
+    plane = [rows_of(plane_ref, i, 6) for i in range(plane_ref.shape[0])]
+    plane[0][1] = plane[0][1] + moved[0]
+    plane[0][3] = plane[0][3] + moved[1]
     entering, after, last, _, _ = ends(plane, where[1], entering, after, last)
-    smoothed = keep[3] + keep[4] * entering + keep[2] * after
     decay = decay_ref[...]
     kappa = 1.0 - leak[...]
+    nothing = jnp.zeros((frames - DMAX, modes), F32)
+    drive = scale[...] * (here[...] + jnp.concatenate([tail[...], nothing], 0))
+    _, _, links, base, slope = recursions(decay, kappa, drive)
+    smoothed = base + slope * entering + links * after
     prior = (1.0 - kappa * last * last) * entering + kappa * last * smoothed[:1]
     first = jnp.logical_and(where[0] == 0, where[1] == 0)
     prior = jnp.where(first, 0.0, prior)
     row = lax.broadcasted_iota(jnp.int32, smoothed.shape, 0)
     shifted = jnp.where(row == 0, prior, pltpu.roll(smoothed, 1, 0))
-    resid = (smoothed - decay * shifted - keep[5]).astype(BF16)
+    resid = (smoothed - decay * shifted - drive).astype(BF16)
     smoothed_out[...] = smoothed.T
     for i in range(resid_out.shape[0]):
         resid_out[i] = resid
@@ -291,6 +334,16 @@
             jnp.stack([lax.axis_index(Z), lax.axis_index(YX), lax.axis_index("state")]).astype(jnp.int32),
             dilation,
         ]
+    )
+    rate_t = rate.T
+    decay = jnp.exp(-rate_t)
+    scale = jnp.sqrt(-jnp.expm1(-2.0 * rate_t))
+    leak_row = leak[None]
+    response = call(
+        response_body, jax.ShapeDtypeStruct((2 * DMAX + 8, modes), F32), smem=(), n_in=3
+    )(decay, scale, leak_row)
+    response_after = lax.ppermute(
+        response, TM, [(i + 1, i) for i in range(planes * blocks - 1)]
     )
     other = swapped(record)
     group = sensors // planes // blocks
@@ -320,33 +373,28 @@
         ),
         n_in=4,
     )(where, other, gain_rest, part)
-    tail = lax.ppermute(onward, TM, [(i, i + 1) for i in range(planes * blocks - 1)])
-    rate_t = behind(rate, here).T
-    decay = jnp.exp(-rate_t)
-    scale = jnp.sqrt(-jnp.expm1(-2.0 * rate_t))
-    leak_row = leak[None]
     by_sensor = behind(record, here).T.reshape(planes, blocks, group, frames).swapaxes(0, 1)
     by_sensor = by_sensor.reshape(blocks, planes * group, frames)
-    keep, sent = call(
+    sent = call(
         local_body,
-        (
-            jax.ShapeDtypeStruct((6, frames, modes), F32),
-            jax.ShapeDtypeStruct((blocks, planes * group + 24, frames), BF16),
-        ),
+        jax.ShapeDtypeStruct((blocks, planes * group + 3 * ROWS, frames), BF16),
         smem=(),
-        n_in=7,
-    )(here, tail, decay, scale, leak_row, by_sensor, peak)
+        n_in=8,
+    )(here, onward, response_after, decay, scale, leak_row, by_sensor, peak)
     mine = lax.all_to_all(sent, YX, 0, 0, tiled=True)
+    tail = lax.ppermute(
+        behind(onward, sent), TM, [(i, i + 1) for i in range(planes * blocks - 1)]
+    )
     plane, plane_summary = call(
         plane_body,
         (
-            jax.ShapeDtypeStruct((blocks, 8, modes), F32),
-            jax.ShapeDtypeStruct((planes, 8, modes), F32),
+            jax.ShapeDtypeStruct((blocks, ROWS, modes), F32),
+            jax.ShapeDtypeStruct((planes, ROWS, modes), F32),
         ),
         smem=(),
         n_in=1,
-    )(mine)
-    theirs = swapped(mine[:, :-24])
+    )(behind(mine, tail))
+    theirs = swapped(mine[:, : planes * group])
     every_plane = lax.all_to_all(plane_summary, Z, 0, 0, tiled=True)
     smoothed, resid, reach = call(
         finish_body,
@@ -355,10 +403,10 @@
             jax.ShapeDtypeStruct((blocks, frames, modes), BF16),
             jax.ShapeDtypeStruct((2, planes, modes), F32),
         ),
-        n_in=6,
-    )(where, plane, every_plane, keep, decay, leak_row)
+        n_in=8,
+    )(where, plane, every_plane, here, tail, decay, scale, leak_row)
     resid_all = lax.all_to_all(resid, YX, 0, 0, tiled=True)
-    tails = behind(jnp.stack([mine[-1, :-24], theirs[-1]]), resid)
+    tails = behind(jnp.stack([mine[-1, : planes * group], theirs[-1]]), resid)
     tails = lax.ppermute(tails, Z, [(i, i + 1) for i in range(planes - 1)])
     reach_other = swapped(reach)
     partial = call(

time: 101 us -> 107 us (1.059)
  blocking collectives: 38.5 us -> 24.2 us
  waiting for transfers between devices: 8.23 us -> 17.9 us
  starting transfers between devices: 43.1 us -> 51.5 us
  local copies, waits for them, and re-layouts: 0.57 us -> 2.05 us
    all_to_all x1 -> x0, blocking collectives: 14.8 us -> none  [per_device(): mine = lax.all_to_all(sent, YX, 0, 0, tiled=True)]
    all_to_all x0 -> x1, starting transfers between devices: none -> 5.15 us  [per_device(): mine = lax.all_to_all(sent, YX, 0, 0, tiled=True)]
    ppermute x1 -> x2, waiting for transfers between devices: 0.41 us -> 5.15 us  [the longest x1 4.49 us: per_device(): lax.ppermute(behind(onward, sent), TM, [(i, i + 1) for i in range(planes...]
    all_to_all x0 -> x1, waiting for transfers between devices: none -> 4.59 us  [per_device(): mine = lax.all_to_all(sent, YX, 0, 0, tiled=True)]
    ppermute x1 -> x2, starting transfers between devices: 1.29 us -> 4.55 us  [the longest x1 3.26 us: per_device(): lax.ppermute(behind(onward, sent), TM, [(i, i + 1) for i in range(planes...]
    unnamed x8 -> x9, local copies, waits for them, and re-layouts: 0.02 us -> 1.59 us
    all_to_all x1, starting transfers between devices: 16.3 us -> 15.1 us  [per_device(): every_plane = lax.all_to_all(plane_summary, Z, 0, 0, tiled=True)]
  transfers between devices with their start and end apart: 7 -> 9, of which waited for: 3 -> 5; matrix products, arithmetic and copies ran while one was open for 1% -> 1% of each run, Pallas kernels for 4% -> 5%
where the time goes in v9:
time: 107 us; the launch traced here: 106 us
  starting transfers between devices  51.5 us (48%)
  blocking collectives  24.2 us (23%)
  waiting for transfers between devices  17.9 us (17%)
  Pallas kernels  9.59 us (9%)
  local copies, waits for them, and re-layouts  2.05 us (2%)
    all_to_all x1, blocking collectives, per_device(): pieces = lax.all_to_all(pieces, (Z, 'state'), 0, 0, tiled=True)  24.2 us
    ppermute x3, starting transfers between devices, swapped(): return lax.ppermute(x, 'state', [(0, 1), (1, 0)])  19.1 us
    all_to_all x1, starting transfers between devices, per_device(): every_plane = lax.all_to_all(plane_summary, Z, 0, 0, tiled=True)  15.1 us
    all_to_all x1, waiting for transfers between devices, per_device(): every_plane = lax.all_to_all(plane_summary, Z, 0, 0, tiled=True)  7.31 us
    all_to_all x1, starting transfers between devices, per_device(): mine = lax.all_to_all(sent, YX, 0, 0, tiled=True)  5.15 us
    all_to_all x1, waiting for transfers between devices, per_device(): mine = lax.all_to_all(sent, YX, 0, 0, tiled=True)  4.59 us
    ppermute x1, waiting for transfers between devices, per_device(): lax.ppermute(behind(onward, sent), TM, [(i, i + 1) for i in range(planes...  4.49 us
    all_to_all x1, starting transfers between devices, per_device(): resid_all = lax.all_to_all(resid, YX, 0, 0, tiled=True)  4.17 us
  transfers between devices with their start and end apart: 9, of which 5 were waited for; matrix products, arithmetic and copies ran while one was open for 1% of the time, Pallas kernels for 5%

profile of v9, /device:TPU:1, one launch (start us, length us, event | category | flops | bytes accessed | tf_op | source)
XLA Modules:
  0.0 106.2 jit_solution(189621137626505963)
XLA Ops:
  0.6 8.8 %collective-permute-start = (bf16[128,2048]{1,0:T(8,128)(2,1)}, bf16[128,2048]{1,0:T(8,128)(2,1)S(1)}, u32[]{:S(2)}, u32[]{:S(2)}) collective-permute-start(bf16[128,2048]{1,0:T(8,128)(2,1)} %record.1), channel_id=1, source_target_pairs={{0,1},{1,0},{2,3},{3,2},{4,5},{5,4},{6,7},{7,6},{8,9},{9,8},{10,11... | collective-permute-start | bytes 1572872 | tf_op jit(solution)/shard_map/ppermute | solution.py:324
  9.4 0.9 copy.10
  10.4 0.1 sqrt_bitcast_fusion
  10.4 0.0 copy-start
  10.4 0.6 copy-done
  11.1 0.1 shard_map.70
  11.2 1.3 %collective-permute-start.1 = (f32[136,128]{1,0:T(8,128)S(1)}, f32[136,128]{1,0:T(8,128)S(1)}, u32[]{:S(2)}, u32[]{:S(2)}) collective-permute-start(f32[136,128]{1,0:T(8,128)S(1)} %shard_map.70), channel_id=1, source_target_pairs={{2,0},{4,2},{6,4},{8,6},{10,8},{12,10},{14,12},{16,14},{18,16},{20... | collective-permute-start | bytes 208904 | tf_op jit(solution)/shard_map/ppermute | solution.py:345
  12.5 0.0 copy-start.2
  12.5 2.1 %shard_map.68 = (f32[128,256]{1,0:T(8,128)S(1)}, bf16[2,128,2048]{2,1,0:T(8,128)(2,1)S(1)}, f32[8,128]{1,0:T(8,128)S(1)}) custom-call(bf16[128,2048]{1,0:T(8,128)(2,1)} %record.1, bf16[2,128,4096]{2,1,0:T(8,128)(2,1)} %gain.1), custom_call_target="tpu_custom_call" | custom-call | tf_op jit(solution)/shard_map/pallas_call | solution.py:352
  14.7 0.0 copy-start.1
  14.7 0.1 pad_add_fusion.where
  14.8 1.0 shard_map.69
  15.8 0.3 copy.12
  16.1 0.1 copy.15
  16.3 0.7 collective-permute-done.1.response
  16.9 1.1 %shard_map.71 = bf16[16,176,128]{2,1,0:T(8,128)(2,1)} custom-call(f32[128,128]{1,0:T(8,128)S(1)} %get-tuple-element.18.here, f32[64,128]{1,0:T(8,128)S(1)} %get-tuple-element.22.onward, f32[136,128]{1,0:T(8,128)S(1)} %collective-permute-done.1.response, f32[128,128]{1,0:T(8,128)S(1)} %get-tuple-element.31.decay_ref, ...), custom_call_target="tpu_custom_call" | custom-call | tf_op jit(solution)/shard_map/pallas_call | solution.py:378
  18.0 5.2 %all-to-all-start = ((bf16[16,176,128]{2,1,0:T(8,128)(2,1)}), bf16[16,176,128]{2,1,0:T(8,128)(2,1)S(1)}, u32[]{:S(2)}, u32[]{:S(2)}) async-start(bf16[16,176,128]{2,1,0:T(8,128)(2,1)} %shard_map.71), calls=%async_computation | async-start | bytes 1441792 | tf_op jit(solution)/shard_map/all_to_all | solution.py:384
  23.2 3.3 %collective-permute-start.2 = (f32[64,128]{1,0:T(8,128)S(1)}, f32[64,128]{1,0:T(8,128)S(1)}, u32[]{:S(2)}, u32[]{:S(2)}) collective-permute-start(f32[64,128]{1,0:T(8,128)S(1)} %get-tuple-element.22.onward), channel_id=1, source_target_pairs={{0,2},{2,4},{4,6},{6,8},{8,10},{10,12},{12,14},{14,16},{16,18},{18... | collective-permute-start | bytes 98312 | tf_op jit(solution)/shard_map/ppermute | solution.py:385
  26.5 4.5 %collective-permute-done.2.tail = f32[64,128]{1,0:T(8,128)S(1)} collective-permute-done((f32[64,128]{1,0:T(8,128)S(1)}, f32[64,128]{1,0:T(8,128)S(1)}, u32[]{:S(2)}, u32[]{:S(2)}) %collective-permute-start.2) | collective-permute-done | bytes 32800 | tf_op jit(solution)/shard_map/ppermute | solution.py:385
  30.9 4.6 %all-to-all-done.sent.own = bf16[16,176,128]{2,1,0:T(8,128)(2,1)S(1)} async-done(((bf16[16,176,128]{2,1,0:T(8,128)(2,1)}), bf16[16,176,128]{2,1,0:T(8,128)(2,1)S(1)}, u32[]{:S(2)}, u32[]{:S(2)}) %all-to-all-start) | async-done | bytes 720928 | tf_op jit(solution)/shard_map/all_to_all | solution.py:384
  35.5 0.7 shard_map.72
  36.3 15.1 %all-to-all-start.1 = ((f32[16,16,128]{2,1,0:T(8,128)}), f32[16,16,128]{2,1,0:T(8,128)S(1)}, u32[]{:S(2)}, u32[]{:S(2)}) async-start(f32[16,16,128]{2,1,0:T(8,128)} %get-tuple-element.25), calls=%async_computation.1 | async-start | bytes 262144 | tf_op jit(solution)/shard_map/all_to_all | solution.py:398
  51.4 4.6 %collective-permute-start.3 = (bf16[16,128,128]{2,1,0:T(8,128)(2,1)S(1)}, bf16[16,128,128]{2,1,0:T(8,128)(2,1)S(1)}, u32[]{:S(2)}, u32[]{:S(2)}) collective-permute-start(bf16[16,128,128]{2,1,0:T(8,128)(2,1)S(1)} %slice.13), channel_id=1, source_target_pairs={{0,1},{1,0},{2,3},{3,2},{4,5},{5,4},{6,7},{7,6},{8,9},{9,8},{10,11... | collective-permute-start | bytes 1572872 | tf_op jit(solution)/shard_map/ppermute | solution.py:324
  56.1 7.3 %all-to-all-done.1.planes_ref = f32[16,16,128]{2,1,0:T(8,128)S(1)} async-done(((f32[16,16,128]{2,1,0:T(8,128)}), f32[16,16,128]{2,1,0:T(8,128)S(1)}, u32[]{:S(2)}, u32[]{:S(2)}) %all-to-all-start.1) | async-done | bytes 131104 | tf_op jit(solution)/shard_map/all_to_all | solution.py:398
  63.4 1.7 %shard_map.73 = (f32[128,128]{1,0:T(8,128)}, bf16[16,128,128]{2,1,0:T(8,128)(2,1)}, f32[2,16,128]{2,1,0:T(8,128)S(1)}) custom-call(s32[5]{0:T(128)S(1)} %pad_add_fusion.where, f32[16,16,128]{2,1,0:T(8,128)S(1)} %get-tuple-element.24.plane_ref, f32[16,16,128]{2,1,0:T(8,128)S(1)} %all-to-all-done.1.planes_ref, f32[128,128]{1,0:T(8,128)S(1)} %get-tuple-element.18.here, ...), custom_call_target="tpu_custom_call" | custom-call | tf_op jit(solution)/shard_map/pallas_call | solution.py:399
  65.1 4.2 %all-to-all-start.2 = ((bf16[16,128,128]{2,1,0:T(8,128)(2,1)}), bf16[16,128,128]{2,1,0:T(8,128)(2,1)S(1)}, u32[]{:S(2)}, u32[]{:S(2)}) async-start(bf16[16,128,128]{2,1,0:T(8,128)(2,1)} %get-tuple-element.27), calls=%async_computation.2 | async-start | bytes 1048576 | tf_op jit(solution)/shard_map/all_to_all | solution.py:408
  69.3 3.4 %collective-permute-start.4 = (bf16[2,128,128]{2,1,0:T(8,128)(2,1)S(1)}, bf16[2,128,128]{2,1,0:T(8,128)(2,1)S(1)}, u32[]{:S(2)}, u32[]{:S(2)}) collective-permute-start(bf16[2,128,128]{2,1,0:T(8,128)(2,1)S(1)} %pad_maximum_fusion), channel_id=1, source_target_pairs={{0,32},{32,64},{64,96},{96,128},{128,160},{160,192},{192,224},{224... | collective-permute-start | bytes 196616 | tf_op jit(solution)/shard_map/ppermute | solution.py:410
  72.7 5.7 %collective-permute-start.5 = (f32[2,16,128]{2,1,0:T(8,128)S(1)}, f32[2,16,128]{2,1,0:T(8,128)S(1)}, u32[]{:S(2)}, u32[]{:S(2)}) collective-permute-start(f32[2,16,128]{2,1,0:T(8,128)S(1)} %get-tuple-element.29.reach), channel_id=1, source_target_pairs={{0,1},{1,0},{2,3},{3,2},{4,5},{5,4},{6,7},{7,6},{8,9},{9,8},{10,11... | collective-permute-start | bytes 49160 | tf_op jit(solution)/shard_map/ppermute | solution.py:324
  78.4 0.8 collective-permute-done.5.reach_other
  79.2 1.6 %shard_map.74 = f32[16,2,8,256]{3,2,1,0:T(8,128)S(1)} custom-call(s32[5]{0:T(128)S(1)} %pad_add_fusion.where, bf16[2,128,128]{2,1,0:T(8,128)(2,1)S(1)} %collective-permute-done.4.tails, bf16[16,176,128]{2,1,0:T(8,128)(2,1)S(1)} %all-to-all-done.sent.own, bf16[16,128,128]{2,1,0:T(8,128)(2,1)S(1)} %collective-permute-done.3.other, ...), custom_call_target="tpu_custom_call" | custom-call | tf_op jit(solution)/shard_map/pallas_call | solution.py:412
  80.9 24.2 %all_to_all.20 = f16[32,8,256]{2,1,0:T(8,128)(2,1)S(1)} all-to-all(f16[32,8,256]{2,1,0:T(8,128)(2,1)S(1)} %bitcast.22), channel_id=1, replica_groups=mesh['tm_0'=16,'tm_1'=4,'tm_2'=4,'state'=2] {'tm_0','state'}, dimensions={0} | all-to-all | bytes 262144 | tf_op jit(solution)/shard_map/all_to_all | solution.py:419
  105.1 1.2 %shard_map.75 = f32[8,512]{1,0:T(8,128)} custom-call(s32[5]{0:T(128)S(1)} %pad_add_fusion.where, f32[32,8,256]{2,1,0:T(8,128)S(1)} %convert_element_type.11.pieces, f32[2,16,128]{2,1,0:T(8,128)S(1)} %get-tuple-element.29.reach, f32[2,16,128]{2,1,0:T(8,128)S(1)} %collective-permute-done.5.reach_other), custom_call_target="tpu_custom_call" | custom-call | tf_op jit(solution)/shard_map/pallas_call | solution.py:420
  (14 shorter events, 0.1 us)
Async XLA Ops:
  0.6 14.1 %copy-start.3 = (s32[2]{0:T(128)S(1)}, s32[2]{0:T(128)}, u32[]{:S(2)}) copy-start(s32[2]{0:T(128)} %param.9) | copy-start | bytes 28
  0.6 14.2 %collective-permute-start = (bf16[128,2048]{1,0:T(8,128)(2,1)}, bf16[128,2048]{1,0:T(8,128)(2,1)S(1)}, u32[]{:S(2)}, u32[]{:S(2)}) collective-permute-start(bf16[128,2048]{1,0:T(8,128)(2,1)} %record.1), channel_id=1, source_target_pairs={{0,1},{1,0},{2,3},{3,2},{4,5},{5,4},{6,7},{7,6},{8,9},{9,8},{10,11... | collective-permute-start | bytes 1572872 | tf_op jit(solution)/shard_map/ppermute | solution.py:324
  10.4 0.7 copy-start
  11.2 5.7 %collective-permute-start.1 = (f32[136,128]{1,0:T(8,128)S(1)}, f32[136,128]{1,0:T(8,128)S(1)}, u32[]{:S(2)}, u32[]{:S(2)}) collective-permute-start(f32[136,128]{1,0:T(8,128)S(1)} %shard_map.70), channel_id=1, source_target_pairs={{2,0},{4,2},{6,4},{8,6},{10,8},{12,10},{14,12},{16,14},{18,16},{20... | collective-permute-start | bytes 208904 | tf_op jit(solution)/shard_map/ppermute | solution.py:345
  12.5 3.3 %copy-start.2 = (bf16[128,2048]{1,0:T(8,128)(2,1)S(1)}, bf16[128,2048]{1,0:T(8,128)(2,1)}, u32[]{:S(2)}) copy-start(bf16[128,2048]{1,0:T(8,128)(2,1)} %record.1) | copy-start | bytes 1572868
  14.7 2.2 %copy-start.1 = (f32[128]{0:T(128)S(1)}, f32[128]{0:T(128)}, u32[]{:S(2)}) copy-start(f32[128]{0:T(128)} %param.8) | copy-start | bytes 1540
  18.0 17.5 %all-to-all-start = ((bf16[16,176,128]{2,1,0:T(8,128)(2,1)}), bf16[16,176,128]{2,1,0:T(8,128)(2,1)S(1)}, u32[]{:S(2)}, u32[]{:S(2)}) async-start(bf16[16,176,128]{2,1,0:T(8,128)(2,1)} %shard_map.71), calls=%async_computation | async-start | bytes 1441792 | tf_op jit(solution)/shard_map/all_to_all | solution.py:384
  23.2 7.8 %collective-permute-start.2 = (f32[64,128]{1,0:T(8,128)S(1)}, f32[64,128]{1,0:T(8,128)S(1)}, u32[]{:S(2)}, u32[]{:S(2)}) collective-permute-start(f32[64,128]{1,0:T(8,128)S(1)} %get-tuple-element.22.onward), channel_id=1, source_target_pairs={{0,2},{2,4},{4,6},{6,8},{8,10},{10,12},{12,14},{14,16},{16,18},{18... | collective-permute-start | bytes 98312 | tf_op jit(solution)/shard_map/ppermute | solution.py:385
  36.3 27.1 %all-to-all-start.1 = ((f32[16,16,128]{2,1,0:T(8,128)}), f32[16,16,128]{2,1,0:T(8,128)S(1)}, u32[]{:S(2)}, u32[]{:S(2)}) async-start(f32[16,16,128]{2,1,0:T(8,128)} %get-tuple-element.25), calls=%async_computation.1 | async-start | bytes 262144 | tf_op jit(solution)/shard_map/all_to_all | solution.py:398
  51.4 17.8 %collective-permute-start.3 = (bf16[16,128,128]{2,1,0:T(8,128)(2,1)S(1)}, bf16[16,128,128]{2,1,0:T(8,128)(2,1)S(1)}, u32[]{:S(2)}, u32[]{:S(2)}) collective-permute-start(bf16[16,128,128]{2,1,0:T(8,128)(2,1)S(1)} %slice.13), channel_id=1, source_target_pairs={{0,1},{1,0},{2,3},{3,2},{4,5},{5,4},{6,7},{7,6},{8,9},{9,8},{10,11... | collective-permute-start | bytes 1572872 | tf_op jit(solution)/shard_map/ppermute | solution.py:324
  65.1 14.2 %all-to-all-start.2 = ((bf16[16,128,128]{2,1,0:T(8,128)(2,1)}), bf16[16,128,128]{2,1,0:T(8,128)(2,1)S(1)}, u32[]{:S(2)}, u32[]{:S(2)}) async-start(bf16[16,128,128]{2,1,0:T(8,128)(2,1)} %get-tuple-element.27), calls=%async_computation.2 | async-start | bytes 1048576 | tf_op jit(solution)/shard_map/all_to_all | solution.py:408
  69.3 9.9 %collective-permute-start.4 = (bf16[2,128,128]{2,1,0:T(8,128)(2,1)S(1)}, bf16[2,128,128]{2,1,0:T(8,128)(2,1)S(1)}, u32[]{:S(2)}, u32[]{:S(2)}) collective-permute-start(bf16[2,128,128]{2,1,0:T(8,128)(2,1)S(1)} %pad_maximum_fusion), channel_id=1, source_target_pairs={{0,32},{32,64},{64,96},{96,128},{128,160},{160,192},{192,224},{224... | collective-permute-start | bytes 196616 | tf_op jit(solution)/shard_map/ppermute | solution.py:410
  72.7 6.6 %collective-permute-start.5 = (f32[2,16,128]{2,1,0:T(8,128)S(1)}, f32[2,16,128]{2,1,0:T(8,128)S(1)}, u32[]{:S(2)}, u32[]{:S(2)}) collective-permute-start(f32[2,16,128]{2,1,0:T(8,128)S(1)} %get-tuple-element.29.reach), channel_id=1, source_target_pairs={{0,1},{1,0},{2,3},{3,2},{4,5},{5,4},{6,7},{7,6},{8,9},{9,8},{10,11... | collective-permute-start | bytes 49160 | tf_op jit(solution)/shard_map/ppermute | solution.py:324

commit v10 on v8

--- a/solution.py
+++ b/solution.py
@@ -10,7 +10,7 @@
 
 TAPS = 2
 TOP = 32768.0
-PIECES = 4
+PIECES = 1
 DMAX = 64
 Z = "tm_0"
 YX = ("tm_1", "tm_2")
@@ -113,7 +113,7 @@
     tail[...] = onward[:DMAX]
 
 
-def local_body(here, tail, decay_ref, scale, leak, by_sensor, peak, keep, sent):
+def local_body(here, tail, decay_ref, scale, leak, peak, keep, summary):
     frames, modes = decay_ref.shape
     nothing = jnp.zeros((frames - DMAX, modes), F32)
     drive_in = here[...] + jnp.concatenate([tail[...], nothing], 0)
@@ -131,24 +131,9 @@
     keep[5] = drive
     rows = [prods[-1:], offsets[-1:], links[:1], base[:1], slope[:1], decay[-1:]]
     rows += [jnp.max(jnp.abs(offsets), axis=0, keepdims=True), peak[:1]]
-    rest = jnp.concatenate(rows, 0)
-    frames_rows = by_sensor.shape[1]
-    parts = []
-    for _ in range(3):
-        part = rest.astype(BF16)
-        parts.append(part.astype(F32))
-        rest = rest - parts[-1]
-    coded = jnp.concatenate(parts, 0).astype(BF16)
-    for i in range(sent.shape[0]):
-        sent[i, :frames_rows] = by_sensor[i]
-        sent[i, frames_rows:] = coded
-
-
-def decoded(every, out):
-    at = every.shape[1] - 24
-    for i in range(every.shape[0]):
-        rows = every[i, at:].astype(F32)
-        out[i] = rows[:8] + rows[8:16] + rows[16:]
+    rows = jnp.concatenate(rows, 0)
+    for i in range(summary.shape[0]):
+        summary[i] = rows
 
 
 def joined(first, second):
@@ -161,9 +146,8 @@
     return tuple(ref[i, r : r + 1] for r in range(5))
 
 
-def plane_body(sent, every, out):
-    n = sent.shape[0]
-    decoded(sent, every)
+def plane_body(every, out):
+    n = every.shape[0]
     parts = [five(every, i) for i in range(n)]
     while len(parts) > 1:
         parts = [joined(parts[i], parts[i + 1]) for i in range(0, len(parts), 2)]
@@ -327,26 +311,22 @@
     leak_row = leak[None]
     by_sensor = behind(record, here).T.reshape(planes, blocks, group, frames).swapaxes(0, 1)
     by_sensor = by_sensor.reshape(blocks, planes * group, frames)
-    keep, sent = call(
+    mine = lax.all_to_all(by_sensor, YX, 0, 0, tiled=True)
+    keep, summary = call(
         local_body,
         (
             jax.ShapeDtypeStruct((6, frames, modes), F32),
-            jax.ShapeDtypeStruct((blocks, planes * group + 24, frames), BF16),
+            jax.ShapeDtypeStruct((blocks, 8, modes), F32),
         ),
         smem=(),
-        n_in=7,
-    )(here, tail, decay, scale, leak_row, by_sensor, peak)
-    mine = lax.all_to_all(sent, YX, 0, 0, tiled=True)
-    plane, plane_summary = call(
-        plane_body,
-        (
-            jax.ShapeDtypeStruct((blocks, 8, modes), F32),
-            jax.ShapeDtypeStruct((planes, 8, modes), F32),
-        ),
-        smem=(),
-        n_in=1,
-    )(mine)
-    theirs = swapped(mine[:, :-24])
+        n_in=6,
+    )(here, tail, decay, scale, leak_row, peak)
+    summary, mine = lax.optimization_barrier((summary, mine))
+    plane = lax.all_to_all(summary, YX, 0, 0, tiled=True)
+    plane_summary = call(
+        plane_body, jax.ShapeDtypeStruct((planes, 8, modes), F32), smem=(), n_in=1
+    )(plane)
+    theirs = swapped(mine)
     every_plane = lax.all_to_all(plane_summary, Z, 0, 0, tiled=True)
     smoothed, resid, reach = call(
         finish_body,
@@ -358,7 +338,7 @@
         n_in=6,
     )(where, plane, every_plane, keep, decay, leak_row)
     resid_all = lax.all_to_all(resid, YX, 0, 0, tiled=True)
-    tails = behind(jnp.stack([mine[-1, :-24], theirs[-1]]), resid)
+    tails = behind(jnp.stack([mine[-1], theirs[-1]]), resid)
     tails = lax.ppermute(tails, Z, [(i, i + 1) for i in range(planes - 1)])
     reach_other = swapped(reach)
     partial = call(

time: 101 us -> 105 us (1.040)
  waiting for transfers between devices: 8.23 us -> 16.2 us
  blocking collectives: 38.5 us -> 33.8 us
    all_to_all x1, blocking collectives: 14.8 us -> 10 us  [per_device(): plane = lax.all_to_all(summary, YX, 0, 0, tiled=True)]
    all_to_all x0 -> x1, waiting for transfers between devices: none -> 4.37 us  [per_device(): mine = lax.all_to_all(by_sensor, YX, 0, 0, tiled=True)]
    all_to_all x1, starting transfers between devices: 16.3 us -> 12.6 us  [per_device(): every_plane = lax.all_to_all(plane_summary, Z, 0, 0, tiled=True)]
    all_to_all x0 -> x1, starting transfers between devices: none -> 3.57 us  [per_device(): mine = lax.all_to_all(by_sensor, YX, 0, 0, tiled=True)]
    ppermute x1, waiting for transfers between devices: 0.41 us -> 3.44 us  [per_device(): lax.ppermute(onward, TM, [(i, i + 1) for i in range(planes * blocks - 1)])]
    ppermute x1, starting transfers between devices: 1.29 us -> 3.14 us  [per_device(): lax.ppermute(onward, TM, [(i, i + 1) for i in range(planes * blocks - 1)])]
  transfers between devices with their start and end apart: 7 -> 8, of which waited for: 3 -> 5; matrix products, arithmetic and copies ran while one was open for 1% -> 0% of each run, Pallas kernels for 4% -> 4%
where the time goes in v10:
time: 105 us
  starting transfers between devices  43.8 us (42%)
  blocking collectives  33.8 us (32%)
  waiting for transfers between devices  16.2 us (15%)
  Pallas kernels  8.38 us (8%)
  local copies, waits for them, and re-layouts  1.33 us (1%)
    all_to_all x1, blocking collectives, per_device(): pieces = lax.all_to_all(pieces, (Z, 'state'), 0, 0, tiled=True)  23.8 us
    ppermute x3, starting transfers between devices, swapped(): return lax.ppermute(x, 'state', [(0, 1), (1, 0)])  18.2 us
    all_to_all x1, starting transfers between devices, per_device(): every_plane = lax.all_to_all(plane_summary, Z, 0, 0, tiled=True)  12.6 us
    all_to_all x1, blocking collectives, per_device(): plane = lax.all_to_all(summary, YX, 0, 0, tiled=True)  10 us
    all_to_all x1, waiting for transfers between devices, per_device(): every_plane = lax.all_to_all(plane_summary, Z, 0, 0, tiled=True)  7.49 us
    all_to_all x1, waiting for transfers between devices, per_device(): mine = lax.all_to_all(by_sensor, YX, 0, 0, tiled=True)  4.37 us
    all_to_all x1, starting transfers between devices, per_device(): resid_all = lax.all_to_all(resid, YX, 0, 0, tiled=True)  3.57 us
    all_to_all x1, starting transfers between devices, per_device(): mine = lax.all_to_all(by_sensor, YX, 0, 0, tiled=True)  3.57 us
  transfers between devices with their start and end apart: 8, of which 5 were waited for; matrix products, arithmetic and copies ran while one was open for 0% of the time, Pallas kernels for 4%

profile of v10, /device:TPU:1, one launch (start us, length us, event | category | flops | bytes accessed | tf_op | source)
XLA Modules:
  0.0 104.5 jit_solution(5394627092763897081)
XLA Ops:
  0.6 0.0 copy-start.3
  0.6 8.8 %collective-permute-start = (bf16[128,2048]{1,0:T(8,128)(2,1)}, bf16[128,2048]{1,0:T(8,128)(2,1)S(1)}, u32[]{:S(2)}, u32[]{:S(2)}) collective-permute-start(bf16[128,2048]{1,0:T(8,128)(2,1)} %record.1), channel_id=1, source_target_pairs={{0,1},{1,0},{2,3},{3,2},{4,5},{5,4},{6,7},{7,6},{8,9},{9,8},{10,11... | collective-permute-start | bytes 1572872 | tf_op jit(solution)/shard_map/ppermute | solution.py:265
  9.5 2.1 %shard_map.68 = (f32[128,256]{1,0:T(8,128)S(1)}, bf16[2,128,2048]{2,1,0:T(8,128)(2,1)S(1)}, f32[8,128]{1,0:T(8,128)S(1)}) custom-call(bf16[128,2048]{1,0:T(8,128)(2,1)} %record.1, bf16[2,128,4096]{2,1,0:T(8,128)(2,1)} %gain.1), custom_call_target="tpu_custom_call" | custom-call | tf_op jit(solution)/shard_map/pallas_call | solution.py:283
  11.6 0.1 pad_add_fusion.where
  11.7 0.0 collective-permute-done.other
  11.7 1.0 shard_map.69
  12.7 0.0 copy-start
  12.7 0.3 copy.12
  13.0 0.9 copy.15
  14.0 3.6 %all-to-all-start = ((bf16[16,128,128]{2,1,0:T(8,128)(2,1)}), bf16[16,128,128]{2,1,0:T(8,128)(2,1)S(1)}, u32[]{:S(2)}, u32[]{:S(2)}) async-start(bf16[16,128,128]{2,1,0:T(8,128)(2,1)} %bitcast.16), calls=%async_computation | async-start | bytes 1048576 | tf_op jit(solution)/shard_map/all_to_all | solution.py:314
  17.5 3.1 %collective-permute-start.1 = (f32[64,128]{1,0:T(8,128)S(1)}, f32[64,128]{1,0:T(8,128)S(1)}, u32[]{:S(2)}, u32[]{:S(2)}) collective-permute-start(f32[64,128]{1,0:T(8,128)S(1)} %get-tuple-element.20), channel_id=1, source_target_pairs={{0,2},{2,4},{4,6},{6,8},{8,10},{10,12},{12,14},{14,16},{16,18},{18... | collective-permute-start | bytes 98312 | tf_op jit(solution)/shard_map/ppermute | solution.py:307
  20.7 0.1 copy.10
  20.8 0.1 sqrt_bitcast_fusion
  20.9 3.4 %collective-permute-done.1.tail = f32[64,128]{1,0:T(8,128)S(1)} collective-permute-done((f32[64,128]{1,0:T(8,128)S(1)}, f32[64,128]{1,0:T(8,128)S(1)}, u32[]{:S(2)}, u32[]{:S(2)}) %collective-permute-start.1) | collective-permute-done | bytes 32800 | tf_op jit(solution)/shard_map/ppermute | solution.py:307
  24.3 0.2 shard_map.70
  24.5 4.4 %all-to-all-done.own = bf16[16,128,128]{2,1,0:T(8,128)(2,1)S(1)} async-done(((bf16[16,128,128]{2,1,0:T(8,128)(2,1)}), bf16[16,128,128]{2,1,0:T(8,128)(2,1)S(1)}, u32[]{:S(2)}, u32[]{:S(2)}) %all-to-all-start) | async-done | bytes 524320 | tf_op jit(solution)/shard_map/all_to_all | solution.py:314
  28.9 10.0 %all_to_all.25.every.plane = f32[16,8,128]{2,1,0:T(8,128)S(1)} all-to-all(f32[16,8,128]{2,1,0:T(8,128)S(1)} %get-tuple-element.25), channel_id=1, replica_groups=mesh['tm_0'=16,'tm_1'=4,'tm_2'=4,'state'=2] {'tm_1','tm_2'}, dimensions={0} | all-to-all | bytes 131072 | tf_op jit(solution)/shard_map/all_to_all | solution.py:325
  38.9 0.7 shard_map.71
  39.6 12.6 %all-to-all-start.2 = ((f32[16,8,128]{2,1,0:T(8,128)}), f32[16,8,128]{2,1,0:T(8,128)S(1)}, u32[]{:S(2)}, u32[]{:S(2)}) async-start(f32[16,8,128]{2,1,0:T(8,128)} %shard_map.71), calls=%async_computation.2 | async-start | bytes 131072 | tf_op jit(solution)/shard_map/all_to_all | solution.py:330
  52.3 4.1 %collective-permute-start.2 = (bf16[16,128,128]{2,1,0:T(8,128)(2,1)S(1)}, bf16[16,128,128]{2,1,0:T(8,128)(2,1)S(1)}, u32[]{:S(2)}, u32[]{:S(2)}) collective-permute-start(bf16[16,128,128]{2,1,0:T(8,128)(2,1)S(1)} %all-to-all-done.own), channel_id=1, source_target_pairs={{0,1},{1,0},{2,3},{3,2},{4,5},{5,4},{6,7},{7,6},{8,9},{9,8},{10,11... | collective-permute-start | bytes 1572872 | tf_op jit(solution)/shard_map/ppermute | solution.py:265
  56.3 7.5 %all-to-all-done.2.planes = f32[16,8,128]{2,1,0:T(8,128)S(1)} async-done(((f32[16,8,128]{2,1,0:T(8,128)}), f32[16,8,128]{2,1,0:T(8,128)S(1)}, u32[]{:S(2)}, u32[]{:S(2)}) %all-to-all-start.2) | async-done | bytes 65568 | tf_op jit(solution)/shard_map/all_to_all | solution.py:330
  63.8 1.6 %shard_map.72 = (f32[128,128]{1,0:T(8,128)}, bf16[16,128,128]{2,1,0:T(8,128)(2,1)}, f32[2,16,128]{2,1,0:T(8,128)S(1)}) custom-call(s32[5]{0:T(128)S(1)} %pad_add_fusion.where, f32[16,8,128]{2,1,0:T(8,128)S(1)} %all_to_all.25.every.plane, f32[16,8,128]{2,1,0:T(8,128)S(1)} %all-to-all-done.2.planes, f32[6,128,128]{2,1,0:T(8,128)S(1)} %get-tuple-element.26.keep, ...), custom_call_target="tpu_custom_call" | custom-call | tf_op jit(solution)/shard_map/pallas_call | solution.py:331
  65.4 3.6 %all-to-all-start.3 = ((bf16[16,128,128]{2,1,0:T(8,128)(2,1)}), bf16[16,128,128]{2,1,0:T(8,128)(2,1)S(1)}, u32[]{:S(2)}, u32[]{:S(2)}) async-start(bf16[16,128,128]{2,1,0:T(8,128)(2,1)} %get-tuple-element.29), calls=%async_computation.3 | async-start | bytes 1048576 | tf_op jit(solution)/shard_map/all_to_all | solution.py:340
  69.0 0.0 collective-permute-done.2.other
  69.0 2.6 %collective-permute-start.3 = (bf16[2,128,128]{2,1,0:T(8,128)(2,1)S(1)}, bf16[2,128,128]{2,1,0:T(8,128)(2,1)S(1)}, u32[]{:S(2)}, u32[]{:S(2)}) collective-permute-start(bf16[2,128,128]{2,1,0:T(8,128)(2,1)S(1)} %pad_maximum_fusion), channel_id=1, source_target_pairs={{0,32},{32,64},{64,96},{96,128},{128,160},{160,192},{192,224},{224... | collective-permute-start | bytes 196616 | tf_op jit(solution)/shard_map/ppermute | solution.py:342
  71.7 5.4 %collective-permute-start.4 = (f32[2,16,128]{2,1,0:T(8,128)S(1)}, f32[2,16,128]{2,1,0:T(8,128)S(1)}, u32[]{:S(2)}, u32[]{:S(2)}) collective-permute-start(f32[2,16,128]{2,1,0:T(8,128)S(1)} %get-tuple-element.31.reach), channel_id=1, source_target_pairs={{0,1},{1,0},{2,3},{3,2},{4,5},{5,4},{6,7},{7,6},{8,9},{9,8},{10,11... | collective-permute-start | bytes 49160 | tf_op jit(solution)/shard_map/ppermute | solution.py:265
  77.0 0.8 collective-permute-done.4.reach_other
  77.9 0.0 collective-permute-done.3.tails
  77.9 0.1 all-to-all-done.3.resid
  77.9 1.6 %shard_map.73 = f32[16,2,8,256]{3,2,1,0:T(8,128)S(1)} custom-call(s32[5]{0:T(128)S(1)} %pad_add_fusion.where, bf16[2,128,128]{2,1,0:T(8,128)(2,1)S(1)} %collective-permute-done.3.tails, bf16[16,128,128]{2,1,0:T(8,128)(2,1)S(1)} %all-to-all-done.own, bf16[16,128,128]{2,1,0:T(8,128)(2,1)S(1)} %collective-permute-done.2.other, ...), custom_call_target="tpu_custom_call" | custom-call | tf_op jit(solution)/shard_map/pallas_call | solution.py:344
  79.5 23.8 %all_to_all.26 = f16[32,8,256]{2,1,0:T(8,128)(2,1)S(1)} all-to-all(f16[32,8,256]{2,1,0:T(8,128)(2,1)S(1)} %bitcast.20), channel_id=1, replica_groups=mesh['tm_0'=16,'tm_1'=4,'tm_2'=4,'state'=2] {'tm_0','state'}, dimensions={0} | all-to-all | bytes 262144 | tf_op jit(solution)/shard_map/all_to_all | solution.py:351
  103.3 1.2 %shard_map.74 = f32[8,512]{1,0:T(8,128)} custom-call(s32[5]{0:T(128)S(1)} %pad_add_fusion.where, f32[32,8,256]{2,1,0:T(8,128)S(1)} %convert_element_type.11.pieces, f32[2,16,128]{2,1,0:T(8,128)S(1)} %get-tuple-element.31.reach, f32[2,16,128]{2,1,0:T(8,128)S(1)} %collective-permute-done.4.reach_other), custom_call_target="tpu_custom_call" | custom-call | tf_op jit(solution)/shard_map/pallas_call | solution.py:352
  (11 shorter events, 0.1 us)
Async XLA Ops:
  0.6 11.0 %copy-start.3 = (s32[2]{0:T(128)S(1)}, s32[2]{0:T(128)}, u32[]{:S(2)}) copy-start(s32[2]{0:T(128)} %param.9) | copy-start | bytes 28
  0.6 11.1 %collective-permute-start = (bf16[128,2048]{1,0:T(8,128)(2,1)}, bf16[128,2048]{1,0:T(8,128)(2,1)S(1)}, u32[]{:S(2)}, u32[]{:S(2)}) collective-permute-start(bf16[128,2048]{1,0:T(8,128)(2,1)} %record.1), channel_id=1, source_target_pairs={{0,1},{1,0},{2,3},{3,2},{4,5},{5,4},{6,7},{7,6},{8,9},{9,8},{10,11... | collective-permute-start | bytes 1572872 | tf_op jit(solution)/shard_map/ppermute | solution.py:265
  9.4 3.3 %copy-start.1 = (bf16[128,2048]{1,0:T(8,128)(2,1)S(1)}, bf16[128,2048]{1,0:T(8,128)(2,1)}, u32[]{:S(2)}) copy-start(bf16[128,2048]{1,0:T(8,128)(2,1)} %record.1) | copy-start | bytes 1572868
  11.7 9.0 %copy-start.2 = (f32[128,128]{1,0:T(8,128)S(1)}, f32[128,128]{1,0:T(8,128)}, u32[]{:S(2)}) copy-start(f32[128,128]{1,0:T(8,128)} %param.7) | copy-start | bytes 196612
  12.7 11.6 %copy-start = (f32[128]{0:T(128)S(1)}, f32[128]{0:T(128)}, u32[]{:S(2)}) copy-start(f32[128]{0:T(128)} %param.8) | copy-start | bytes 1540
  14.0 14.9 %all-to-all-start = ((bf16[16,128,128]{2,1,0:T(8,128)(2,1)}), bf16[16,128,128]{2,1,0:T(8,128)(2,1)S(1)}, u32[]{:S(2)}, u32[]{:S(2)}) async-start(bf16[16,128,128]{2,1,0:T(8,128)(2,1)} %bitcast.16), calls=%async_computation | async-start | bytes 1048576 | tf_op jit(solution)/shard_map/all_to_all | solution.py:314
  17.5 6.8 %collective-permute-start.1 = (f32[64,128]{1,0:T(8,128)S(1)}, f32[64,128]{1,0:T(8,128)S(1)}, u32[]{:S(2)}, u32[]{:S(2)}) collective-permute-start(f32[64,128]{1,0:T(8,128)S(1)} %get-tuple-element.20), channel_id=1, source_target_pairs={{0,2},{2,4},{4,6},{6,8},{8,10},{10,12},{12,14},{14,16},{16,18},{18... | collective-permute-start | bytes 98312 | tf_op jit(solution)/shard_map/ppermute | solution.py:307
  39.6 24.2 %all-to-all-start.2 = ((f32[16,8,128]{2,1,0:T(8,128)}), f32[16,8,128]{2,1,0:T(8,128)S(1)}, u32[]{:S(2)}, u32[]{:S(2)}) async-start(f32[16,8,128]{2,1,0:T(8,128)} %shard_map.71), calls=%async_computation.2 | async-start | bytes 131072 | tf_op jit(solution)/shard_map/all_to_all | solution.py:330
  52.3 16.7 %collective-permute-start.2 = (bf16[16,128,128]{2,1,0:T(8,128)(2,1)S(1)}, bf16[16,128,128]{2,1,0:T(8,128)(2,1)S(1)}, u32[]{:S(2)}, u32[]{:S(2)}) collective-permute-start(bf16[16,128,128]{2,1,0:T(8,128)(2,1)S(1)} %all-to-all-done.own), channel_id=1, source_target_pairs={{0,1},{1,0},{2,3},{3,2},{4,5},{5,4},{6,7},{7,6},{8,9},{9,8},{10,11... | collective-permute-start | bytes 1572872 | tf_op jit(solution)/shard_map/ppermute | solution.py:265
  65.4 12.5 %all-to-all-start.3 = ((bf16[16,128,128]{2,1,0:T(8,128)(2,1)}), bf16[16,128,128]{2,1,0:T(8,128)(2,1)S(1)}, u32[]{:S(2)}, u32[]{:S(2)}) async-start(bf16[16,128,128]{2,1,0:T(8,128)(2,1)} %get-tuple-element.29), calls=%async_computation.3 | async-start | bytes 1048576 | tf_op jit(solution)/shard_map/all_to_all | solution.py:340
  69.0 8.8 %collective-permute-start.3 = (bf16[2,128,128]{2,1,0:T(8,128)(2,1)S(1)}, bf16[2,128,128]{2,1,0:T(8,128)(2,1)S(1)}, u32[]{:S(2)}, u32[]{:S(2)}) collective-permute-start(bf16[2,128,128]{2,1,0:T(8,128)(2,1)S(1)} %pad_maximum_fusion), channel_id=1, source_target_pairs={{0,32},{32,64},{64,96},{96,128},{128,160},{160,192},{192,224},{224... | collective-permute-start | bytes 196616 | tf_op jit(solution)/shard_map/ppermute | solution.py:342
  71.7 6.2 %collective-permute-start.4 = (f32[2,16,128]{2,1,0:T(8,128)S(1)}, f32[2,16,128]{2,1,0:T(8,128)S(1)}, u32[]{:S(2)}, u32[]{:S(2)}) collective-permute-start(f32[2,16,128]{2,1,0:T(8,128)S(1)} %get-tuple-element.31.reach), channel_id=1, source_target_pairs={{0,1},{1,0},{2,3},{3,2},{4,5},{5,4},{6,7},{7,6},{8,9},{9,8},{10,11... | collective-permute-start | bytes 49160 | tf_op jit(solution)/shard_map/ppermute | solution.py:265

commit v11 on v8

--- a/solution.py
+++ b/solution.py
@@ -10,7 +10,7 @@
 
 TAPS = 2
 TOP = 32768.0
-PIECES = 4
+PIECES = 1
 DMAX = 64
 Z = "tm_0"
 YX = ("tm_1", "tm_2")
@@ -97,20 +97,31 @@
         copy.wait()
 
 
-def rest_body(where, other, gain, part, out, tail):
+def onward_body(where, other, gain, part, out):
+    modes = gain.shape[1]
+    at = part.shape[0] - DMAX
+    row = lax.broadcasted_iota(jnp.int32, out.shape, 0)
+    total = jnp.zeros(out.shape, F32)
+    for k in range(TAPS):
+        u = part[at:, k * modes : (k + 1) * modes] + lax.dot_general(
+            other[at:], gain[k], NT, preferred_element_type=F32
+        )
+        delayed = pltpu.roll(u, where[3 + k] % DMAX, 0)
+        total += jnp.where(row < where[3 + k], delayed, 0.0)
+    out[...] = total
+
+
+def here_body(where, other, gain, part, onward, out):
     modes = gain.shape[1]
     row = lax.broadcasted_iota(jnp.int32, out.shape, 0)
-    here = jnp.zeros(out.shape, F32)
-    onward = jnp.zeros(out.shape, F32)
+    total = jnp.zeros(out.shape, F32)
     for k in range(TAPS):
         u = part[:, k * modes : (k + 1) * modes] + lax.dot_general(
             other[...], gain[k], NT, preferred_element_type=F32
         )
         delayed = pltpu.roll(u, where[3 + k], 0)
-        here += jnp.where(row >= where[3 + k], delayed, 0.0)
-        onward += jnp.where(row < where[3 + k], delayed, 0.0)
-    out[...] = here
-    tail[...] = onward[:DMAX]
+        total += jnp.where(row >= where[3 + k], delayed, 0.0)
+    out[...] = total
 
 
 def local_body(here, tail, decay_ref, scale, leak, by_sensor, peak, keep, sent):
@@ -206,12 +217,14 @@
 def finish_body(where, plane, planes, keep, decay_ref, leak, smoothed_out, resid_out, reach):
     zero = jnp.zeros((1, decay_ref.shape[1]), F32)
     entering, after, last, states, afters = ends(planes, where[0], zero, zero, zero)
-    peak = zero
+    peaks = [zero]
+    bound = []
     for i in range(planes.shape[0]):
-        bound = 6.0 * (planes[i, 6:7] + jnp.abs(states[i])) + 2.0 * jnp.abs(afters[i])
-        reach[0, i : i + 1] = jnp.broadcast_to(jnp.max(bound, axis=1, keepdims=True), zero.shape)
-        reach[1, i : i + 1] = jnp.maximum(peak, planes[i, 7:8])
-        peak = planes[i, 7:8]
+        bound.append(6.0 * (planes[i, 6:7] + jnp.abs(states[i])) + 2.0 * jnp.abs(afters[i]))
+        peaks.append(planes[i, 7:8])
+    bound = jnp.concatenate(bound, 0)
+    reach[0] = jnp.broadcast_to(jnp.max(bound, axis=1, keepdims=True), bound.shape)
+    reach[1] = jnp.maximum(jnp.concatenate(peaks[:-1], 0), jnp.concatenate(peaks[1:], 0))
     entering, after, last, _, _ = ends(plane, where[1], entering, after, last)
     smoothed = keep[3] + keep[4] * entering + keep[2] * after
     decay = decay_ref[...]
@@ -235,15 +248,19 @@
     blocks, frames, modes = resid.shape
     row = lax.broadcasted_iota(jnp.int32, (frames, 2 * frames), 0)
     column = lax.broadcasted_iota(jnp.int32, (frames, 2 * frames), 1)
-    picks = [(column == row + where[3 + k]).astype(F32).astype(BF16) for k in range(TAPS)]
+    picks = jnp.concatenate(
+        [(column == row + where[3 + k]).astype(F32).astype(BF16) for k in range(TAPS)], 0
+    )
     nothing = jnp.zeros((frames, modes), BF16)
     for b in range(blocks + 1):
         pair = jnp.concatenate(
             [resid[b - 1] if b > 0 else nothing, resid[b] if b < blocks else nothing], 0
         )
+        moved = jnp.dot(picks, pair, preferred_element_type=F32).astype(BF16)
         for k in range(TAPS):
-            moved = jnp.dot(picks[k], pair, preferred_element_type=F32)
-            padded[b * frames : (b + 1) * frames, k * modes : (k + 1) * modes] = moved.astype(BF16)
+            padded[b * frames : (b + 1) * frames, k * modes : (k + 1) * modes] = moved[
+                k * frames : (k + 1) * frames
+            ]
     rhs = padded[...]
     bound = bounds(reach, reach_other, float(blocks * frames))
     plane = lax.broadcasted_iota(jnp.int32, bound.shape, 0)
@@ -312,14 +329,12 @@
         whole=(0, 1),
         n_in=2,
     )(*(pltpu.with_memory_space_constraint(x, pltpu.HBM) for x in (record, gain)))
-    here, onward = call(
-        rest_body,
-        (
-            jax.ShapeDtypeStruct((frames, modes), F32),
-            jax.ShapeDtypeStruct((DMAX, modes), F32),
-        ),
-        n_in=4,
-    )(where, other, gain_rest, part)
+    onward = call(onward_body, jax.ShapeDtypeStruct((DMAX, modes), F32), n_in=4)(
+        where, other, gain_rest, part
+    )
+    here = call(here_body, jax.ShapeDtypeStruct((frames, modes), F32), n_in=5)(
+        where, other, gain_rest, part, onward
+    )
     tail = lax.ppermute(onward, TM, [(i, i + 1) for i in range(planes * blocks - 1)])
     rate_t = behind(rate, here).T
     decay = jnp.exp(-rate_t)

time: 101 us -> 100 us (0.990)
    pallas_call x1 -> x2, Pallas kernels: 1.01 us -> 2.03 us  [the longest x1 1.03 us: per_device(): call(onward_body, jax.ShapeDtypeStruct((DMAX, modes), F32), n_in=4)]
  transfers between devices with their start and end apart: 7 -> 7, of which waited for: 3 -> 2; matrix products, arithmetic and copies ran while one was open for 1% -> 1% of each run, Pallas kernels for 4% -> 5%
where the time goes in v11:
time: 100 us; the launch traced here: 99.8 us
  starting transfers between devices  43.1 us (43%)
  blocking collectives  37.9 us (38%)
  Pallas kernels  9.36 us (9%)
  waiting for transfers between devices  7.82 us (8%)
    all_to_all x1, blocking collectives, per_device(): pieces = lax.all_to_all(pieces, (Z, 'state'), 0, 0, tiled=True)  23.8 us
    ppermute x3, starting transfers between devices, swapped(): return lax.ppermute(x, 'state', [(0, 1), (1, 0)])  19.3 us
    all_to_all x1, starting transfers between devices, per_device(): every_plane = lax.all_to_all(plane_summary, Z, 0, 0, tiled=True)  16.3 us
    all_to_all x1, blocking collectives, per_device(): mine = lax.all_to_all(sent, YX, 0, 0, tiled=True)  14.2 us
    all_to_all x1, waiting for transfers between devices, per_device(): every_plane = lax.all_to_all(plane_summary, Z, 0, 0, tiled=True)  6.99 us
    all_to_all x1, starting transfers between devices, per_device(): resid_all = lax.all_to_all(resid, YX, 0, 0, tiled=True)  3.57 us
    ppermute x1, starting transfers between devices, per_device(): tails = lax.ppermute(tails, Z, [(i, i + 1) for i in range(planes - 1)])  2.66 us
    pallas_call x1, Pallas kernels, per_device(): call(own_body, (both, jax.ShapeDtypeStruct(half_gain, BF16), jax.ShapeDty...  2.09 us
  transfers between devices with their start and end apart: 7, of which 2 were waited for; matrix products, arithmetic and copies ran while one was open for 1% of the time, Pallas kernels for 5%

profile of v11, /device:TPU:1, one launch (start us, length us, event | category | flops | bytes accessed | tf_op | source)
XLA Modules:
  0.0 99.8 jit_solution(8873517922794639209)
XLA Ops:
  0.6 8.8 %collective-permute-start = (bf16[128,2048]{1,0:T(8,128)(2,1)}, bf16[128,2048]{1,0:T(8,128)(2,1)S(1)}, u32[]{:S(2)}, u32[]{:S(2)}) collective-permute-start(bf16[128,2048]{1,0:T(8,128)(2,1)} %record.1), channel_id=1, source_target_pairs={{0,1},{1,0},{2,3},{3,2},{4,5},{5,4},{6,7},{7,6},{8,9},{9,8},{10,11... | collective-permute-start | bytes 1572872 | tf_op jit(solution)/shard_map/ppermute | solution.py:298
  9.4 2.1 %shard_map.68 = (f32[128,256]{1,0:T(8,128)S(1)}, bf16[2,128,2048]{2,1,0:T(8,128)(2,1)S(1)}, f32[8,128]{1,0:T(8,128)S(1)}) custom-call(bf16[128,2048]{1,0:T(8,128)(2,1)} %record.1, bf16[2,128,4096]{2,1,0:T(8,128)(2,1)} %gain.1), custom_call_target="tpu_custom_call" | custom-call | tf_op jit(solution)/shard_map/pallas_call | solution.py:316
  11.5 0.0 copy-start.2
  11.6 0.0 copy-start.1
  11.6 0.1 pad_add_fusion.where
  11.7 0.0 collective-permute-done.other
  11.7 1.0 %shard_map.69.onward = f32[64,128]{1,0:T(8,128)S(1)} custom-call(s32[5]{0:T(128)S(1)} %pad_add_fusion.where, bf16[128,2048]{1,0:T(8,128)(2,1)S(1)} %collective-permute-done.other, bf16[2,128,2048]{2,1,0:T(8,128)(2,1)S(1)} %get-tuple-element.15.gain, f32[128,256]{1,0:T(8,128)S(1)} %get-tuple-element.16.part), custom_call_target="tpu_custom_call" | custom-call | tf_op jit(solution)/shard_map/pallas_call | solution.py:332
  12.7 0.0 copy-start
  12.7 1.3 %collective-permute-start.1 = (f32[64,128]{1,0:T(8,128)S(1)}, f32[64,128]{1,0:T(8,128)S(1)}, u32[]{:S(2)}, u32[]{:S(2)}) collective-permute-start(f32[64,128]{1,0:T(8,128)S(1)} %shard_map.69.onward), channel_id=1, source_target_pairs={{0,2},{2,4},{4,6},{6,8},{8,10},{10,12},{12,14},{14,16},{16,18},{18... | collective-permute-start | bytes 98312 | tf_op jit(solution)/shard_map/ppermute | solution.py:338
  14.0 1.0 %shard_map.70.here = f32[128,128]{1,0:T(8,128)S(1)} custom-call(s32[5]{0:T(128)S(1)} %pad_add_fusion.where, bf16[128,2048]{1,0:T(8,128)(2,1)S(1)} %collective-permute-done.other, bf16[2,128,2048]{2,1,0:T(8,128)(2,1)S(1)} %get-tuple-element.15.gain, f32[128,256]{1,0:T(8,128)S(1)} %get-tuple-element.16.part, f32[64,128]{1,0:T(8,128)S(1)} %shard_map.69.onward), custom_call_target="tpu_custom_call" | custom-call | tf_op jit(solution)/shard_map/pallas_call | solution.py:335
  15.0 0.1 copy.10
  15.1 0.1 sqrt_bitcast_fusion
  15.2 0.3 copy.12
  15.5 0.1 copy.15
  15.6 0.0 collective-permute-done.1.tail
  15.6 0.2 shard_map.71
  15.9 14.2 %all_to_all.20.sent.own = bf16[16,152,128]{2,1,0:T(8,128)(2,1)S(1)} all-to-all(bf16[16,152,128]{2,1,0:T(8,128)(2,1)S(1)} %get-tuple-element.20), channel_id=1, replica_groups=mesh['tm_0'=16,'tm_1'=4,'tm_2'=4,'state'=2] {'tm_1','tm_2'}, dimensions={0} | all-to-all | bytes 1245184 | tf_op jit(solution)/shard_map/all_to_all | solution.py:354
  30.1 0.7 shard_map.72
  30.8 16.3 %all-to-all-start.1 = ((f32[16,8,128]{2,1,0:T(8,128)}), f32[16,8,128]{2,1,0:T(8,128)S(1)}, u32[]{:S(2)}, u32[]{:S(2)}) async-start(f32[16,8,128]{2,1,0:T(8,128)} %get-tuple-element.22), calls=%async_computation.1 | async-start | bytes 131072 | tf_op jit(solution)/shard_map/all_to_all | solution.py:365
  47.2 4.5 %collective-permute-start.2 = (bf16[16,128,128]{2,1,0:T(8,128)(2,1)S(1)}, bf16[16,128,128]{2,1,0:T(8,128)(2,1)S(1)}, u32[]{:S(2)}, u32[]{:S(2)}) collective-permute-start(bf16[16,128,128]{2,1,0:T(8,128)(2,1)S(1)} %slice.13), channel_id=1, source_target_pairs={{0,1},{1,0},{2,3},{3,2},{4,5},{5,4},{6,7},{7,6},{8,9},{9,8},{10,11... | collective-permute-start | bytes 1572872 | tf_op jit(solution)/shard_map/ppermute | solution.py:298
  51.7 7.0 %all-to-all-done.1.planes = f32[16,8,128]{2,1,0:T(8,128)S(1)} async-done(((f32[16,8,128]{2,1,0:T(8,128)}), f32[16,8,128]{2,1,0:T(8,128)S(1)}, u32[]{:S(2)}, u32[]{:S(2)}) %all-to-all-start.1) | async-done | bytes 65568 | tf_op jit(solution)/shard_map/all_to_all | solution.py:365
  58.7 1.5 %shard_map.73 = (f32[128,128]{1,0:T(8,128)}, bf16[16,128,128]{2,1,0:T(8,128)(2,1)}, f32[2,16,128]{2,1,0:T(8,128)S(1)}) custom-call(s32[5]{0:T(128)S(1)} %pad_add_fusion.where, f32[16,8,128]{2,1,0:T(8,128)S(1)} %get-tuple-element.21.plane, f32[16,8,128]{2,1,0:T(8,128)S(1)} %all-to-all-done.1.planes, f32[6,128,128]{2,1,0:T(8,128)S(1)} %get-tuple-element.23.keep, ...), custom_call_target="tpu_custom_call" | custom-call | tf_op jit(solution)/shard_map/pallas_call | solution.py:366
  60.2 3.6 %all-to-all-start.2 = ((bf16[16,128,128]{2,1,0:T(8,128)(2,1)}), bf16[16,128,128]{2,1,0:T(8,128)(2,1)S(1)}, u32[]{:S(2)}, u32[]{:S(2)}) async-start(bf16[16,128,128]{2,1,0:T(8,128)(2,1)} %get-tuple-element.25), calls=%async_computation.2 | async-start | bytes 1048576 | tf_op jit(solution)/shard_map/all_to_all | solution.py:375
  63.8 0.0 collective-permute-done.2.other
  63.8 2.7 %collective-permute-start.3 = (bf16[2,128,128]{2,1,0:T(8,128)(2,1)S(1)}, bf16[2,128,128]{2,1,0:T(8,128)(2,1)S(1)}, u32[]{:S(2)}, u32[]{:S(2)}) collective-permute-start(bf16[2,128,128]{2,1,0:T(8,128)(2,1)S(1)} %pad_maximum_fusion), channel_id=1, source_target_pairs={{0,32},{32,64},{64,96},{96,128},{128,160},{160,192},{192,224},{224... | collective-permute-start | bytes 196616 | tf_op jit(solution)/shard_map/ppermute | solution.py:377
  66.5 5.9 %collective-permute-start.4 = (f32[2,16,128]{2,1,0:T(8,128)S(1)}, f32[2,16,128]{2,1,0:T(8,128)S(1)}, u32[]{:S(2)}, u32[]{:S(2)}) collective-permute-start(f32[2,16,128]{2,1,0:T(8,128)S(1)} %get-tuple-element.27.reach), channel_id=1, source_target_pairs={{0,1},{1,0},{2,3},{3,2},{4,5},{5,4},{6,7},{7,6},{8,9},{9,8},{10,11... | collective-permute-start | bytes 49160 | tf_op jit(solution)/shard_map/ppermute | solution.py:298
  72.5 0.8 collective-permute-done.4.reach_other
  73.3 0.0 collective-permute-done.3.tails
  73.3 0.0 all-to-all-done.2.resid
  73.3 1.6 %shard_map.74 = f32[16,2,8,256]{3,2,1,0:T(8,128)S(1)} custom-call(s32[5]{0:T(128)S(1)} %pad_add_fusion.where, bf16[2,128,128]{2,1,0:T(8,128)(2,1)S(1)} %collective-permute-done.3.tails, bf16[16,152,128]{2,1,0:T(8,128)(2,1)S(1)} %all_to_all.20.sent.own, bf16[16,128,128]{2,1,0:T(8,128)(2,1)S(1)} %collective-permute-done.2.other, ...), custom_call_target="tpu_custom_call" | custom-call | tf_op jit(solution)/shard_map/pallas_call | solution.py:379
  74.9 23.8 %all_to_all.21 = f16[32,8,256]{2,1,0:T(8,128)(2,1)S(1)} all-to-all(f16[32,8,256]{2,1,0:T(8,128)(2,1)S(1)} %bitcast.21), channel_id=1, replica_groups=mesh['tm_0'=16,'tm_1'=4,'tm_2'=4,'state'=2] {'tm_0','state'}, dimensions={0} | all-to-all | bytes 262144 | tf_op jit(solution)/shard_map/all_to_all | solution.py:386
  98.7 1.2 %shard_map.75 = f32[8,512]{1,0:T(8,128)} custom-call(s32[5]{0:T(128)S(1)} %pad_add_fusion.where, f32[32,8,256]{2,1,0:T(8,128)S(1)} %convert_element_type.11.pieces, f32[2,16,128]{2,1,0:T(8,128)S(1)} %get-tuple-element.27.reach, f32[2,16,128]{2,1,0:T(8,128)S(1)} %collective-permute-done.4.reach_other), custom_call_target="tpu_custom_call" | custom-call | tf_op jit(solution)/shard_map/pallas_call | solution.py:387
  (11 shorter events, 0.1 us)
Async XLA Ops:
  0.6 10.9 %copy-start.3 = (s32[2]{0:T(128)S(1)}, s32[2]{0:T(128)}, u32[]{:S(2)}) copy-start(s32[2]{0:T(128)} %param.9) | copy-start | bytes 28
  0.6 11.0 %collective-permute-start = (bf16[128,2048]{1,0:T(8,128)(2,1)}, bf16[128,2048]{1,0:T(8,128)(2,1)S(1)}, u32[]{:S(2)}, u32[]{:S(2)}) collective-permute-start(bf16[128,2048]{1,0:T(8,128)(2,1)} %record.1), channel_id=1, source_target_pairs={{0,1},{1,0},{2,3},{3,2},{4,5},{5,4},{6,7},{7,6},{8,9},{9,8},{10,11... | collective-permute-start | bytes 1572872 | tf_op jit(solution)/shard_map/ppermute | solution.py:298
  11.5 3.5 %copy-start.2 = (f32[128,128]{1,0:T(8,128)S(1)}, f32[128,128]{1,0:T(8,128)}, u32[]{:S(2)}) copy-start(f32[128,128]{1,0:T(8,128)} %param.7) | copy-start | bytes 196612
  11.6 3.6 %copy-start.1 = (bf16[128,2048]{1,0:T(8,128)(2,1)S(1)}, bf16[128,2048]{1,0:T(8,128)(2,1)}, u32[]{:S(2)}) copy-start(bf16[128,2048]{1,0:T(8,128)(2,1)} %record.1) | copy-start | bytes 1572868
  12.7 2.9 %copy-start = (f32[128]{0:T(128)S(1)}, f32[128]{0:T(128)}, u32[]{:S(2)}) copy-start(f32[128]{0:T(128)} %param.8) | copy-start | bytes 1540
  12.7 2.9 %collective-permute-start.1 = (f32[64,128]{1,0:T(8,128)S(1)}, f32[64,128]{1,0:T(8,128)S(1)}, u32[]{:S(2)}, u32[]{:S(2)}) collective-permute-start(f32[64,128]{1,0:T(8,128)S(1)} %shard_map.69.onward), channel_id=1, source_target_pairs={{0,2},{2,4},{4,6},{6,8},{8,10},{10,12},{12,14},{14,16},{16,18},{18... | collective-permute-start | bytes 98312 | tf_op jit(solution)/shard_map/ppermute | solution.py:338
  30.8 27.9 %all-to-all-start.1 = ((f32[16,8,128]{2,1,0:T(8,128)}), f32[16,8,128]{2,1,0:T(8,128)S(1)}, u32[]{:S(2)}, u32[]{:S(2)}) async-start(f32[16,8,128]{2,1,0:T(8,128)} %get-tuple-element.22), calls=%async_computation.1 | async-start | bytes 131072 | tf_op jit(solution)/shard_map/all_to_all | solution.py:365
  47.2 16.6 %collective-permute-start.2 = (bf16[16,128,128]{2,1,0:T(8,128)(2,1)S(1)}, bf16[16,128,128]{2,1,0:T(8,128)(2,1)S(1)}, u32[]{:S(2)}, u32[]{:S(2)}) collective-permute-start(bf16[16,128,128]{2,1,0:T(8,128)(2,1)S(1)} %slice.13), channel_id=1, source_target_pairs={{0,1},{1,0},{2,3},{3,2},{4,5},{5,4},{6,7},{7,6},{8,9},{9,8},{10,11... | collective-permute-start | bytes 1572872 | tf_op jit(solution)/shard_map/ppermute | solution.py:298
  60.2 13.1 %all-to-all-start.2 = ((bf16[16,128,128]{2,1,0:T(8,128)(2,1)}), bf16[16,128,128]{2,1,0:T(8,128)(2,1)S(1)}, u32[]{:S(2)}, u32[]{:S(2)}) async-start(bf16[16,128,128]{2,1,0:T(8,128)(2,1)} %get-tuple-element.25), calls=%async_computation.2 | async-start | bytes 1048576 | tf_op jit(solution)/shard_map/all_to_all | solution.py:375
  63.8 9.4 %collective-permute-start.3 = (bf16[2,128,128]{2,1,0:T(8,128)(2,1)S(1)}, bf16[2,128,128]{2,1,0:T(8,128)(2,1)S(1)}, u32[]{:S(2)}, u32[]{:S(2)}) collective-permute-start(bf16[2,128,128]{2,1,0:T(8,128)(2,1)S(1)} %pad_maximum_fusion), channel_id=1, source_target_pairs={{0,32},{32,64},{64,96},{96,128},{128,160},{160,192},{192,224},{224... | collective-permute-start | bytes 196616 | tf_op jit(solution)/shard_map/ppermute | solution.py:377
  66.5 6.8 %collective-permute-start.4 = (f32[2,16,128]{2,1,0:T(8,128)S(1)}, f32[2,16,128]{2,1,0:T(8,128)S(1)}, u32[]{:S(2)}, u32[]{:S(2)}) collective-permute-start(f32[2,16,128]{2,1,0:T(8,128)S(1)} %get-tuple-element.27.reach), channel_id=1, source_target_pairs={{0,1},{1,0},{2,3},{3,2},{4,5},{5,4},{6,7},{7,6},{8,9},{9,8},{10,11... | collective-permute-start | bytes 49160 | tf_op jit(solution)/shard_map/ppermute | solution.py:298

commit v12 on v11

--- a/solution.py
+++ b/solution.py
@@ -19,13 +19,12 @@
 F32 = jnp.float32
 BF16 = jnp.bfloat16
 VMEM = pl.BlockSpec(memory_space=pltpu.VMEM)
-SMEM = pl.BlockSpec(memory_space=pltpu.SMEM)
 WHOLE = pl.BlockSpec(memory_space=pltpu.HBM)
 NT = (((1,), (1,)), ((), ()))
 
 
-def call(body, outs, scratch=(), smem=(0,), whole=(), n_in=1):
-    specs = [WHOLE if i in whole else SMEM if i in smem else VMEM for i in range(n_in)]
+def call(body, outs, scratch=(), whole=(), n_in=1):
+    specs = [WHOLE if i in whole else VMEM for i in range(n_in)]
     return pl.pallas_call(
         body,
         out_shape=outs,
@@ -97,30 +96,36 @@
         copy.wait()
 
 
-def onward_body(where, other, gain, part, out):
+def moved(delay, rows, ahead, values):
+    shape = (rows, values.shape[0])
+    row = lax.broadcasted_iota(jnp.int32, shape, 0)
+    column = lax.broadcasted_iota(jnp.int32, shape, 1)
+    pick = (column + delay[:, : shape[1]] == row + ahead).astype(F32)
+    return jnp.dot(
+        pick, values, precision=lax.Precision.HIGHEST, preferred_element_type=F32
+    )
+
+
+def onward_body(delays, other, gain, part, out):
     modes = gain.shape[1]
     at = part.shape[0] - DMAX
-    row = lax.broadcasted_iota(jnp.int32, out.shape, 0)
     total = jnp.zeros(out.shape, F32)
     for k in range(TAPS):
         u = part[at:, k * modes : (k + 1) * modes] + lax.dot_general(
             other[at:], gain[k], NT, preferred_element_type=F32
         )
-        delayed = pltpu.roll(u, where[3 + k] % DMAX, 0)
-        total += jnp.where(row < where[3 + k], delayed, 0.0)
+        total += moved(delays[k : k + 1], DMAX, DMAX, u)
     out[...] = total
 
 
-def here_body(where, other, gain, part, onward, out):
+def here_body(delays, other, gain, part, onward, out):
     modes = gain.shape[1]
-    row = lax.broadcasted_iota(jnp.int32, out.shape, 0)
     total = jnp.zeros(out.shape, F32)
     for k in range(TAPS):
         u = part[:, k * modes : (k + 1) * modes] + lax.dot_general(
             other[...], gain[k], NT, preferred_element_type=F32
         )
-        delayed = pltpu.roll(u, where[3 + k], 0)
-        total += jnp.where(row >= where[3 + k], delayed, 0.0)
+        total += moved(delays[k : k + 1], u.shape[0], 0, u)
     out[...] = total
 
 
@@ -214,9 +219,11 @@
     return own_state, own_after, own_last, states, afters
 
 
-def finish_body(where, plane, planes, keep, decay_ref, leak, smoothed_out, resid_out, reach):
+def finish_body(plane, planes, keep, decay_ref, leak, smoothed_out, resid_out, reach):
+    at_plane = lax.axis_index(Z)
+    at_block = lax.axis_index(YX)
     zero = jnp.zeros((1, decay_ref.shape[1]), F32)
-    entering, after, last, states, afters = ends(planes, where[0], zero, zero, zero)
+    entering, after, last, states, afters = ends(planes, at_plane, zero, zero, zero)
     peaks = [zero]
     bound = []
     for i in range(planes.shape[0]):
@@ -225,12 +232,12 @@
     bound = jnp.concatenate(bound, 0)
     reach[0] = jnp.broadcast_to(jnp.max(bound, axis=1, keepdims=True), bound.shape)
     reach[1] = jnp.maximum(jnp.concatenate(peaks[:-1], 0), jnp.concatenate(peaks[1:], 0))
-    entering, after, last, _, _ = ends(plane, where[1], entering, after, last)
+    entering, after, last, _, _ = ends(plane, at_block, entering, after, last)
     smoothed = keep[3] + keep[4] * entering + keep[2] * after
     decay = decay_ref[...]
     kappa = 1.0 - leak[...]
     prior = (1.0 - kappa * last * last) * entering + kappa * last * smoothed[:1]
-    first = jnp.logical_and(where[0] == 0, where[1] == 0)
+    first = jnp.logical_and(at_plane == 0, at_block == 0)
     prior = jnp.where(first, 0.0, prior)
     row = lax.broadcasted_iota(jnp.int32, smoothed.shape, 0)
     shifted = jnp.where(row == 0, prior, pltpu.roll(smoothed, 1, 0))
@@ -244,12 +251,12 @@
     return jnp.maximum(span * first[0] * jnp.maximum(first[1], second[1]), 1e-30)
 
 
-def gradient_body(where, tails, own, other, resid, reach, reach_other, out, padded):
+def gradient_body(delays, tails, own, other, resid, reach, reach_other, out, padded):
     blocks, frames, modes = resid.shape
     row = lax.broadcasted_iota(jnp.int32, (frames, 2 * frames), 0)
     column = lax.broadcasted_iota(jnp.int32, (frames, 2 * frames), 1)
     picks = jnp.concatenate(
-        [(column == row + where[3 + k]).astype(F32).astype(BF16) for k in range(TAPS)], 0
+        [(column == row + delays[k : k + 1, : 2 * frames]).astype(F32).astype(BF16) for k in range(TAPS)], 0
     )
     nothing = jnp.zeros((frames, modes), BF16)
     for b in range(blocks + 1):
@@ -264,23 +271,23 @@
     rhs = padded[...]
     bound = bounds(reach, reach_other, float(blocks * frames))
     plane = lax.broadcasted_iota(jnp.int32, bound.shape, 0)
-    factor = jnp.sum(jnp.where(plane == where[0], TOP / bound, 0.0), axis=0, keepdims=True)
+    factor = jnp.sum(jnp.where(plane == lax.axis_index(Z), TOP / bound, 0.0), axis=0, keepdims=True)
     factor = jnp.concatenate([factor] * TAPS, 1)
     for which, (before, rows) in enumerate(((tails[0], own), (tails[1], other))):
         lhs = jnp.concatenate(
             [before] + [rows[i, : before.shape[0]] for i in range(blocks)], 1
         )
         sums = jnp.dot(lhs, rhs, preferred_element_type=F32) * factor
-        half = jnp.where(where[2] == which, 0, 1)
+        half = jnp.where(lax.axis_index("state") == which, 0, 1)
         for i in range(out.shape[0]):
             out[i, half] = sums[i * 8 : (i + 1) * 8]
 
 
-def total_body(where, pieces, reach, reach_other, out, *, span):
+def total_body(pieces, reach, reach_other, out, *, span):
     modes = out.shape[1] // TAPS // 2
     pair = (bounds(reach, reach_other, span) / TOP, bounds(reach_other, reach, span) / TOP)
     for core in range(2):
-        factor = jnp.where(where[2] == core, pair[0], pair[1])
+        factor = jnp.where(lax.axis_index("state") == core, pair[0], pair[1])
         factor = jnp.concatenate([factor] * TAPS, 1)
         total = pieces[core] * factor[:1]
         for i in range(1, factor.shape[0]):
@@ -303,12 +310,7 @@
     modes = rate.shape[0]
     planes = lax.axis_size(Z)
     blocks = lax.axis_size(YX)
-    where = jnp.concatenate(
-        [
-            jnp.stack([lax.axis_index(Z), lax.axis_index(YX), lax.axis_index("state")]).astype(jnp.int32),
-            dilation,
-        ]
-    )
+    delays = jnp.broadcast_to(dilation[:, None], (TAPS, 2 * frames))
     other = swapped(record)
     group = sensors // planes // blocks
     both = jax.ShapeDtypeStruct((frames, TAPS * modes), F32)
@@ -325,15 +327,14 @@
             pltpu.VMEM(half_gain, BF16),
             pltpu.SemaphoreType.DMA(((1 + 2 * TAPS) * PIECES,)),
         ],
-        smem=(),
         whole=(0, 1),
         n_in=2,
     )(*(pltpu.with_memory_space_constraint(x, pltpu.HBM) for x in (record, gain)))
     onward = call(onward_body, jax.ShapeDtypeStruct((DMAX, modes), F32), n_in=4)(
-        where, other, gain_rest, part
+        delays, other, gain_rest, part
     )
     here = call(here_body, jax.ShapeDtypeStruct((frames, modes), F32), n_in=5)(
-        where, other, gain_rest, part, onward
+        delays, other, gain_rest, part, onward
     )
     tail = lax.ppermute(onward, TM, [(i, i + 1) for i in range(planes * blocks - 1)])
     rate_t = behind(rate, here).T
@@ -348,7 +349,6 @@
             jax.ShapeDtypeStruct((6, frames, modes), F32),
             jax.ShapeDtypeStruct((blocks, planes * group + 24, frames), BF16),
         ),
-        smem=(),
         n_in=7,
     )(here, tail, decay, scale, leak_row, by_sensor, peak)
     mine = lax.all_to_all(sent, YX, 0, 0, tiled=True)
@@ -358,7 +358,6 @@
             jax.ShapeDtypeStruct((blocks, 8, modes), F32),
             jax.ShapeDtypeStruct((planes, 8, modes), F32),
         ),
-        smem=(),
         n_in=1,
     )(mine)
     theirs = swapped(mine[:, :-24])
@@ -370,8 +369,8 @@
             jax.ShapeDtypeStruct((blocks, frames, modes), BF16),
             jax.ShapeDtypeStruct((2, planes, modes), F32),
         ),
-        n_in=6,
-    )(where, plane, every_plane, keep, decay, leak_row)
+        n_in=5,
+    )(plane, every_plane, keep, decay, leak_row)
     resid_all = lax.all_to_all(resid, YX, 0, 0, tiled=True)
     tails = behind(jnp.stack([mine[-1, :-24], theirs[-1]]), resid)
     tails = lax.ppermute(tails, Z, [(i, i + 1) for i in range(planes - 1)])
@@ -381,14 +380,14 @@
         jax.ShapeDtypeStruct((planes, 2, group, TAPS * modes), F32),
         scratch=[pltpu.VMEM(((blocks + 1) * frames, TAPS * modes), BF16)],
         n_in=7,
-    )(where, tails, mine, theirs, resid_all, reach, reach_other)
+    )(delays, tails, mine, theirs, resid_all, reach, reach_other)
     pieces = partial.reshape(planes * 2, group, TAPS * modes).astype(jnp.float16)
     pieces = lax.all_to_all(pieces, (Z, "state"), 0, 0, tiled=True)
     grad = call(
         functools.partial(total_body, span=float(blocks * frames)),
         jax.ShapeDtypeStruct((group, TAPS * 2 * modes), F32),
-        n_in=4,
-    )(where, pieces.astype(F32), reach, reach_other)
+        n_in=3,
+    )(pieces.astype(F32), reach, reach_other)
     return (smoothed, grad)
 
 

time: 100 us -> 98.4 us (0.984)
  Pallas kernels: 9.36 us -> 7.24 us
  transfers between devices with their start and end apart: 7 -> 7, of which waited for: 2 -> 2; matrix products, arithmetic and copies ran while one was open for 1% -> 1% of each run, Pallas kernels for 5% -> 4%
where the time goes in v12:
time: 98.4 us; the launch traced here: 97.9 us
  starting transfers between devices  43.1 us (44%)
  blocking collectives  38.1 us (39%)
  waiting for transfers between devices  7.82 us (8%)
  Pallas kernels  7.24 us (7%)
    all_to_all x1, blocking collectives, per_device(): pieces = lax.all_to_all(pieces, (Z, 'state'), 0, 0, tiled=True)  23.7 us
    ppermute x3, starting transfers between devices, swapped(): return lax.ppermute(x, 'state', [(0, 1), (1, 0)])  19.2 us
    all_to_all x1, starting transfers between devices, per_device(): every_plane = lax.all_to_all(plane_summary, Z, 0, 0, tiled=True)  16.4 us
    all_to_all x1, blocking collectives, per_device(): mine = lax.all_to_all(sent, YX, 0, 0, tiled=True)  14.3 us
    all_to_all x1, waiting for transfers between devices, per_device(): every_plane = lax.all_to_all(plane_summary, Z, 0, 0, tiled=True)  6.99 us
    all_to_all x1, starting transfers between devices, per_device(): resid_all = lax.all_to_all(resid, YX, 0, 0, tiled=True)  3.57 us
    ppermute x1, starting transfers between devices, per_device(): tails = lax.ppermute(tails, Z, [(i, i + 1) for i in range(planes - 1)])  2.66 us
    pallas_call x1, Pallas kernels, per_device(): call(own_body, (both, jax.ShapeDtypeStruct(half_gain, BF16), jax.ShapeDty...  2.09 us
  transfers between devices with their start and end apart: 7, of which 2 were waited for; matrix products, arithmetic and copies ran while one was open for 1% of the time, Pallas kernels for 4%

profile of v12, /device:TPU:1, one launch (start us, length us, event | category | flops | bytes accessed | tf_op | source)
XLA Modules:
  0.0 97.9 jit_solution(6847910177940972021)
XLA Ops:
  0.6 8.8 %collective-permute-start = (bf16[128,2048]{1,0:T(8,128)(2,1)}, bf16[128,2048]{1,0:T(8,128)(2,1)S(1)}, u32[]{:S(2)}, u32[]{:S(2)}) collective-permute-start(bf16[128,2048]{1,0:T(8,128)(2,1)} %record.1), channel_id=1, source_target_pairs={{0,1},{1,0},{2,3},{3,2},{4,5},{5,4},{6,7},{7,6},{8,9},{9,8},{10,11... | collective-permute-start | bytes 1572872 | tf_op jit(solution)/shard_map/ppermute | solution.py:305
  9.4 2.1 %shard_map.68 = (f32[128,256]{1,0:T(8,128)S(1)}, bf16[2,128,2048]{2,1,0:T(8,128)(2,1)S(1)}, f32[8,128]{1,0:T(8,128)S(1)}) custom-call(bf16[128,2048]{1,0:T(8,128)(2,1)} %record.1, bf16[2,128,4096]{2,1,0:T(8,128)(2,1)} %gain.1), custom_call_target="tpu_custom_call" | custom-call | tf_op jit(solution)/shard_map/pallas_call | solution.py:318
  11.5 0.0 copy-start.2
  11.5 0.0 copy-start.1
  11.6 0.0 collective-permute-done.other
  11.6 0.1 broadcast_in_dim.4.delays
  11.6 0.7 shard_map.69.onward
  12.3 0.0 copy-start
  12.4 1.3 %collective-permute-start.1 = (f32[64,128]{1,0:T(8,128)S(1)}, f32[64,128]{1,0:T(8,128)S(1)}, u32[]{:S(2)}, u32[]{:S(2)}) collective-permute-start(f32[64,128]{1,0:T(8,128)S(1)} %shard_map.69.onward), channel_id=1, source_target_pairs={{0,2},{2,4},{4,6},{6,8},{8,10},{10,12},{12,14},{14,16},{16,18},{18... | collective-permute-start | bytes 98312 | tf_op jit(solution)/shard_map/ppermute | solution.py:339
  13.7 0.8 shard_map.70.here
  14.6 0.1 copy.10
  14.6 0.1 sqrt_bitcast_fusion
  14.7 0.3 copy.12
  15.0 0.1 copy.15
  15.1 0.0 collective-permute-done.1.tail
  15.2 0.2 shard_map.71
  15.4 14.3 %all_to_all.20.sent.own = bf16[16,152,128]{2,1,0:T(8,128)(2,1)S(1)} all-to-all(bf16[16,152,128]{2,1,0:T(8,128)(2,1)S(1)} %get-tuple-element.20), channel_id=1, replica_groups=mesh['tm_0'=16,'tm_1'=4,'tm_2'=4,'state'=2] {'tm_1','tm_2'}, dimensions={0} | all-to-all | bytes 1245184 | tf_op jit(solution)/shard_map/all_to_all | solution.py:354
  29.7 0.7 shard_map.72
  30.4 16.4 %all-to-all-start.1 = ((f32[16,8,128]{2,1,0:T(8,128)}), f32[16,8,128]{2,1,0:T(8,128)S(1)}, u32[]{:S(2)}, u32[]{:S(2)}) async-start(f32[16,8,128]{2,1,0:T(8,128)} %get-tuple-element.22), calls=%async_computation.1 | async-start | bytes 131072 | tf_op jit(solution)/shard_map/all_to_all | solution.py:364
  46.8 4.5 %collective-permute-start.2 = (bf16[16,128,128]{2,1,0:T(8,128)(2,1)S(1)}, bf16[16,128,128]{2,1,0:T(8,128)(2,1)S(1)}, u32[]{:S(2)}, u32[]{:S(2)}) collective-permute-start(bf16[16,128,128]{2,1,0:T(8,128)(2,1)S(1)} %slice.13), channel_id=1, source_target_pairs={{0,1},{1,0},{2,3},{3,2},{4,5},{5,4},{6,7},{7,6},{8,9},{9,8},{10,11... | collective-permute-start | bytes 1572872 | tf_op jit(solution)/shard_map/ppermute | solution.py:305
  51.4 7.0 %all-to-all-done.1.planes = f32[16,8,128]{2,1,0:T(8,128)S(1)} async-done(((f32[16,8,128]{2,1,0:T(8,128)}), f32[16,8,128]{2,1,0:T(8,128)S(1)}, u32[]{:S(2)}, u32[]{:S(2)}) %all-to-all-start.1) | async-done | bytes 65568 | tf_op jit(solution)/shard_map/all_to_all | solution.py:364
  58.4 1.0 %shard_map.73 = (f32[128,128]{1,0:T(8,128)}, bf16[16,128,128]{2,1,0:T(8,128)(2,1)}, f32[2,16,128]{2,1,0:T(8,128)S(1)}) custom-call(f32[16,8,128]{2,1,0:T(8,128)S(1)} %get-tuple-element.21.plane, f32[16,8,128]{2,1,0:T(8,128)S(1)} %all-to-all-done.1.planes, f32[6,128,128]{2,1,0:T(8,128)S(1)} %get-tuple-element.23.keep, ...), custom_call_target="tpu_custom_call" | custom-call | tf_op jit(solution)/shard_map/pallas_call | solution.py:365
  59.4 3.6 %all-to-all-start.2 = ((bf16[16,128,128]{2,1,0:T(8,128)(2,1)}), bf16[16,128,128]{2,1,0:T(8,128)(2,1)S(1)}, u32[]{:S(2)}, u32[]{:S(2)}) async-start(bf16[16,128,128]{2,1,0:T(8,128)(2,1)} %get-tuple-element.25), calls=%async_computation.2 | async-start | bytes 1048576 | tf_op jit(solution)/shard_map/all_to_all | solution.py:374
  62.9 0.0 collective-permute-done.2.other
  63.0 2.7 %collective-permute-start.3 = (bf16[2,128,128]{2,1,0:T(8,128)(2,1)S(1)}, bf16[2,128,128]{2,1,0:T(8,128)(2,1)S(1)}, u32[]{:S(2)}, u32[]{:S(2)}) collective-permute-start(bf16[2,128,128]{2,1,0:T(8,128)(2,1)S(1)} %pad_maximum_fusion), channel_id=1, source_target_pairs={{0,32},{32,64},{64,96},{96,128},{128,160},{160,192},{192,224},{224... | collective-permute-start | bytes 196616 | tf_op jit(solution)/shard_map/ppermute | solution.py:376
  65.7 5.9 %collective-permute-start.4 = (f32[2,16,128]{2,1,0:T(8,128)S(1)}, f32[2,16,128]{2,1,0:T(8,128)S(1)}, u32[]{:S(2)}, u32[]{:S(2)}) collective-permute-start(f32[2,16,128]{2,1,0:T(8,128)S(1)} %get-tuple-element.27.reach), channel_id=1, source_target_pairs={{0,1},{1,0},{2,3},{3,2},{4,5},{5,4},{6,7},{7,6},{8,9},{9,8},{10,11... | collective-permute-start | bytes 49160 | tf_op jit(solution)/shard_map/ppermute | solution.py:305
  71.6 0.8 collective-permute-done.4.reach_other
  72.4 0.0 collective-permute-done.3.tails
  72.4 0.0 all-to-all-done.2.resid
  72.4 1.0 %shard_map.74 = f32[16,2,8,256]{3,2,1,0:T(8,128)S(1)} custom-call(s32[2,256]{1,0:T(2,128)S(1)} %broadcast_in_dim.4.delays, bf16[2,128,128]{2,1,0:T(8,128)(2,1)S(1)} %collective-permute-done.3.tails, bf16[16,152,128]{2,1,0:T(8,128)(2,1)S(1)} %all_to_all.20.sent.own, bf16[16,128,128]{2,1,0:T(8,128)(2,1)S(1)} %collective-permute-done.2.other, ...), custom_call_target="tpu_custom_call" | custom-call | tf_op jit(solution)/shard_map/pallas_call | solution.py:378
  73.5 23.7 %all_to_all.21 = f16[32,8,256]{2,1,0:T(8,128)(2,1)S(1)} all-to-all(f16[32,8,256]{2,1,0:T(8,128)(2,1)S(1)} %bitcast.18), channel_id=1, replica_groups=mesh['tm_0'=16,'tm_1'=4,'tm_2'=4,'state'=2] {'tm_0','state'}, dimensions={0} | all-to-all | bytes 262144 | tf_op jit(solution)/shard_map/all_to_all | solution.py:385
  97.3 0.6 shard_map.75
  (11 shorter events, 0.1 us)
Async XLA Ops:
  0.6 10.9 %copy-start.3 = (s32[2]{0:T(128)S(1)}, s32[2]{0:T(128)}, u32[]{:S(2)}) copy-start(s32[2]{0:T(128)} %param.9) | copy-start | bytes 28
  0.6 10.9 %collective-permute-start = (bf16[128,2048]{1,0:T(8,128)(2,1)}, bf16[128,2048]{1,0:T(8,128)(2,1)S(1)}, u32[]{:S(2)}, u32[]{:S(2)}) collective-permute-start(bf16[128,2048]{1,0:T(8,128)(2,1)} %record.1), channel_id=1, source_target_pairs={{0,1},{1,0},{2,3},{3,2},{4,5},{5,4},{6,7},{7,6},{8,9},{9,8},{10,11... | collective-permute-start | bytes 1572872 | tf_op jit(solution)/shard_map/ppermute | solution.py:305
  11.5 3.0 %copy-start.2 = (f32[128,128]{1,0:T(8,128)S(1)}, f32[128,128]{1,0:T(8,128)}, u32[]{:S(2)}) copy-start(f32[128,128]{1,0:T(8,128)} %param.7) | copy-start | bytes 196612
  11.5 3.2 %copy-start.1 = (bf16[128,2048]{1,0:T(8,128)(2,1)S(1)}, bf16[128,2048]{1,0:T(8,128)(2,1)}, u32[]{:S(2)}) copy-start(bf16[128,2048]{1,0:T(8,128)(2,1)} %record.1) | copy-start | bytes 1572868
  12.3 2.8 %copy-start = (f32[128]{0:T(128)S(1)}, f32[128]{0:T(128)}, u32[]{:S(2)}) copy-start(f32[128]{0:T(128)} %param.8) | copy-start | bytes 1540
  12.4 2.7 %collective-permute-start.1 = (f32[64,128]{1,0:T(8,128)S(1)}, f32[64,128]{1,0:T(8,128)S(1)}, u32[]{:S(2)}, u32[]{:S(2)}) collective-permute-start(f32[64,128]{1,0:T(8,128)S(1)} %shard_map.69.onward), channel_id=1, source_target_pairs={{0,2},{2,4},{4,6},{6,8},{8,10},{10,12},{12,14},{14,16},{16,18},{18... | collective-permute-start | bytes 98312 | tf_op jit(solution)/shard_map/ppermute | solution.py:339
  30.4 27.9 %all-to-all-start.1 = ((f32[16,8,128]{2,1,0:T(8,128)}), f32[16,8,128]{2,1,0:T(8,128)S(1)}, u32[]{:S(2)}, u32[]{:S(2)}) async-start(f32[16,8,128]{2,1,0:T(8,128)} %get-tuple-element.22), calls=%async_computation.1 | async-start | bytes 131072 | tf_op jit(solution)/shard_map/all_to_all | solution.py:364
  46.8 16.1 %collective-permute-start.2 = (bf16[16,128,128]{2,1,0:T(8,128)(2,1)S(1)}, bf16[16,128,128]{2,1,0:T(8,128)(2,1)S(1)}, u32[]{:S(2)}, u32[]{:S(2)}) collective-permute-start(bf16[16,128,128]{2,1,0:T(8,128)(2,1)S(1)} %slice.13), channel_id=1, source_target_pairs={{0,1},{1,0},{2,3},{3,2},{4,5},{5,4},{6,7},{7,6},{8,9},{9,8},{10,11... | collective-permute-start | bytes 1572872 | tf_op jit(solution)/shard_map/ppermute | solution.py:305
  59.4 13.1 %all-to-all-start.2 = ((bf16[16,128,128]{2,1,0:T(8,128)(2,1)}), bf16[16,128,128]{2,1,0:T(8,128)(2,1)S(1)}, u32[]{:S(2)}, u32[]{:S(2)}) async-start(bf16[16,128,128]{2,1,0:T(8,128)(2,1)} %get-tuple-element.25), calls=%async_computation.2 | async-start | bytes 1048576 | tf_op jit(solution)/shard_map/all_to_all | solution.py:374
  63.0 9.4 %collective-permute-start.3 = (bf16[2,128,128]{2,1,0:T(8,128)(2,1)S(1)}, bf16[2,128,128]{2,1,0:T(8,128)(2,1)S(1)}, u32[]{:S(2)}, u32[]{:S(2)}) collective-permute-start(bf16[2,128,128]{2,1,0:T(8,128)(2,1)S(1)} %pad_maximum_fusion), channel_id=1, source_target_pairs={{0,32},{32,64},{64,96},{96,128},{128,160},{160,192},{192,224},{224... | collective-permute-start | bytes 196616 | tf_op jit(solution)/shard_map/ppermute | solution.py:376
  65.7 6.8 %collective-permute-start.4 = (f32[2,16,128]{2,1,0:T(8,128)S(1)}, f32[2,16,128]{2,1,0:T(8,128)S(1)}, u32[]{:S(2)}, u32[]{:S(2)}) collective-permute-start(f32[2,16,128]{2,1,0:T(8,128)S(1)} %get-tuple-element.27.reach), channel_id=1, source_target_pairs={{0,1},{1,0},{2,3},{3,2},{4,5},{5,4},{6,7},{7,6},{8,9},{9,8},{10,11... | collective-permute-start | bytes 49160 | tf_op jit(solution)/shard_map/ppermute | solution.py:305

commit v13 on v12

--- a/solution.py
+++ b/solution.py
@@ -242,7 +242,7 @@
     row = lax.broadcasted_iota(jnp.int32, smoothed.shape, 0)
     shifted = jnp.where(row == 0, prior, pltpu.roll(smoothed, 1, 0))
     resid = (smoothed - decay * shifted - keep[5]).astype(BF16)
-    smoothed_out[...] = smoothed.T
+    smoothed_out[...] = smoothed
     for i in range(resid_out.shape[0]):
         resid_out[i] = resid
 
@@ -365,7 +365,7 @@
     smoothed, resid, reach = call(
         finish_body,
         (
-            jax.ShapeDtypeStruct((modes, frames), F32),
+            jax.ShapeDtypeStruct((frames, modes), F32),
             jax.ShapeDtypeStruct((blocks, frames, modes), BF16),
             jax.ShapeDtypeStruct((2, planes, modes), F32),
         ),
@@ -388,7 +388,7 @@
         jax.ShapeDtypeStruct((group, TAPS * 2 * modes), F32),
         n_in=3,
     )(pieces.astype(F32), reach, reach_other)
-    return (smoothed, grad)
+    return (behind(smoothed, partial).T, grad)
 
 
 def solution(mesh):

time: 98.4 us -> 99.3 us (level)
  blocking collectives: 38.1 us -> 14.3 us
  waiting for transfers between devices: 7.82 us -> 22.9 us
  starting transfers between devices: 43.1 us -> 51.2 us
    all_to_all x1 -> x0, blocking collectives: 23.7 us -> none  [per_device(): pieces = lax.all_to_all(pieces, (Z, 'state'), 0, 0, tiled=True)]
    all_to_all x0 -> x1, waiting for transfers between devices: none -> 15.1 us  [per_device(): pieces = lax.all_to_all(pieces, (Z, 'state'), 0, 0, tiled=True)]
    all_to_all x0 -> x1, starting transfers between devices: none -> 8.09 us  [per_device(): pieces = lax.all_to_all(pieces, (Z, 'state'), 0, 0, tiled=True)]
  transfers between devices with their start and end apart: 7 -> 8, of which waited for: 2 -> 3; matrix products, arithmetic and copies ran while one was open for 1% -> 1% of each run, Pallas kernels for 4% -> 4%
where the time goes in v13:
time: 99.3 us; the launch traced here: 98.8 us
  starting transfers between devices  51.2 us (52%)
  waiting for transfers between devices  22.9 us (23%)
  blocking collectives  14.3 us (14%)
  Pallas kernels  7.24 us (7%)
  local copies, waits for them, and re-layouts  1.41 us (1%)
    ppermute x3, starting transfers between devices, swapped(): return lax.ppermute(x, 'state', [(0, 1), (1, 0)])  19.2 us
    all_to_all x1, starting transfers between devices, per_device(): every_plane = lax.all_to_all(plane_summary, Z, 0, 0, tiled=True)  16.4 us
    all_to_all x1, waiting for transfers between devices, per_device(): pieces = lax.all_to_all(pieces, (Z, 'state'), 0, 0, tiled=True)  15.1 us
    all_to_all x1, blocking collectives, per_device(): mine = lax.all_to_all(sent, YX, 0, 0, tiled=True)  14.3 us
    all_to_all x1, starting transfers between devices, per_device(): pieces = lax.all_to_all(pieces, (Z, 'state'), 0, 0, tiled=True)  8.09 us
    all_to_all x1, waiting for transfers between devices, per_device(): every_plane = lax.all_to_all(plane_summary, Z, 0, 0, tiled=True)  6.99 us
    all_to_all x1, starting transfers between devices, per_device(): resid_all = lax.all_to_all(resid, YX, 0, 0, tiled=True)  3.57 us
    ppermute x1, starting transfers between devices, per_device(): tails = lax.ppermute(tails, Z, [(i, i + 1) for i in range(planes - 1)])  2.66 us
  transfers between devices with their start and end apart: 8, of which 3 were waited for; matrix products, arithmetic and copies ran while one was open for 1% of the time, Pallas kernels for 4%

profile of v13, /device:TPU:1, one launch (start us, length us, event | category | flops | bytes accessed | tf_op | source)
XLA Modules:
  0.0 98.8 jit_solution(7051789316624138409)
XLA Ops:
  0.6 8.8 %collective-permute-start = (bf16[128,2048]{1,0:T(8,128)(2,1)}, bf16[128,2048]{1,0:T(8,128)(2,1)S(1)}, u32[]{:S(2)}, u32[]{:S(2)}) collective-permute-start(bf16[128,2048]{1,0:T(8,128)(2,1)} %record.1), channel_id=1, source_target_pairs={{0,1},{1,0},{2,3},{3,2},{4,5},{5,4},{6,7},{7,6},{8,9},{9,8},{10,11... | collective-permute-start | bytes 1572872 | tf_op jit(solution)/shard_map/ppermute | solution.py:305
  9.4 2.1 %shard_map.68 = (f32[128,256]{1,0:T(8,128)S(1)}, bf16[2,128,2048]{2,1,0:T(8,128)(2,1)S(1)}, f32[8,128]{1,0:T(8,128)S(1)}) custom-call(bf16[128,2048]{1,0:T(8,128)(2,1)} %record.1, bf16[2,128,4096]{2,1,0:T(8,128)(2,1)} %gain.1), custom_call_target="tpu_custom_call" | custom-call | tf_op jit(solution)/shard_map/pallas_call | solution.py:318
  11.5 0.0 copy-start.2
  11.5 0.0 copy-start.1
  11.6 0.1 broadcast_in_dim.4.delays
  11.6 0.7 shard_map.69.onward
  12.3 0.0 copy-start
  12.4 1.3 %collective-permute-start.1 = (f32[64,128]{1,0:T(8,128)S(1)}, f32[64,128]{1,0:T(8,128)S(1)}, u32[]{:S(2)}, u32[]{:S(2)}) collective-permute-start(f32[64,128]{1,0:T(8,128)S(1)} %shard_map.69.onward), channel_id=1, source_target_pairs={{0,2},{2,4},{4,6},{6,8},{8,10},{10,12},{12,14},{14,16},{16,18},{18... | collective-permute-start | bytes 98312 | tf_op jit(solution)/shard_map/ppermute | solution.py:339
  13.7 0.8 shard_map.70.here
  14.6 0.1 copy.11
  14.6 0.1 sqrt_bitcast_fusion
  14.7 0.3 copy.13
  15.0 0.1 copy.17
  15.1 0.0 collective-permute-done.1.tail
  15.2 0.2 shard_map.71
  15.4 14.3 %all_to_all.20.sent.own = bf16[16,152,128]{2,1,0:T(8,128)(2,1)S(1)} all-to-all(bf16[16,152,128]{2,1,0:T(8,128)(2,1)S(1)} %get-tuple-element.21), channel_id=1, replica_groups=mesh['tm_0'=16,'tm_1'=4,'tm_2'=4,'state'=2] {'tm_1','tm_2'}, dimensions={0} | all-to-all | bytes 1245184 | tf_op jit(solution)/shard_map/all_to_all | solution.py:354
  29.7 0.7 shard_map.72
  30.4 16.4 %all-to-all-start.1 = ((f32[16,8,128]{2,1,0:T(8,128)}), f32[16,8,128]{2,1,0:T(8,128)S(1)}, u32[]{:S(2)}, u32[]{:S(2)}) async-start(f32[16,8,128]{2,1,0:T(8,128)} %get-tuple-element.23), calls=%async_computation.1 | async-start | bytes 131072 | tf_op jit(solution)/shard_map/all_to_all | solution.py:364
  46.8 4.5 %collective-permute-start.2 = (bf16[16,128,128]{2,1,0:T(8,128)(2,1)S(1)}, bf16[16,128,128]{2,1,0:T(8,128)(2,1)S(1)}, u32[]{:S(2)}, u32[]{:S(2)}) collective-permute-start(bf16[16,128,128]{2,1,0:T(8,128)(2,1)S(1)} %slice.13), channel_id=1, source_target_pairs={{0,1},{1,0},{2,3},{3,2},{4,5},{5,4},{6,7},{7,6},{8,9},{9,8},{10,11... | collective-permute-start | bytes 1572872 | tf_op jit(solution)/shard_map/ppermute | solution.py:305
  51.4 7.0 %all-to-all-done.1.planes = f32[16,8,128]{2,1,0:T(8,128)S(1)} async-done(((f32[16,8,128]{2,1,0:T(8,128)}), f32[16,8,128]{2,1,0:T(8,128)S(1)}, u32[]{:S(2)}, u32[]{:S(2)}) %all-to-all-start.1) | async-done | bytes 65568 | tf_op jit(solution)/shard_map/all_to_all | solution.py:364
  58.4 1.0 shard_map.73
  59.3 3.6 %all-to-all-start.2 = ((bf16[16,128,128]{2,1,0:T(8,128)(2,1)}), bf16[16,128,128]{2,1,0:T(8,128)(2,1)S(1)}, u32[]{:S(2)}, u32[]{:S(2)}) async-start(bf16[16,128,128]{2,1,0:T(8,128)(2,1)} %get-tuple-element.26), calls=%async_computation.2 | async-start | bytes 1048576 | tf_op jit(solution)/shard_map/all_to_all | solution.py:374
  62.9 0.0 collective-permute-done.2.other
  63.0 2.7 %collective-permute-start.3 = (bf16[2,128,128]{2,1,0:T(8,128)(2,1)S(1)}, bf16[2,128,128]{2,1,0:T(8,128)(2,1)S(1)}, u32[]{:S(2)}, u32[]{:S(2)}) collective-permute-start(bf16[2,128,128]{2,1,0:T(8,128)(2,1)S(1)} %pad_maximum_fusion), channel_id=1, source_target_pairs={{0,32},{32,64},{64,96},{96,128},{128,160},{160,192},{192,224},{224... | collective-permute-start | bytes 196616 | tf_op jit(solution)/shard_map/ppermute | solution.py:376
  65.6 5.9 %collective-permute-start.4 = (f32[2,16,128]{2,1,0:T(8,128)S(1)}, f32[2,16,128]{2,1,0:T(8,128)S(1)}, u32[]{:S(2)}, u32[]{:S(2)}) collective-permute-start(f32[2,16,128]{2,1,0:T(8,128)S(1)} %get-tuple-element.28.reach), channel_id=1, source_target_pairs={{0,1},{1,0},{2,3},{3,2},{4,5},{5,4},{6,7},{7,6},{8,9},{9,8},{10,11... | collective-permute-start | bytes 49160 | tf_op jit(solution)/shard_map/ppermute | solution.py:305
  71.6 0.8 collective-permute-done.4.reach_other
  72.4 1.0 %shard_map.74 = f32[16,2,8,256]{3,2,1,0:T(8,128)S(1)} custom-call(s32[2,256]{1,0:T(2,128)S(1)} %broadcast_in_dim.4.delays, bf16[2,128,128]{2,1,0:T(8,128)(2,1)S(1)} %collective-permute-done.3.tails, bf16[16,152,128]{2,1,0:T(8,128)(2,1)S(1)} %all_to_all.20.sent.own, bf16[16,128,128]{2,1,0:T(8,128)(2,1)S(1)} %collective-permute-done.2.other, ...), custom_call_target="tpu_custom_call" | custom-call | tf_op jit(solution)/shard_map/pallas_call | solution.py:378
  73.5 0.7 convert_element_type.9
  74.1 8.1 %all-to-all-start.3 = ((f16[32,8,256]{2,1,0:T(8,128)(2,1)}), f16[32,8,256]{2,1,0:T(8,128)(2,1)S(1)}, u32[]{:S(2)}, u32[]{:S(2)}) async-start(f16[32,8,256]{2,1,0:T(8,128)(2,1)} %bitcast.8), calls=%async_computation.3 | async-start | bytes 262144 | tf_op jit(solution)/shard_map/all_to_all | solution.py:385
  82.2 0.7 copy.15
  83.0 15.1 %all-to-all-done.3 = f16[32,8,256]{2,1,0:T(8,128)(2,1)S(1)} async-done(((f16[32,8,256]{2,1,0:T(8,128)(2,1)}), f16[32,8,256]{2,1,0:T(8,128)(2,1)S(1)}, u32[]{:S(2)}, u32[]{:S(2)}) %all-to-all-start.3) | async-done | bytes 131104 | tf_op jit(solution)/shard_map/all_to_all | solution.py:385
  98.1 0.6 shard_map.75
  (13 shorter events, 0.1 us)
Async XLA Ops:
  0.6 10.9 %copy-start.3 = (s32[2]{0:T(128)S(1)}, s32[2]{0:T(128)}, u32[]{:S(2)}) copy-start(s32[2]{0:T(128)} %param.9) | copy-start | bytes 28
  0.6 10.9 %collective-permute-start = (bf16[128,2048]{1,0:T(8,128)(2,1)}, bf16[128,2048]{1,0:T(8,128)(2,1)S(1)}, u32[]{:S(2)}, u32[]{:S(2)}) collective-permute-start(bf16[128,2048]{1,0:T(8,128)(2,1)} %record.1), channel_id=1, source_target_pairs={{0,1},{1,0},{2,3},{3,2},{4,5},{5,4},{6,7},{7,6},{8,9},{9,8},{10,11... | collective-permute-start | bytes 1572872 | tf_op jit(solution)/shard_map/ppermute | solution.py:305
  11.5 3.0 %copy-start.2 = (f32[128,128]{1,0:T(8,128)S(1)}, f32[128,128]{1,0:T(8,128)}, u32[]{:S(2)}) copy-start(f32[128,128]{1,0:T(8,128)} %param.7) | copy-start | bytes 196612
  11.5 3.2 %copy-start.1 = (bf16[128,2048]{1,0:T(8,128)(2,1)S(1)}, bf16[128,2048]{1,0:T(8,128)(2,1)}, u32[]{:S(2)}) copy-start(bf16[128,2048]{1,0:T(8,128)(2,1)} %record.1) | copy-start | bytes 1572868
  12.3 2.8 %copy-start = (f32[128]{0:T(128)S(1)}, f32[128]{0:T(128)}, u32[]{:S(2)}) copy-start(f32[128]{0:T(128)} %param.8) | copy-start | bytes 1540
  12.4 2.7 %collective-permute-start.1 = (f32[64,128]{1,0:T(8,128)S(1)}, f32[64,128]{1,0:T(8,128)S(1)}, u32[]{:S(2)}, u32[]{:S(2)}) collective-permute-start(f32[64,128]{1,0:T(8,128)S(1)} %shard_map.69.onward), channel_id=1, source_target_pairs={{0,2},{2,4},{4,6},{6,8},{8,10},{10,12},{12,14},{14,16},{16,18},{18... | collective-permute-start | bytes 98312 | tf_op jit(solution)/shard_map/ppermute | solution.py:339
  30.4 27.9 %all-to-all-start.1 = ((f32[16,8,128]{2,1,0:T(8,128)}), f32[16,8,128]{2,1,0:T(8,128)S(1)}, u32[]{:S(2)}, u32[]{:S(2)}) async-start(f32[16,8,128]{2,1,0:T(8,128)} %get-tuple-element.23), calls=%async_computation.1 | async-start | bytes 131072 | tf_op jit(solution)/shard_map/all_to_all | solution.py:364
  46.8 16.1 %collective-permute-start.2 = (bf16[16,128,128]{2,1,0:T(8,128)(2,1)S(1)}, bf16[16,128,128]{2,1,0:T(8,128)(2,1)S(1)}, u32[]{:S(2)}, u32[]{:S(2)}) collective-permute-start(bf16[16,128,128]{2,1,0:T(8,128)(2,1)S(1)} %slice.13), channel_id=1, source_target_pairs={{0,1},{1,0},{2,3},{3,2},{4,5},{5,4},{6,7},{7,6},{8,9},{9,8},{10,11... | collective-permute-start | bytes 1572872 | tf_op jit(solution)/shard_map/ppermute | solution.py:305
  59.3 13.1 %all-to-all-start.2 = ((bf16[16,128,128]{2,1,0:T(8,128)(2,1)}), bf16[16,128,128]{2,1,0:T(8,128)(2,1)S(1)}, u32[]{:S(2)}, u32[]{:S(2)}) async-start(bf16[16,128,128]{2,1,0:T(8,128)(2,1)} %get-tuple-element.26), calls=%async_computation.2 | async-start | bytes 1048576 | tf_op jit(solution)/shard_map/all_to_all | solution.py:374
  63.0 9.4 %collective-permute-start.3 = (bf16[2,128,128]{2,1,0:T(8,128)(2,1)S(1)}, bf16[2,128,128]{2,1,0:T(8,128)(2,1)S(1)}, u32[]{:S(2)}, u32[]{:S(2)}) collective-permute-start(bf16[2,128,128]{2,1,0:T(8,128)(2,1)S(1)} %pad_maximum_fusion), channel_id=1, source_target_pairs={{0,32},{32,64},{64,96},{96,128},{128,160},{160,192},{192,224},{224... | collective-permute-start | bytes 196616 | tf_op jit(solution)/shard_map/ppermute | solution.py:376
  65.6 6.8 %collective-permute-start.4 = (f32[2,16,128]{2,1,0:T(8,128)S(1)}, f32[2,16,128]{2,1,0:T(8,128)S(1)}, u32[]{:S(2)}, u32[]{:S(2)}) collective-permute-start(f32[2,16,128]{2,1,0:T(8,128)S(1)} %get-tuple-element.28.reach), channel_id=1, source_target_pairs={{0,1},{1,0},{2,3},{3,2},{4,5},{5,4},{6,7},{7,6},{8,9},{9,8},{10,11... | collective-permute-start | bytes 49160 | tf_op jit(solution)/shard_map/ppermute | solution.py:305
  74.1 24.0 %all-to-all-start.3 = ((f16[32,8,256]{2,1,0:T(8,128)(2,1)}), f16[32,8,256]{2,1,0:T(8,128)(2,1)S(1)}, u32[]{:S(2)}, u32[]{:S(2)}) async-start(f16[32,8,256]{2,1,0:T(8,128)(2,1)} %bitcast.8), calls=%async_computation.3 | async-start | bytes 262144 | tf_op jit(solution)/shard_map/all_to_all | solution.py:385

commit v14 on v12

--- a/solution.py
+++ b/solution.py
@@ -57,6 +57,11 @@
         link = link * shift(link, k, 1.0)
         k *= 2
     return link, sums
+
+
+def product(rows, gain):
+    both = gain[...].reshape(TAPS * gain.shape[1], gain.shape[2])
+    return lax.dot_general(rows, both, NT, preferred_element_type=F32)
 
 
 def own_body(record, gain, out, gain_rest, peak, own, gain_own, arrived):
@@ -86,12 +91,9 @@
         copy.wait()
     largest = jnp.max(jnp.abs(own[...].astype(F32)), axis=0, keepdims=True)
     peak[...] = jnp.broadcast_to(jnp.max(largest, axis=1, keepdims=True), peak.shape)
-    for k in range(TAPS):
-        for copy in copies[(1 + k) * PIECES : (2 + k) * PIECES]:
-            copy.wait()
-        out[:, k * modes : (k + 1) * modes] = lax.dot_general(
-            own[...], gain_own[k], NT, preferred_element_type=F32
-        )
+    for copy in copies[PIECES : (1 + TAPS) * PIECES]:
+        copy.wait()
+    out[...] = product(own[...], gain_own)
     for copy in copies[(1 + TAPS) * PIECES :]:
         copy.wait()
 
@@ -109,23 +111,19 @@
 def onward_body(delays, other, gain, part, out):
     modes = gain.shape[1]
     at = part.shape[0] - DMAX
+    u = part[at:] + product(other[at:], gain)
     total = jnp.zeros(out.shape, F32)
     for k in range(TAPS):
-        u = part[at:, k * modes : (k + 1) * modes] + lax.dot_general(
-            other[at:], gain[k], NT, preferred_element_type=F32
-        )
-        total += moved(delays[k : k + 1], DMAX, DMAX, u)
+        total += moved(delays[k : k + 1], DMAX, DMAX, u[:, k * modes : (k + 1) * modes])
     out[...] = total
 
 
 def here_body(delays, other, gain, part, onward, out):
     modes = gain.shape[1]
+    u = part[...] + product(other[...], gain)
     total = jnp.zeros(out.shape, F32)
     for k in range(TAPS):
-        u = part[:, k * modes : (k + 1) * modes] + lax.dot_general(
-            other[...], gain[k], NT, preferred_element_type=F32
-        )
-        total += moved(delays[k : k + 1], u.shape[0], 0, u)
+        total += moved(delays[k : k + 1], u.shape[0], 0, u[:, k * modes : (k + 1) * modes])
     out[...] = total
 
 
@@ -273,14 +271,16 @@
     plane = lax.broadcasted_iota(jnp.int32, bound.shape, 0)
     factor = jnp.sum(jnp.where(plane == lax.axis_index(Z), TOP / bound, 0.0), axis=0, keepdims=True)
     factor = jnp.concatenate([factor] * TAPS, 1)
-    for which, (before, rows) in enumerate(((tails[0], own), (tails[1], other))):
-        lhs = jnp.concatenate(
-            [before] + [rows[i, : before.shape[0]] for i in range(blocks)], 1
-        )
-        sums = jnp.dot(lhs, rhs, preferred_element_type=F32) * factor
+    lhs = [
+        jnp.concatenate([tails[which]] + [rows[i, : tails.shape[1]] for i in range(blocks)], 1)
+        for which, rows in enumerate((own, other))
+    ]
+    sums = jnp.dot(jnp.concatenate(lhs, 0), rhs, preferred_element_type=F32) * factor
+    for which in range(2):
         half = jnp.where(lax.axis_index("state") == which, 0, 1)
         for i in range(out.shape[0]):
-            out[i, half] = sums[i * 8 : (i + 1) * 8]
+            row = which * tails.shape[1] + i * 8
+            out[i, half] = sums[row : row + 8]
 
 
 def total_body(pieces, reach, reach_other, out, *, span):

time: 98.4 us -> 98.7 us (level)
  no operation moved by 1% of the time
where the time goes in v14:
time: 98.7 us; the launch traced here: 98.2 us
  starting transfers between devices  43.3 us (44%)
  blocking collectives  37.9 us (38%)
  waiting for transfers between devices  7.86 us (8%)
  Pallas kernels  7.48 us (8%)
    all_to_all x1, blocking collectives, per_device(): pieces = lax.all_to_all(pieces, (Z, 'state'), 0, 0, tiled=True)  23.7 us
    ppermute x3, starting transfers between devices, swapped(): return lax.ppermute(x, 'state', [(0, 1), (1, 0)])  19.2 us
    all_to_all x1, starting transfers between devices, per_device(): every_plane = lax.all_to_all(plane_summary, Z, 0, 0, tiled=True)  16.5 us
    all_to_all x1, blocking collectives, per_device(): mine = lax.all_to_all(sent, YX, 0, 0, tiled=True)  14.1 us
    all_to_all x1, waiting for transfers between devices, per_device(): every_plane = lax.all_to_all(plane_summary, Z, 0, 0, tiled=True)  7.03 us
    all_to_all x1, starting transfers between devices, per_device(): resid_all = lax.all_to_all(resid, YX, 0, 0, tiled=True)  3.57 us
    ppermute x1, starting transfers between devices, per_device(): tails = lax.ppermute(tails, Z, [(i, i + 1) for i in range(planes - 1)])  2.66 us
  transfers between devices with their start and end apart: 7, of which 2 were waited for; matrix products, arithmetic and copies ran while one was open for 1% of the time, Pallas kernels for 4%

profile of v14, /device:TPU:1, one launch (start us, length us, event | category | flops | bytes accessed | tf_op | source)
XLA Modules:
  0.0 98.2 jit_solution(14223500497542514812)
XLA Ops:
  0.6 0.0 copy-start.3
  0.6 8.8 %collective-permute-start = (bf16[128,2048]{1,0:T(8,128)(2,1)}, bf16[128,2048]{1,0:T(8,128)(2,1)S(1)}, u32[]{:S(2)}, u32[]{:S(2)}) collective-permute-start(bf16[128,2048]{1,0:T(8,128)(2,1)} %record.1), channel_id=1, source_target_pairs={{0,1},{1,0},{2,3},{3,2},{4,5},{5,4},{6,7},{7,6},{8,9},{9,8},{10,11... | collective-permute-start | bytes 1572872 | tf_op jit(solution)/shard_map/ppermute | solution.py:305
  9.4 1.9 %shard_map.68 = (f32[128,256]{1,0:T(8,128)S(1)}, bf16[2,128,2048]{2,1,0:T(8,128)(2,1)S(1)}, f32[8,128]{1,0:T(8,128)S(1)}) custom-call(bf16[128,2048]{1,0:T(8,128)(2,1)} %record.1, bf16[2,128,4096]{2,1,0:T(8,128)(2,1)} %gain.1), custom_call_target="tpu_custom_call" | custom-call | tf_op jit(solution)/shard_map/pallas_call | solution.py:318
  11.3 0.0 copy-start.2
  11.3 0.0 copy-start.1
  11.4 0.0 collective-permute-done.other
  11.4 0.1 broadcast_in_dim.4.delays
  11.4 0.7 shard_map.69.onward
  12.2 1.4 %collective-permute-start.1 = (f32[64,128]{1,0:T(8,128)S(1)}, f32[64,128]{1,0:T(8,128)S(1)}, u32[]{:S(2)}, u32[]{:S(2)}) collective-permute-start(f32[64,128]{1,0:T(8,128)S(1)} %shard_map.69.onward), channel_id=1, source_target_pairs={{0,2},{2,4},{4,6},{6,8},{8,10},{10,12},{12,14},{14,16},{16,18},{18... | collective-permute-start | bytes 98312 | tf_op jit(solution)/shard_map/ppermute | solution.py:339
  13.6 0.9 shard_map.70.here
  14.5 0.1 copy.10
  14.6 0.1 sqrt_bitcast_fusion
  14.7 0.3 copy.12
  15.0 0.1 copy.15
  15.1 0.0 collective-permute-done.1.tail
  15.1 0.2 shard_map.71
  15.4 14.1 %all_to_all.20.sent.own = bf16[16,152,128]{2,1,0:T(8,128)(2,1)S(1)} all-to-all(bf16[16,152,128]{2,1,0:T(8,128)(2,1)S(1)} %get-tuple-element.20), channel_id=1, replica_groups=mesh['tm_0'=16,'tm_1'=4,'tm_2'=4,'state'=2] {'tm_1','tm_2'}, dimensions={0} | all-to-all | bytes 1245184 | tf_op jit(solution)/shard_map/all_to_all | solution.py:354
  29.5 0.7 shard_map.72
  30.2 16.5 %all-to-all-start.1 = ((f32[16,8,128]{2,1,0:T(8,128)}), f32[16,8,128]{2,1,0:T(8,128)S(1)}, u32[]{:S(2)}, u32[]{:S(2)}) async-start(f32[16,8,128]{2,1,0:T(8,128)} %get-tuple-element.22), calls=%async_computation.1 | async-start | bytes 131072 | tf_op jit(solution)/shard_map/all_to_all | solution.py:364
  46.8 4.5 %collective-permute-start.2 = (bf16[16,128,128]{2,1,0:T(8,128)(2,1)S(1)}, bf16[16,128,128]{2,1,0:T(8,128)(2,1)S(1)}, u32[]{:S(2)}, u32[]{:S(2)}) collective-permute-start(bf16[16,128,128]{2,1,0:T(8,128)(2,1)S(1)} %slice.13), channel_id=1, source_target_pairs={{0,1},{1,0},{2,3},{3,2},{4,5},{5,4},{6,7},{7,6},{8,9},{9,8},{10,11... | collective-permute-start | bytes 1572872 | tf_op jit(solution)/shard_map/ppermute | solution.py:305
  51.3 7.0 %all-to-all-done.1.planes = f32[16,8,128]{2,1,0:T(8,128)S(1)} async-done(((f32[16,8,128]{2,1,0:T(8,128)}), f32[16,8,128]{2,1,0:T(8,128)S(1)}, u32[]{:S(2)}, u32[]{:S(2)}) %all-to-all-start.1) | async-done | bytes 65568 | tf_op jit(solution)/shard_map/all_to_all | solution.py:364
  58.3 1.0 %shard_map.73 = (f32[128,128]{1,0:T(8,128)}, bf16[16,128,128]{2,1,0:T(8,128)(2,1)}, f32[2,16,128]{2,1,0:T(8,128)S(1)}) custom-call(f32[16,8,128]{2,1,0:T(8,128)S(1)} %get-tuple-element.21.plane, f32[16,8,128]{2,1,0:T(8,128)S(1)} %all-to-all-done.1.planes, f32[6,128,128]{2,1,0:T(8,128)S(1)} %get-tuple-element.23.keep, ...), custom_call_target="tpu_custom_call" | custom-call | tf_op jit(solution)/shard_map/pallas_call | solution.py:365
  59.3 3.6 %all-to-all-start.2 = ((bf16[16,128,128]{2,1,0:T(8,128)(2,1)}), bf16[16,128,128]{2,1,0:T(8,128)(2,1)S(1)}, u32[]{:S(2)}, u32[]{:S(2)}) async-start(bf16[16,128,128]{2,1,0:T(8,128)(2,1)} %get-tuple-element.25), calls=%async_computation.2 | async-start | bytes 1048576 | tf_op jit(solution)/shard_map/all_to_all | solution.py:374
  62.9 0.0 collective-permute-done.2.other
  62.9 2.7 %collective-permute-start.3 = (bf16[2,128,128]{2,1,0:T(8,128)(2,1)S(1)}, bf16[2,128,128]{2,1,0:T(8,128)(2,1)S(1)}, u32[]{:S(2)}, u32[]{:S(2)}) collective-permute-start(bf16[2,128,128]{2,1,0:T(8,128)(2,1)S(1)} %pad_maximum_fusion), channel_id=1, source_target_pairs={{0,32},{32,64},{64,96},{96,128},{128,160},{160,192},{192,224},{224... | collective-permute-start | bytes 196616 | tf_op jit(solution)/shard_map/ppermute | solution.py:376
  65.6 5.9 %collective-permute-start.4 = (f32[2,16,128]{2,1,0:T(8,128)S(1)}, f32[2,16,128]{2,1,0:T(8,128)S(1)}, u32[]{:S(2)}, u32[]{:S(2)}) collective-permute-start(f32[2,16,128]{2,1,0:T(8,128)S(1)} %get-tuple-element.27.reach), channel_id=1, source_target_pairs={{0,1},{1,0},{2,3},{3,2},{4,5},{5,4},{6,7},{7,6},{8,9},{9,8},{10,11... | collective-permute-start | bytes 49160 | tf_op jit(solution)/shard_map/ppermute | solution.py:305
  71.5 0.8 collective-permute-done.4.reach_other
  72.3 0.0 collective-permute-done.3.tails
  72.3 0.0 all-to-all-done.2.resid
  72.3 1.4 %shard_map.74 = f32[16,2,8,256]{3,2,1,0:T(8,128)S(1)} custom-call(s32[2,256]{1,0:T(2,128)S(1)} %broadcast_in_dim.4.delays, bf16[2,128,128]{2,1,0:T(8,128)(2,1)S(1)} %collective-permute-done.3.tails, bf16[16,152,128]{2,1,0:T(8,128)(2,1)S(1)} %all_to_all.20.sent.own, bf16[16,128,128]{2,1,0:T(8,128)(2,1)S(1)} %collective-permute-done.2.other, ...), custom_call_target="tpu_custom_call" | custom-call | tf_op jit(solution)/shard_map/pallas_call | solution.py:378
  73.8 23.7 %all_to_all.21 = f16[32,8,256]{2,1,0:T(8,128)(2,1)S(1)} all-to-all(f16[32,8,256]{2,1,0:T(8,128)(2,1)S(1)} %bitcast.18), channel_id=1, replica_groups=mesh['tm_0'=16,'tm_1'=4,'tm_2'=4,'state'=2] {'tm_0','state'}, dimensions={0} | all-to-all | bytes 262144 | tf_op jit(solution)/shard_map/all_to_all | solution.py:385
  97.5 0.6 shard_map.75
  (11 shorter events, 0.1 us)
Async XLA Ops:
  0.6 10.7 %copy-start.3 = (s32[2]{0:T(128)S(1)}, s32[2]{0:T(128)}, u32[]{:S(2)}) copy-start(s32[2]{0:T(128)} %param.9) | copy-start | bytes 28
  0.6 10.7 %collective-permute-start = (bf16[128,2048]{1,0:T(8,128)(2,1)}, bf16[128,2048]{1,0:T(8,128)(2,1)S(1)}, u32[]{:S(2)}, u32[]{:S(2)}) collective-permute-start(bf16[128,2048]{1,0:T(8,128)(2,1)} %record.1), channel_id=1, source_target_pairs={{0,1},{1,0},{2,3},{3,2},{4,5},{5,4},{6,7},{7,6},{8,9},{9,8},{10,11... | collective-permute-start | bytes 1572872 | tf_op jit(solution)/shard_map/ppermute | solution.py:305
  11.3 3.2 %copy-start.2 = (f32[128,128]{1,0:T(8,128)S(1)}, f32[128,128]{1,0:T(8,128)}, u32[]{:S(2)}) copy-start(f32[128,128]{1,0:T(8,128)} %param.7) | copy-start | bytes 196612
  11.3 3.3 %copy-start.1 = (bf16[128,2048]{1,0:T(8,128)(2,1)S(1)}, bf16[128,2048]{1,0:T(8,128)(2,1)}, u32[]{:S(2)}) copy-start(bf16[128,2048]{1,0:T(8,128)(2,1)} %record.1) | copy-start | bytes 1572868
  12.2 2.9 %copy-start = (f32[128]{0:T(128)S(1)}, f32[128]{0:T(128)}, u32[]{:S(2)}) copy-start(f32[128]{0:T(128)} %param.8) | copy-start | bytes 1540
  12.2 2.9 %collective-permute-start.1 = (f32[64,128]{1,0:T(8,128)S(1)}, f32[64,128]{1,0:T(8,128)S(1)}, u32[]{:S(2)}, u32[]{:S(2)}) collective-permute-start(f32[64,128]{1,0:T(8,128)S(1)} %shard_map.69.onward), channel_id=1, source_target_pairs={{0,2},{2,4},{4,6},{6,8},{8,10},{10,12},{12,14},{14,16},{16,18},{18... | collective-permute-start | bytes 98312 | tf_op jit(solution)/shard_map/ppermute | solution.py:339
  30.2 28.1 %all-to-all-start.1 = ((f32[16,8,128]{2,1,0:T(8,128)}), f32[16,8,128]{2,1,0:T(8,128)S(1)}, u32[]{:S(2)}, u32[]{:S(2)}) async-start(f32[16,8,128]{2,1,0:T(8,128)} %get-tuple-element.22), calls=%async_computation.1 | async-start | bytes 131072 | tf_op jit(solution)/shard_map/all_to_all | solution.py:364
  46.8 16.1 %collective-permute-start.2 = (bf16[16,128,128]{2,1,0:T(8,128)(2,1)S(1)}, bf16[16,128,128]{2,1,0:T(8,128)(2,1)S(1)}, u32[]{:S(2)}, u32[]{:S(2)}) collective-permute-start(bf16[16,128,128]{2,1,0:T(8,128)(2,1)S(1)} %slice.13), channel_id=1, source_target_pairs={{0,1},{1,0},{2,3},{3,2},{4,5},{5,4},{6,7},{7,6},{8,9},{9,8},{10,11... | collective-permute-start | bytes 1572872 | tf_op jit(solution)/shard_map/ppermute | solution.py:305
  59.3 13.0 %all-to-all-start.2 = ((bf16[16,128,128]{2,1,0:T(8,128)(2,1)}), bf16[16,128,128]{2,1,0:T(8,128)(2,1)S(1)}, u32[]{:S(2)}, u32[]{:S(2)}) async-start(bf16[16,128,128]{2,1,0:T(8,128)(2,1)} %get-tuple-element.25), calls=%async_computation.2 | async-start | bytes 1048576 | tf_op jit(solution)/shard_map/all_to_all | solution.py:374
  62.9 9.4 %collective-permute-start.3 = (bf16[2,128,128]{2,1,0:T(8,128)(2,1)S(1)}, bf16[2,128,128]{2,1,0:T(8,128)(2,1)S(1)}, u32[]{:S(2)}, u32[]{:S(2)}) collective-permute-start(bf16[2,128,128]{2,1,0:T(8,128)(2,1)S(1)} %pad_maximum_fusion), channel_id=1, source_target_pairs={{0,32},{32,64},{64,96},{96,128},{128,160},{160,192},{192,224},{224... | collective-permute-start | bytes 196616 | tf_op jit(solution)/shard_map/ppermute | solution.py:376
  65.6 6.7 %collective-permute-start.4 = (f32[2,16,128]{2,1,0:T(8,128)S(1)}, f32[2,16,128]{2,1,0:T(8,128)S(1)}, u32[]{:S(2)}, u32[]{:S(2)}) collective-permute-start(f32[2,16,128]{2,1,0:T(8,128)S(1)} %get-tuple-element.27.reach), channel_id=1, source_target_pairs={{0,1},{1,0},{2,3},{3,2},{4,5},{5,4},{6,7},{7,6},{8,9},{9,8},{10,11... | collective-permute-start | bytes 49160 | tf_op jit(solution)/shard_map/ppermute | solution.py:305

commit v15 on v14

--- a/solution.py
+++ b/solution.py
@@ -271,16 +271,14 @@
     plane = lax.broadcasted_iota(jnp.int32, bound.shape, 0)
     factor = jnp.sum(jnp.where(plane == lax.axis_index(Z), TOP / bound, 0.0), axis=0, keepdims=True)
     factor = jnp.concatenate([factor] * TAPS, 1)
-    lhs = [
-        jnp.concatenate([tails[which]] + [rows[i, : tails.shape[1]] for i in range(blocks)], 1)
-        for which, rows in enumerate((own, other))
-    ]
-    sums = jnp.dot(jnp.concatenate(lhs, 0), rhs, preferred_element_type=F32) * factor
-    for which in range(2):
+    for which, (before, rows) in enumerate(((tails[0], own), (tails[1], other))):
+        lhs = jnp.concatenate(
+            [before] + [rows[i, : before.shape[0]] for i in range(blocks)], 1
+        )
+        sums = jnp.dot(lhs, rhs, preferred_element_type=F32) * factor
         half = jnp.where(lax.axis_index("state") == which, 0, 1)
-        for i in range(out.shape[0]):
-            row = which * tails.shape[1] + i * 8
-            out[i, half] = sums[row : row + 8]
+        for i in range(out.shape[1]):
+            out[half, i] = sums[i * 8 : (i + 1) * 8]
 
 
 def total_body(pieces, reach, reach_other, out, *, span):
@@ -289,9 +287,10 @@
     for core in range(2):
         factor = jnp.where(lax.axis_index("state") == core, pair[0], pair[1])
         factor = jnp.concatenate([factor] * TAPS, 1)
-        total = pieces[core] * factor[:1]
-        for i in range(1, factor.shape[0]):
-            total += pieces[2 * i + core] * factor[i : i + 1]
+        planes = factor.shape[0]
+        total = pieces[core * planes] * factor[:1]
+        for i in range(1, planes):
+            total += pieces[core * planes + i] * factor[i : i + 1]
         for k in range(TAPS):
             column = (2 * k + core) * modes
             out[:, column : column + modes] = total[:, k * modes : (k + 1) * modes]
@@ -377,12 +376,12 @@
     reach_other = swapped(reach)
     partial = call(
         gradient_body,
-        jax.ShapeDtypeStruct((planes, 2, group, TAPS * modes), F32),
+        jax.ShapeDtypeStruct((2, planes, group, TAPS * modes), F32),
         scratch=[pltpu.VMEM(((blocks + 1) * frames, TAPS * modes), BF16)],
         n_in=7,
     )(delays, tails, mine, theirs, resid_all, reach, reach_other)
     pieces = partial.reshape(planes * 2, group, TAPS * modes).astype(jnp.float16)
-    pieces = lax.all_to_all(pieces, (Z, "state"), 0, 0, tiled=True)
+    pieces = lax.all_to_all(pieces, ("state", Z), 0, 0, tiled=True)
     grad = call(
         functools.partial(total_body, span=float(blocks * frames)),
         jax.ShapeDtypeStruct((group, TAPS * 2 * modes), F32),

time: 98.7 us -> 98.8 us (level)
  no operation moved by 1% of the time
where the time goes in v15:
time: 98.8 us; the launch traced here: 98.3 us
  starting transfers between devices  43.3 us (44%)
  blocking collectives  38.4 us (39%)
  waiting for transfers between devices  7.86 us (8%)
  Pallas kernels  7.13 us (7%)
    all_to_all x1, blocking collectives, per_device(): pieces = lax.all_to_all(pieces, ('state', Z), 0, 0, tiled=True)  24.3 us
    ppermute x3, starting transfers between devices, swapped(): return lax.ppermute(x, 'state', [(0, 1), (1, 0)])  19.2 us
    all_to_all x1, starting transfers between devices, per_device(): every_plane = lax.all_to_all(plane_summary, Z, 0, 0, tiled=True)  16.5 us
    all_to_all x1, blocking collectives, per_device(): mine = lax.all_to_all(sent, YX, 0, 0, tiled=True)  14.1 us
    all_to_all x1, waiting for transfers between devices, per_device(): every_plane = lax.all_to_all(plane_summary, Z, 0, 0, tiled=True)  7.03 us
    all_to_all x1, starting transfers between devices, per_device(): resid_all = lax.all_to_all(resid, YX, 0, 0, tiled=True)  3.57 us
    ppermute x1, starting transfers between devices, per_device(): tails = lax.ppermute(tails, Z, [(i, i + 1) for i in range(planes - 1)])  2.66 us
  transfers between devices with their start and end apart: 7, of which 2 were waited for; matrix products, arithmetic and copies ran while one was open for 1% of the time, Pallas kernels for 4%

profile of v15, /device:TPU:1, one launch (start us, length us, event | category | flops | bytes accessed | tf_op | source)
XLA Modules:
  0.0 98.3 jit_solution(7527480383716676251)
XLA Ops:
  0.6 8.8 %collective-permute-start = (bf16[128,2048]{1,0:T(8,128)(2,1)}, bf16[128,2048]{1,0:T(8,128)(2,1)S(1)}, u32[]{:S(2)}, u32[]{:S(2)}) collective-permute-start(bf16[128,2048]{1,0:T(8,128)(2,1)} %record.1), channel_id=1, source_target_pairs={{0,1},{1,0},{2,3},{3,2},{4,5},{5,4},{6,7},{7,6},{8,9},{9,8},{10,11... | collective-permute-start | bytes 1572872 | tf_op jit(solution)/shard_map/ppermute | solution.py:304
  9.4 1.9 %shard_map.68 = (f32[128,256]{1,0:T(8,128)S(1)}, bf16[2,128,2048]{2,1,0:T(8,128)(2,1)S(1)}, f32[8,128]{1,0:T(8,128)S(1)}) custom-call(bf16[128,2048]{1,0:T(8,128)(2,1)} %record.1, bf16[2,128,4096]{2,1,0:T(8,128)(2,1)} %gain.1), custom_call_target="tpu_custom_call" | custom-call | tf_op jit(solution)/shard_map/pallas_call | solution.py:317
  11.3 0.0 copy-start.2
  11.3 0.0 copy-start.1
  11.4 0.0 collective-permute-done.other
  11.4 0.1 broadcast_in_dim.4.delays
  11.4 0.7 shard_map.69.onward
  12.2 1.4 %collective-permute-start.1 = (f32[64,128]{1,0:T(8,128)S(1)}, f32[64,128]{1,0:T(8,128)S(1)}, u32[]{:S(2)}, u32[]{:S(2)}) collective-permute-start(f32[64,128]{1,0:T(8,128)S(1)} %shard_map.69.onward), channel_id=1, source_target_pairs={{0,2},{2,4},{4,6},{6,8},{8,10},{10,12},{12,14},{14,16},{16,18},{18... | collective-permute-start | bytes 98312 | tf_op jit(solution)/shard_map/ppermute | solution.py:338
  13.6 0.9 shard_map.70.here
  14.5 0.0 copy-done.2
  14.5 0.1 copy.10
  14.6 0.1 sqrt_bitcast_fusion
  14.7 0.3 copy.12
  15.0 0.1 copy.15
  15.1 0.0 collective-permute-done.1.tail
  15.1 0.2 shard_map.71
  15.4 14.1 %all_to_all.20.sent.own = bf16[16,152,128]{2,1,0:T(8,128)(2,1)S(1)} all-to-all(bf16[16,152,128]{2,1,0:T(8,128)(2,1)S(1)} %get-tuple-element.20), channel_id=1, replica_groups=mesh['tm_0'=16,'tm_1'=4,'tm_2'=4,'state'=2] {'tm_1','tm_2'}, dimensions={0} | all-to-all | bytes 1245184 | tf_op jit(solution)/shard_map/all_to_all | solution.py:353
  29.5 0.7 shard_map.72
  30.2 16.5 %all-to-all-start.1 = ((f32[16,8,128]{2,1,0:T(8,128)}), f32[16,8,128]{2,1,0:T(8,128)S(1)}, u32[]{:S(2)}, u32[]{:S(2)}) async-start(f32[16,8,128]{2,1,0:T(8,128)} %get-tuple-element.22), calls=%async_computation.1 | async-start | bytes 131072 | tf_op jit(solution)/shard_map/all_to_all | solution.py:363
  46.8 4.5 %collective-permute-start.2 = (bf16[16,128,128]{2,1,0:T(8,128)(2,1)S(1)}, bf16[16,128,128]{2,1,0:T(8,128)(2,1)S(1)}, u32[]{:S(2)}, u32[]{:S(2)}) collective-permute-start(bf16[16,128,128]{2,1,0:T(8,128)(2,1)S(1)} %slice.13), channel_id=1, source_target_pairs={{0,1},{1,0},{2,3},{3,2},{4,5},{5,4},{6,7},{7,6},{8,9},{9,8},{10,11... | collective-permute-start | bytes 1572872 | tf_op jit(solution)/shard_map/ppermute | solution.py:304
  51.3 7.0 %all-to-all-done.1.planes = f32[16,8,128]{2,1,0:T(8,128)S(1)} async-done(((f32[16,8,128]{2,1,0:T(8,128)}), f32[16,8,128]{2,1,0:T(8,128)S(1)}, u32[]{:S(2)}, u32[]{:S(2)}) %all-to-all-start.1) | async-done | bytes 65568 | tf_op jit(solution)/shard_map/all_to_all | solution.py:363
  58.3 1.0 %shard_map.73 = (f32[128,128]{1,0:T(8,128)}, bf16[16,128,128]{2,1,0:T(8,128)(2,1)}, f32[2,16,128]{2,1,0:T(8,128)S(1)}) custom-call(f32[16,8,128]{2,1,0:T(8,128)S(1)} %get-tuple-element.21.plane, f32[16,8,128]{2,1,0:T(8,128)S(1)} %all-to-all-done.1.planes, f32[6,128,128]{2,1,0:T(8,128)S(1)} %get-tuple-element.23.keep, ...), custom_call_target="tpu_custom_call" | custom-call | tf_op jit(solution)/shard_map/pallas_call | solution.py:364
  59.3 3.6 %all-to-all-start.2 = ((bf16[16,128,128]{2,1,0:T(8,128)(2,1)}), bf16[16,128,128]{2,1,0:T(8,128)(2,1)S(1)}, u32[]{:S(2)}, u32[]{:S(2)}) async-start(bf16[16,128,128]{2,1,0:T(8,128)(2,1)} %get-tuple-element.25), calls=%async_computation.2 | async-start | bytes 1048576 | tf_op jit(solution)/shard_map/all_to_all | solution.py:373
  62.9 0.0 collective-permute-done.2.other
  62.9 2.7 %collective-permute-start.3 = (bf16[2,128,128]{2,1,0:T(8,128)(2,1)S(1)}, bf16[2,128,128]{2,1,0:T(8,128)(2,1)S(1)}, u32[]{:S(2)}, u32[]{:S(2)}) collective-permute-start(bf16[2,128,128]{2,1,0:T(8,128)(2,1)S(1)} %pad_maximum_fusion), channel_id=1, source_target_pairs={{0,32},{32,64},{64,96},{96,128},{128,160},{160,192},{192,224},{224... | collective-permute-start | bytes 196616 | tf_op jit(solution)/shard_map/ppermute | solution.py:375
  65.6 5.9 %collective-permute-start.4 = (f32[2,16,128]{2,1,0:T(8,128)S(1)}, f32[2,16,128]{2,1,0:T(8,128)S(1)}, u32[]{:S(2)}, u32[]{:S(2)}) collective-permute-start(f32[2,16,128]{2,1,0:T(8,128)S(1)} %get-tuple-element.27.reach), channel_id=1, source_target_pairs={{0,1},{1,0},{2,3},{3,2},{4,5},{5,4},{6,7},{7,6},{8,9},{9,8},{10,11... | collective-permute-start | bytes 49160 | tf_op jit(solution)/shard_map/ppermute | solution.py:304
  71.5 0.8 collective-permute-done.4.reach_other
  72.3 0.0 collective-permute-done.3.tails
  72.3 0.0 all-to-all-done.2.resid
  72.3 1.0 %shard_map.74 = f32[2,16,8,256]{3,2,1,0:T(8,128)S(1)} custom-call(s32[2,256]{1,0:T(2,128)S(1)} %broadcast_in_dim.4.delays, bf16[2,128,128]{2,1,0:T(8,128)(2,1)S(1)} %collective-permute-done.3.tails, bf16[16,152,128]{2,1,0:T(8,128)(2,1)S(1)} %all_to_all.20.sent.own, bf16[16,128,128]{2,1,0:T(8,128)(2,1)S(1)} %collective-permute-done.2.other, ...), custom_call_target="tpu_custom_call" | custom-call | tf_op jit(solution)/shard_map/pallas_call | solution.py:377
  73.4 24.3 %all_to_all.21 = f16[32,8,256]{2,1,0:T(8,128)(2,1)S(1)} all-to-all(f16[32,8,256]{2,1,0:T(8,128)(2,1)S(1)} %bitcast.18), channel_id=1, replica_groups=mesh['tm_0'=16,'tm_1'=4,'tm_2'=4,'state'=2] {'state','tm_0'}, dimensions={0} | all-to-all | bytes 262144 | tf_op jit(solution)/shard_map/all_to_all | solution.py:384
  97.7 0.6 shard_map.75
  (11 shorter events, 0.1 us)
Async XLA Ops:
  0.6 10.7 %copy-start.3 = (s32[2]{0:T(128)S(1)}, s32[2]{0:T(128)}, u32[]{:S(2)}) copy-start(s32[2]{0:T(128)} %param.9) | copy-start | bytes 28
  0.6 10.7 %collective-permute-start = (bf16[128,2048]{1,0:T(8,128)(2,1)}, bf16[128,2048]{1,0:T(8,128)(2,1)S(1)}, u32[]{:S(2)}, u32[]{:S(2)}) collective-permute-start(bf16[128,2048]{1,0:T(8,128)(2,1)} %record.1), channel_id=1, source_target_pairs={{0,1},{1,0},{2,3},{3,2},{4,5},{5,4},{6,7},{7,6},{8,9},{9,8},{10,11... | collective-permute-start | bytes 1572872 | tf_op jit(solution)/shard_map/ppermute | solution.py:304
  11.3 3.2 %copy-start.2 = (f32[128,128]{1,0:T(8,128)S(1)}, f32[128,128]{1,0:T(8,128)}, u32[]{:S(2)}) copy-start(f32[128,128]{1,0:T(8,128)} %param.7) | copy-start | bytes 196612
  11.3 3.3 %copy-start.1 = (bf16[128,2048]{1,0:T(8,128)(2,1)S(1)}, bf16[128,2048]{1,0:T(8,128)(2,1)}, u32[]{:S(2)}) copy-start(bf16[128,2048]{1,0:T(8,128)(2,1)} %record.1) | copy-start | bytes 1572868
  12.2 2.9 %copy-start = (f32[128]{0:T(128)S(1)}, f32[128]{0:T(128)}, u32[]{:S(2)}) copy-start(f32[128]{0:T(128)} %param.8) | copy-start | bytes 1540
  12.2 2.9 %collective-permute-start.1 = (f32[64,128]{1,0:T(8,128)S(1)}, f32[64,128]{1,0:T(8,128)S(1)}, u32[]{:S(2)}, u32[]{:S(2)}) collective-permute-start(f32[64,128]{1,0:T(8,128)S(1)} %shard_map.69.onward), channel_id=1, source_target_pairs={{0,2},{2,4},{4,6},{6,8},{8,10},{10,12},{12,14},{14,16},{16,18},{18... | collective-permute-start | bytes 98312 | tf_op jit(solution)/shard_map/ppermute | solution.py:338
  30.2 28.1 %all-to-all-start.1 = ((f32[16,8,128]{2,1,0:T(8,128)}), f32[16,8,128]{2,1,0:T(8,128)S(1)}, u32[]{:S(2)}, u32[]{:S(2)}) async-start(f32[16,8,128]{2,1,0:T(8,128)} %get-tuple-element.22), calls=%async_computation.1 | async-start | bytes 131072 | tf_op jit(solution)/shard_map/all_to_all | solution.py:363
  46.8 16.1 %collective-permute-start.2 = (bf16[16,128,128]{2,1,0:T(8,128)(2,1)S(1)}, bf16[16,128,128]{2,1,0:T(8,128)(2,1)S(1)}, u32[]{:S(2)}, u32[]{:S(2)}) collective-permute-start(bf16[16,128,128]{2,1,0:T(8,128)(2,1)S(1)} %slice.13), channel_id=1, source_target_pairs={{0,1},{1,0},{2,3},{3,2},{4,5},{5,4},{6,7},{7,6},{8,9},{9,8},{10,11... | collective-permute-start | bytes 1572872 | tf_op jit(solution)/shard_map/ppermute | solution.py:304
  59.3 13.0 %all-to-all-start.2 = ((bf16[16,128,128]{2,1,0:T(8,128)(2,1)}), bf16[16,128,128]{2,1,0:T(8,128)(2,1)S(1)}, u32[]{:S(2)}, u32[]{:S(2)}) async-start(bf16[16,128,128]{2,1,0:T(8,128)(2,1)} %get-tuple-element.25), calls=%async_computation.2 | async-start | bytes 1048576 | tf_op jit(solution)/shard_map/all_to_all | solution.py:373
  62.9 9.4 %collective-permute-start.3 = (bf16[2,128,128]{2,1,0:T(8,128)(2,1)S(1)}, bf16[2,128,128]{2,1,0:T(8,128)(2,1)S(1)}, u32[]{:S(2)}, u32[]{:S(2)}) collective-permute-start(bf16[2,128,128]{2,1,0:T(8,128)(2,1)S(1)} %pad_maximum_fusion), channel_id=1, source_target_pairs={{0,32},{32,64},{64,96},{96,128},{128,160},{160,192},{192,224},{224... | collective-permute-start | bytes 196616 | tf_op jit(solution)/shard_map/ppermute | solution.py:375
  65.6 6.7 %collective-permute-start.4 = (f32[2,16,128]{2,1,0:T(8,128)S(1)}, f32[2,16,128]{2,1,0:T(8,128)S(1)}, u32[]{:S(2)}, u32[]{:S(2)}) collective-permute-start(f32[2,16,128]{2,1,0:T(8,128)S(1)} %get-tuple-element.27.reach), channel_id=1, source_target_pairs={{0,1},{1,0},{2,3},{3,2},{4,5},{5,4},{6,7},{7,6},{8,9},{9,8},{10,11... | collective-permute-start | bytes 49160 | tf_op jit(solution)/shard_map/ppermute | solution.py:304

commit v16 on v15

--- a/solution.py
+++ b/solution.py
@@ -181,13 +181,14 @@
     parts = [five(every, i) for i in range(n)]
     while len(parts) > 1:
         parts = [joined(parts[i], parts[i + 1]) for i in range(0, len(parts), 2)]
-    state = jnp.zeros_like(every[0, :1])
-    reach = state
-    peak = state
-    for i in range(n):
-        reach = jnp.maximum(reach, every[i, 6:7] + jnp.abs(state))
+    reach = every[0, 6:7]
+    peak = every[0, 7:8]
+    spread = jnp.abs(every[0, 1:2])
+    for i in range(1, n):
+        reach = jnp.maximum(reach, every[i, 6:7])
         peak = jnp.maximum(peak, every[i, 7:8])
-        state = every[i, 0:1] * state + every[i, 1:2]
+        spread += jnp.abs(every[i, 1:2])
+    reach += spread
     rows = list(parts[0]) + [every[n - 1, 5:6], reach, peak]
     for r, row in enumerate(rows):
         for i in range(out.shape[0]):
@@ -217,19 +218,11 @@
     return own_state, own_after, own_last, states, afters
 
 
-def finish_body(plane, planes, keep, decay_ref, leak, smoothed_out, resid_out, reach):
+def finish_body(plane, planes, keep, decay_ref, leak, smoothed_out, resid_out):
     at_plane = lax.axis_index(Z)
     at_block = lax.axis_index(YX)
     zero = jnp.zeros((1, decay_ref.shape[1]), F32)
-    entering, after, last, states, afters = ends(planes, at_plane, zero, zero, zero)
-    peaks = [zero]
-    bound = []
-    for i in range(planes.shape[0]):
-        bound.append(6.0 * (planes[i, 6:7] + jnp.abs(states[i])) + 2.0 * jnp.abs(afters[i]))
-        peaks.append(planes[i, 7:8])
-    bound = jnp.concatenate(bound, 0)
-    reach[0] = jnp.broadcast_to(jnp.max(bound, axis=1, keepdims=True), bound.shape)
-    reach[1] = jnp.maximum(jnp.concatenate(peaks[:-1], 0), jnp.concatenate(peaks[1:], 0))
+    entering, after, last, _, _ = ends(planes, at_plane, zero, zero, zero)
     entering, after, last, _, _ = ends(plane, at_block, entering, after, last)
     smoothed = keep[3] + keep[4] * entering + keep[2] * after
     decay = decay_ref[...]
@@ -243,6 +236,19 @@
     smoothed_out[...] = smoothed.T
     for i in range(resid_out.shape[0]):
         resid_out[i] = resid
+
+
+def reach_body(planes, resid, reach):
+    zero = jnp.zeros((1, planes.shape[2]), F32)
+    _, _, _, states, afters = ends(planes, 0, zero, zero, zero)
+    peaks = [zero]
+    bound = []
+    for i in range(planes.shape[0]):
+        bound.append(6.0 * (planes[i, 6:7] + jnp.abs(states[i])) + 2.0 * jnp.abs(afters[i]))
+        peaks.append(planes[i, 7:8])
+    bound = jnp.concatenate(bound, 0)
+    reach[0] = jnp.broadcast_to(jnp.max(bound, axis=1, keepdims=True), bound.shape)
+    reach[1] = jnp.maximum(jnp.concatenate(peaks[:-1], 0), jnp.concatenate(peaks[1:], 0))
 
 
 def bounds(first, second, span):
@@ -361,18 +367,20 @@
     )(mine)
     theirs = swapped(mine[:, :-24])
     every_plane = lax.all_to_all(plane_summary, Z, 0, 0, tiled=True)
-    smoothed, resid, reach = call(
+    smoothed, resid = call(
         finish_body,
         (
             jax.ShapeDtypeStruct((modes, frames), F32),
             jax.ShapeDtypeStruct((blocks, frames, modes), BF16),
-            jax.ShapeDtypeStruct((2, planes, modes), F32),
         ),
         n_in=5,
     )(plane, every_plane, keep, decay, leak_row)
     resid_all = lax.all_to_all(resid, YX, 0, 0, tiled=True)
     tails = behind(jnp.stack([mine[-1, :-24], theirs[-1]]), resid)
     tails = lax.ppermute(tails, Z, [(i, i + 1) for i in range(planes - 1)])
+    reach = call(reach_body, jax.ShapeDtypeStruct((2, planes, modes), F32), whole=(1,), n_in=2)(
+        every_plane, resid
+    )
     reach_other = swapped(reach)
     partial = call(
         gradient_body,

time: 98.8 us -> 98.8 us (level)
  no operation moved by 1% of the time
where the time goes in v16:
time: 98.8 us; the launch traced here: 98.3 us
  starting transfers between devices  43.3 us (44%)
  blocking collectives  38.2 us (39%)
  waiting for transfers between devices  7.86 us (8%)
  Pallas kernels  7.28 us (7%)
    all_to_all x1, blocking collectives, per_device(): pieces = lax.all_to_all(pieces, ('state', Z), 0, 0, tiled=True)  24.1 us
    ppermute x3, starting transfers between devices, swapped(): return lax.ppermute(x, 'state', [(0, 1), (1, 0)])  19.2 us
    all_to_all x1, starting transfers between devices, per_device(): every_plane = lax.all_to_all(plane_summary, Z, 0, 0, tiled=True)  16.5 us
    all_to_all x1, blocking collectives, per_device(): mine = lax.all_to_all(sent, YX, 0, 0, tiled=True)  14.1 us
    all_to_all x1, waiting for transfers between devices, per_device(): every_plane = lax.all_to_all(plane_summary, Z, 0, 0, tiled=True)  7.03 us
    all_to_all x1, starting transfers between devices, per_device(): resid_all = lax.all_to_all(resid, YX, 0, 0, tiled=True)  3.57 us
    ppermute x1, starting transfers between devices, per_device(): tails = lax.ppermute(tails, Z, [(i, i + 1) for i in range(planes - 1)])  2.66 us
  transfers between devices with their start and end apart: 7, of which 2 were waited for; matrix products, arithmetic and copies ran while one was open for 1% of the time, Pallas kernels for 4%

profile of v16, /device:TPU:1, one launch (start us, length us, event | category | flops | bytes accessed | tf_op | source)
XLA Modules:
  0.0 98.3 jit_solution(15308071170206178109)
XLA Ops:
  0.6 8.8 %collective-permute-start = (bf16[128,2048]{1,0:T(8,128)(2,1)}, bf16[128,2048]{1,0:T(8,128)(2,1)S(1)}, u32[]{:S(2)}, u32[]{:S(2)}) collective-permute-start(bf16[128,2048]{1,0:T(8,128)(2,1)} %record.1), channel_id=1, source_target_pairs={{0,1},{1,0},{2,3},{3,2},{4,5},{5,4},{6,7},{7,6},{8,9},{9,8},{10,11... | collective-permute-start | bytes 1572872 | tf_op jit(solution)/shard_map/ppermute | solution.py:310
  9.4 1.9 %shard_map.68 = (f32[128,256]{1,0:T(8,128)S(1)}, bf16[2,128,2048]{2,1,0:T(8,128)(2,1)S(1)}, f32[8,128]{1,0:T(8,128)S(1)}) custom-call(bf16[128,2048]{1,0:T(8,128)(2,1)} %record.1, bf16[2,128,4096]{2,1,0:T(8,128)(2,1)} %gain.1), custom_call_target="tpu_custom_call" | custom-call | tf_op jit(solution)/shard_map/pallas_call | solution.py:323
  11.3 0.0 copy-start.2
  11.3 0.0 copy-start.1
  11.4 0.0 collective-permute-done.other
  11.4 0.1 broadcast_in_dim.4.delays
  11.4 0.7 shard_map.69.onward
  12.2 1.4 %collective-permute-start.1 = (f32[64,128]{1,0:T(8,128)S(1)}, f32[64,128]{1,0:T(8,128)S(1)}, u32[]{:S(2)}, u32[]{:S(2)}) collective-permute-start(f32[64,128]{1,0:T(8,128)S(1)} %shard_map.69.onward), channel_id=1, source_target_pairs={{0,2},{2,4},{4,6},{6,8},{8,10},{10,12},{12,14},{14,16},{16,18},{18... | collective-permute-start | bytes 98312 | tf_op jit(solution)/shard_map/ppermute | solution.py:344
  13.6 0.9 shard_map.70.here
  14.5 0.1 copy.10
  14.6 0.1 sqrt_bitcast_fusion
  14.7 0.3 copy.12
  15.0 0.1 copy.15
  15.1 0.0 collective-permute-done.1.tail
  15.1 0.2 shard_map.71
  15.4 14.1 %all_to_all.20.sent.own = bf16[16,152,128]{2,1,0:T(8,128)(2,1)S(1)} all-to-all(bf16[16,152,128]{2,1,0:T(8,128)(2,1)S(1)} %get-tuple-element.19), channel_id=1, replica_groups=mesh['tm_0'=16,'tm_1'=4,'tm_2'=4,'state'=2] {'tm_1','tm_2'}, dimensions={0} | all-to-all | bytes 1245184 | tf_op jit(solution)/shard_map/all_to_all | solution.py:359
  29.5 0.7 shard_map.72
  30.2 16.5 %all-to-all-start.1 = ((f32[16,8,128]{2,1,0:T(8,128)}), f32[16,8,128]{2,1,0:T(8,128)S(1)}, u32[]{:S(2)}, u32[]{:S(2)}) async-start(f32[16,8,128]{2,1,0:T(8,128)} %get-tuple-element.21), calls=%async_computation.1 | async-start | bytes 131072 | tf_op jit(solution)/shard_map/all_to_all | solution.py:369
  46.8 4.5 %collective-permute-start.2 = (bf16[16,128,128]{2,1,0:T(8,128)(2,1)S(1)}, bf16[16,128,128]{2,1,0:T(8,128)(2,1)S(1)}, u32[]{:S(2)}, u32[]{:S(2)}) collective-permute-start(bf16[16,128,128]{2,1,0:T(8,128)(2,1)S(1)} %slice.13), channel_id=1, source_target_pairs={{0,1},{1,0},{2,3},{3,2},{4,5},{5,4},{6,7},{7,6},{8,9},{9,8},{10,11... | collective-permute-start | bytes 1572872 | tf_op jit(solution)/shard_map/ppermute | solution.py:310
  51.3 7.0 %all-to-all-done.1.planes = f32[16,8,128]{2,1,0:T(8,128)S(1)} async-done(((f32[16,8,128]{2,1,0:T(8,128)}), f32[16,8,128]{2,1,0:T(8,128)S(1)}, u32[]{:S(2)}, u32[]{:S(2)}) %all-to-all-start.1) | async-done | bytes 65568 | tf_op jit(solution)/shard_map/all_to_all | solution.py:369
  58.3 1.0 %shard_map.73 = (f32[128,128]{1,0:T(8,128)}, bf16[16,128,128]{2,1,0:T(8,128)(2,1)}) custom-call(f32[16,8,128]{2,1,0:T(8,128)S(1)} %get-tuple-element.20.plane, f32[16,8,128]{2,1,0:T(8,128)S(1)} %all-to-all-done.1.planes, f32[6,128,128]{2,1,0:T(8,128)S(1)} %get-tuple-element.22.keep, f32[128,128]{1,0:T(8,128)S(1)} %get-tuple-element.27.decay_ref, ...), custom_call_target="tpu_custom_call" | custom-call | tf_op jit(solution)/shard_map/pallas_call | solution.py:370
  59.3 3.6 %all-to-all-start.2 = ((bf16[16,128,128]{2,1,0:T(8,128)(2,1)}), bf16[16,128,128]{2,1,0:T(8,128)(2,1)S(1)}, u32[]{:S(2)}, u32[]{:S(2)}) async-start(bf16[16,128,128]{2,1,0:T(8,128)(2,1)} %get-tuple-element.24.resid), calls=%async_computation.2 | async-start | bytes 1048576 | tf_op jit(solution)/shard_map/all_to_all | solution.py:378
  62.9 0.0 collective-permute-done.2.other
  62.9 2.7 %collective-permute-start.3 = (bf16[2,128,128]{2,1,0:T(8,128)(2,1)S(1)}, bf16[2,128,128]{2,1,0:T(8,128)(2,1)S(1)}, u32[]{:S(2)}, u32[]{:S(2)}) collective-permute-start(bf16[2,128,128]{2,1,0:T(8,128)(2,1)S(1)} %pad_maximum_fusion), channel_id=1, source_target_pairs={{0,32},{32,64},{64,96},{96,128},{128,160},{160,192},{192,224},{224... | collective-permute-start | bytes 196616 | tf_op jit(solution)/shard_map/ppermute | solution.py:380
  65.6 0.2 shard_map.74.reach
  65.7 5.9 %collective-permute-start.4 = (f32[2,16,128]{2,1,0:T(8,128)S(1)}, f32[2,16,128]{2,1,0:T(8,128)S(1)}, u32[]{:S(2)}, u32[]{:S(2)}) collective-permute-start(f32[2,16,128]{2,1,0:T(8,128)S(1)} %shard_map.74.reach), channel_id=1, source_target_pairs={{0,1},{1,0},{2,3},{3,2},{4,5},{5,4},{6,7},{7,6},{8,9},{9,8},{10,11... | collective-permute-start | bytes 49160 | tf_op jit(solution)/shard_map/ppermute | solution.py:310
  71.6 0.8 collective-permute-done.4.reach_other
  72.5 0.0 collective-permute-done.3.tails
  72.5 0.0 all-to-all-done.2.resid
  72.5 1.0 %shard_map.75 = f32[2,16,8,256]{3,2,1,0:T(8,128)S(1)} custom-call(s32[2,256]{1,0:T(2,128)S(1)} %broadcast_in_dim.4.delays, bf16[2,128,128]{2,1,0:T(8,128)(2,1)S(1)} %collective-permute-done.3.tails, bf16[16,152,128]{2,1,0:T(8,128)(2,1)S(1)} %all_to_all.20.sent.own, bf16[16,128,128]{2,1,0:T(8,128)(2,1)S(1)} %collective-permute-done.2.other, ...), custom_call_target="tpu_custom_call" | custom-call | tf_op jit(solution)/shard_map/pallas_call | solution.py:385
  73.5 24.1 %all_to_all.21 = f16[32,8,256]{2,1,0:T(8,128)(2,1)S(1)} all-to-all(f16[32,8,256]{2,1,0:T(8,128)(2,1)S(1)} %bitcast.18), channel_id=1, replica_groups=mesh['tm_0'=16,'tm_1'=4,'tm_2'=4,'state'=2] {'state','tm_0'}, dimensions={0} | all-to-all | bytes 262144 | tf_op jit(solution)/shard_map/all_to_all | solution.py:392
  97.7 0.6 shard_map.76
  (12 shorter events, 0.1 us)
Async XLA Ops:
  0.6 10.7 %copy-start.3 = (s32[2]{0:T(128)S(1)}, s32[2]{0:T(128)}, u32[]{:S(2)}) copy-start(s32[2]{0:T(128)} %param.9) | copy-start | bytes 28
  0.6 10.7 %collective-permute-start = (bf16[128,2048]{1,0:T(8,128)(2,1)}, bf16[128,2048]{1,0:T(8,128)(2,1)S(1)}, u32[]{:S(2)}, u32[]{:S(2)}) collective-permute-start(bf16[128,2048]{1,0:T(8,128)(2,1)} %record.1), channel_id=1, source_target_pairs={{0,1},{1,0},{2,3},{3,2},{4,5},{5,4},{6,7},{7,6},{8,9},{9,8},{10,11... | collective-permute-start | bytes 1572872 | tf_op jit(solution)/shard_map/ppermute | solution.py:310
  11.3 3.2 %copy-start.2 = (f32[128,128]{1,0:T(8,128)S(1)}, f32[128,128]{1,0:T(8,128)}, u32[]{:S(2)}) copy-start(f32[128,128]{1,0:T(8,128)} %param.7) | copy-start | bytes 196612
  11.3 3.3 %copy-start.1 = (bf16[128,2048]{1,0:T(8,128)(2,1)S(1)}, bf16[128,2048]{1,0:T(8,128)(2,1)}, u32[]{:S(2)}) copy-start(bf16[128,2048]{1,0:T(8,128)(2,1)} %record.1) | copy-start | bytes 1572868
  12.2 2.9 %copy-start = (f32[128]{0:T(128)S(1)}, f32[128]{0:T(128)}, u32[]{:S(2)}) copy-start(f32[128]{0:T(128)} %param.8) | copy-start | bytes 1540
  12.2 2.9 %collective-permute-start.1 = (f32[64,128]{1,0:T(8,128)S(1)}, f32[64,128]{1,0:T(8,128)S(1)}, u32[]{:S(2)}, u32[]{:S(2)}) collective-permute-start(f32[64,128]{1,0:T(8,128)S(1)} %shard_map.69.onward), channel_id=1, source_target_pairs={{0,2},{2,4},{4,6},{6,8},{8,10},{10,12},{12,14},{14,16},{16,18},{18... | collective-permute-start | bytes 98312 | tf_op jit(solution)/shard_map/ppermute | solution.py:344
  30.2 28.1 %all-to-all-start.1 = ((f32[16,8,128]{2,1,0:T(8,128)}), f32[16,8,128]{2,1,0:T(8,128)S(1)}, u32[]{:S(2)}, u32[]{:S(2)}) async-start(f32[16,8,128]{2,1,0:T(8,128)} %get-tuple-element.21), calls=%async_computation.1 | async-start | bytes 131072 | tf_op jit(solution)/shard_map/all_to_all | solution.py:369
  46.8 16.1 %collective-permute-start.2 = (bf16[16,128,128]{2,1,0:T(8,128)(2,1)S(1)}, bf16[16,128,128]{2,1,0:T(8,128)(2,1)S(1)}, u32[]{:S(2)}, u32[]{:S(2)}) collective-permute-start(bf16[16,128,128]{2,1,0:T(8,128)(2,1)S(1)} %slice.13), channel_id=1, source_target_pairs={{0,1},{1,0},{2,3},{3,2},{4,5},{5,4},{6,7},{7,6},{8,9},{9,8},{10,11... | collective-permute-start | bytes 1572872 | tf_op jit(solution)/shard_map/ppermute | solution.py:310
  59.3 13.2 %all-to-all-start.2 = ((bf16[16,128,128]{2,1,0:T(8,128)(2,1)}), bf16[16,128,128]{2,1,0:T(8,128)(2,1)S(1)}, u32[]{:S(2)}, u32[]{:S(2)}) async-start(bf16[16,128,128]{2,1,0:T(8,128)(2,1)} %get-tuple-element.24.resid), calls=%async_computation.2 | async-start | bytes 1048576 | tf_op jit(solution)/shard_map/all_to_all | solution.py:378
  62.9 9.6 %collective-permute-start.3 = (bf16[2,128,128]{2,1,0:T(8,128)(2,1)S(1)}, bf16[2,128,128]{2,1,0:T(8,128)(2,1)S(1)}, u32[]{:S(2)}, u32[]{:S(2)}) collective-permute-start(bf16[2,128,128]{2,1,0:T(8,128)(2,1)S(1)} %pad_maximum_fusion), channel_id=1, source_target_pairs={{0,32},{32,64},{64,96},{96,128},{128,160},{160,192},{192,224},{224... | collective-permute-start | bytes 196616 | tf_op jit(solution)/shard_map/ppermute | solution.py:380
  65.7 6.7 %collective-permute-start.4 = (f32[2,16,128]{2,1,0:T(8,128)S(1)}, f32[2,16,128]{2,1,0:T(8,128)S(1)}, u32[]{:S(2)}, u32[]{:S(2)}) collective-permute-start(f32[2,16,128]{2,1,0:T(8,128)S(1)} %shard_map.74.reach), channel_id=1, source_target_pairs={{0,1},{1,0},{2,3},{3,2},{4,5},{5,4},{6,7},{7,6},{8,9},{9,8},{10,11... | collective-permute-start | bytes 49160 | tf_op jit(solution)/shard_map/ppermute | solution.py:310

commit v17 on v15

--- a/solution.py
+++ b/solution.py
@@ -102,10 +102,14 @@
     shape = (rows, values.shape[0])
     row = lax.broadcasted_iota(jnp.int32, shape, 0)
     column = lax.broadcasted_iota(jnp.int32, shape, 1)
-    pick = (column + delay[:, : shape[1]] == row + ahead).astype(F32)
-    return jnp.dot(
-        pick, values, precision=lax.Precision.HIGHEST, preferred_element_type=F32
-    )
+    pick = (column + delay[:, : shape[1]] == row + ahead).astype(F32).astype(BF16)
+    parts = []
+    for _ in range(3):
+        parts.append(values.astype(BF16))
+        values = values - parts[-1].astype(F32)
+    sums = jnp.dot(pick, jnp.concatenate(parts, 1), preferred_element_type=F32)
+    wide = values.shape[1]
+    return sums[:, :wide] + sums[:, wide : 2 * wide] + sums[:, 2 * wide :]
 
 
 def onward_body(delays, other, gain, part, out):

time: 98.8 us -> 98.6 us (level)
  no operation moved by 1% of the time
where the time goes in v17:
time: 98.6 us; the launch traced here: 98.1 us
  starting transfers between devices  43.2 us (44%)
  blocking collectives  38.5 us (39%)
  waiting for transfers between devices  7.86 us (8%)
  Pallas kernels  6.88 us (7%)
    all_to_all x1, blocking collectives, per_device(): pieces = lax.all_to_all(pieces, ('state', Z), 0, 0, tiled=True)  24.3 us
    ppermute x3, starting transfers between devices, swapped(): return lax.ppermute(x, 'state', [(0, 1), (1, 0)])  19.2 us
    all_to_all x1, starting transfers between devices, per_device(): every_plane = lax.all_to_all(plane_summary, Z, 0, 0, tiled=True)  16.5 us
    all_to_all x1, blocking collectives, per_device(): mine = lax.all_to_all(sent, YX, 0, 0, tiled=True)  14.3 us
    all_to_all x1, waiting for transfers between devices, per_device(): every_plane = lax.all_to_all(plane_summary, Z, 0, 0, tiled=True)  7.03 us
    all_to_all x1, starting transfers between devices, per_device(): resid_all = lax.all_to_all(resid, YX, 0, 0, tiled=True)  3.57 us
    ppermute x1, starting transfers between devices, per_device(): tails = lax.ppermute(tails, Z, [(i, i + 1) for i in range(planes - 1)])  2.66 us
  transfers between devices with their start and end apart: 7, of which 2 were waited for; matrix products, arithmetic and copies ran while one was open for 1% of the time, Pallas kernels for 4%

profile of v17, /device:TPU:1, one launch (start us, length us, event | category | flops | bytes accessed | tf_op | source)
XLA Modules:
  0.0 98.1 jit_solution(17412682944682067886)
XLA Ops:
  0.6 8.8 %collective-permute-start = (bf16[128,2048]{1,0:T(8,128)(2,1)}, bf16[128,2048]{1,0:T(8,128)(2,1)S(1)}, u32[]{:S(2)}, u32[]{:S(2)}) collective-permute-start(bf16[128,2048]{1,0:T(8,128)(2,1)} %record.1), channel_id=1, source_target_pairs={{0,1},{1,0},{2,3},{3,2},{4,5},{5,4},{6,7},{7,6},{8,9},{9,8},{10,11... | collective-permute-start | bytes 1572872 | tf_op jit(solution)/shard_map/ppermute | solution.py:308
  9.4 1.9 %shard_map.68 = (f32[128,256]{1,0:T(8,128)S(1)}, bf16[2,128,2048]{2,1,0:T(8,128)(2,1)S(1)}, f32[8,128]{1,0:T(8,128)S(1)}) custom-call(bf16[128,2048]{1,0:T(8,128)(2,1)} %record.1, bf16[2,128,4096]{2,1,0:T(8,128)(2,1)} %gain.1), custom_call_target="tpu_custom_call" | custom-call | tf_op jit(solution)/shard_map/pallas_call | solution.py:321
  11.3 0.0 copy-start.2
  11.3 0.0 copy-start.1
  11.4 0.0 collective-permute-done.other
  11.4 0.1 broadcast_in_dim.4.delays
  11.4 0.6 shard_map.69.onward
  12.1 0.0 copy-start
  12.1 1.3 %collective-permute-start.1 = (f32[64,128]{1,0:T(8,128)S(1)}, f32[64,128]{1,0:T(8,128)S(1)}, u32[]{:S(2)}, u32[]{:S(2)}) collective-permute-start(f32[64,128]{1,0:T(8,128)S(1)} %shard_map.69.onward), channel_id=1, source_target_pairs={{0,2},{2,4},{4,6},{6,8},{8,10},{10,12},{12,14},{14,16},{16,18},{18... | collective-permute-start | bytes 98312 | tf_op jit(solution)/shard_map/ppermute | solution.py:342
  13.4 0.8 shard_map.70.here
  14.1 0.1 copy.10
  14.2 0.1 sqrt_bitcast_fusion
  14.3 0.3 copy.12
  14.6 0.1 copy.15
  14.7 0.0 collective-permute-done.1.tail
  14.8 0.2 shard_map.71
  15.0 14.3 %all_to_all.20.sent.own = bf16[16,152,128]{2,1,0:T(8,128)(2,1)S(1)} all-to-all(bf16[16,152,128]{2,1,0:T(8,128)(2,1)S(1)} %get-tuple-element.20), channel_id=1, replica_groups=mesh['tm_0'=16,'tm_1'=4,'tm_2'=4,'state'=2] {'tm_1','tm_2'}, dimensions={0} | all-to-all | bytes 1245184 | tf_op jit(solution)/shard_map/all_to_all | solution.py:357
  29.3 0.7 shard_map.72
  30.0 16.5 %all-to-all-start.1 = ((f32[16,8,128]{2,1,0:T(8,128)}), f32[16,8,128]{2,1,0:T(8,128)S(1)}, u32[]{:S(2)}, u32[]{:S(2)}) async-start(f32[16,8,128]{2,1,0:T(8,128)} %get-tuple-element.22), calls=%async_computation.1 | async-start | bytes 131072 | tf_op jit(solution)/shard_map/all_to_all | solution.py:367
  46.6 4.5 %collective-permute-start.2 = (bf16[16,128,128]{2,1,0:T(8,128)(2,1)S(1)}, bf16[16,128,128]{2,1,0:T(8,128)(2,1)S(1)}, u32[]{:S(2)}, u32[]{:S(2)}) collective-permute-start(bf16[16,128,128]{2,1,0:T(8,128)(2,1)S(1)} %slice.13), channel_id=1, source_target_pairs={{0,1},{1,0},{2,3},{3,2},{4,5},{5,4},{6,7},{7,6},{8,9},{9,8},{10,11... | collective-permute-start | bytes 1572872 | tf_op jit(solution)/shard_map/ppermute | solution.py:308
  51.0 7.0 %all-to-all-done.1.planes = f32[16,8,128]{2,1,0:T(8,128)S(1)} async-done(((f32[16,8,128]{2,1,0:T(8,128)}), f32[16,8,128]{2,1,0:T(8,128)S(1)}, u32[]{:S(2)}, u32[]{:S(2)}) %all-to-all-start.1) | async-done | bytes 65568 | tf_op jit(solution)/shard_map/all_to_all | solution.py:367
  58.1 1.0 %shard_map.73 = (f32[128,128]{1,0:T(8,128)}, bf16[16,128,128]{2,1,0:T(8,128)(2,1)}, f32[2,16,128]{2,1,0:T(8,128)S(1)}) custom-call(f32[16,8,128]{2,1,0:T(8,128)S(1)} %get-tuple-element.21.plane, f32[16,8,128]{2,1,0:T(8,128)S(1)} %all-to-all-done.1.planes, f32[6,128,128]{2,1,0:T(8,128)S(1)} %get-tuple-element.23.keep, ...), custom_call_target="tpu_custom_call" | custom-call | tf_op jit(solution)/shard_map/pallas_call | solution.py:368
  59.1 3.6 %all-to-all-start.2 = ((bf16[16,128,128]{2,1,0:T(8,128)(2,1)}), bf16[16,128,128]{2,1,0:T(8,128)(2,1)S(1)}, u32[]{:S(2)}, u32[]{:S(2)}) async-start(bf16[16,128,128]{2,1,0:T(8,128)(2,1)} %get-tuple-element.25), calls=%async_computation.2 | async-start | bytes 1048576 | tf_op jit(solution)/shard_map/all_to_all | solution.py:377
  62.7 0.0 collective-permute-done.2.other
  62.7 2.7 %collective-permute-start.3 = (bf16[2,128,128]{2,1,0:T(8,128)(2,1)S(1)}, bf16[2,128,128]{2,1,0:T(8,128)(2,1)S(1)}, u32[]{:S(2)}, u32[]{:S(2)}) collective-permute-start(bf16[2,128,128]{2,1,0:T(8,128)(2,1)S(1)} %pad_maximum_fusion), channel_id=1, source_target_pairs={{0,32},{32,64},{64,96},{96,128},{128,160},{160,192},{192,224},{224... | collective-permute-start | bytes 196616 | tf_op jit(solution)/shard_map/ppermute | solution.py:379
  65.4 5.9 %collective-permute-start.4 = (f32[2,16,128]{2,1,0:T(8,128)S(1)}, f32[2,16,128]{2,1,0:T(8,128)S(1)}, u32[]{:S(2)}, u32[]{:S(2)}) collective-permute-start(f32[2,16,128]{2,1,0:T(8,128)S(1)} %get-tuple-element.27.reach), channel_id=1, source_target_pairs={{0,1},{1,0},{2,3},{3,2},{4,5},{5,4},{6,7},{7,6},{8,9},{9,8},{10,11... | collective-permute-start | bytes 49160 | tf_op jit(solution)/shard_map/ppermute | solution.py:308
  71.3 0.8 collective-permute-done.4.reach_other
  72.1 0.0 collective-permute-done.3.tails
  72.1 0.0 all-to-all-done.2.resid
  72.1 1.0 %shard_map.74 = f32[2,16,8,256]{3,2,1,0:T(8,128)S(1)} custom-call(s32[2,256]{1,0:T(2,128)S(1)} %broadcast_in_dim.4.delays, bf16[2,128,128]{2,1,0:T(8,128)(2,1)S(1)} %collective-permute-done.3.tails, bf16[16,152,128]{2,1,0:T(8,128)(2,1)S(1)} %all_to_all.20.sent.own, bf16[16,128,128]{2,1,0:T(8,128)(2,1)S(1)} %collective-permute-done.2.other, ...), custom_call_target="tpu_custom_call" | custom-call | tf_op jit(solution)/shard_map/pallas_call | solution.py:381
  73.2 24.3 %all_to_all.21 = f16[32,8,256]{2,1,0:T(8,128)(2,1)S(1)} all-to-all(f16[32,8,256]{2,1,0:T(8,128)(2,1)S(1)} %bitcast.18), channel_id=1, replica_groups=mesh['tm_0'=16,'tm_1'=4,'tm_2'=4,'state'=2] {'state','tm_0'}, dimensions={0} | all-to-all | bytes 262144 | tf_op jit(solution)/shard_map/all_to_all | solution.py:388
  97.5 0.6 shard_map.75
  (11 shorter events, 0.1 us)
Async XLA Ops:
  0.6 10.7 %copy-start.3 = (s32[2]{0:T(128)S(1)}, s32[2]{0:T(128)}, u32[]{:S(2)}) copy-start(s32[2]{0:T(128)} %param.9) | copy-start | bytes 28
  0.6 10.7 %collective-permute-start = (bf16[128,2048]{1,0:T(8,128)(2,1)}, bf16[128,2048]{1,0:T(8,128)(2,1)S(1)}, u32[]{:S(2)}, u32[]{:S(2)}) collective-permute-start(bf16[128,2048]{1,0:T(8,128)(2,1)} %record.1), channel_id=1, source_target_pairs={{0,1},{1,0},{2,3},{3,2},{4,5},{5,4},{6,7},{7,6},{8,9},{9,8},{10,11... | collective-permute-start | bytes 1572872 | tf_op jit(solution)/shard_map/ppermute | solution.py:308
  11.3 2.8 %copy-start.2 = (f32[128,128]{1,0:T(8,128)S(1)}, f32[128,128]{1,0:T(8,128)}, u32[]{:S(2)}) copy-start(f32[128,128]{1,0:T(8,128)} %param.7) | copy-start | bytes 196612
  11.3 3.0 %copy-start.1 = (bf16[128,2048]{1,0:T(8,128)(2,1)S(1)}, bf16[128,2048]{1,0:T(8,128)(2,1)}, u32[]{:S(2)}) copy-start(bf16[128,2048]{1,0:T(8,128)(2,1)} %record.1) | copy-start | bytes 1572868
  12.1 2.7 %copy-start = (f32[128]{0:T(128)S(1)}, f32[128]{0:T(128)}, u32[]{:S(2)}) copy-start(f32[128]{0:T(128)} %param.8) | copy-start | bytes 1540
  12.1 2.7 %collective-permute-start.1 = (f32[64,128]{1,0:T(8,128)S(1)}, f32[64,128]{1,0:T(8,128)S(1)}, u32[]{:S(2)}, u32[]{:S(2)}) collective-permute-start(f32[64,128]{1,0:T(8,128)S(1)} %shard_map.69.onward), channel_id=1, source_target_pairs={{0,2},{2,4},{4,6},{6,8},{8,10},{10,12},{12,14},{14,16},{16,18},{18... | collective-permute-start | bytes 98312 | tf_op jit(solution)/shard_map/ppermute | solution.py:342
  30.0 28.1 %all-to-all-start.1 = ((f32[16,8,128]{2,1,0:T(8,128)}), f32[16,8,128]{2,1,0:T(8,128)S(1)}, u32[]{:S(2)}, u32[]{:S(2)}) async-start(f32[16,8,128]{2,1,0:T(8,128)} %get-tuple-element.22), calls=%async_computation.1 | async-start | bytes 131072 | tf_op jit(solution)/shard_map/all_to_all | solution.py:367
  46.6 16.1 %collective-permute-start.2 = (bf16[16,128,128]{2,1,0:T(8,128)(2,1)S(1)}, bf16[16,128,128]{2,1,0:T(8,128)(2,1)S(1)}, u32[]{:S(2)}, u32[]{:S(2)}) collective-permute-start(bf16[16,128,128]{2,1,0:T(8,128)(2,1)S(1)} %slice.13), channel_id=1, source_target_pairs={{0,1},{1,0},{2,3},{3,2},{4,5},{5,4},{6,7},{7,6},{8,9},{9,8},{10,11... | collective-permute-start | bytes 1572872 | tf_op jit(solution)/shard_map/ppermute | solution.py:308
  59.1 13.0 %all-to-all-start.2 = ((bf16[16,128,128]{2,1,0:T(8,128)(2,1)}), bf16[16,128,128]{2,1,0:T(8,128)(2,1)S(1)}, u32[]{:S(2)}, u32[]{:S(2)}) async-start(bf16[16,128,128]{2,1,0:T(8,128)(2,1)} %get-tuple-element.25), calls=%async_computation.2 | async-start | bytes 1048576 | tf_op jit(solution)/shard_map/all_to_all | solution.py:377
  62.7 9.4 %collective-permute-start.3 = (bf16[2,128,128]{2,1,0:T(8,128)(2,1)S(1)}, bf16[2,128,128]{2,1,0:T(8,128)(2,1)S(1)}, u32[]{:S(2)}, u32[]{:S(2)}) collective-permute-start(bf16[2,128,128]{2,1,0:T(8,128)(2,1)S(1)} %pad_maximum_fusion), channel_id=1, source_target_pairs={{0,32},{32,64},{64,96},{96,128},{128,160},{160,192},{192,224},{224... | collective-permute-start | bytes 196616 | tf_op jit(solution)/shard_map/ppermute | solution.py:379
  65.4 6.7 %collective-permute-start.4 = (f32[2,16,128]{2,1,0:T(8,128)S(1)}, f32[2,16,128]{2,1,0:T(8,128)S(1)}, u32[]{:S(2)}, u32[]{:S(2)}) collective-permute-start(f32[2,16,128]{2,1,0:T(8,128)S(1)} %get-tuple-element.27.reach), channel_id=1, source_target_pairs={{0,1},{1,0},{2,3},{3,2},{4,5},{5,4},{6,7},{7,6},{8,9},{9,8},{10,11... | collective-permute-start | bytes 49160 | tf_op jit(solution)/shard_map/ppermute | solution.py:308
